TPU v7x, 32 devices: a whole 2x2x4 slice. The times are simulated.
32 devices in a mesh: shot: 4 (over y, x), sub: 8 (over z, core).
Axes of the slice: x: 2, y: 2, z: 4, core: 2. Of those that a mesh axis runs over, the one named last changes fastest.
Arguments:
- vel_model: bfloat16 [4, 32, 320, 128], P('shot', 'sub'), may hold values from 0.5 to 1
- den_model: bfloat16 [4, 32, 320, 128], P('shot', 'sub'), may hold values from 1 to 4
- cover: int32 [4, 8], replicated, may hold values from 0 to 3
- receivers: int32 [4, 512], P('shot'), may hold values from 0 to 1310719
- observed: float32 [4, 4, 512], P('shot'), may hold values from -6 to 6
- p_now: float32 [4, 32, 320, 128], P('shot', 'sub'), may hold values from -6 to 6
- p_before: float32 [4, 32, 320, 128], P('shot', 'sub'), may hold values from -6 to 6
- q_now: float32 [4, 32, 320, 128], P('shot', 'sub'), may hold values from -6 to 6
- q_before: float32 [4, 32, 320, 128], P('shot', 'sub'), may hold values from -6 to 6
Outputs:
- grad_vel: float32 [4, 32, 320, 128], P('shot', 'sub')
- grad_den: float32 [4, 32, 320, 128], P('shot', 'sub')
All inputs are finite; a program needn't handle non-finite values.
Results may differ from a plain program's by a relative error of at most 0.011.
Values may be sent and summed in bfloat16 or wider, within the bound.
No kernel may reach another device: no remote copies, remote signals or barrier semaphores. Data moves between devices by JAX's collectives and lax.ppermute only.
A program may use at most 64 MiB of HBM per device.

v0:
```python
import jax
import jax.numpy as jnp
from jax import lax
from jax.sharding import PartitionSpec as P

ITERS = 4


SECOND = (-205.0 / 72.0, 8.0 / 5.0, -1.0 / 5.0, 8.0 / 315.0, -1.0 / 560.0)
FIRST = (4.0 / 5.0, -1.0 / 5.0, 4.0 / 105.0, -1.0 / 280.0)
SPEED = 0.15


def padded_2(cells, sides, width):
    for axis, dim in sides:
        count = lax.axis_size(axis)
        ends = count - 1
        head = lax.slice_in_dim(cells, 0, width, axis=dim)
        tail = lax.slice_in_dim(cells, cells.shape[dim] - width, cells.shape[dim], axis=dim)
        cells = jnp.concatenate(
            [
                lax.ppermute(tail, axis, [(i, (i + 1) % count) for i in range(ends)]),
                cells,
                lax.ppermute(head, axis, [((i + 1) % count, i) for i in range(ends)]),
            ],
            axis=dim,
        )
    return cells


def moved(padded, direction, offset):
    window = [
        slice(4, padded.shape[0] - 4),
        slice(4, padded.shape[1] - 4),
        slice(4, padded.shape[2] - 4),
    ]
    window[direction] = slice(4 + offset, padded.shape[direction] - 4 + offset)
    return padded[tuple(window)]


def stencil(padded):
    center = moved(padded, 0, 0)
    laplace = 3.0 * SECOND[0] * center
    first_diffs = []
    for direction in range(3):
        slope_sum = jnp.zeros_like(center)
        for distance in range(1, 5):
            above_part = moved(padded, direction, distance)
            below_part = moved(padded, direction, -distance)
            laplace = laplace + SECOND[distance] * (above_part + below_part)
            slope_sum = slope_sum + FIRST[distance - 1] * (above_part - below_part)
        first_diffs.append(slope_sum)
    return (laplace, first_diffs)


def operate(laplace, first_diffs, slopes):
    return laplace - (
        slopes[0] * first_diffs[0] + slopes[1] * first_diffs[1] + slopes[2] * first_diffs[2]
    )


def side_pad(wide):
    return jnp.pad(wide, ((0, 0), (4, 4), (4, 4)))


def body(vel_model, den_model, cover, receivers, observed, p_now, p_before, q_now, q_before):
    shot_index = lax.axis_index("shot")
    column = lax.axis_index("sub")
    groups = lax.axis_size("shot")
    wanted = cover[shot_index, column]
    owners = cover[:, column]
    mine = (owners == shot_index)[:, None, None, None]
    send_vel = jnp.where(mine, vel_model, jnp.zeros_like(vel_model))
    send_den = jnp.where(mine, den_model, jnp.zeros_like(den_model))
    got_vel, got_den = (
        lax.all_to_all(send_vel, "shot", split_axis=0, concat_axis=0, tiled=True),
        lax.all_to_all(send_den, "shot", split_axis=0, concat_axis=0, tiled=True),
    )
    vel_tile = jnp.sum(got_vel, axis=0)
    den_tile = jnp.sum(got_den, axis=0)
    velocity = vel_tile.astype(jnp.float32)
    density = den_tile.astype(jnp.float32)
    log_den = jnp.log(density)
    wide_log = padded_2(log_den.astype(jnp.bfloat16), (("sub", 0),), 4).astype(log_den.dtype)
    unused_lap, slopes = stencil(side_pad(wide_log))
    scale = SPEED * velocity * velocity
    shape = velocity.shape
    cells = velocity.size
    local_cell = receivers[0] - column * cells
    valid = (local_cell >= 0) & (local_cell < cells)
    station = jnp.where(valid, local_cell, 0)

    def field_terms(field):
        wide = padded_2(field.astype(jnp.bfloat16), (("sub", 0),), 4).astype(field.dtype)
        laplace, diffs = stencil(side_pad(wide))
        return (operate(laplace, diffs, slopes), diffs)

    stored = []
    misfits = []
    previous, current = (p_before[0], p_now[0])
    for time_step in range(ITERS):
        applied, diffs = field_terms(current)
        stored.append((applied, diffs))
        previous, current = (current, 2.0 * current - previous + scale * applied)
        sampled = current.reshape(-1)[station]
        misfits.append(jnp.where(valid, sampled - observed[0, time_step], 0.0))
    sum_vel = jnp.zeros(shape, jnp.float32)
    sum_den = jnp.zeros(shape, jnp.float32)
    previous, current = (q_before[0], q_now[0])
    for time_step in range(ITERS):
        source = (
            jnp.zeros((cells,), jnp.float32)
            .at[station]
            .add(misfits[ITERS - 1 - time_step])
            .reshape(shape)
        )
        adjoint = current + source
        applied, diffs = field_terms(adjoint)
        forward_applied, forward_diffs = stored[ITERS - 1 - time_step]
        sum_vel = sum_vel + adjoint * forward_applied
        sum_den = sum_den + (
            diffs[0] * forward_diffs[0] + diffs[1] * forward_diffs[1] + diffs[2] * forward_diffs[2]
        )
        previous, current = (current, 2.0 * adjoint - previous + scale * applied)
    shot_vel = (2.0 * SPEED * velocity * sum_vel).astype(jnp.bfloat16)
    shot_den = (scale / density * sum_den).astype(jnp.bfloat16)
    targets = (jnp.arange(groups, dtype=jnp.int32) == wanted)[:, None, None, None]
    exact_vel = lax.optimization_barrier(shot_vel).astype(jnp.float32)
    exact_den = lax.optimization_barrier(shot_den).astype(jnp.float32)
    term_vel = jnp.where(targets, exact_vel[None], 0.0)
    term_den = jnp.where(targets, exact_den[None], 0.0)
    summed_vel, summed_den = (
        lax.psum_scatter(
            term_vel.astype(jnp.bfloat16), "shot", scatter_dimension=0, tiled=True
        ).astype(jnp.float32),
        lax.psum_scatter(
            term_den.astype(jnp.bfloat16), "shot", scatter_dimension=0, tiled=True
        ).astype(jnp.float32),
    )
    return (summed_vel, summed_den)


def solution(mesh):
    return jax.shard_map(
        body,
        mesh=mesh,
        in_specs=(
            P("shot", "sub", None, None),
            P("shot", "sub", None, None),
            P(),
            P("shot", None),
            P("shot", None, None),
            P("shot", "sub", None, None),
            P("shot", "sub", None, None),
            P("shot", "sub", None, None),
            P("shot", "sub", None, None),
        ),
        out_specs=(P("shot", "sub", None, None), P("shot", "sub", None, None)),
        check_vma=False,
    )
```

profile of v0, /device:TPU:0, one launch (start us, length us, event | category | flops | bytes accessed | tf_op | source)
XLA Modules:
  0.0 290.7 jit_solution(530717518243873821)
XLA Ops:
  8.0 2.4 broadcast_select_fusion
  10.4 21.9 %all_to_all.10 = bf16[4,4,320,128]{3,2,1,0:T(8,128)(2,1)S(1)} all-to-all(bf16[4,4,320,128]{3,2,1,0:T(8,128)(2,1)S(1)} %get-tuple-element.53), channel_id=1, replica_groups=mesh['shot'=4,'sub'=8] {'shot'}, dimensions={0} | all-to-all | bytes 2621440 | tf_op jit(solution)/shard_map/all_to_all | solution.py:77
  32.4 4.4 %all-to-all-start = ((bf16[4,4,320,128]{3,2,1,0:T(8,128)(2,1)}), bf16[4,4,320,128]{3,2,1,0:T(8,128)(2,1)}, u32[]{:S(2)}, u32[]{:S(2)}) async-start(bf16[4,4,320,128]{3,2,1,0:T(8,128)(2,1)} %get-tuple-element.54), calls=%async_computation | async-start | bytes 2621440 | tf_op jit(solution)/shard_map/all_to_all | solution.py:76
  36.9 1.3 collective-permute-start.1
  38.2 3.8 %collective-permute-start = (bf16[4,320,128]{2,1,0:T(8,128)(2,1)S(1)}, bf16[4,320,128]{2,1,0:T(8,128)(2,1)}, u32[]{:S(2)}, u32[]{:S(2)}) collective-permute-start(bf16[4,320,128]{2,1,0:T(8,128)(2,1)S(1)} %bitcast_convert_fusion), channel_id=1, source_target_pairs={{0,1},{1,2},{2,3},{3,4},{4,5},{5,6},{6,7},{8,9},{9,10},{10,11},{11... | collective-permute-start | bytes 983048 | tf_op jit(solution)/shard_map/ppermute | solution.py:22
  42.4 1.3 collective-permute-start.3
  43.7 3.8 %collective-permute-start.2 = (bf16[4,320,128]{2,1,0:T(8,128)(2,1)S(1)}, bf16[4,320,128]{2,1,0:T(8,128)(2,1)}, u32[]{:S(2)}, u32[]{:S(2)}) collective-permute-start(bf16[4,320,128]{2,1,0:T(8,128)(2,1)S(1)} %fusion.18), channel_id=1, source_target_pairs={{0,1},{1,2},{2,3},{3,4},{4,5},{5,6},{6,7},{8,9},{9,10},{10,11},{11... | collective-permute-start | bytes 983048 | tf_op jit(solution)/shard_map/ppermute | solution.py:22
  49.4 2.7 all-to-all-done
  52.1 1.6 reduce_sum.24
  54.9 6.7 %fusion.198 = (bf16[4,320,128]{2,1,0:T(8,128)(2,1)}, f32[4,320,128]{2,1,0:T(8,128)}, f32[4,320,128]{2,1,0:T(8,128)}, f32[4,320,128]{2,1,0:T(8,128)}, f32[4,320,1...) fusion(bf16[4,320,128]{2,1,0:T(8,128)(2,1)S(1)} %reduce_sum.24,, ...), kind=kLoop, calls=%fused_computation.413 | loop fusion | flops 19169280 | bytes 22282240 | tf_op jit(solution)/shard_map/convert_element_type | solution.py:94
  61.6 1.4 collective-permute-start.5
  63.0 3.8 %collective-permute-start.4 = (bf16[4,320,128]{2,1,0:T(8,128)(2,1)}, bf16[4,320,128]{2,1,0:T(8,128)(2,1)}, u32[]{:S(2)}, u32[]{:S(2)}) collective-permute-start(bf16[4,320,128]{2,1,0:T(8,128)(2,1)} %get-tuple-element.34), channel_id=1, source_target_pairs={{0,1},{1,2},{2,3},{3,4},{4,5},{5,6},{6,7},{8,9},{9,10},{10,11},{11... | collective-permute-start | bytes 983048 | tf_op jit(solution)/shard_map/ppermute | solution.py:22
  67.6 1.3 maximum_convert_fusion.2
  69.0 3.9 %fusion.195 = (bf16[4,320,128]{2,1,0:T(8,128)(2,1)S(1)}, f32[4,320,128]{2,1,0:T(8,128)S(1)}, f32[4,320,128]{2,1,0:T(8,128)}, f32[4,320,128]{2,1,0:T(8,128)}, f32[4,320,128]{2,1,0:T(8,128)}, /*index=5*/f32[4,320,128]{2,1,0:T(8,128)}) fusion(bf16[4,320,128]{2,1,0:T(8,128)(2,1)S(1)} %reduce_sum.24, f32[1,4,320,128]{3,2,1,0:T(8,128)S(1)} %copy-done.15, ...), kind=kLoop, calls=%fused_computation.412 | loop fusion | flops 13762560 | bytes 15073280 | tf_op jit(solution)/shard_map/convert_element_type | solution.py:94
  72.9 1.3 collective-permute-start.7
  74.2 6.5 %collective-permute-start.6 = (bf16[4,320,128]{2,1,0:T(8,128)(2,1)S(1)}, bf16[4,320,128]{2,1,0:T(8,128)(2,1)S(1)}, u32[]{:S(2)}, u32[]{:S(2)}) collective-permute-start(bf16[4,320,128]{2,1,0:T(8,128)(2,1)S(1)} %get-tuple-element.28), channel_id=1, source_target_pairs={{0,1},{1,2},{2,3},{3,4},{4,5},{5,6},{6,7},{8,9},{9,10},{10,11},{11... | collective-permute-start | bytes 983048 | tf_op jit(solution)/shard_map/ppermute | solution.py:22
  82.1 4.1 %fusion.192 = (bf16[4,320,128]{2,1,0:T(8,128)(2,1)}, f32[4,320,128]{2,1,0:T(8,128)}, f32[4,320,128]{2,1,0:T(8,128)}, f32[4,320,128]{2,1,0:T(8,128)}, f32[4,320,128]{2,1,0:T(8,128)}, /*index=5*/f32[4,320,128]{2,1,0:T(8,128)}) fusion(bf16[4,320,128]{2,1,0:T(8,128)(2,1)S(1)} %reduce_sum.24, f32[4,320,128]{2,1,0:T(8,128)S(1)} %copy-done.2, ...), kind=kLoop, calls=%fused_computation.411 | loop fusion | flops 13762560 | bytes 15073280 | tf_op jit(solution)/shard_map/convert_element_type | solution.py:94
  86.2 1.3 collective-permute-start.9
  87.4 8.5 %collective-permute-start.8 = (bf16[4,320,128]{2,1,0:T(8,128)(2,1)}, bf16[4,320,128]{2,1,0:T(8,128)(2,1)}, u32[]{:S(2)}, u32[]{:S(2)}) collective-permute-start(bf16[4,320,128]{2,1,0:T(8,128)(2,1)} %get-tuple-element.22), channel_id=1, source_target_pairs={{0,1},{1,2},{2,3},{3,4},{4,5},{5,6},{6,7},{8,9},{9,10},{10,11},{11... | collective-permute-start | bytes 983048 | tf_op jit(solution)/shard_map/ppermute | solution.py:22
  96.0 3.1 %gather_fusion.3 = f32[512]{0:T(512)S(1)} fusion(f32[163840]{0:T(1024)S(1)} %bitcast.52, s32[1024]{0:T(1024)S(1)} %pad_clamp_fusion), kind=kCustom, calls=%fused_computation.3 | custom fusion | bytes 6144 | tf_op jit(solution)/shard_map/gather | solution.py:105
  99.2 18.5 %gather_fusion.2 = f32[512]{0:T(512)S(1)} fusion(f32[163840]{0:T(1024)} %bitcast.53, s32[1024]{0:T(1024)S(1)} %pad_clamp_fusion), kind=kCustom, calls=%fused_computation.2 | custom fusion | bytes 6144 | tf_op jit(solution)/shard_map/gather | solution.py:105
  117.7 3.1 %gather_fusion.1 = f32[512]{0:T(512)S(1)} fusion(f32[163840]{0:T(1024)S(1)} %bitcast.54, s32[1024]{0:T(1024)S(1)} %pad_clamp_fusion), kind=kCustom, calls=%fused_computation.1 | custom fusion | bytes 6144 | tf_op jit(solution)/shard_map/gather | solution.py:105
  120.9 1.4 maximum_convert_fusion.4
  122.2 4.1 %fusion.10 = (f32[4,320,128]{2,1,0:T(8,128)}, f32[4,320,128]{2,1,0:T(8,128)}, f32[4,320,128]{2,1,0:T(8,128)}, f32[4,320,128]{2,1,0:T(8,128)}, f32[4,320,128]{2,1,0:T(8,128)}) fusion(bf16[4,320,128]{2,1,0:T(8,128)(2,1)S(1)} %reduce_sum.24, f32[4,320,128]{2,1,0:T(8,128)S(1)} %copy-done.4, f32[4,320,128]{2,1,0:T(8,128)S(1)} %copy-done.5, ...), kind=kLoop, calls=%fused_computation.179 | loop fusion | flops 13598720 | bytes 14745600 | tf_op jit(solution)/shard_map/add | solution.py:104
  126.3 18.5 %gather_fusion = f32[512]{0:T(512)S(1)} fusion(f32[163840]{0:T(1024)} %bitcast.55, s32[1024]{0:T(1024)S(1)} %pad_clamp_fusion), kind=kCustom, calls=%fused_computation | custom fusion | bytes 6144 | tf_op jit(solution)/shard_map/gather | solution.py:105
  144.8 3.8 %scatter_custom_fusion = f32[163840]{0:T(1024)S(1)} fusion(s32[512]{0:T(512)S(1)} %bitcast.67, f32[512]{0:T(512)S(1)} %get-tuple-element.49, f32[]{:T(128)} %constant.9.clone.1), kind=kCustom, calls=%fused_computation.394 | custom fusion | flops 512 | bytes 655364 | tf_op jit(solution)/shard_map/scatter-add | solution.py:114
  148.6 1.9 fusion.185
  150.5 1.3 collective-permute-start.11
  151.8 4.6 %collective-permute-start.10 = (bf16[4,320,128]{2,1,0:T(8,128)(2,1)}, bf16[4,320,128]{2,1,0:T(8,128)(2,1)}, u32[]{:S(2)}, u32[]{:S(2)}) collective-permute-start(bf16[4,320,128]{2,1,0:T(8,128)(2,1)} %fusion.185), channel_id=1, source_target_pairs={{0,1},{1,2},{2,3},{3,4},{4,5},{5,6},{6,7},{8,9},{9,10},{10,11},{11... | collective-permute-start | bytes 983048 | tf_op jit(solution)/shard_map/ppermute | solution.py:22
  156.4 4.5 %scatter_custom_fusion.1 = f32[163840]{0:T(1024)} fusion(s32[512]{0:T(512)S(1)} %bitcast.68, f32[512]{0:T(512)S(1)} %get-tuple-element.52, f32[]{:T(128)} %constant.9.clone.1), kind=kCustom, calls=%fused_computation.392 | custom fusion | flops 512 | bytes 655364 | tf_op jit(solution)/shard_map/scatter-add | solution.py:114
  160.9 1.5 maximum_convert_fusion.5
  162.6 4.0 %add_convert_fusion = (bf16[4,320,128]{2,1,0:T(8,128)(2,1)}, f32[4,320,128]{2,1,0:T(8,128)}, f32[4,320,128]{2,1,0:T(8,128)}, f32[4,320,128]{2,1,0:T(8,128)}, f32[4,320,128]{2,1,0:T(8,128)}) fusion(f32[4,320,128]{2,1,0:T(8,128)S(1)} %bitcast.59, f32[4,320,128]{2,1,0:T(8,128)S(1)} %copy-done.1, f32[4,320,128]{2,1,0:T(8,128)S(1)} %copy-done, ...), kind=kLoop, calls=%fused_computation.408 | loop fusion | flops 14090240 | bytes 15728640 | tf_op jit(solution)/shard_map/convert_element_type | solution.py:94
  167.9 5.5 %collective-permute-start.12 = (bf16[4,320,128]{2,1,0:T(8,128)(2,1)}, bf16[4,320,128]{2,1,0:T(8,128)(2,1)}, u32[]{:S(2)}, u32[]{:S(2)}) collective-permute-start(bf16[4,320,128]{2,1,0:T(8,128)(2,1)} %get-tuple-element.12), channel_id=1, source_target_pairs={{0,1},{1,2},{2,3},{3,4},{4,5},{5,6},{6,7},{8,9},{9,10},{10,11},{11... | collective-permute-start | bytes 983048 | tf_op jit(solution)/shard_map/ppermute | solution.py:22
  173.4 4.5 %scatter_custom_fusion.2 = f32[163840]{0:T(1024)} fusion(s32[512]{0:T(512)S(1)} %bitcast.69, f32[512]{0:T(512)S(1)} %get-tuple-element.51, f32[]{:T(128)} %constant.9.clone.1), kind=kCustom, calls=%fused_computation.390 | custom fusion | flops 512 | bytes 655364 | tf_op jit(solution)/shard_map/scatter-add | solution.py:114
  177.9 1.5 maximum_convert_fusion.6
  179.9 4.0 %fusion.188 = (bf16[4,320,128]{2,1,0:T(8,128)(2,1)}, f32[4,320,128]{2,1,0:T(8,128)}, f32[4,320,128]{2,1,0:T(8,128)}, f32[4,320,128]{2,1,0:T(8,128)}, f32[4,320,128]{2,1,0:T(8,128)}) fusion(f32[4,320,128]{2,1,0:T(8,128)S(1)} %bitcast.63, f32[4,320,128]{2,1,0:T(8,128)S(1)} %copy-done.1, f32[4,320,128]{2,1,0:T(8,128)S(1)} %copy-done, ...), kind=kLoop, calls=%fused_computation.410 | loop fusion | flops 14090240 | bytes 15728640 | tf_op jit(solution)/shard_map/convert_element_type | solution.py:94
  185.1 4.4 %collective-permute-start.14 = (bf16[4,320,128]{2,1,0:T(8,128)(2,1)}, bf16[4,320,128]{2,1,0:T(8,128)(2,1)}, u32[]{:S(2)}, u32[]{:S(2)}) collective-permute-start(bf16[4,320,128]{2,1,0:T(8,128)(2,1)} %get-tuple-element.7), channel_id=1, source_target_pairs={{0,1},{1,2},{2,3},{3,4},{4,5},{5,6},{6,7},{8,9},{9,10},{10,11},{11... | collective-permute-start | bytes 983048 | tf_op jit(solution)/shard_map/ppermute | solution.py:22
  191.4 4.5 %scatter_custom_fusion.3 = f32[163840]{0:T(1024)} fusion(s32[512]{0:T(512)S(1)} %bitcast.70, f32[512]{0:T(512)S(1)} %get-tuple-element.50, f32[]{:T(128)} %constant.9.clone.1), kind=kCustom, calls=%fused_computation.388 | custom fusion | flops 512 | bytes 655364 | tf_op jit(solution)/shard_map/scatter-add | solution.py:114
  195.9 1.5 maximum_convert_fusion.7
  197.7 2.9 %fusion.186 = (bf16[4,320,128]{2,1,0:T(8,128)(2,1)S(1)}, f32[4,320,128]{2,1,0:T(8,128)S(1)}, f32[4,320,128]{2,1,0:T(8,128)S(1)}, f32[4,320,128]{2,1,0:T(8,128)S(1)}, f32[4,320,128]{2,1,0:T(8,128)S(1)}) fusion(f32[4,320,128]{2,1,0:T(8,128)S(1)} %bitcast.62, f32[4,320,128]{2,1,0:T(8,128)S(1)} %copy-done.1, f32[4,320,128]{2,1,0:T(8,128)S(1)} %copy-done, ...), kind=kLoop, calls=%fused_computation.409 | loop fusion | flops 13926400 | bytes 15073280 | tf_op jit(solution)/shard_map/convert_element_type | solution.py:94
  200.7 1.3 collective-permute-start.17
  202.0 3.8 %collective-permute-start.16 = (bf16[4,320,128]{2,1,0:T(8,128)(2,1)S(1)}, bf16[4,320,128]{2,1,0:T(8,128)(2,1)S(1)}, u32[]{:S(2)}, u32[]{:S(2)}) collective-permute-start(bf16[4,320,128]{2,1,0:T(8,128)(2,1)S(1)} %get-tuple-element.2), channel_id=1, source_target_pairs={{0,1},{1,2},{2,3},{3,4},{4,5},{5,6},{6,7},{8,9},{9,10},{10,11},{11... | collective-permute-start | bytes 983048 | tf_op jit(solution)/shard_map/ppermute | solution.py:22
  209.7 2.7 fusion.175
  212.4 2.2 select_convert_fusion
  215.4 34.2 %reduce-scatter.7.cloned.1.call-done = bf16[1,4,320,128]{3,2,1,0:T(8,128)(2,1)} async-done(((bf16[4,4,320,128]{3,2,1,0:T(8,128)(2,1)}), bf16[1,4,320,128]{3,2,1,0:T(8,128)(2,1)}) %reduce-scatter.7.cloned.1.call-update) | async-done | bytes 327696
  249.6 1.9 convert_element_type.119
  251.4 30.6 %reduce-scatter.9.cloned.1.call-done = bf16[1,4,320,128]{3,2,1,0:T(8,128)(2,1)} async-done(((bf16[4,4,320,128]{3,2,1,0:T(8,128)(2,1)}), bf16[1,4,320,128]{3,2,1,0:T(8,128)(2,1)}) %reduce-scatter.9.cloned.1.call-update) | async-done | bytes 327696
  282.0 1.9 convert_element_type.125
  (132 shorter events, 16.7 us)
Async XLA Ops:
  32.4 4.5 %copy-start.14 = (f32[1,4,320,128]{3,2,1,0:T(8,128)S(1)}, f32[1,4,320,128]{3,2,1,0:T(8,128)}, u32[]{:S(2)}) copy-start(f32[1,4,320,128]{3,2,1,0:T(8,128)} %param.14) | copy-start | bytes 1966084
  32.4 19.7 %all-to-all-start = ((bf16[4,4,320,128]{3,2,1,0:T(8,128)(2,1)}), bf16[4,4,320,128]{3,2,1,0:T(8,128)(2,1)}, u32[]{:S(2)}, u32[]{:S(2)}) async-start(bf16[4,4,320,128]{3,2,1,0:T(8,128)(2,1)} %get-tuple-element.54), calls=%async_computation | async-start | bytes 2621440 | tf_op jit(solution)/shard_map/all_to_all | solution.py:76
  36.8 212.8 %reduce-scatter.7.cloned.1.call-start = ((), (), s32[]{:S(2)}) async-start(), calls=%async_computation.4 | async-start | bytes 1638400
  36.9 10.5 %collective-permute-start.1 = (bf16[4,320,128]{2,1,0:T(8,128)(2,1)S(1)}, bf16[4,320,128]{2,1,0:T(8,128)(2,1)S(1)}, u32[]{:S(2)}, u32[]{:S(2)}) collective-permute-start(bf16[4,320,128]{2,1,0:T(8,128)(2,1)S(1)} %bitcast_convert_fusion), channel_id=1, source_target_pairs={{1,0},{2,1},{3,2},{4,3},{5,4},{6,5},{7,6},{9,8},{10,9},{11,10},{12... | collective-permute-start | bytes 983048 | tf_op jit(solution)/shard_map/ppermute | solution.py:24
  38.2 10.0 %collective-permute-start = (bf16[4,320,128]{2,1,0:T(8,128)(2,1)S(1)}, bf16[4,320,128]{2,1,0:T(8,128)(2,1)}, u32[]{:S(2)}, u32[]{:S(2)}) collective-permute-start(bf16[4,320,128]{2,1,0:T(8,128)(2,1)S(1)} %bitcast_convert_fusion), channel_id=1, source_target_pairs={{0,1},{1,2},{2,3},{3,4},{4,5},{5,6},{6,7},{8,9},{9,10},{10,11},{11... | collective-permute-start | bytes 983048 | tf_op jit(solution)/shard_map/ppermute | solution.py:22
  42.4 11.3 %collective-permute-start.3 = (bf16[4,320,128]{2,1,0:T(8,128)(2,1)S(1)}, bf16[4,320,128]{2,1,0:T(8,128)(2,1)S(1)}, u32[]{:S(2)}, u32[]{:S(2)}) collective-permute-start(bf16[4,320,128]{2,1,0:T(8,128)(2,1)S(1)} %fusion.18), channel_id=1, source_target_pairs={{1,0},{2,1},{3,2},{4,3},{5,4},{6,5},{7,6},{9,8},{10,9},{11,10},{12... | collective-permute-start | bytes 983048 | tf_op jit(solution)/shard_map/ppermute | solution.py:24
  43.7 10.0 %collective-permute-start.2 = (bf16[4,320,128]{2,1,0:T(8,128)(2,1)S(1)}, bf16[4,320,128]{2,1,0:T(8,128)(2,1)}, u32[]{:S(2)}, u32[]{:S(2)}) collective-permute-start(bf16[4,320,128]{2,1,0:T(8,128)(2,1)S(1)} %fusion.18), channel_id=1, source_target_pairs={{0,1},{1,2},{2,3},{3,4},{4,5},{5,6},{6,7},{8,9},{9,10},{10,11},{11... | collective-permute-start | bytes 983048 | tf_op jit(solution)/shard_map/ppermute | solution.py:22
  61.5 7.4 %copy-start = (f32[4,320,128]{2,1,0:T(8,128)S(1)}, f32[4,320,128]{2,1,0:T(8,128)}, u32[]{:S(2)}) copy-start(f32[4,320,128]{2,1,0:T(8,128)} %get-tuple-element.40) | copy-start | bytes 1966084
  61.5 7.4 %copy-start.1 = (f32[4,320,128]{2,1,0:T(8,128)S(1)}, f32[4,320,128]{2,1,0:T(8,128)}, u32[]{:S(2)}) copy-start(f32[4,320,128]{2,1,0:T(8,128)} %get-tuple-element.42) | copy-start | bytes 1966084
  61.6 7.4 %copy-start.2 = (f32[4,320,128]{2,1,0:T(8,128)S(1)}, f32[4,320,128]{2,1,0:T(8,128)}, u32[]{:S(2)}) copy-start(f32[4,320,128]{2,1,0:T(8,128)} %get-tuple-element.35) | copy-start | bytes 1966084
  61.6 5.2 %collective-permute-start.5 = (bf16[4,320,128]{2,1,0:T(8,128)(2,1)}, bf16[4,320,128]{2,1,0:T(8,128)(2,1)}, u32[]{:S(2)}, u32[]{:S(2)}) collective-permute-start(bf16[4,320,128]{2,1,0:T(8,128)(2,1)} %get-tuple-element.34), channel_id=1, source_target_pairs={{1,0},{2,1},{3,2},{4,3},{5,4},{6,5},{7,6},{9,8},{10,9},{11,10},{12... | collective-permute-start | bytes 983048 | tf_op jit(solution)/shard_map/ppermute | solution.py:24
  63.0 4.6 %collective-permute-start.4 = (bf16[4,320,128]{2,1,0:T(8,128)(2,1)}, bf16[4,320,128]{2,1,0:T(8,128)(2,1)}, u32[]{:S(2)}, u32[]{:S(2)}) collective-permute-start(bf16[4,320,128]{2,1,0:T(8,128)(2,1)} %get-tuple-element.34), channel_id=1, source_target_pairs={{0,1},{1,2},{2,3},{3,4},{4,5},{5,6},{6,7},{8,9},{9,10},{10,11},{11... | collective-permute-start | bytes 983048 | tf_op jit(solution)/shard_map/ppermute | solution.py:22
  66.8 2.2 copy-start.15
  69.0 11.7 %copy-start.45 = (s32[1,512]{1,0:T(1,128)S(1)}, s32[1,512]{1,0:T(1,128)}, u32[]{:S(2)}) copy-start(s32[1,512]{1,0:T(1,128)} %param.12) | copy-start | bytes 6148
  72.9 13.3 %copy-start.3 = (f32[4,320,128]{2,1,0:T(8,128)}, f32[4,320,128]{2,1,0:T(8,128)S(1)}, u32[]{:S(2)}) copy-start(f32[4,320,128]{2,1,0:T(8,128)S(1)} %get-tuple-element.29) | copy-start | bytes 1966084
  72.9 7.8 %collective-permute-start.7 = (bf16[4,320,128]{2,1,0:T(8,128)(2,1)S(1)}, bf16[4,320,128]{2,1,0:T(8,128)(2,1)S(1)}, u32[]{:S(2)}, u32[]{:S(2)}) collective-permute-start(bf16[4,320,128]{2,1,0:T(8,128)(2,1)S(1)} %get-tuple-element.28), channel_id=1, source_target_pairs={{1,0},{2,1},{3,2},{4,3},{5,4},{6,5},{7,6},{9,8},{10,9},{11,10},{12... | collective-permute-start | bytes 983048 | tf_op jit(solution)/shard_map/ppermute | solution.py:24
  74.2 7.7 %collective-permute-start.6 = (bf16[4,320,128]{2,1,0:T(8,128)(2,1)S(1)}, bf16[4,320,128]{2,1,0:T(8,128)(2,1)S(1)}, u32[]{:S(2)}, u32[]{:S(2)}) collective-permute-start(bf16[4,320,128]{2,1,0:T(8,128)(2,1)S(1)} %get-tuple-element.28), channel_id=1, source_target_pairs={{0,1},{1,2},{2,3},{3,4},{4,5},{5,6},{6,7},{8,9},{9,10},{10,11},{11... | collective-permute-start | bytes 983048 | tf_op jit(solution)/shard_map/ppermute | solution.py:22
  82.0 13.9 %copy-start.44 = (f32[1,4,512]{2,1,0:T(4,128)S(1)}, f32[1,4,512]{2,1,0:T(4,128)}, u32[]{:S(2)}) copy-start(f32[1,4,512]{2,1,0:T(4,128)} %param.13) | copy-start | bytes 24580
  86.2 34.7 %collective-permute-start.9 = (bf16[4,320,128]{2,1,0:T(8,128)(2,1)}, bf16[4,320,128]{2,1,0:T(8,128)(2,1)}, u32[]{:S(2)}, u32[]{:S(2)}) collective-permute-start(bf16[4,320,128]{2,1,0:T(8,128)(2,1)} %get-tuple-element.22), channel_id=1, source_target_pairs={{1,0},{2,1},{3,2},{4,3},{5,4},{6,5},{7,6},{9,8},{10,9},{11,10},{12... | collective-permute-start | bytes 983048 | tf_op jit(solution)/shard_map/ppermute | solution.py:24
  87.4 33.4 %collective-permute-start.8 = (bf16[4,320,128]{2,1,0:T(8,128)(2,1)}, bf16[4,320,128]{2,1,0:T(8,128)(2,1)}, u32[]{:S(2)}, u32[]{:S(2)}) collective-permute-start(bf16[4,320,128]{2,1,0:T(8,128)(2,1)} %get-tuple-element.22), channel_id=1, source_target_pairs={{0,1},{1,2},{2,3},{3,4},{4,5},{5,6},{6,7},{8,9},{9,10},{10,11},{11... | collective-permute-start | bytes 983048 | tf_op jit(solution)/shard_map/ppermute | solution.py:22
  99.2 18.5 %copy-start.5 = (f32[4,320,128]{2,1,0:T(8,128)S(1)}, f32[4,320,128]{2,1,0:T(8,128)}, u32[]{:S(2)}) copy-start(f32[4,320,128]{2,1,0:T(8,128)} %get-tuple-element.23) | copy-start | bytes 1966084
  150.5 10.4 %collective-permute-start.11 = (bf16[4,320,128]{2,1,0:T(8,128)(2,1)}, bf16[4,320,128]{2,1,0:T(8,128)(2,1)}, u32[]{:S(2)}, u32[]{:S(2)}) collective-permute-start(bf16[4,320,128]{2,1,0:T(8,128)(2,1)} %fusion.185), channel_id=1, source_target_pairs={{1,0},{2,1},{3,2},{4,3},{5,4},{6,5},{7,6},{9,8},{10,9},{11,10},{12... | collective-permute-start | bytes 983048 | tf_op jit(solution)/shard_map/ppermute | solution.py:24
  151.8 9.1 %collective-permute-start.10 = (bf16[4,320,128]{2,1,0:T(8,128)(2,1)}, bf16[4,320,128]{2,1,0:T(8,128)(2,1)}, u32[]{:S(2)}, u32[]{:S(2)}) collective-permute-start(bf16[4,320,128]{2,1,0:T(8,128)(2,1)} %fusion.185), channel_id=1, source_target_pairs={{0,1},{1,2},{2,3},{3,4},{4,5},{5,6},{6,7},{8,9},{9,10},{10,11},{11... | collective-permute-start | bytes 983048 | tf_op jit(solution)/shard_map/ppermute | solution.py:22
  166.6 11.3 %collective-permute-start.13 = (bf16[4,320,128]{2,1,0:T(8,128)(2,1)}, bf16[4,320,128]{2,1,0:T(8,128)(2,1)}, u32[]{:S(2)}, u32[]{:S(2)}) collective-permute-start(bf16[4,320,128]{2,1,0:T(8,128)(2,1)} %get-tuple-element.12), channel_id=1, source_target_pairs={{1,0},{2,1},{3,2},{4,3},{5,4},{6,5},{7,6},{9,8},{10,9},{11,10},{12... | collective-permute-start | bytes 983048 | tf_op jit(solution)/shard_map/ppermute | solution.py:24
  167.9 10.0 %collective-permute-start.12 = (bf16[4,320,128]{2,1,0:T(8,128)(2,1)}, bf16[4,320,128]{2,1,0:T(8,128)(2,1)}, u32[]{:S(2)}, u32[]{:S(2)}) collective-permute-start(bf16[4,320,128]{2,1,0:T(8,128)(2,1)} %get-tuple-element.12), channel_id=1, source_target_pairs={{0,1},{1,2},{2,3},{3,4},{4,5},{5,6},{6,7},{8,9},{9,10},{10,11},{11... | collective-permute-start | bytes 983048 | tf_op jit(solution)/shard_map/ppermute | solution.py:22
  183.8 12.1 %collective-permute-start.15 = (bf16[4,320,128]{2,1,0:T(8,128)(2,1)}, bf16[4,320,128]{2,1,0:T(8,128)(2,1)}, u32[]{:S(2)}, u32[]{:S(2)}) collective-permute-start(bf16[4,320,128]{2,1,0:T(8,128)(2,1)} %get-tuple-element.7), channel_id=1, source_target_pairs={{1,0},{2,1},{3,2},{4,3},{5,4},{6,5},{7,6},{9,8},{10,9},{11,10},{12... | collective-permute-start | bytes 983048 | tf_op jit(solution)/shard_map/ppermute | solution.py:24
  185.1 10.8 %collective-permute-start.14 = (bf16[4,320,128]{2,1,0:T(8,128)(2,1)}, bf16[4,320,128]{2,1,0:T(8,128)(2,1)}, u32[]{:S(2)}, u32[]{:S(2)}) collective-permute-start(bf16[4,320,128]{2,1,0:T(8,128)(2,1)} %get-tuple-element.7), channel_id=1, source_target_pairs={{0,1},{1,2},{2,3},{3,4},{4,5},{5,6},{6,7},{8,9},{9,10},{10,11},{11... | collective-permute-start | bytes 983048 | tf_op jit(solution)/shard_map/ppermute | solution.py:22
  197.6 8.1 %copy-start.10 = (f32[1,4,320,128]{3,2,1,0:T(8,128)S(1)}, f32[1,4,320,128]{3,2,1,0:T(8,128)}, u32[]{:S(2)}) copy-start(f32[1,4,320,128]{3,2,1,0:T(8,128)} %param.16) | copy-start | bytes 1966084
  197.7 8.1 %copy-start.13 = (f32[163840]{0:T(1024)S(1)}, f32[163840]{0:T(1024)}, u32[]{:S(2)}) copy-start(f32[163840]{0:T(1024)} %scatter_custom_fusion.1) | copy-start | bytes 1966084
  197.7 8.1 %copy-start.29 = (f32[4,320,128]{2,1,0:T(8,128)S(1)}, f32[4,320,128]{2,1,0:T(8,128)}, u32[]{:S(2)}) copy-start(f32[4,320,128]{2,1,0:T(8,128)} %get-tuple-element.36) | copy-start | bytes 1966084
  197.7 8.1 %copy-start.30 = (f32[4,320,128]{2,1,0:T(8,128)S(1)}, f32[4,320,128]{2,1,0:T(8,128)}, u32[]{:S(2)}) copy-start(f32[4,320,128]{2,1,0:T(8,128)} %get-tuple-element.30) | copy-start | bytes 1966084
  197.7 8.1 %copy-start.31 = (f32[4,320,128]{2,1,0:T(8,128)S(1)}, f32[4,320,128]{2,1,0:T(8,128)}, u32[]{:S(2)}) copy-start(f32[4,320,128]{2,1,0:T(8,128)} %get-tuple-element.24) | copy-start | bytes 1966084
  197.7 8.1 %copy-start.32 = (f32[4,320,128]{2,1,0:T(8,128)S(1)}, f32[4,320,128]{2,1,0:T(8,128)}, u32[]{:S(2)}) copy-start(f32[4,320,128]{2,1,0:T(8,128)} %get-tuple-element.18) | copy-start | bytes 1966084
  197.7 9.4 %copy-start.37 = (f32[4,320,128]{2,1,0:T(8,128)S(1)}, f32[4,320,128]{2,1,0:T(8,128)}, u32[]{:S(2)}) copy-start(f32[4,320,128]{2,1,0:T(8,128)} %get-tuple-element.9) | copy-start | bytes 1966084
  197.7 9.4 %copy-start.38 = (f32[4,320,128]{2,1,0:T(8,128)S(1)}, f32[4,320,128]{2,1,0:T(8,128)}, u32[]{:S(2)}) copy-start(f32[4,320,128]{2,1,0:T(8,128)} %get-tuple-element.10) | copy-start | bytes 1966084
  197.7 9.4 %copy-start.39 = (f32[4,320,128]{2,1,0:T(8,128)S(1)}, f32[4,320,128]{2,1,0:T(8,128)}, u32[]{:S(2)}) copy-start(f32[4,320,128]{2,1,0:T(8,128)} %get-tuple-element.11) | copy-start | bytes 1966084
  200.7 5.8 %collective-permute-start.17 = (bf16[4,320,128]{2,1,0:T(8,128)(2,1)S(1)}, bf16[4,320,128]{2,1,0:T(8,128)(2,1)S(1)}, u32[]{:S(2)}, u32[]{:S(2)}) collective-permute-start(bf16[4,320,128]{2,1,0:T(8,128)(2,1)S(1)} %get-tuple-element.2), channel_id=1, source_target_pairs={{1,0},{2,1},{3,2},{4,3},{5,4},{6,5},{7,6},{9,8},{10,9},{11,10},{12... | collective-permute-start | bytes 983048 | tf_op jit(solution)/shard_map/ppermute | solution.py:24
  202.0 5.0 %collective-permute-start.16 = (bf16[4,320,128]{2,1,0:T(8,128)(2,1)S(1)}, bf16[4,320,128]{2,1,0:T(8,128)(2,1)S(1)}, u32[]{:S(2)}, u32[]{:S(2)}) collective-permute-start(bf16[4,320,128]{2,1,0:T(8,128)(2,1)S(1)} %get-tuple-element.2), channel_id=1, source_target_pairs={{0,1},{1,2},{2,3},{3,4},{4,5},{5,6},{6,7},{8,9},{9,10},{10,11},{11... | collective-permute-start | bytes 983048 | tf_op jit(solution)/shard_map/ppermute | solution.py:22
  205.9 2.2 copy-start.27
  205.9 2.4 copy-start.28
  205.9 2.6 copy-start.34
  205.9 2.8 copy-start.35
  205.9 3.0 %copy-start.36 = (f32[4,320,128]{2,1,0:T(8,128)S(1)}, f32[4,320,128]{2,1,0:T(8,128)}, u32[]{:S(2)}) copy-start(f32[4,320,128]{2,1,0:T(8,128)} %get-tuple-element.16) | copy-start | bytes 1966084
  206.4 2.8 copy-start.17
  206.4 3.0 %copy-start.18 = (f32[4,320,128]{2,1,0:T(8,128)S(1)}, f32[4,320,128]{2,1,0:T(8,128)}, u32[]{:S(2)}) copy-start(f32[4,320,128]{2,1,0:T(8,128)} %get-tuple-element.39) | copy-start | bytes 1966084
  206.4 3.2 %copy-start.19 = (f32[4,320,128]{2,1,0:T(8,128)S(1)}, f32[4,320,128]{2,1,0:T(8,128)}, u32[]{:S(2)}) copy-start(f32[4,320,128]{2,1,0:T(8,128)} %get-tuple-element.41) | copy-start | bytes 1966084
  206.4 3.3 %copy-start.20 = (f32[4,320,128]{2,1,0:T(8,128)S(1)}, f32[4,320,128]{2,1,0:T(8,128)}, u32[]{:S(2)}) copy-start(f32[4,320,128]{2,1,0:T(8,128)} %get-tuple-element.31) | copy-start | bytes 1966084
  214.7 67.4 %reduce-scatter.9.cloned.1.call-start = ((), (), s32[]{:S(2)}) async-start(), calls=%async_computation.5 | async-start | bytes 1638400
  (19 other events, 29.5 us)
Sparse Core Ops, SparseCore 0:
  214.8 34.7 reduce-scatter.6
  252.5 29.4 reduce-scatter.8
where the time goes:
time: 293 us; the launch traced here: 291 us
  other arithmetic  73.5 us (25%)
  waiting for transfers between devices  70.7 us (24%)
  starting transfers between devices  60.8 us (21%)
  local copies, waits for them, and re-layouts  49 us (17%)
  blocking collectives  21.9 us (7%)
  between operations  14.8 us (5%)
    unnamed x4, waiting for transfers between devices  65.5 us
    ppermute x9, starting transfers between devices, padded_2(): lax.ppermute(tail, axis, [(i, (i + 1) % count) for i in range(ends)])  44.6 us
    gather x4, local copies, waits for them, and re-layouts, body(): sampled = current.reshape(-1)[station]  43.2 us
    convert_element_type x8, other arithmetic, field_terms(): field.astype(jnp.bfloat16)  27.5 us
    all_to_all x1, blocking collectives, body(): lax.all_to_all(send_den, 'shot', split_axis=0, concat_axis=0, tiled=True)  21.9 us
    scatter-add x4, other arithmetic, body(): source = jnp.zeros((cells,), jnp.float32).at[station].add(misfits[ITERS -...  17.3 us
    ppermute x9, starting transfers between devices, padded_2(): lax.ppermute(head, axis, [((i + 1) % count, i) for i in range(ends)])  11.7 us
    convert_element_type x8, other arithmetic, field_terms(): padded_2(field.astype(jnp.bfloat16), (('sub', 0),), 4).astype(field.dtype)  8.58 us
  transfers between devices with their start and end apart: 21, of which 6 were waited for; matrix products, arithmetic and copies ran while one was open for 16% of the time, Pallas kernels for 0%

commit v1 on v0

v1 whole, which is shorter than its diff:
```python
import math

import jax
import jax.numpy as jnp
from jax import lax
from jax.experimental import pallas as pl
from jax.experimental.pallas import tpu as pltpu
from jax.sharding import PartitionSpec as P

ITERS = 4
SECOND = (-205.0 / 72.0, 8.0 / 5.0, -1.0 / 5.0, 8.0 / 315.0, -1.0 / 560.0)
FIRST = (4.0 / 5.0, -1.0 / 5.0, 4.0 / 105.0, -1.0 / 280.0)
SPEED = 0.15
PAD = 8
F32, BF16 = jnp.float32, jnp.bfloat16
VMEM_LIMIT = 4 << 20

VM = pl.BlockSpec(memory_space=pltpu.VMEM)
SM = pl.BlockSpec(memory_space=pltpu.SMEM)


def call(kernel, outs, ins, specs, out_specs=None, scratch=(), flops=0):
    outs = tuple(jax.ShapeDtypeStruct(shape, dtype) for shape, dtype in outs)
    moved_bytes = sum(math.prod(x.shape) * x.dtype.itemsize for x in (*ins, *outs))
    return pl.pallas_call(
        kernel,
        out_shape=outs,
        in_specs=list(specs),
        out_specs=tuple(out_specs or [VM] * len(outs)),
        scratch_shapes=list(scratch),
        cost_estimate=pl.CostEstimate(flops=flops, bytes_accessed=moved_bytes, transcendentals=0),
        compiler_params=pltpu.CompilerParams(vmem_limit_bytes=VMEM_LIMIT),
    )(*ins)


def weighted(pairs):
    lap, first = None, None
    for m, (ahead, behind) in enumerate(pairs, 1):
        s = SECOND[m] * (ahead + behind)
        t = FIRST[m - 1] * (ahead - behind)
        lap = s if lap is None else lap + s
        first = t if first is None else first + t
    return lap, first


def y_pairs(ref, layer, row, rows):
    return [
        (ref[layer, pl.ds(row + m, rows), :], ref[layer, pl.ds(row - m, rows), :])
        for m in range(1, 5)
    ]


def z_masks(rows, depth):
    lane = lax.broadcasted_iota(jnp.int32, (rows, depth), 1)
    return [(lane < depth - m, lane >= m) for m in range(1, 5)]


def z_pairs(value, masks):
    depth = value.shape[1]
    return [
        (
            jnp.where(ahead, pltpu.roll(value, depth - m, 1), 0.0),
            jnp.where(behind, pltpu.roll(value, m, 1), 0.0),
        )
        for m, (ahead, behind) in enumerate(masks, 1)
    ]


def x_values(flags_ref, own, on_ref, off_ref, rows):
    even = flags_ref[0] == 1
    valid = flags_ref[1] == 1
    count = len(own)
    on = [on_ref[l, rows, :].astype(F32) for l in range(count)]
    off = [jnp.where(valid, off_ref[l, rows, :].astype(F32), 0.0) for l in range(count)]
    low = [jnp.where(even, b, a) for a, b in zip(on, off)]
    high = [jnp.where(even, a, b) for a, b in zip(on, off)]
    return low[count - 4 :] + own + high[:4]


def x_pairs(values, layer):
    return [(values[4 + layer + m], values[4 + layer - m]) for m in range(1, 5)]


def zero_pads(ref):
    layers, tall, depth = ref.shape
    zeros = jnp.zeros((PAD, depth), F32)
    for l in range(layers):
        ref[l, pl.ds(0, PAD), :] = zeros
        ref[l, pl.ds(tall - PAD, PAD), :] = zeros


def prepare_kernel(p_ref, q_ref, pw_ref, qw_ref, ph_ref, qh_ref):
    layers, width, _ = p_ref.shape
    for src, wide, half in ((p_ref, pw_ref, ph_ref), (q_ref, qw_ref, qh_ref)):
        zero_pads(wide)

        @pl.loop(0, width // 16)
        def _(j, src=src, wide=wide, half=half):
            at = pl.multiple_of(16 * j, 16)
            for l in range(layers):
                v = src[l, pl.ds(at, 16), :]
                wide[l, pl.ds(at + PAD, 16), :] = v
                half[l, pl.ds(at, 16), :] = v.astype(BF16)


def list_kernel(row_ref, lane_ref, list_row, list_lane, list_at, count_ref):
    def step(i, count):
        row = row_ref[i]
        list_row[count] = row
        list_lane[count] = lane_ref[i]
        list_at[count] = i
        return count + jnp.where(row >= 0, 1, 0)

    count_ref[0] = lax.fori_loop(0, row_ref.shape[0], step, jnp.int32(0))


def add_receivers(n, field_ref, into_ref, lists, observed_ref):
    list_row, list_lane, list_at, count_ref = lists
    tall = field_ref.shape[1]
    lane = lax.broadcasted_iota(jnp.int32, (1, field_ref.shape[2]), 1)

    def step(c, carry):
        row = list_row[c]
        layer = row // tall
        y = row - layer * tall
        seen = observed_ref[n, list_at[c]]
        term = jnp.where(lane == list_lane[c], field_ref[layer, pl.ds(y, 1), :] - seen, 0.0)
        into_ref[layer, pl.ds(y, 1), :] += term
        return carry

    lax.fori_loop(0, count_ref[0], step, 0)


def receivers_kernel(n, field_ref, lr, ll, la, lc, observed_ref, source_ref):
    source_ref[...] = jnp.zeros(source_ref.shape, F32)
    add_receivers(n, field_ref, source_ref, (lr, ll, la, lc), observed_ref)


def first_adjoint_kernel(n, p_ref, q_ref, lr, ll, la, lc, observed_ref, a_ref, half_ref):
    a_ref[...] = q_ref[...]
    add_receivers(n, p_ref, a_ref, (lr, ll, la, lc), observed_ref)
    layers, width, _ = half_ref.shape

    @pl.loop(0, width // 16)
    def _(j):
        at = pl.multiple_of(16 * j, 16)
        for l in range(layers):
            half_ref[l, pl.ds(at, 16), :] = a_ref[l, pl.ds(at + PAD, 16), :].astype(BF16)


def log_kernel(den_ref, log_ref, s2_ref, s3_ref):
    layers, width, depth = den_ref.shape
    zero_pads(log_ref)

    @pl.loop(0, width // 16)
    def _(j):
        at = pl.multiple_of(16 * j, 16)
        for l in range(layers):
            log_ref[l, pl.ds(at + PAD, 16), :] = jnp.log(den_ref[l, pl.ds(at, 16), :].astype(F32))

    masks = z_masks(8, depth)

    @pl.loop(0, width // 8)
    def _(j):
        at = pl.multiple_of(8 * j, 8)
        for l in range(layers):
            s2_ref[l, pl.ds(at, 8), :] = weighted(y_pairs(log_ref, l, at + PAD, 8))[1]
            s3_ref[l, pl.ds(at, 8), :] = weighted(z_pairs(log_ref[l, pl.ds(at + PAD, 8), :], masks))[1]


def slope_x_kernel(flags_ref, log_ref, on_ref, off_ref, vel_ref, s1_ref, scale_ref):
    layers, width, _ = s1_ref.shape
    even = flags_ref[0] == 1
    valid = flags_ref[1] == 1

    @pl.loop(0, width // 16)
    def _(j):
        at = pl.multiple_of(16 * j, 16)
        rows = pl.ds(at, 16)
        own = [log_ref[l, pl.ds(at + PAD, 16), :] for l in range(layers)]
        on = [jnp.log(on_ref[l, rows, :].astype(F32)) for l in range(layers)]
        off = [jnp.log(jnp.where(valid, off_ref[l, rows, :].astype(F32), 1.0)) for l in range(layers)]
        low = [jnp.where(even, b, a) for a, b in zip(on, off)]
        high = [jnp.where(even, a, b) for a, b in zip(on, off)]
        values = low[layers - 4 :] + own + high[:4]
        for l in range(layers):
            s1_ref[l, rows, :] = weighted(x_pairs(values, l))[1]
            v = vel_ref[l, rows, :].astype(F32)
            scale_ref[l, rows, :] = SPEED * v * v


def yz_terms(f_ref, s2_ref, s3_ref, l, at, masks):
    f = f_ref[l, pl.ds(at + PAD, 8), :]
    lap_y, d_y = weighted(y_pairs(f_ref, l, at + PAD, 8))
    lap_z, d_z = weighted(z_pairs(f, masks))
    rows = pl.ds(at, 8)
    part = (3.0 * SECOND[0]) * f + lap_y + lap_z
    part = part - (s2_ref[l, rows, :] * d_y + s3_ref[l, rows, :] * d_z)
    return f, part, d_y, d_z


def forward_yz_kernel(f_ref, s2_ref, s3_ref, part_ref, dy_ref, dz_ref):
    layers, width, depth = part_ref.shape
    masks = z_masks(8, depth)

    @pl.loop(0, width // 8)
    def _(j):
        at = pl.multiple_of(8 * j, 8)
        rows = pl.ds(at, 8)
        for l in range(layers):
            f, part, d_y, d_z = yz_terms(f_ref, s2_ref, s3_ref, l, at, masks)
            part_ref[l, rows, :] = part
            dy_ref[l, rows, :] = d_y
            dz_ref[l, rows, :] = d_z


def forward_x_kernel(
    flags_ref, f_ref, on_ref, off_ref, part_ref, s1_ref, scale_ref, before_ref,
    dx_ref, applied_ref, next_ref, half_ref,
):
    layers, width, _ = part_ref.shape
    zero_pads(next_ref)
    shift = before_ref.shape[1] != width

    @pl.loop(0, width // 16)
    def _(j):
        at = pl.multiple_of(16 * j, 16)
        rows = pl.ds(at, 16)
        wide = pl.ds(at + PAD, 16)
        own = [f_ref[l, wide, :] for l in range(layers)]
        values = x_values(flags_ref, own, on_ref, off_ref, rows)
        for l in range(layers):
            lap, d_x = weighted(x_pairs(values, l))
            applied = part_ref[l, rows, :] + (lap - s1_ref[l, rows, :] * d_x)
            before = before_ref[l, wide if shift else rows, :]
            later = 2.0 * own[l] - before + scale_ref[l, rows, :] * applied
            dx_ref[l, rows, :] = d_x
            applied_ref[l, rows, :] = applied
            next_ref[l, wide, :] = later
            half_ref[l, rows, :] = later.astype(BF16)


def adjoint_yz_kernel(
    first, f_ref, s2_ref, s3_ref, fdy_ref, fdz_ref, fapplied_ref, *refs,
):
    if first:
        part_ref, vel_ref, den_ref = refs
    else:
        vel_in, den_in, part_ref, vel_ref, den_ref = refs
    layers, width, depth = part_ref.shape
    masks = z_masks(8, depth)

    @pl.loop(0, width // 8)
    def _(j):
        at = pl.multiple_of(8 * j, 8)
        rows = pl.ds(at, 8)
        for l in range(layers):
            f, part, d_y, d_z = yz_terms(f_ref, s2_ref, s3_ref, l, at, masks)
            part_ref[l, rows, :] = part
            sum_vel = f * fapplied_ref[l, rows, :]
            sum_den = d_y * fdy_ref[l, rows, :] + d_z * fdz_ref[l, rows, :]
            if not first:
                sum_vel = vel_in[l, rows, :] + sum_vel
                sum_den = den_in[l, rows, :] + sum_den
            vel_ref[l, rows, :] = sum_vel
            den_ref[l, rows, :] = sum_den


def adjoint_x_kernel(
    last, flags_ref, f_ref, on_ref, off_ref, part_ref, s1_ref, scale_ref, before_ref,
    source_ref, fdx_ref, den_in, *refs,
):
    if last:
        vel_in, fapplied_ref, vmodel_ref, q_ref, a_ref, half_ref, den_ref, shot_ref = refs
    else:
        q_ref, a_ref, half_ref, den_ref = refs
    layers, width, _ = part_ref.shape
    zero_pads(a_ref)
    shift = before_ref.shape[1] != width

    @pl.loop(0, width // 16)
    def _(j):
        at = pl.multiple_of(16 * j, 16)
        rows = pl.ds(at, 16)
        wide = pl.ds(at + PAD, 16)
        own = [f_ref[l, wide, :] for l in range(layers)]
        values = x_values(flags_ref, own, on_ref, off_ref, rows)
        for l in range(layers):
            lap, d_x = weighted(x_pairs(values, l))
            applied = part_ref[l, rows, :] + (lap - s1_ref[l, rows, :] * d_x)
            before = before_ref[l, wide if shift else rows, :]
            later = 2.0 * own[l] - before + scale_ref[l, rows, :] * applied
            if not last:
                q_ref[l, rows, :] = later
            adjoint = later + source_ref[l, wide, :]
            a_ref[l, wide, :] = adjoint
            half_ref[l, rows, :] = adjoint.astype(BF16)
            den_ref[l, rows, :] = den_in[l, rows, :] + d_x * fdx_ref[l, rows, :]
            if last:
                total = vel_in[l, rows, :] + adjoint * fapplied_ref[l, rows, :]
                v = vmodel_ref[l, rows, :].astype(F32)
                shot_ref[l, rows, :] = ((2.0 * SPEED) * v * total).astype(BF16)
    if last:
        q_ref[...] = jnp.zeros(q_ref.shape, F32)


def last_yz_kernel(f_ref, fdy_ref, fdz_ref, den_in, den_ref):
    layers, width, depth = den_ref.shape
    masks = z_masks(8, depth)

    @pl.loop(0, width // 8)
    def _(j):
        at = pl.multiple_of(8 * j, 8)
        rows = pl.ds(at, 8)
        for l in range(layers):
            d_y = weighted(y_pairs(f_ref, l, at + PAD, 8))[1]
            d_z = weighted(z_pairs(f_ref[l, pl.ds(at + PAD, 8), :], masks))[1]
            den_ref[l, rows, :] = den_in[l, rows, :] + (
                d_y * fdy_ref[l, rows, :] + d_z * fdz_ref[l, rows, :]
            )


def last_x_kernel(flags_ref, f_ref, on_ref, off_ref, fdx_ref, den_in, scale_ref, dmodel_ref, shot_ref):
    layers, width, _ = shot_ref.shape

    @pl.loop(0, width // 16)
    def _(j):
        at = pl.multiple_of(16 * j, 16)
        rows = pl.ds(at, 16)
        own = [f_ref[l, pl.ds(at + PAD, 16), :] for l in range(layers)]
        values = x_values(flags_ref, own, on_ref, off_ref, rows)
        for l in range(layers):
            d_x = weighted(x_pairs(values, l))[1]
            total = den_in[l, rows, :] + d_x * fdx_ref[l, rows, :]
            density = dmodel_ref[l, rows, :].astype(F32)
            shot_ref[l, rows, :] = (scale_ref[l, rows, :] / density * total).astype(BF16)


def swap_over(axis, count, bit, value):
    return lax.ppermute(value, axis, [(i, i ^ bit) for i in range(count)])


def beside(half):
    groups, count = lax.axis_size("shot"), lax.axis_size("sub")
    on = lax.ppermute(half, "sub", [(i, i ^ 1) for i in range(count)])
    pairs = []
    for s in range(groups):
        for i in range(1, count - 1, 2):
            pairs += [(s * count + i, s * count + i + 1), (s * count + i + 1, s * count + i)]
        if groups % 2 == 0:
            for i in (0, count - 1):
                pairs.append((s * count + i, (s ^ 1) * count + i))
    off = lax.ppermute(half, ("shot", "sub"), pairs)
    return on, off


def bits_of(groups):
    return [1 << k for k in range(groups.bit_length() - 1)]


def fetch(tile, wanted_all, me, bits):
    groups = wanted_all.shape[0]
    held = [(0, tile)]
    for bit in bits[:-1]:
        block = jnp.concatenate([t for _, t in held], axis=0) if len(held) > 1 else held[0][1]
        got = swap_over("shot", groups, bit, block)
        size = tile.shape[0]
        held = held + [
            (offset ^ bit, lax.slice_in_dim(got, n * size, (n + 1) * size, axis=0))
            for n, (offset, _) in enumerate(held)
        ]
    bit = bits[-1]

    def pick(row):
        out = held[0][1]
        for offset, t in held[1:]:
            out = jnp.where(row == (me ^ offset), t, out)
        return out

    far = swap_over("shot", groups, bit, pick(wanted_all[me ^ bit]))
    mine = wanted_all[me]
    return jnp.where((mine & bit) == (me & bit), pick(mine), far)


def give_back(tile, wanted_all, me, bits):
    groups = wanted_all.shape[0]
    mine, bit = wanted_all[me], bits[0]
    got = swap_over("shot", groups, bit, tile)
    parts = [(mine, tile), (wanted_all[me ^ bit], got)]

    def bucket(row):
        total = None
        for target, t in parts:
            term = jnp.where(target == row, t, jnp.zeros_like(t)).astype(F32)
            total = term if total is None else total + term
        return total

    offsets = [0]
    for b in reversed(bits[1:]):
        offsets = offsets + [o ^ b for o in offsets]
    sums = {o: bucket(me ^ o) for o in offsets}
    for b in bits[1:]:
        away = [o for o in sums if o & b]
        got = swap_over(
            "shot", groups, b, jnp.stack([sums[o].astype(BF16) for o in away], axis=0)
        )
        kept = [o ^ b for o in away]
        sums = {o: sums[o] + got[n].astype(F32) for n, o in enumerate(kept)}
    return sums[0]


def split_fetch(tile, wanted_all, me, groups):
    bits = bits_of(groups)
    layers = tile.shape[0] // 2
    return jnp.concatenate(
        [
            fetch(tile[:layers], wanted_all, me, bits),
            fetch(tile[layers:], wanted_all, me, bits[::-1]),
        ],
        axis=0,
    )


def split_give_back(tile, wanted_all, me, groups):
    bits = bits_of(groups)
    layers = tile.shape[0] // 2
    return jnp.concatenate(
        [
            give_back(tile[:layers], wanted_all, me, bits),
            give_back(tile[layers:], wanted_all, me, bits[::-1]),
        ],
        axis=0,
    )


def body(vel_model, den_model, cover, receivers, observed, p_now, p_before, q_now, q_before):
    me = lax.axis_index("shot")
    column = lax.axis_index("sub")
    groups, columns = lax.axis_size("shot"), lax.axis_size("sub")
    layers, width, depth = p_now.shape[1:]
    tall = width + 2 * PAD
    narrow, padded = ((layers, width, depth), F32), ((layers, tall, depth), F32)
    half = ((layers, width, depth), BF16)
    wanted_all = cover[:, column]

    even = (column & 1) == 0
    valid = (column > 0) & (column < columns - 1)
    flags = jnp.stack([even, valid]).astype(jnp.int32)

    den = split_fetch(den_model[0], wanted_all, me, groups)
    vel = split_fetch(vel_model[0], wanted_all, me, groups)

    p, q, p_half, q_half = call(prepare_kernel, [padded, padded, half, half], [p_now[0], q_now[0]], [VM] * 2)

    cells = layers * width * depth
    local = receivers[0] - column * cells
    inside = (local >= 0) & (local < cells)
    line = local // depth
    row = jnp.where(inside, line + (2 * PAD) * (line // width) + PAD, -1)
    lane = local & (depth - 1) if depth & (depth - 1) == 0 else local % depth
    n_rec = row.shape[0]
    ints = ((n_rec,), jnp.int32)
    lists = call(
        list_kernel, [ints, ints, ints, ((1,), jnp.int32)], [row, lane], [SM, SM], [SM] * 4
    )
    seen = observed[0]
    list_specs = [SM] * 5

    log_den, s2, s3 = call(log_kernel, [padded, narrow, narrow], [den], [VM])
    den_on, den_off = beside(den)
    s1, scale = call(
        slope_x_kernel, [narrow, narrow], [flags, log_den, den_on, den_off, vel], [SM] + [VM] * 4
    )

    stored, sources = [], []
    before = p_before[0]
    for step in range(ITERS):
        on, off = beside(p_half)
        part, d_y, d_z = call(forward_yz_kernel, [narrow] * 3, [p, s2, s3], [VM] * 3)
        if step > 0:
            sources += call(
                lambda *refs, n=step - 1: receivers_kernel(n, *refs),
                [padded], [p, *lists, seen], [VM] + list_specs,
            )
        d_x, applied, later, p_half = call(
            forward_x_kernel, [narrow, narrow, padded, half],
            [flags, p, on, off, part, s1, scale, before], [SM] + [VM] * 7,
        )
        stored.append((applied, d_x, d_y, d_z))
        before, p = p, later

    a, a_half = call(
        lambda *refs: first_adjoint_kernel(ITERS - 1, *refs),
        [padded, half], [p, q, *lists, seen], [VM, VM] + list_specs,
    )
    before, current = q_before[0], q
    sums = ()
    for step in range(ITERS - 1):
        f_applied, f_dx, f_dy, f_dz = stored[ITERS - 1 - step]
        last = step == ITERS - 2
        on, off = beside(a_half)
        part, sum_vel, sum_den = call(
            lambda *refs, first=step == 0: adjoint_yz_kernel(first, *refs),
            [narrow] * 3, [a, s2, s3, f_dy, f_dz, f_applied, *sums], [VM] * (6 + len(sums)),
        )
        extra = [sum_vel, stored[0][0], vel] if last else []
        later, a, a_half, sum_den, *shot = call(
            lambda *refs, last=last: adjoint_x_kernel(last, *refs),
            [((8, 128), F32) if last else narrow, padded, half, narrow] + ([half] if last else []),
            [flags, a, on, off, part, s1, scale, before, sources[ITERS - 2 - step], f_dx, sum_den, *extra],
            [SM] + [VM] * (10 + len(extra)),
        )
        before, current = current, later
        sums = (sum_vel, sum_den)
    shot_vel = shot[0]
    _, f_dx, f_dy, f_dz = stored[0]
    on, off = beside(a_half)
    grad_vel = split_give_back(shot_vel, wanted_all, me, groups)
    (sum_den,) = call(last_yz_kernel, [narrow], [a, f_dy, f_dz, sum_den], [VM] * 4)
    (shot_den,) = call(
        last_x_kernel, [half], [flags, a, on, off, f_dx, sum_den, scale, den], [SM] + [VM] * 7
    )
    grad_den = split_give_back(shot_den, wanted_all, me, groups)
    return grad_vel[None], grad_den[None]


def solution(mesh):
    return jax.shard_map(
        body,
        mesh=mesh,
        in_specs=(
            P("shot", "sub", None, None),
            P("shot", "sub", None, None),
            P(),
            P("shot", None),
            P("shot", None, None),
            P("shot", "sub", None, None),
            P("shot", "sub", None, None),
            P("shot", "sub", None, None),
            P("shot", "sub", None, None),
        ),
        out_specs=(P("shot", "sub", None, None), P("shot", "sub", None, None)),
        check_vma=False,
    )
```

time: 293 us -> 156 us (0.53)
  Pallas kernels: 0 us -> 72.8 us
  other arithmetic: 73.5 us -> 2.77 us
  waiting for transfers between devices: 70.7 us -> 22.9 us
  local copies, waits for them, and re-layouts: 49 us -> 16.7 us
  starting transfers between devices: 60.8 us -> 33.1 us
  blocking collectives: 21.9 us -> 0 us
  between operations: 14.8 us -> 7.1 us
    pallas_call x0 -> x24, Pallas kernels: none -> 72.8 us  [call(): pl.pallas_call(kernel, out_shape=outs, in_specs=list(specs), out_specs=tu...]
    unnamed x4 -> x0, waiting for transfers between devices: 65.5 us -> none
    convert_element_type x23 -> x1, other arithmetic: 46.4 us -> 0.08 us  [body(): flags = jnp.stack([even, valid]).astype(jnp.int32)]
    gather x4 -> x0, local copies, waits for them, and re-layouts: 43.2 us -> none  [body(): sampled = current.reshape(-1)[station]]
    ppermute x18 -> x34, starting transfers between devices: 56.3 us -> 33.1 us  [the longest x16 17.6 us: swap_over(): return lax.ppermute(value, axis, [(i, i ^ bit) for i in range(count)])]
    all_to_all x1 -> x0, blocking collectives: 21.9 us -> none  [body(): lax.all_to_all(send_den, 'shot', split_axis=0, concat_axis=0, tiled=True)]
    ppermute x18 -> x34, waiting for transfers between devices: 2.57 us -> 22.9 us  [the longest x16 17 us: swap_over(): return lax.ppermute(value, axis, [(i, i ^ bit) for i in range(count)])]
    scatter-add x4 -> x0, other arithmetic: 17.3 us -> none  [body(): source = jnp.zeros((cells,), jnp.float32).at[station].add(misfits[ITERS -...]
  transfers between devices with their start and end apart: 21 -> 34, of which waited for: 6 -> 10; matrix products, arithmetic and copies ran while one was open for 16% -> 2% of each run, Pallas kernels for 0% -> 35%
where the time goes in v1:
time: 156 us; the launch traced here: 155 us
  Pallas kernels  72.8 us (47%)
  starting transfers between devices  33.1 us (21%)
  waiting for transfers between devices  22.9 us (15%)
  local copies, waits for them, and re-layouts  16.7 us (11%)
  between operations  7.1 us (5%)
  other arithmetic  2.77 us (2%)
    pallas_call x24, Pallas kernels, call(): pl.pallas_call(kernel, out_shape=outs, in_specs=list(specs), out_specs=tu...  72.8 us
    ppermute x16, starting transfers between devices, swap_over(): return lax.ppermute(value, axis, [(i, i ^ bit) for i in range(count)])  17.6 us
    ppermute x16, waiting for transfers between devices, swap_over(): return lax.ppermute(value, axis, [(i, i ^ bit) for i in range(count)])  17 us
    unnamed x84, local copies, waits for them, and re-layouts  16 us
    ppermute x9, starting transfers between devices, beside(): off = lax.ppermute(half, ('shot', 'sub'), pairs)  13 us
    ppermute x9, waiting for transfers between devices, beside(): off = lax.ppermute(half, ('shot', 'sub'), pairs)  5.86 us
  transfers between devices with their start and end apart: 34, of which 10 were waited for; matrix products, arithmetic and copies ran while one was open for 2% of the time, Pallas kernels for 35%

profile of v1, /device:TPU:0, one launch (start us, length us, event | category | flops | bytes accessed | tf_op | source)
XLA Modules:
  0.0 155.4 jit_solution(7446629943160661165)
XLA Ops:
  5.3 2.5 %collective-permute-start.1 = (bf16[4,320,128]{2,1,0:T(8,128)(2,1)}, bf16[4,320,128]{2,1,0:T(8,128)(2,1)S(1)}, u32[]{:S(2)}, u32[]{:S(2)}) collective-permute-start(bf16[4,320,128]{2,1,0:T(8,128)(2,1)} %get-tuple-element.64), channel_id=1, source_target_pairs={{1,2},{2,1},{3,4},{4,3},{5,6},{6,5},{0,8},{7,15},{9,10},{10,9},{11... | collective-permute-start | bytes 983048 | tf_op jit(solution)/shard_map/ppermute | solution.py:353
  7.9 2.0 %collective-permute-start.4 = (bf16[2,320,128]{2,1,0:T(8,128)(2,1)S(1)}, bf16[2,320,128]{2,1,0:T(8,128)(2,1)S(1)}, u32[]{:S(2)}, u32[]{:S(2)}) collective-permute-start(bf16[2,320,128]{2,1,0:T(8,128)(2,1)S(1)} %get-tuple-element.143), channel_id=1, source_target_pairs={{0,16},{8,24},{16,0},{24,8},{1,17},{9,25},{17,1},{25,9},{2,18},{10... | collective-permute-start | bytes 491528 | tf_op jit(solution)/shard_map/ppermute | solution.py:340
  15.4 1.1 collective-permute-done.2
  16.5 2.0 %collective-permute-start.8 = (bf16[2,320,128]{2,1,0:T(8,128)(2,1)S(1)}, bf16[2,320,128]{2,1,0:T(8,128)(2,1)S(1)}, u32[]{:S(2)}, u32[]{:S(2)}) collective-permute-start(bf16[2,320,128]{2,1,0:T(8,128)(2,1)S(1)} %get-tuple-element.136), channel_id=1, source_target_pairs={{0,8},{8,0},{16,24},{24,16},{1,9},{9,1},{17,25},{25,17},{2,10},{10... | collective-permute-start | bytes 491528 | tf_op jit(solution)/shard_map/ppermute | solution.py:340
  18.6 1.6 %collective-permute-start.3 = (bf16[2,320,128]{2,1,0:T(8,128)(2,1)S(1)}, bf16[2,320,128]{2,1,0:T(8,128)(2,1)S(1)}, u32[]{:S(2)}, u32[]{:S(2)}) collective-permute-start(bf16[2,320,128]{2,1,0:T(8,128)(2,1)S(1)} %get-tuple-element.140), channel_id=1, source_target_pairs={{0,16},{8,24},{16,0},{24,8},{1,17},{9,25},{17,1},{25,9},{2,18},{10... | collective-permute-start | bytes 491528 | tf_op jit(solution)/shard_map/ppermute | solution.py:340
  20.7 2.9 %collective-permute-done.8 = bf16[2,320,128]{2,1,0:T(8,128)(2,1)S(1)} collective-permute-done((bf16[2,320,128]{2,1,0:T(8,128)(2,1)S(1)}, bf16[2,320,128]{2,1,0:T(8,128)(2,1)S(1)}, u32[]{:S(2)}, u32[]{:S(2)}) %collective-permute-start.8) | collective-permute-done | bytes 163872 | tf_op jit(solution)/shard_map/ppermute | solution.py:340
  23.6 2.1 %collective-permute-start.11 = (bf16[2,320,128]{2,1,0:T(8,128)(2,1)S(1)}, bf16[2,320,128]{2,1,0:T(8,128)(2,1)S(1)}, u32[]{:S(2)}, u32[]{:S(2)}) collective-permute-start(bf16[2,320,128]{2,1,0:T(8,128)(2,1)S(1)} %get-tuple-element.135), channel_id=1, source_target_pairs={{0,8},{8,0},{16,24},{24,16},{1,9},{9,1},{17,25},{25,17},{2,10},{10... | collective-permute-start | bytes 491528 | tf_op jit(solution)/shard_map/ppermute | solution.py:340
  25.7 1.5 collective-permute-start.9
  27.4 4.6 %shard_map.105 = (f32[4,336,128]{2,1,0:T(8,128)S(1)}, f32[4,320,128]{2,1,0:T(8,128)S(1)}, f32[4,320,128]{2,1,0:T(8,128)S(1)}) custom-call(bf16[4,320,128]{2,1,0:T(8,128)(2,1)S(1)} %pad_maximum_fusion.den_ref.dmodel_ref), custom_call_target="tpu_custom_call" | custom-call | bytes 2326528 | tf_op jit(solution)/shard_map/pallas_call | solution.py:25
  32.0 4.3 %shard_map.106 = (f32[4,320,128]{2,1,0:T(8,128)S(1)}, f32[4,320,128]{2,1,0:T(8,128)S(1)}, f32[4,320,128]{2,1,0:T(8,128)S(1)}) custom-call(f32[4,336,128]{2,1,0:T(8,128)S(1)} %get-tuple-element.63.f_ref.before_ref, f32[4,320,128]{2,1,0:T(8,128)S(1)} %get-tuple-element.65.s2_ref.refs_1_, f32[4,320,128]{2,1,0:T(8,128)S(1)} %get-tuple-element.66.s3_ref.refs_2_), custom_call_target="tpu_custom_call" | custom-call | bytes 3964928 | tf_op jit(solution)/shard_map/pallas_call | solution.py:25
  38.0 1.7 %collective-permute-start.7 = (bf16[4,320,128]{2,1,0:T(8,128)(2,1)S(1)}, bf16[4,320,128]{2,1,0:T(8,128)(2,1)S(1)}, u32[]{:S(2)}, u32[]{:S(2)}) collective-permute-start(bf16[4,320,128]{2,1,0:T(8,128)(2,1)S(1)} %pad_maximum_fusion.den_ref.dmodel_ref), channel_id=1, source_target_pairs={{1,2},{2,1},{3,4},{4,3},{5,6},{6,5},{0,8},{7,15},{9,10},{10,9},{11... | collective-permute-start | bytes 983048 | tf_op jit(solution)/shard_map/ppermute | solution.py:353
  39.8 5.3 %collective-permute-done.7.off_ref = bf16[4,320,128]{2,1,0:T(8,128)(2,1)S(1)} collective-permute-done((bf16[4,320,128]{2,1,0:T(8,128)(2,1)S(1)}, bf16[4,320,128]{2,1,0:T(8,128)(2,1)S(1)}, u32[]{:S(2)}, u32[]{:S(2)}) %collective-permute-start.7) | collective-permute-done | bytes 327712 | tf_op jit(solution)/shard_map/ppermute | solution.py:353
  45.1 1.2 shard_map.107
  49.7 1.5 shard_map.108
  51.3 1.7 %collective-permute-start.13 = (bf16[4,320,128]{2,1,0:T(8,128)(2,1)S(1)}, bf16[4,320,128]{2,1,0:T(8,128)(2,1)S(1)}, u32[]{:S(2)}, u32[]{:S(2)}) collective-permute-start(bf16[4,320,128]{2,1,0:T(8,128)(2,1)S(1)} %get-tuple-element.72), channel_id=1, source_target_pairs={{1,2},{2,1},{3,4},{4,3},{5,6},{6,5},{0,8},{7,15},{9,10},{10,9},{11... | collective-permute-start | bytes 983048 | tf_op jit(solution)/shard_map/ppermute | solution.py:353
  53.0 4.3 %shard_map.109 = (f32[4,320,128]{2,1,0:T(8,128)S(1)}, f32[4,320,128]{2,1,0:T(8,128)S(1)}, f32[4,320,128]{2,1,0:T(8,128)S(1)}) custom-call(f32[4,336,128]{2,1,0:T(8,128)S(1)} %get-tuple-element.71.f_ref.before_ref.refs_0_, f32[4,320,128]{2,1,0:T(8,128)S(1)} %get-tuple-element.65.s2_ref.refs_1_, f32[4,320,128]{2,1,0:T(8,128)S(1)} %get-tuple-element.66.s3_ref.refs_2_), custom_call_target="tpu_custom_call" | custom-call | bytes 3964928 | tf_op jit(solution)/shard_map/pallas_call | solution.py:25
  58.4 2.2 %shard_map.110 = (f32[4,320,128]{2,1,0:T(8,128)S(1)}, f32[4,320,128]{2,1,0:T(8,128)S(1)}, f32[4,336,128]{2,1,0:T(8,128)S(1)}, bf16[4,320,128]{2,1,0:T(8,128)(2,1)}) custom-call(s32[2]{0:T(128)S(1)} %add_convert_fusion.4.flags_ref.refs_0_, f32[4,336,128]{2,1,0:T(8,128)S(1)} %get-tuple-element.71.f_ref.before_ref.refs_0_, ...), custom_call_target="tpu_custom_call" | custom-call | bytes 6324232 | tf_op jit(solution)/shard_map/pallas_call | solution.py:25
  63.3 1.7 %collective-permute-start.15 = (bf16[4,320,128]{2,1,0:T(8,128)(2,1)}, bf16[4,320,128]{2,1,0:T(8,128)(2,1)}, u32[]{:S(2)}, u32[]{:S(2)}) collective-permute-start(bf16[4,320,128]{2,1,0:T(8,128)(2,1)} %get-tuple-element.75), channel_id=1, source_target_pairs={{1,2},{2,1},{3,4},{4,3},{5,6},{6,5},{0,8},{7,15},{9,10},{10,9},{11... | collective-permute-start | bytes 983048 | tf_op jit(solution)/shard_map/ppermute | solution.py:353
  64.9 1.1 copy-done.1
  66.0 4.3 %shard_map.111 = (f32[4,320,128]{2,1,0:T(8,128)S(1)}, f32[4,320,128]{2,1,0:T(8,128)S(1)}, f32[4,320,128]{2,1,0:T(8,128)S(1)}) custom-call(f32[4,336,128]{2,1,0:T(8,128)S(1)} %copy-done.1, f32[4,320,128]{2,1,0:T(8,128)S(1)} %get-tuple-element.65.s2_ref.refs_1_, f32[4,320,128]{2,1,0:T(8,128)S(1)} %get-tuple-element.66.s3_ref.refs_2_), custom_call_target="tpu_custom_call" | custom-call | bytes 3964928 | tf_op jit(solution)/shard_map/pallas_call | solution.py:25
  70.7 2.0 %shard_map.112 = (f32[4,320,128]{2,1,0:T(8,128)S(1)}, f32[4,320,128]{2,1,0:T(8,128)S(1)}, f32[4,336,128]{2,1,0:T(8,128)S(1)}, bf16[4,320,128]{2,1,0:T(8,128)(2,1)S(1)}) custom-call(s32[2]{0:T(128)S(1)} %add_convert_fusion.4.flags_ref.refs_0_, f32[4,336,128]{2,1,0:T(8,128)S(1)} %copy-done.2, bf16[4,320,128]{2,1,0:T(8,128)(2,1)} %collective-permute-done.14.on_ref, ...), custom_call_target="tpu_custom_call" | custom-call | bytes 6324232 | tf_op jit(solution)/shard_map/pallas_call | solution.py:25
  72.9 1.7 %collective-permute-start.17 = (bf16[4,320,128]{2,1,0:T(8,128)(2,1)S(1)}, bf16[4,320,128]{2,1,0:T(8,128)(2,1)S(1)}, u32[]{:S(2)}, u32[]{:S(2)}) collective-permute-start(bf16[4,320,128]{2,1,0:T(8,128)(2,1)S(1)} %get-tuple-element.78), channel_id=1, source_target_pairs={{1,2},{2,1},{3,4},{4,3},{5,6},{6,5},{0,8},{7,15},{9,10},{10,9},{11... | collective-permute-start | bytes 983048 | tf_op jit(solution)/shard_map/ppermute | solution.py:353
  74.6 5.3 %shard_map.115 = (s32[512]{0:T(512)S(1)}, s32[512]{0:T(512)S(1)}, s32[512]{0:T(512)S(1)}, s32[1]{0:T(128)}) custom-call(s32[512]{0:T(512)S(1)} %get-tuple-element.145.row_ref, s32[512]{0:T(512)S(1)} %get-tuple-element.144.lane_ref), custom_call_target="tpu_custom_call" | custom-call | bytes 10244 | tf_op jit(solution)/shard_map/pallas_call | solution.py:25
  79.9 4.3 %shard_map.113 = (f32[4,320,128]{2,1,0:T(8,128)S(1)}, f32[4,320,128]{2,1,0:T(8,128)S(1)}, f32[4,320,128]{2,1,0:T(8,128)S(1)}) custom-call(f32[4,336,128]{2,1,0:T(8,128)S(1)} %get-tuple-element.77.f_ref.refs_0_, f32[4,320,128]{2,1,0:T(8,128)S(1)} %get-tuple-element.65.s2_ref.refs_1_, f32[4,320,128]{2,1,0:T(8,128)S(1)} %get-tuple-element.66.s3_ref.refs_2_), custom_call_target="tpu_custom_call" | custom-call | bytes 3964928 | tf_op jit(solution)/shard_map/pallas_call | solution.py:25
  84.3 2.2 %shard_map.114 = (f32[4,320,128]{2,1,0:T(8,128)S(1)}, f32[4,320,128]{2,1,0:T(8,128)S(1)}, f32[4,336,128]{2,1,0:T(8,128)S(1)}, bf16[4,320,128]{2,1,0:T(8,128)(2,1)}) custom-call(s32[2]{0:T(128)S(1)} %add_convert_fusion.4.flags_ref.refs_0_, f32[4,336,128]{2,1,0:T(8,128)S(1)} %get-tuple-element.77.f_ref.refs_0_, ...), custom_call_target="tpu_custom_call" | custom-call | bytes 6324232 | tf_op jit(solution)/shard_map/pallas_call | solution.py:25
  87.2 2.6 %shard_map.116 = (f32[4,336,128]{2,1,0:T(8,128)S(1)}, bf16[4,320,128]{2,1,0:T(8,128)(2,1)S(1)}) custom-call(f32[4,336,128]{2,1,0:T(8,128)S(1)} %get-tuple-element.80.refs_0_, f32[4,336,128]{2,1,0:T(8,128)S(1)} %copy-done.10, s32[512]{0:T(512)S(1)} %get-tuple-element.82.refs_2_.refs_1_, s32[512]{0:T(512)S(1)} %get-tuple-element.83.refs_3_.refs_2_, ...), custom_call_target="tpu_custom_call" | custom-call | bytes 2406404 | tf_op jit(solution)/shard_map/pallas_call | solution.py:25
  90.5 2.5 %shard_map.118.refs_8_ = f32[4,336,128]{2,1,0:T(8,128)S(1)} custom-call(f32[4,336,128]{2,1,0:T(8,128)S(1)} %get-tuple-element.77.f_ref.refs_0_, s32[512]{0:T(512)S(1)} %get-tuple-element.82.refs_2_.refs_1_, s32[512]{0:T(512)S(1)} %get-tuple-element.83.refs_3_.refs_2_, s32[512]{0:T(512)S(1)} %get-tuple-element.84.refs_4_.refs_3_, ...), custom_call_target="tpu_custom_call" | custom-call | bytes 1390596 | tf_op jit(solution)/shard_map/pallas_call | solution.py:25
  93.1 4.3 %shard_map.117 = (f32[4,320,128]{2,1,0:T(8,128)S(1)}, f32[4,320,128]{2,1,0:T(8,128)S(1)}, f32[4,320,128]{2,1,0:T(8,128)S(1)}) custom-call(f32[4,336,128]{2,1,0:T(8,128)S(1)} %get-tuple-element.86.refs_0_.refs_1_, f32[4,320,128]{2,1,0:T(8,128)S(1)} %get-tuple-element.65.s2_ref.refs_1_, f32[4,320,128]{2,1,0:T(8,128)S(1)} %get-tuple-element.66.s3_ref.refs_2_, ...), custom_call_target="tpu_custom_call" | custom-call | bytes 5931008 | tf_op jit(solution)/shard_map/pallas_call | solution.py:25
  97.5 1.6 %shard_map.119 = (f32[4,320,128]{2,1,0:T(8,128)S(1)}, f32[4,336,128]{2,1,0:T(8,128)S(1)}, bf16[4,320,128]{2,1,0:T(8,128)(2,1)S(1)}, f32[4,320,128]{2,1,0:T(8,128)S(1)}) custom-call(s32[2]{0:T(128)S(1)} %add_convert_fusion.4.flags_ref.refs_0_, f32[4,336,128]{2,1,0:T(8,128)S(1)} %get-tuple-element.86.refs_0_.refs_1_, ...), custom_call_target="tpu_custom_call" | custom-call | bytes 8290312 | tf_op jit(solution)/shard_map/pallas_call | solution.py:25
  99.7 1.5 collective-permute-start.21
  101.2 2.5 %shard_map.121.refs_8_ = f32[4,336,128]{2,1,0:T(8,128)S(1)} custom-call(f32[4,336,128]{2,1,0:T(8,128)S(1)} %copy-done.2, s32[512]{0:T(512)S(1)} %get-tuple-element.82.refs_2_.refs_1_, s32[512]{0:T(512)S(1)} %get-tuple-element.83.refs_3_.refs_2_, s32[512]{0:T(512)S(1)} %get-tuple-element.84.refs_4_.refs_3_, s32[1]{0:T(128)} %get-tuple-element.85.refs_5_.refs_4_, ...), custom_call_target="tpu_custom_call" | custom-call | bytes 1390596 | tf_op jit(solution)/shard_map/pallas_call | solution.py:25
  103.7 4.3 %shard_map.120 = (f32[4,320,128]{2,1,0:T(8,128)S(1)}, f32[4,320,128]{2,1,0:T(8,128)S(1)}, f32[4,320,128]{2,1,0:T(8,128)S(1)}) custom-call(f32[4,336,128]{2,1,0:T(8,128)S(1)} %get-tuple-element.94.refs_0_.refs_1_, f32[4,320,128]{2,1,0:T(8,128)S(1)} %get-tuple-element.65.s2_ref.refs_1_, f32[4,320,128]{2,1,0:T(8,128)S(1)} %get-tuple-element.66.s3_ref.refs_2_, ...), custom_call_target="tpu_custom_call" | custom-call | bytes 7241728 | tf_op jit(solution)/shard_map/pallas_call | solution.py:25
  108.1 2.4 %shard_map.122 = (f32[4,320,128]{2,1,0:T(8,128)}, f32[4,336,128]{2,1,0:T(8,128)S(1)}, bf16[4,320,128]{2,1,0:T(8,128)(2,1)S(1)}, f32[4,320,128]{2,1,0:T(8,128)S(1)}) custom-call(s32[2]{0:T(128)S(1)} %add_convert_fusion.4.flags_ref.refs_0_, f32[4,336,128]{2,1,0:T(8,128)S(1)} %get-tuple-element.94.refs_0_.refs_1_, ...), custom_call_target="tpu_custom_call" | custom-call | bytes 8323080 | tf_op jit(solution)/shard_map/pallas_call | solution.py:25
  111.2 2.5 %shard_map.124.refs_8_ = f32[4,336,128]{2,1,0:T(8,128)S(1)} custom-call(f32[4,336,128]{2,1,0:T(8,128)S(1)} %get-tuple-element.71.f_ref.before_ref.refs_0_, s32[512]{0:T(512)S(1)} %get-tuple-element.82.refs_2_.refs_1_, s32[512]{0:T(512)S(1)} %get-tuple-element.83.refs_3_.refs_2_, s32[512]{0:T(512)S(1)} %get-tuple-element.84.refs_4_.refs_3_, ...), custom_call_target="tpu_custom_call" | custom-call | bytes 1390596 | tf_op jit(solution)/shard_map/pallas_call | solution.py:25
  113.8 4.3 %shard_map.123 = (f32[4,320,128]{2,1,0:T(8,128)S(1)}, f32[4,320,128]{2,1,0:T(8,128)S(1)}, f32[4,320,128]{2,1,0:T(8,128)S(1)}) custom-call(f32[4,336,128]{2,1,0:T(8,128)S(1)} %get-tuple-element.104.refs_0_.refs_1_, f32[4,320,128]{2,1,0:T(8,128)S(1)} %get-tuple-element.65.s2_ref.refs_1_, f32[4,320,128]{2,1,0:T(8,128)S(1)} %get-tuple-element.66.s3_ref.refs_2_, ...), custom_call_target="tpu_custom_call" | custom-call | bytes 7241728 | tf_op jit(solution)/shard_map/pallas_call | solution.py:25
  118.2 2.5 %shard_map.125 = (f32[8,128]{1,0:T(8,128)}, f32[4,336,128]{2,1,0:T(8,128)S(1)}, bf16[4,320,128]{2,1,0:T(8,128)(2,1)}, f32[4,320,128]{2,1,0:T(8,128)S(1)}, bf16[4,320,128]{2,1,0:T(8,128)(2,1)S(1)}) custom-call(s32[2]{0:T(128)S(1)} %add_convert_fusion.4.flags_ref.refs_0_, f32[4,336,128]{2,1,0:T(8,128)S(1)} %get-tuple-element.104.refs_0_.refs_1_, ...), custom_call_target="tpu_custom_call" | custom-call | bytes 9605128 | tf_op jit(solution)/shard_map/pallas_call | solution.py:25
  122.0 1.2 collective-permute-start.29
  126.0 1.5 collective-permute-start.26
  127.5 1.1 copy-done.23
  128.6 4.3 %shard_map.126.den_in = f32[4,320,128]{2,1,0:T(8,128)S(1)} custom-call(f32[4,336,128]{2,1,0:T(8,128)S(1)} %get-tuple-element.118.f_ref, f32[4,320,128]{2,1,0:T(8,128)S(1)} %copy-done.13, f32[4,320,128]{2,1,0:T(8,128)S(1)} %copy-done.15, f32[4,320,128]{2,1,0:T(8,128)S(1)} %copy-done.23), custom_call_target="tpu_custom_call" | custom-call | bytes 3309568 | tf_op jit(solution)/shard_map/pallas_call | solution.py:25
  132.9 1.8 %shard_map.127 = bf16[4,320,128]{2,1,0:T(8,128)(2,1)S(1)} custom-call(s32[2]{0:T(128)S(1)} %add_convert_fusion.4.flags_ref.refs_0_, f32[4,336,128]{2,1,0:T(8,128)S(1)} %get-tuple-element.118.f_ref, bf16[4,320,128]{2,1,0:T(8,128)(2,1)} %collective-permute-done.28.on_ref, bf16[4,320,128]{2,1,0:T(8,128)(2,1)} %collective-permute-done.29.off_ref, ...), custom_call_target="tpu_custom_call" | custom-call | bytes 3964936 | tf_op jit(solution)/shard_map/pallas_call | solution.py:25
  134.8 1.9 %collective-permute-start.30 = (bf16[2,320,128]{2,1,0:T(8,128)(2,1)S(1)}, bf16[2,320,128]{2,1,0:T(8,128)(2,1)S(1)}, u32[]{:S(2)}, u32[]{:S(2)}) collective-permute-start(bf16[2,320,128]{2,1,0:T(8,128)(2,1)S(1)} %get-tuple-element.126), channel_id=1, source_target_pairs={{0,8},{8,0},{16,24},{24,16},{1,9},{9,1},{17,25},{25,17},{2,10},{10... | collective-permute-start | bytes 491528 | tf_op jit(solution)/shard_map/ppermute | solution.py:340
  136.8 2.0 %collective-permute-start.32 = (bf16[2,320,128]{2,1,0:T(8,128)(2,1)S(1)}, bf16[2,320,128]{2,1,0:T(8,128)(2,1)S(1)}, u32[]{:S(2)}, u32[]{:S(2)}) collective-permute-start(bf16[2,320,128]{2,1,0:T(8,128)(2,1)S(1)} %get-tuple-element.127), channel_id=1, source_target_pairs={{0,16},{8,24},{16,0},{24,8},{1,17},{9,25},{17,1},{25,9},{2,18},{10... | collective-permute-start | bytes 491528 | tf_op jit(solution)/shard_map/ppermute | solution.py:340
  138.8 1.9 %collective-permute-done.30 = bf16[2,320,128]{2,1,0:T(8,128)(2,1)S(1)} collective-permute-done((bf16[2,320,128]{2,1,0:T(8,128)(2,1)S(1)}, bf16[2,320,128]{2,1,0:T(8,128)(2,1)S(1)}, u32[]{:S(2)}, u32[]{:S(2)}) %collective-permute-start.30) | collective-permute-done | bytes 163872 | tf_op jit(solution)/shard_map/ppermute | solution.py:340
  141.1 2.8 %collective-permute-done.25 = bf16[1,2,320,128]{3,2,1,0:T(8,128)(2,1)S(1)} collective-permute-done((bf16[1,2,320,128]{3,2,1,0:T(8,128)(2,1)S(1)}, bf16[1,2,320,128]{3,2,1,0:T(8,128)(2,1)S(1)}, u32[]{:S(2)}, u32[]{:S(2)}) %collective-permute-start.25) | collective-permute-done | bytes 163872 | tf_op jit(solution)/shard_map/ppermute | solution.py:340
  144.3 2.9 %collective-permute-done.32 = bf16[2,320,128]{2,1,0:T(8,128)(2,1)S(1)} collective-permute-done((bf16[2,320,128]{2,1,0:T(8,128)(2,1)S(1)}, bf16[2,320,128]{2,1,0:T(8,128)(2,1)S(1)}, u32[]{:S(2)}, u32[]{:S(2)}) %collective-permute-start.32) | collective-permute-done | bytes 163872 | tf_op jit(solution)/shard_map/ppermute | solution.py:340
  147.2 1.8 %collective-permute-done.31 = bf16[1,2,320,128]{3,2,1,0:T(8,128)(2,1)S(1)} collective-permute-done((bf16[1,2,320,128]{3,2,1,0:T(8,128)(2,1)S(1)}, bf16[1,2,320,128]{3,2,1,0:T(8,128)(2,1)S(1)}, u32[]{:S(2)}, u32[]{:S(2)}) %collective-permute-start.31) | collective-permute-done | bytes 163872 | tf_op jit(solution)/shard_map/ppermute | solution.py:340
  150.8 3.7 %collective-permute-done.33 = bf16[1,2,320,128]{3,2,1,0:T(8,128)(2,1)S(1)} collective-permute-done((bf16[1,2,320,128]{3,2,1,0:T(8,128)(2,1)S(1)}, bf16[1,2,320,128]{3,2,1,0:T(8,128)(2,1)S(1)}, u32[]{:S(2)}, u32[]{:S(2)}) %collective-permute-start.33) | collective-permute-done | bytes 163872 | tf_op jit(solution)/shard_map/ppermute | solution.py:340
  (150 shorter events, 25.6 us)
Async XLA Ops:
  2.8 4.9 %copy-start.38 = (bf16[1,4,320,128]{3,2,1,0:T(8,128)(2,1)S(1)}, bf16[1,4,320,128]{3,2,1,0:T(8,128)(2,1)}, u32[]{:S(2)}) copy-start(bf16[1,4,320,128]{3,2,1,0:T(8,128)(2,1)} %param.10) | copy-start | bytes 983044
  4.8 27.3 %copy-start.3 = (f32[4,336,128]{2,1,0:T(8,128)}, f32[4,336,128]{2,1,0:T(8,128)S(1)}, u32[]{:S(2)}) copy-start(f32[4,336,128]{2,1,0:T(8,128)S(1)} %get-tuple-element.63.f_ref.before_ref) | copy-start | bytes 2064388
  4.8 5.1 %copy-start.39 = (bf16[1,4,320,128]{3,2,1,0:T(8,128)(2,1)S(1)}, bf16[1,4,320,128]{3,2,1,0:T(8,128)(2,1)}, u32[]{:S(2)}) copy-start(bf16[1,4,320,128]{3,2,1,0:T(8,128)(2,1)} %param.9) | copy-start | bytes 983044
  4.8 41.5 %collective-permute-start = (bf16[4,320,128]{2,1,0:T(8,128)(2,1)}, bf16[4,320,128]{2,1,0:T(8,128)(2,1)S(1)}, u32[]{:S(2)}, u32[]{:S(2)}) collective-permute-start(bf16[4,320,128]{2,1,0:T(8,128)(2,1)} %get-tuple-element.64), channel_id=1, source_target_pairs={{0,1},{1,0},{2,3},{3,2},{4,5},{5,4},{6,7},{7,6},{8,9},{9,8},{10,11... | collective-permute-start | bytes 983048 | tf_op jit(solution)/shard_map/ppermute | solution.py:345
  5.3 41.8 %collective-permute-start.1 = (bf16[4,320,128]{2,1,0:T(8,128)(2,1)}, bf16[4,320,128]{2,1,0:T(8,128)(2,1)S(1)}, u32[]{:S(2)}, u32[]{:S(2)}) collective-permute-start(bf16[4,320,128]{2,1,0:T(8,128)(2,1)} %get-tuple-element.64), channel_id=1, source_target_pairs={{1,2},{2,1},{3,4},{4,3},{5,6},{6,5},{0,8},{7,15},{9,10},{10,9},{11... | collective-permute-start | bytes 983048 | tf_op jit(solution)/shard_map/ppermute | solution.py:353
  7.8 8.7 %collective-permute-start.2 = (bf16[2,320,128]{2,1,0:T(8,128)(2,1)S(1)}, bf16[2,320,128]{2,1,0:T(8,128)(2,1)S(1)}, u32[]{:S(2)}, u32[]{:S(2)}) collective-permute-start(bf16[2,320,128]{2,1,0:T(8,128)(2,1)S(1)} %get-tuple-element.142), channel_id=1, source_target_pairs={{0,8},{8,0},{16,24},{24,16},{1,9},{9,1},{17,25},{25,17},{2,10},{10... | collective-permute-start | bytes 491528 | tf_op jit(solution)/shard_map/ppermute | solution.py:340
  7.9 10.7 %collective-permute-start.4 = (bf16[2,320,128]{2,1,0:T(8,128)(2,1)S(1)}, bf16[2,320,128]{2,1,0:T(8,128)(2,1)S(1)}, u32[]{:S(2)}, u32[]{:S(2)}) collective-permute-start(bf16[2,320,128]{2,1,0:T(8,128)(2,1)S(1)} %get-tuple-element.143), channel_id=1, source_target_pairs={{0,16},{8,24},{16,0},{24,8},{1,17},{9,25},{17,1},{25,9},{2,18},{10... | collective-permute-start | bytes 491528 | tf_op jit(solution)/shard_map/ppermute | solution.py:340
  9.9 10.2 %collective-permute-start.10 = (bf16[2,320,128]{2,1,0:T(8,128)(2,1)S(1)}, bf16[2,320,128]{2,1,0:T(8,128)(2,1)S(1)}, u32[]{:S(2)}, u32[]{:S(2)}) collective-permute-start(bf16[2,320,128]{2,1,0:T(8,128)(2,1)S(1)} %get-tuple-element.137), channel_id=1, source_target_pairs={{0,16},{8,24},{16,0},{24,8},{1,17},{9,25},{17,1},{25,9},{2,18},{10... | collective-permute-start | bytes 491528 | tf_op jit(solution)/shard_map/ppermute | solution.py:340
  16.5 7.1 %collective-permute-start.8 = (bf16[2,320,128]{2,1,0:T(8,128)(2,1)S(1)}, bf16[2,320,128]{2,1,0:T(8,128)(2,1)S(1)}, u32[]{:S(2)}, u32[]{:S(2)}) collective-permute-start(bf16[2,320,128]{2,1,0:T(8,128)(2,1)S(1)} %get-tuple-element.136), channel_id=1, source_target_pairs={{0,8},{8,0},{16,24},{24,16},{1,9},{9,1},{17,25},{25,17},{2,10},{10... | collective-permute-start | bytes 491528 | tf_op jit(solution)/shard_map/ppermute | solution.py:340
  18.6 7.2 %collective-permute-start.3 = (bf16[2,320,128]{2,1,0:T(8,128)(2,1)S(1)}, bf16[2,320,128]{2,1,0:T(8,128)(2,1)S(1)}, u32[]{:S(2)}, u32[]{:S(2)}) collective-permute-start(bf16[2,320,128]{2,1,0:T(8,128)(2,1)S(1)} %get-tuple-element.140), channel_id=1, source_target_pairs={{0,16},{8,24},{16,0},{24,8},{1,17},{9,25},{17,1},{25,9},{2,18},{10... | collective-permute-start | bytes 491528 | tf_op jit(solution)/shard_map/ppermute | solution.py:340
  20.2 7.1 %collective-permute-start.5 = (bf16[2,320,128]{2,1,0:T(8,128)(2,1)S(1)}, bf16[2,320,128]{2,1,0:T(8,128)(2,1)S(1)}, u32[]{:S(2)}, u32[]{:S(2)}) collective-permute-start(bf16[2,320,128]{2,1,0:T(8,128)(2,1)S(1)} %get-tuple-element.141), channel_id=1, source_target_pairs={{0,8},{8,0},{16,24},{24,16},{1,9},{9,1},{17,25},{25,17},{2,10},{10... | collective-permute-start | bytes 491528 | tf_op jit(solution)/shard_map/ppermute | solution.py:340
  23.6 14.4 %collective-permute-start.11 = (bf16[2,320,128]{2,1,0:T(8,128)(2,1)S(1)}, bf16[2,320,128]{2,1,0:T(8,128)(2,1)S(1)}, u32[]{:S(2)}, u32[]{:S(2)}) collective-permute-start(bf16[2,320,128]{2,1,0:T(8,128)(2,1)S(1)} %get-tuple-element.135), channel_id=1, source_target_pairs={{0,8},{8,0},{16,24},{24,16},{1,9},{9,1},{17,25},{25,17},{2,10},{10... | collective-permute-start | bytes 491528 | tf_op jit(solution)/shard_map/ppermute | solution.py:340
  25.7 14.0 %collective-permute-start.9 = (bf16[2,320,128]{2,1,0:T(8,128)(2,1)S(1)}, bf16[2,320,128]{2,1,0:T(8,128)(2,1)S(1)}, u32[]{:S(2)}, u32[]{:S(2)}) collective-permute-start(bf16[2,320,128]{2,1,0:T(8,128)(2,1)S(1)} %get-tuple-element.134), channel_id=1, source_target_pairs={{0,16},{8,24},{16,0},{24,8},{1,17},{9,25},{17,1},{25,9},{2,18},{10... | collective-permute-start | bytes 491528 | tf_op jit(solution)/shard_map/ppermute | solution.py:340
  27.4 10.6 %copy-start.5 = (bf16[4,320,128]{2,1,0:T(8,128)(2,1)}, bf16[4,320,128]{2,1,0:T(8,128)(2,1)S(1)}, u32[]{:S(2)}) copy-start(bf16[4,320,128]{2,1,0:T(8,128)(2,1)S(1)} %pad_maximum_fusion.den_ref.dmodel_ref) | copy-start | bytes 983044
  31.9 7.9 %collective-permute-start.6 = (bf16[4,320,128]{2,1,0:T(8,128)(2,1)S(1)}, bf16[4,320,128]{2,1,0:T(8,128)(2,1)S(1)}, u32[]{:S(2)}, u32[]{:S(2)}) collective-permute-start(bf16[4,320,128]{2,1,0:T(8,128)(2,1)S(1)} %pad_maximum_fusion.den_ref.dmodel_ref), channel_id=1, source_target_pairs={{0,1},{1,0},{2,3},{3,2},{4,5},{5,4},{6,7},{7,6},{8,9},{9,8},{10,11... | collective-permute-start | bytes 983048 | tf_op jit(solution)/shard_map/ppermute | solution.py:345
  38.0 7.1 %collective-permute-start.7 = (bf16[4,320,128]{2,1,0:T(8,128)(2,1)S(1)}, bf16[4,320,128]{2,1,0:T(8,128)(2,1)S(1)}, u32[]{:S(2)}, u32[]{:S(2)}) collective-permute-start(bf16[4,320,128]{2,1,0:T(8,128)(2,1)S(1)} %pad_maximum_fusion.den_ref.dmodel_ref), channel_id=1, source_target_pairs={{1,2},{2,1},{3,4},{4,3},{5,6},{6,5},{0,8},{7,15},{9,10},{10,9},{11... | collective-permute-start | bytes 983048 | tf_op jit(solution)/shard_map/ppermute | solution.py:353
  39.8 6.4 %copy-start.7 = (bf16[4,320,128]{2,1,0:T(8,128)(2,1)}, bf16[4,320,128]{2,1,0:T(8,128)(2,1)S(1)}, u32[]{:S(2)}) copy-start(bf16[4,320,128]{2,1,0:T(8,128)(2,1)S(1)} %pad_maximum_fusion.1.vel_ref.refs_13_) | copy-start | bytes 983044
  51.1 6.2 %copy-start.27 = (f32[4,320,128]{2,1,0:T(8,128)}, f32[4,320,128]{2,1,0:T(8,128)S(1)}, u32[]{:S(2)}) copy-start(f32[4,320,128]{2,1,0:T(8,128)S(1)} %get-tuple-element.120.fdx_ref) | copy-start | bytes 1966084
  51.2 6.2 %copy-start.29 = (f32[4,320,128]{2,1,0:T(8,128)}, f32[4,320,128]{2,1,0:T(8,128)S(1)}, u32[]{:S(2)}) copy-start(f32[4,320,128]{2,1,0:T(8,128)S(1)} %get-tuple-element.116.refs_12_) | copy-start | bytes 1966084
  51.2 7.0 %collective-permute-start.12 = (bf16[4,320,128]{2,1,0:T(8,128)(2,1)S(1)}, bf16[4,320,128]{2,1,0:T(8,128)(2,1)S(1)}, u32[]{:S(2)}, u32[]{:S(2)}) collective-permute-start(bf16[4,320,128]{2,1,0:T(8,128)(2,1)S(1)} %get-tuple-element.72), channel_id=1, source_target_pairs={{0,1},{1,0},{2,3},{3,2},{4,5},{5,4},{6,7},{7,6},{8,9},{9,8},{10,11... | collective-permute-start | bytes 983048 | tf_op jit(solution)/shard_map/ppermute | solution.py:345
  51.3 7.1 %collective-permute-start.13 = (bf16[4,320,128]{2,1,0:T(8,128)(2,1)S(1)}, bf16[4,320,128]{2,1,0:T(8,128)(2,1)S(1)}, u32[]{:S(2)}, u32[]{:S(2)}) collective-permute-start(bf16[4,320,128]{2,1,0:T(8,128)(2,1)S(1)} %get-tuple-element.72), channel_id=1, source_target_pairs={{1,2},{2,1},{3,4},{4,3},{5,6},{6,5},{0,8},{7,15},{9,10},{10,9},{11... | collective-permute-start | bytes 983048 | tf_op jit(solution)/shard_map/ppermute | solution.py:353
  63.2 7.2 %collective-permute-start.14 = (bf16[4,320,128]{2,1,0:T(8,128)(2,1)}, bf16[4,320,128]{2,1,0:T(8,128)(2,1)}, u32[]{:S(2)}, u32[]{:S(2)}) collective-permute-start(bf16[4,320,128]{2,1,0:T(8,128)(2,1)} %get-tuple-element.75), channel_id=1, source_target_pairs={{0,1},{1,0},{2,3},{3,2},{4,5},{5,4},{6,7},{7,6},{8,9},{9,8},{10,11... | collective-permute-start | bytes 983048 | tf_op jit(solution)/shard_map/ppermute | solution.py:345
  63.3 7.4 %collective-permute-start.15 = (bf16[4,320,128]{2,1,0:T(8,128)(2,1)}, bf16[4,320,128]{2,1,0:T(8,128)(2,1)}, u32[]{:S(2)}, u32[]{:S(2)}) collective-permute-start(bf16[4,320,128]{2,1,0:T(8,128)(2,1)} %get-tuple-element.75), channel_id=1, source_target_pairs={{1,2},{2,1},{3,4},{4,3},{5,6},{6,5},{0,8},{7,15},{9,10},{10,9},{11... | collective-permute-start | bytes 983048 | tf_op jit(solution)/shard_map/ppermute | solution.py:353
  66.0 4.6 %copy-start.2 = (f32[4,336,128]{2,1,0:T(8,128)S(1)}, f32[4,336,128]{2,1,0:T(8,128)}, u32[]{:S(2)}) copy-start(f32[4,336,128]{2,1,0:T(8,128)} %copy-done) | copy-start | bytes 2064388
  72.7 11.5 %collective-permute-start.16 = (bf16[4,320,128]{2,1,0:T(8,128)(2,1)S(1)}, bf16[4,320,128]{2,1,0:T(8,128)(2,1)S(1)}, u32[]{:S(2)}, u32[]{:S(2)}) collective-permute-start(bf16[4,320,128]{2,1,0:T(8,128)(2,1)S(1)} %get-tuple-element.78), channel_id=1, source_target_pairs={{0,1},{1,0},{2,3},{3,2},{4,5},{5,4},{6,7},{7,6},{8,9},{9,8},{10,11... | collective-permute-start | bytes 983048 | tf_op jit(solution)/shard_map/ppermute | solution.py:345
  72.9 11.4 %collective-permute-start.17 = (bf16[4,320,128]{2,1,0:T(8,128)(2,1)S(1)}, bf16[4,320,128]{2,1,0:T(8,128)(2,1)S(1)}, u32[]{:S(2)}, u32[]{:S(2)}) collective-permute-start(bf16[4,320,128]{2,1,0:T(8,128)(2,1)S(1)} %get-tuple-element.78), channel_id=1, source_target_pairs={{1,2},{2,1},{3,4},{4,3},{5,6},{6,5},{0,8},{7,15},{9,10},{10,9},{11... | collective-permute-start | bytes 983048 | tf_op jit(solution)/shard_map/ppermute | solution.py:353
  89.8 7.6 %collective-permute-start.18 = (bf16[4,320,128]{2,1,0:T(8,128)(2,1)S(1)}, bf16[4,320,128]{2,1,0:T(8,128)(2,1)S(1)}, u32[]{:S(2)}, u32[]{:S(2)}) collective-permute-start(bf16[4,320,128]{2,1,0:T(8,128)(2,1)S(1)} %get-tuple-element.87), channel_id=1, source_target_pairs={{0,1},{1,0},{2,3},{3,2},{4,5},{5,4},{6,7},{7,6},{8,9},{9,8},{10,11... | collective-permute-start | bytes 983048 | tf_op jit(solution)/shard_map/ppermute | solution.py:345
  89.9 7.6 %collective-permute-start.19 = (bf16[4,320,128]{2,1,0:T(8,128)(2,1)S(1)}, bf16[4,320,128]{2,1,0:T(8,128)(2,1)S(1)}, u32[]{:S(2)}, u32[]{:S(2)}) collective-permute-start(bf16[4,320,128]{2,1,0:T(8,128)(2,1)S(1)} %get-tuple-element.87), channel_id=1, source_target_pairs={{1,2},{2,1},{3,4},{4,3},{5,6},{6,5},{0,8},{7,15},{9,10},{10,9},{11... | collective-permute-start | bytes 983048 | tf_op jit(solution)/shard_map/ppermute | solution.py:353
  99.0 9.0 %collective-permute-start.20 = (bf16[4,320,128]{2,1,0:T(8,128)(2,1)S(1)}, bf16[4,320,128]{2,1,0:T(8,128)(2,1)S(1)}, u32[]{:S(2)}, u32[]{:S(2)}) collective-permute-start(bf16[4,320,128]{2,1,0:T(8,128)(2,1)S(1)} %get-tuple-element.95), channel_id=1, source_target_pairs={{0,1},{1,0},{2,3},{3,2},{4,5},{5,4},{6,7},{7,6},{8,9},{9,8},{10,11... | collective-permute-start | bytes 983048 | tf_op jit(solution)/shard_map/ppermute | solution.py:345
  99.7 8.4 %collective-permute-start.21 = (bf16[4,320,128]{2,1,0:T(8,128)(2,1)S(1)}, bf16[4,320,128]{2,1,0:T(8,128)(2,1)S(1)}, u32[]{:S(2)}, u32[]{:S(2)}) collective-permute-start(bf16[4,320,128]{2,1,0:T(8,128)(2,1)S(1)} %get-tuple-element.95), channel_id=1, source_target_pairs={{1,2},{2,1},{3,4},{4,3},{5,6},{6,5},{0,8},{7,15},{9,10},{10,9},{11... | collective-permute-start | bytes 983048 | tf_op jit(solution)/shard_map/ppermute | solution.py:353
  108.1 5.7 %copy-start.21 = (f32[4,320,128]{2,1,0:T(8,128)S(1)}, f32[4,320,128]{2,1,0:T(8,128)}, u32[]{:S(2)}) copy-start(f32[4,320,128]{2,1,0:T(8,128)} %copy-done.20) | copy-start | bytes 1966084
  110.5 7.6 %collective-permute-start.22 = (bf16[4,320,128]{2,1,0:T(8,128)(2,1)S(1)}, bf16[4,320,128]{2,1,0:T(8,128)(2,1)S(1)}, u32[]{:S(2)}, u32[]{:S(2)}) collective-permute-start(bf16[4,320,128]{2,1,0:T(8,128)(2,1)S(1)} %get-tuple-element.105), channel_id=1, source_target_pairs={{0,1},{1,0},{2,3},{3,2},{4,5},{5,4},{6,7},{7,6},{8,9},{9,8},{10,11... | collective-permute-start | bytes 983048 | tf_op jit(solution)/shard_map/ppermute | solution.py:345
  110.8 7.4 %collective-permute-start.23 = (bf16[4,320,128]{2,1,0:T(8,128)(2,1)S(1)}, bf16[4,320,128]{2,1,0:T(8,128)(2,1)S(1)}, u32[]{:S(2)}, u32[]{:S(2)}) collective-permute-start(bf16[4,320,128]{2,1,0:T(8,128)(2,1)S(1)} %get-tuple-element.105), channel_id=1, source_target_pairs={{1,2},{2,1},{3,4},{4,3},{5,6},{6,5},{0,8},{7,15},{9,10},{10,9},{11... | collective-permute-start | bytes 983048 | tf_op jit(solution)/shard_map/ppermute | solution.py:353
  113.8 4.4 %copy-start.8 = (bf16[4,320,128]{2,1,0:T(8,128)(2,1)S(1)}, bf16[4,320,128]{2,1,0:T(8,128)(2,1)}, u32[]{:S(2)}) copy-start(bf16[4,320,128]{2,1,0:T(8,128)(2,1)} %copy-done.7) | copy-start | bytes 983044
  113.8 4.4 %copy-start.30 = (f32[4,320,128]{2,1,0:T(8,128)S(1)}, f32[4,320,128]{2,1,0:T(8,128)}, u32[]{:S(2)}) copy-start(f32[4,320,128]{2,1,0:T(8,128)} %copy-done.29) | copy-start | bytes 1966084
  113.8 4.4 %copy-start.32 = (f32[4,320,128]{2,1,0:T(8,128)S(1)}, f32[4,320,128]{2,1,0:T(8,128)}, u32[]{:S(2)}) copy-start(f32[4,320,128]{2,1,0:T(8,128)} %copy-done.31) | copy-start | bytes 1966084
  118.2 9.3 %copy-start.15 = (f32[4,320,128]{2,1,0:T(8,128)S(1)}, f32[4,320,128]{2,1,0:T(8,128)}, u32[]{:S(2)}) copy-start(f32[4,320,128]{2,1,0:T(8,128)} %copy-done.14) | copy-start | bytes 1966084
  121.5 6.0 %copy-start.13 = (f32[4,320,128]{2,1,0:T(8,128)S(1)}, f32[4,320,128]{2,1,0:T(8,128)}, u32[]{:S(2)}) copy-start(f32[4,320,128]{2,1,0:T(8,128)} %copy-done.12) | copy-start | bytes 1966084
  121.5 11.4 %collective-permute-start.28 = (bf16[4,320,128]{2,1,0:T(8,128)(2,1)}, bf16[4,320,128]{2,1,0:T(8,128)(2,1)}, u32[]{:S(2)}, u32[]{:S(2)}) collective-permute-start(bf16[4,320,128]{2,1,0:T(8,128)(2,1)} %get-tuple-element.119), channel_id=1, source_target_pairs={{0,1},{1,0},{2,3},{3,2},{4,5},{5,4},{6,7},{7,6},{8,9},{9,8},{10,11... | collective-permute-start | bytes 983048 | tf_op jit(solution)/shard_map/ppermute | solution.py:345
  122.0 10.9 %collective-permute-start.29 = (bf16[4,320,128]{2,1,0:T(8,128)(2,1)}, bf16[4,320,128]{2,1,0:T(8,128)(2,1)}, u32[]{:S(2)}, u32[]{:S(2)}) collective-permute-start(bf16[4,320,128]{2,1,0:T(8,128)(2,1)} %get-tuple-element.119), channel_id=1, source_target_pairs={{1,2},{2,1},{3,4},{4,3},{5,6},{6,5},{0,8},{7,15},{9,10},{10,9},{11... | collective-permute-start | bytes 983048 | tf_op jit(solution)/shard_map/ppermute | solution.py:353
  125.2 11.5 %collective-permute-start.24 = (bf16[2,320,128]{2,1,0:T(8,128)(2,1)S(1)}, bf16[2,320,128]{2,1,0:T(8,128)(2,1)S(1)}, u32[]{:S(2)}, u32[]{:S(2)}) collective-permute-start(bf16[2,320,128]{2,1,0:T(8,128)(2,1)S(1)} %get-tuple-element.130), channel_id=1, source_target_pairs={{0,8},{8,0},{16,24},{24,16},{1,9},{9,1},{17,25},{25,17},{2,10},{10... | collective-permute-start | bytes 491528 | tf_op jit(solution)/shard_map/ppermute | solution.py:340
  126.0 15.0 %collective-permute-start.26 = (bf16[2,320,128]{2,1,0:T(8,128)(2,1)S(1)}, bf16[2,320,128]{2,1,0:T(8,128)(2,1)S(1)}, u32[]{:S(2)}, u32[]{:S(2)}) collective-permute-start(bf16[2,320,128]{2,1,0:T(8,128)(2,1)S(1)} %get-tuple-element.131), channel_id=1, source_target_pairs={{0,16},{8,24},{16,0},{24,8},{1,17},{9,25},{17,1},{25,9},{2,18},{10... | collective-permute-start | bytes 491528 | tf_op jit(solution)/shard_map/ppermute | solution.py:340
  134.8 5.9 %collective-permute-start.30 = (bf16[2,320,128]{2,1,0:T(8,128)(2,1)S(1)}, bf16[2,320,128]{2,1,0:T(8,128)(2,1)S(1)}, u32[]{:S(2)}, u32[]{:S(2)}) collective-permute-start(bf16[2,320,128]{2,1,0:T(8,128)(2,1)S(1)} %get-tuple-element.126), channel_id=1, source_target_pairs={{0,8},{8,0},{16,24},{24,16},{1,9},{9,1},{17,25},{25,17},{2,10},{10... | collective-permute-start | bytes 491528 | tf_op jit(solution)/shard_map/ppermute | solution.py:340
  136.7 7.1 %collective-permute-start.25 = (bf16[1,2,320,128]{3,2,1,0:T(8,128)(2,1)S(1)}, bf16[1,2,320,128]{3,2,1,0:T(8,128)(2,1)S(1)}, u32[]{:S(2)}, u32[]{:S(2)}) collective-permute-start(bf16[1,2,320,128]{3,2,1,0:T(8,128)(2,1)S(1)} %fusion), channel_id=1, source_target_pairs={{0,16},{8,24},{16,0},{24,8},{1,17},{9,25},{17,1},{25,9},{2,18},{10... | collective-permute-start | bytes 491528 | tf_op jit(solution)/shard_map/ppermute | solution.py:340
  136.8 10.4 %collective-permute-start.32 = (bf16[2,320,128]{2,1,0:T(8,128)(2,1)S(1)}, bf16[2,320,128]{2,1,0:T(8,128)(2,1)S(1)}, u32[]{:S(2)}, u32[]{:S(2)}) collective-permute-start(bf16[2,320,128]{2,1,0:T(8,128)(2,1)S(1)} %get-tuple-element.127), channel_id=1, source_target_pairs={{0,16},{8,24},{16,0},{24,8},{1,17},{9,25},{17,1},{25,9},{2,18},{10... | collective-permute-start | bytes 491528 | tf_op jit(solution)/shard_map/ppermute | solution.py:340
  140.7 8.2 %collective-permute-start.31 = (bf16[1,2,320,128]{3,2,1,0:T(8,128)(2,1)S(1)}, bf16[1,2,320,128]{3,2,1,0:T(8,128)(2,1)S(1)}, u32[]{:S(2)}, u32[]{:S(2)}) collective-permute-start(bf16[1,2,320,128]{3,2,1,0:T(8,128)(2,1)S(1)} %fusion.2), channel_id=1, source_target_pairs={{0,16},{8,24},{16,0},{24,8},{1,17},{9,25},{17,1},{25,9},{2,18},{10... | collective-permute-start | bytes 491528 | tf_op jit(solution)/shard_map/ppermute | solution.py:340
  144.0 5.8 %collective-permute-start.27 = (bf16[1,2,320,128]{3,2,1,0:T(8,128)(2,1)S(1)}, bf16[1,2,320,128]{3,2,1,0:T(8,128)(2,1)S(1)}, u32[]{:S(2)}, u32[]{:S(2)}) collective-permute-start(bf16[1,2,320,128]{3,2,1,0:T(8,128)(2,1)S(1)} %get-tuple-element.129), channel_id=1, source_target_pairs={{0,8},{8,0},{16,24},{24,16},{1,9},{9,1},{17,25},{25,17},{2,10},{10... | collective-permute-start | bytes 491528 | tf_op jit(solution)/shard_map/ppermute | solution.py:340
  149.1 5.4 %collective-permute-start.33 = (bf16[1,2,320,128]{3,2,1,0:T(8,128)(2,1)S(1)}, bf16[1,2,320,128]{3,2,1,0:T(8,128)(2,1)S(1)}, u32[]{:S(2)}, u32[]{:S(2)}) collective-permute-start(bf16[1,2,320,128]{3,2,1,0:T(8,128)(2,1)S(1)} %get-tuple-element.125), channel_id=1, source_target_pairs={{0,8},{8,0},{16,24},{24,16},{1,9},{9,1},{17,25},{25,17},{2,10},{10... | collective-permute-start | bytes 491528 | tf_op jit(solution)/shard_map/ppermute | solution.py:340
  (28 other events, 49.3 us)

commit v2 on v1

v2 whole, which is shorter than its diff:
```python
import math

import jax
import jax.numpy as jnp
import numpy as np
from jax import lax
from jax.experimental import pallas as pl
from jax.experimental.pallas import tpu as pltpu
from jax.sharding import PartitionSpec as P

ITERS = 4
SECOND = (-205.0 / 72.0, 8.0 / 5.0, -1.0 / 5.0, 8.0 / 315.0, -1.0 / 560.0)
FIRST = (4.0 / 5.0, -1.0 / 5.0, 4.0 / 105.0, -1.0 / 280.0)
SPEED = 0.15
PAD = 8
UNROLL = 4
F32, BF16 = jnp.float32, jnp.bfloat16
VMEM_LIMIT = 4 << 20

VM = pl.BlockSpec(memory_space=pltpu.VMEM)
SM = pl.BlockSpec(memory_space=pltpu.SMEM)


def call(kernel, outs, ins, specs, out_specs=None, scratch=(), flops=0):
    outs = tuple(jax.ShapeDtypeStruct(shape, dtype) for shape, dtype in outs)
    moved_bytes = sum(math.prod(x.shape) * x.dtype.itemsize for x in (*ins, *outs))
    return pl.pallas_call(
        kernel,
        out_shape=outs,
        in_specs=list(specs),
        out_specs=tuple(out_specs or [VM] * len(outs)),
        scratch_shapes=list(scratch),
        cost_estimate=pl.CostEstimate(flops=flops, bytes_accessed=moved_bytes, transcendentals=0),
        compiler_params=pltpu.CompilerParams(vmem_limit_bytes=VMEM_LIMIT),
    )(*ins)


def weighted(pairs):
    lap, first = None, None
    for m, (ahead, behind) in enumerate(pairs, 1):
        s = SECOND[m] * (ahead + behind)
        t = FIRST[m - 1] * (ahead - behind)
        lap = s if lap is None else lap + s
        first = t if first is None else first + t
    return lap, first


def y_pairs(ref, layer, row, rows):
    return [
        (ref[layer, pl.ds(row + m, rows), :], ref[layer, pl.ds(row - m, rows), :])
        for m in range(1, 5)
    ]


def z_matrix(depth):
    both = np.zeros((depth, 2 * depth), np.float64)
    for out in range(depth):
        for m in range(1, 5):
            for source, sign in ((out + m, 1.0), (out - m, -1.0)):
                if 0 <= source < depth:
                    both[source, out] += SECOND[m]
                    both[source, depth + out] += sign * FIRST[m - 1]
    high = both.astype(np.float32).astype(jnp.bfloat16)
    low = (both - high.astype(np.float64)).astype(np.float32).astype(jnp.bfloat16)
    return jnp.asarray(np.concatenate([high, high, low], axis=0))


def z_terms(f_ref, matrix_ref, z_ref):
    layers, width, _ = z_ref.shape
    for l in range(layers):
        f = f_ref[l, pl.ds(PAD, width), :]
        high = f.astype(BF16)
        low = (f - high.astype(F32)).astype(BF16)
        split = jnp.concatenate([high, low, high], axis=1)
        z_ref[l, :, :] = jnp.dot(split, matrix_ref[...], preferred_element_type=F32)


def where_am_i():
    column, columns = lax.axis_index("sub"), lax.axis_size("sub")
    even = (column & 1) == 0
    valid = jnp.logical_and(column > 0, column < columns - 1)
    return even, valid


def x_values(own, on_ref, off_ref, rows):
    even, valid = where_am_i()
    count = len(own)
    on = [on_ref[l, rows, :].astype(F32) for l in range(count)]
    off = [jnp.where(valid, off_ref[l, rows, :].astype(F32), 0.0) for l in range(count)]
    low = [jnp.where(even, b, a) for a, b in zip(on, off)]
    high = [jnp.where(even, a, b) for a, b in zip(on, off)]
    return low[count - 4 :] + own + high[:4]


def x_pairs(values, layer):
    return [(values[4 + layer + m], values[4 + layer - m]) for m in range(1, 5)]


def zero_pads(ref):
    layers, tall, depth = ref.shape
    zeros = jnp.zeros((PAD, depth), F32)
    for l in range(layers):
        ref[l, pl.ds(0, PAD), :] = zeros
        ref[l, pl.ds(tall - PAD, PAD), :] = zeros


def prepare_kernel(p_ref, q_ref, pw_ref, qw_ref, ph_ref, qh_ref):
    layers, width, _ = p_ref.shape
    for src, wide, half in ((p_ref, pw_ref, ph_ref), (q_ref, qw_ref, qh_ref)):
        zero_pads(wide)

        @pl.loop(0, width // 16)
        def _(j, src=src, wide=wide, half=half):
            at = pl.multiple_of(16 * j, 16)
            for l in range(layers):
                v = src[l, pl.ds(at, 16), :]
                wide[l, pl.ds(at + PAD, 16), :] = v
                half[l, pl.ds(at, 16), :] = v.astype(BF16)


def list_kernel(rec_ref, layers, width, depth, list_ref):
    total = rec_ref.shape[1]
    cells = layers * width * depth
    first = lax.axis_index("sub") * cells

    def step(i, count):
        local = rec_ref[0, i] - first
        inside = jnp.logical_and(local >= 0, local < cells)
        skip = jnp.int32(PAD * depth)
        for l in range(1, layers):
            skip += jnp.where(local >= l * width * depth, 2 * PAD * depth, 0)
        list_ref[count] = local + skip
        list_ref[total + UNROLL + count] = i
        return count + jnp.where(inside, 1, 0)

    count = lax.fori_loop(0, total, step, jnp.int32(0))
    for n in range(UNROLL):
        list_ref[count + n] = -1
        list_ref[total + UNROLL + count + n] = 0
    list_ref[2 * (total + UNROLL)] = count


def add_receivers(n, field_ref, into_ref, list_ref, observed_ref):
    depth = field_ref.shape[1]
    lane = lax.broadcasted_iota(jnp.int32, (1, depth), 1)
    start = (list_ref.shape[0] - 1) // 2
    count = list_ref[2 * start]

    @pl.loop(0, (count + UNROLL - 1) // UNROLL)
    def _(c):
        rows, terms = [], []
        for k in range(UNROLL):
            at = list_ref[c * UNROLL + k]
            real = at >= 0
            row = jnp.where(real, lax.div(at, depth), 0)
            spot = jnp.where(real, lax.rem(at, depth), depth)
            seen = observed_ref[n, list_ref[start + c * UNROLL + k]]
            rows.append(row)
            terms.append(jnp.where(lane == spot, field_ref[pl.ds(row, 1), :] - seen, 0.0))
        for row, term in zip(rows, terms):
            into_ref[pl.ds(row, 1), :] += term


def receivers_kernel(n, field_ref, list_ref, observed_ref, source_ref):
    source_ref[...] = jnp.zeros(source_ref.shape, F32)
    add_receivers(n, field_ref, source_ref, list_ref, observed_ref)


def first_adjoint_kernel(n, p_ref, q_ref, list_ref, observed_ref, a_ref, half_ref):
    a_ref[...] = q_ref[...]
    add_receivers(n, p_ref, a_ref, list_ref, observed_ref)
    layers, width, _ = half_ref.shape
    tall = width + 2 * PAD

    @pl.loop(0, width // 16)
    def _(j):
        at = pl.multiple_of(16 * j, 16)
        for l in range(layers):
            from_row = pl.multiple_of(at + l * tall + PAD, 8)
            half_ref[l, pl.ds(at, 16), :] = a_ref[pl.ds(from_row, 16), :].astype(BF16)


def log_kernel(den_ref, matrix_ref, log_ref, s2_ref, s3_ref, z_ref):
    layers, width, depth = den_ref.shape
    zero_pads(log_ref)

    @pl.loop(0, width // 16)
    def _(j):
        at = pl.multiple_of(16 * j, 16)
        for l in range(layers):
            log_ref[l, pl.ds(at + PAD, 16), :] = jnp.log(den_ref[l, pl.ds(at, 16), :].astype(F32))

    z_terms(log_ref, matrix_ref, z_ref)

    @pl.loop(0, width // 8)
    def _(j):
        at = pl.multiple_of(8 * j, 8)
        for l in range(layers):
            s2_ref[l, pl.ds(at, 8), :] = weighted(y_pairs(log_ref, l, at + PAD, 8))[1]
            s3_ref[l, pl.ds(at, 8), :] = z_ref[l, pl.ds(at, 8), pl.ds(depth, depth)]


def slope_x_kernel(log_ref, on_ref, off_ref, vel_ref, s1_ref, scale_ref):
    layers, width, _ = s1_ref.shape
    even, valid = where_am_i()

    @pl.loop(0, width // 16)
    def _(j):
        at = pl.multiple_of(16 * j, 16)
        rows = pl.ds(at, 16)
        own = [log_ref[l, pl.ds(at + PAD, 16), :] for l in range(layers)]
        on = [jnp.log(on_ref[l, rows, :].astype(F32)) for l in range(layers)]
        off = [jnp.log(jnp.where(valid, off_ref[l, rows, :].astype(F32), 1.0)) for l in range(layers)]
        low = [jnp.where(even, b, a) for a, b in zip(on, off)]
        high = [jnp.where(even, a, b) for a, b in zip(on, off)]
        values = low[layers - 4 :] + own + high[:4]
        for l in range(layers):
            s1_ref[l, rows, :] = weighted(x_pairs(values, l))[1]
            v = vel_ref[l, rows, :].astype(F32)
            scale_ref[l, rows, :] = SPEED * v * v


def yz_terms(f_ref, s2_ref, s3_ref, z_ref, l, at):
    f = f_ref[l, pl.ds(at + PAD, 8), :]
    lap_y, d_y = weighted(y_pairs(f_ref, l, at + PAD, 8))
    rows, depth = pl.ds(at, 8), f.shape[1]
    lap_z, d_z = z_ref[l, rows, pl.ds(0, depth)], z_ref[l, rows, pl.ds(depth, depth)]
    part = (3.0 * SECOND[0]) * f + lap_y + lap_z
    part = part - (s2_ref[l, rows, :] * d_y + s3_ref[l, rows, :] * d_z)
    return f, part, d_y, d_z


def forward_yz_kernel(f_ref, s2_ref, s3_ref, matrix_ref, part_ref, dy_ref, dz_ref, z_ref):
    layers, width, depth = part_ref.shape
    z_terms(f_ref, matrix_ref, z_ref)

    @pl.loop(0, width // 8)
    def _(j):
        at = pl.multiple_of(8 * j, 8)
        rows = pl.ds(at, 8)
        for l in range(layers):
            f, part, d_y, d_z = yz_terms(f_ref, s2_ref, s3_ref, z_ref, l, at)
            part_ref[l, rows, :] = part
            dy_ref[l, rows, :] = d_y
            dz_ref[l, rows, :] = d_z


def forward_x_kernel(
    f_ref, on_ref, off_ref, part_ref, s1_ref, scale_ref, before_ref,
    dx_ref, applied_ref, next_ref, half_ref,
):
    layers, width, _ = part_ref.shape
    zero_pads(next_ref)
    shift = before_ref.shape[1] != width

    @pl.loop(0, width // 16)
    def _(j):
        at = pl.multiple_of(16 * j, 16)
        rows = pl.ds(at, 16)
        wide = pl.ds(at + PAD, 16)
        own = [f_ref[l, wide, :] for l in range(layers)]
        values = x_values(own, on_ref, off_ref, rows)
        for l in range(layers):
            lap, d_x = weighted(x_pairs(values, l))
            applied = part_ref[l, rows, :] + (lap - s1_ref[l, rows, :] * d_x)
            before = before_ref[l, wide if shift else rows, :]
            later = 2.0 * own[l] - before + scale_ref[l, rows, :] * applied
            dx_ref[l, rows, :] = d_x
            applied_ref[l, rows, :] = applied
            next_ref[l, wide, :] = later
            half_ref[l, rows, :] = later.astype(BF16)


def adjoint_yz_kernel(
    first, f_ref, s2_ref, s3_ref, matrix_ref, fdy_ref, fdz_ref, fapplied_ref, *refs,
):
    if first:
        part_ref, vel_ref, den_ref, z_ref = refs
    else:
        vel_in, den_in, part_ref, vel_ref, den_ref, z_ref = refs
    layers, width, depth = part_ref.shape
    z_terms(f_ref, matrix_ref, z_ref)

    @pl.loop(0, width // 8)
    def _(j):
        at = pl.multiple_of(8 * j, 8)
        rows = pl.ds(at, 8)
        for l in range(layers):
            f, part, d_y, d_z = yz_terms(f_ref, s2_ref, s3_ref, z_ref, l, at)
            part_ref[l, rows, :] = part
            sum_vel = f * fapplied_ref[l, rows, :]
            sum_den = d_y * fdy_ref[l, rows, :] + d_z * fdz_ref[l, rows, :]
            if not first:
                sum_vel = vel_in[l, rows, :] + sum_vel
                sum_den = den_in[l, rows, :] + sum_den
            vel_ref[l, rows, :] = sum_vel
            den_ref[l, rows, :] = sum_den


def adjoint_x_kernel(
    last, f_ref, on_ref, off_ref, part_ref, s1_ref, scale_ref, before_ref,
    source_ref, fdx_ref, den_in, *refs,
):
    if last:
        vel_in, fapplied_ref, vmodel_ref, q_ref, a_ref, half_ref, den_ref, shot_ref = refs
    else:
        q_ref, a_ref, half_ref, den_ref = refs
    layers, width, _ = part_ref.shape
    zero_pads(a_ref)
    shift = before_ref.shape[1] != width

    @pl.loop(0, width // 16)
    def _(j):
        at = pl.multiple_of(16 * j, 16)
        rows = pl.ds(at, 16)
        wide = pl.ds(at + PAD, 16)
        own = [f_ref[l, wide, :] for l in range(layers)]
        values = x_values(own, on_ref, off_ref, rows)
        for l in range(layers):
            lap, d_x = weighted(x_pairs(values, l))
            applied = part_ref[l, rows, :] + (lap - s1_ref[l, rows, :] * d_x)
            before = before_ref[l, wide if shift else rows, :]
            later = 2.0 * own[l] - before + scale_ref[l, rows, :] * applied
            if not last:
                q_ref[l, rows, :] = later
            adjoint = later + source_ref[l, wide, :]
            a_ref[l, wide, :] = adjoint
            half_ref[l, rows, :] = adjoint.astype(BF16)
            den_ref[l, rows, :] = den_in[l, rows, :] + d_x * fdx_ref[l, rows, :]
            if last:
                total = vel_in[l, rows, :] + adjoint * fapplied_ref[l, rows, :]
                v = vmodel_ref[l, rows, :].astype(F32)
                shot_ref[l, rows, :] = ((2.0 * SPEED) * v * total).astype(BF16)
    if last:
        q_ref[...] = jnp.zeros(q_ref.shape, F32)


def last_yz_kernel(f_ref, matrix_ref, fdy_ref, fdz_ref, den_in, den_ref, z_ref):
    layers, width, depth = den_ref.shape
    z_terms(f_ref, matrix_ref, z_ref)

    @pl.loop(0, width // 8)
    def _(j):
        at = pl.multiple_of(8 * j, 8)
        rows = pl.ds(at, 8)
        for l in range(layers):
            d_y = weighted(y_pairs(f_ref, l, at + PAD, 8))[1]
            d_z = z_ref[l, rows, pl.ds(depth, depth)]
            den_ref[l, rows, :] = den_in[l, rows, :] + (
                d_y * fdy_ref[l, rows, :] + d_z * fdz_ref[l, rows, :]
            )


def last_x_kernel(f_ref, on_ref, off_ref, fdx_ref, den_in, scale_ref, dmodel_ref, shot_ref):
    layers, width, _ = shot_ref.shape

    @pl.loop(0, width // 16)
    def _(j):
        at = pl.multiple_of(16 * j, 16)
        rows = pl.ds(at, 16)
        own = [f_ref[l, pl.ds(at + PAD, 16), :] for l in range(layers)]
        values = x_values(own, on_ref, off_ref, rows)
        for l in range(layers):
            d_x = weighted(x_pairs(values, l))[1]
            total = den_in[l, rows, :] + d_x * fdx_ref[l, rows, :]
            density = dmodel_ref[l, rows, :].astype(F32)
            shot_ref[l, rows, :] = (scale_ref[l, rows, :] / density * total).astype(BF16)


def swap_over(axis, count, bit, value):
    return lax.ppermute(value, axis, [(i, i ^ bit) for i in range(count)])


def beside(half):
    groups, count = lax.axis_size("shot"), lax.axis_size("sub")
    on = lax.ppermute(half, "sub", [(i, i ^ 1) for i in range(count)])
    pairs = []
    for s in range(groups):
        for i in range(1, count - 1, 2):
            pairs += [(s * count + i, s * count + i + 1), (s * count + i + 1, s * count + i)]
        if groups % 2 == 0:
            for i in (0, count - 1):
                pairs.append((s * count + i, (s ^ 1) * count + i))
    off = lax.ppermute(half, ("shot", "sub"), pairs)
    return on, off


def bits_of(groups):
    return [1 << k for k in range(groups.bit_length() - 1)]


def pick_into(out_ref, spot, held, me, row):
    for offset, ref in held:

        @pl.when(row == (me ^ offset))
        def _(ref=ref):
            if spot is None:
                out_ref[...] = ref[...]
            else:
                out_ref[spot, :, :] = ref[...]


def pick_kernel(offsets, bits, cover_ref, *refs):
    me, column = lax.axis_index("shot"), lax.axis_index("sub")
    outs = refs[-2:]
    count = len(refs) // 2 - 1
    for way in range(2):
        held = list(zip(offsets[way], refs[way * count : (way + 1) * count]))
        pick_into(outs[way], None, held, me, cover_ref[me ^ bits[way], column])


def gather_kernel(offsets, bits, cover_ref, *refs):
    me, column = lax.axis_index("shot"), lax.axis_index("sub")
    out_ref = refs[-1]
    count = (len(refs) - 1) // 2
    mine = cover_ref[me, column]
    layers = out_ref.shape[0] // 2
    for way in range(2):
        *near, far = refs[way * count : (way + 1) * count]
        spot = pl.ds(way * layers, layers)
        pick_into(out_ref, spot, list(zip(offsets[way], near)), me, mine)

        @pl.when((mine & bits[way]) != (me & bits[way]))
        def _(far=far, spot=spot):
            out_ref[spot, :, :] = far[...]


def fetch(tile, cover):
    groups = cover.shape[0]
    layers = tile.shape[0] // 2
    small = (layers, *tile.shape[1:])
    ways = [bits_of(groups), bits_of(groups)[::-1]]
    held = [[tile[:layers]], [tile[layers:]]]
    offsets = [[0], [0]]
    for stage in range(len(ways[0]) - 1):
        for way in range(2):
            bit = ways[way][stage]
            block = jnp.concatenate(held[way], axis=0) if len(held[way]) > 1 else held[way][0]
            got = swap_over("shot", groups, bit, block)
            held[way] = held[way] + [
                lax.slice_in_dim(got, n * layers, (n + 1) * layers, axis=0)
                for n in range(len(held[way]))
            ]
            offsets[way] = offsets[way] + [o ^ bit for o in offsets[way]]
    last = [way[-1] for way in ways]
    count = len(held[0])
    sends = call(
        lambda *refs: pick_kernel(offsets, last, *refs),
        [(small, BF16)] * 2, [cover, *held[0], *held[1]], [SM] + [VM] * (2 * count),
    )
    far = [swap_over("shot", groups, last[way], sends[way]) for way in range(2)]
    (out,) = call(
        lambda *refs: gather_kernel(offsets, last, *refs),
        [(tile.shape, BF16)], [cover, *held[0], far[0], *held[1], far[1]],
        [SM] + [VM] * (2 * count + 2),
    )
    return out


def bucket_kernel(offsets, bits, cover_ref, tile_ref, *refs):
    me, column = lax.axis_index("shot"), lax.axis_index("sub")
    layers = tile_ref.shape[0] // 2
    got, outs = refs[:2], refs[2:]
    mine = cover_ref[me, column]
    for way in range(2):
        theirs = cover_ref[me ^ bits[way], column]
        own_ref = tile_ref.at[pl.ds(way * layers, layers)]
        for n, offset in enumerate(offsets[way]):
            out = outs[way * len(offsets[way]) + n]
            a = jnp.where(mine == (me ^ offset), own_ref[...].astype(F32), 0.0)
            b = jnp.where(theirs == (me ^ offset), got[way][...].astype(F32), 0.0)
            out[...] = (a + b).astype(out.dtype)


def give_back(tile, cover):
    groups = cover.shape[0]
    layers = tile.shape[0] // 2
    small = (layers, *tile.shape[1:])
    ways = [bits_of(groups), bits_of(groups)[::-1]]
    got = [
        swap_over("shot", groups, ways[way][0], tile[way * layers : (way + 1) * layers])
        for way in range(2)
    ]
    offsets, types = [], []
    for way in ways:
        own = [0]
        for b in reversed(way[1:]):
            own = own + [o ^ b for o in own]
        offsets.append(own)
        types += [BF16 if o & way[1] else F32 for o in own]
    sums = call(
        lambda *refs: bucket_kernel(offsets, [way[0] for way in ways], *refs),
        [(small, kind) for kind in types], [cover, tile, *got], [SM] + [VM] * 3,
    )
    parts = []
    for way in range(2):
        count = len(offsets[way])
        left = dict(zip(offsets[way], sums[way * count : (way + 1) * count]))
        for b in ways[way][1:]:
            away = [o for o in left if o & b]
            block = jnp.concatenate([left[o].astype(BF16) for o in away], axis=0)
            came = swap_over("shot", groups, b, block)
            left = {
                o ^ b: left[o ^ b] + came[n * layers : (n + 1) * layers].astype(F32)
                for n, o in enumerate(away)
            }
        parts.append(left[0])
    return jnp.concatenate(parts, axis=0)


def body(vel_model, den_model, cover, receivers, observed, p_now, p_before, q_now, q_before):
    layers, width, depth = p_now.shape[1:]
    tall = width + 2 * PAD
    narrow, padded = ((layers, width, depth), F32), ((layers, tall, depth), F32)
    half, flat = ((layers, width, depth), BF16), ((layers * tall, depth), F32)
    z_scratch = [pltpu.VMEM((layers, width, 2 * depth), F32)]
    matrix = z_matrix(depth)
    seen = observed[0]

    den = fetch(den_model[0], cover)
    vel = fetch(vel_model[0], cover)

    p, q, p_half, q_half = call(prepare_kernel, [padded, padded, half, half], [p_now[0], q_now[0]], [VM] * 2)
    n_rec = receivers.shape[1]
    (lists,) = call(
        lambda rec, out: list_kernel(rec, layers, width, depth, out),
        [((2 * (n_rec + UNROLL) + 1,), jnp.int32)], [receivers], [SM], [SM],
    )
    p, lists = lax.optimization_barrier((p, lists))

    log_den, s2, s3 = call(log_kernel, [padded, narrow, narrow], [den, matrix], [VM] * 2, scratch=z_scratch)
    den_on, den_off = beside(den)
    s1, scale = call(slope_x_kernel, [narrow, narrow], [log_den, den_on, den_off, vel], [VM] * 4)

    stored, sources = [], []
    before = p_before[0]
    for step in range(ITERS):
        on, off = beside(p_half)
        part, d_y, d_z = call(
            forward_yz_kernel, [narrow] * 3, [p, s2, s3, matrix], [VM] * 4, scratch=z_scratch
        )
        if step > 0:
            (source,) = call(
                lambda *refs, n=step - 1: receivers_kernel(n, *refs),
                [flat], [p.reshape(flat[0]), lists, seen], [VM, SM, SM],
            )
            sources.append(source.reshape(padded[0]))
        d_x, applied, later, p_half = call(
            forward_x_kernel, [narrow, narrow, padded, half],
            [p, on, off, part, s1, scale, before], [VM] * 7,
        )
        stored.append((applied, d_x, d_y, d_z))
        before, p = p, later

    a, a_half = call(
        lambda *refs: first_adjoint_kernel(ITERS - 1, *refs),
        [flat, half], [p.reshape(flat[0]), q.reshape(flat[0]), lists, seen], [VM, VM, SM, SM],
    )
    a = a.reshape(padded[0])
    before, current = q_before[0], q
    sums = ()
    for step in range(ITERS - 1):
        f_applied, f_dx, f_dy, f_dz = stored[ITERS - 1 - step]
        last = step == ITERS - 2
        on, off = beside(a_half)
        part, sum_vel, sum_den = call(
            lambda *refs, first=step == 0: adjoint_yz_kernel(first, *refs),
            [narrow] * 3, [a, s2, s3, matrix, f_dy, f_dz, f_applied, *sums], [VM] * (7 + len(sums)),
            scratch=z_scratch,
        )
        extra = [sum_vel, stored[0][0], vel] if last else []
        later, a, a_half, sum_den, *shot = call(
            lambda *refs, last=last: adjoint_x_kernel(last, *refs),
            [((8, 128), F32) if last else narrow, padded, half, narrow] + ([half] if last else []),
            [a, on, off, part, s1, scale, before, sources[ITERS - 2 - step], f_dx, sum_den, *extra],
            [VM] * (10 + len(extra)),
        )
        before, current = current, later
        sums = (sum_vel, sum_den)
    shot_vel = shot[0]
    _, f_dx, f_dy, f_dz = stored[0]
    on, off = beside(a_half)
    grad_vel = give_back(shot_vel, cover)
    (sum_den,) = call(
        last_yz_kernel, [narrow], [a, matrix, f_dy, f_dz, sum_den], [VM] * 5, scratch=z_scratch
    )
    (shot_den,) = call(
        last_x_kernel, [half], [a, on, off, f_dx, sum_den, scale, den], [VM] * 7
    )
    grad_den = give_back(shot_den, cover)
    return grad_vel[None], grad_den[None]


def solution(mesh):
    return jax.shard_map(
        body,
        mesh=mesh,
        in_specs=(
            P("shot", "sub", None, None),
            P("shot", "sub", None, None),
            P(),
            P("shot", None),
            P("shot", None, None),
            P("shot", "sub", None, None),
            P("shot", "sub", None, None),
            P("shot", "sub", None, None),
            P("shot", "sub", None, None),
        ),
        out_specs=(P("shot", "sub", None, None), P("shot", "sub", None, None)),
        check_vma=False,
    )
```

time: 156 us -> 122 us (0.78)
  Pallas kernels: 72.8 us -> 41.2 us
  waiting for transfers between devices: 22.9 us -> 44.6 us
  local copies, waits for them, and re-layouts: 16.7 us -> 2.3 us
  between operations: 7.1 us -> 1.04 us
  starting transfers between devices: 33.1 us -> 31.2 us
    pallas_call x24 -> x30, Pallas kernels: 72.8 us -> 41.2 us  [call(): pl.pallas_call(kernel, out_shape=outs, in_specs=list(specs), out_specs=tu...]
    ppermute x9, waiting for transfers between devices: 5.86 us -> 21.2 us  [beside(): off = lax.ppermute(half, ('shot', 'sub'), pairs)]
    unnamed x84 -> x18, local copies, waits for them, and re-layouts: 16 us -> 1.17 us
    ppermute x16, waiting for transfers between devices: 17 us -> 23.3 us  [swap_over(): return lax.ppermute(value, axis, [(i, i ^ bit) for i in range(count)])]
    ppermute x9, starting transfers between devices: 13 us -> 10.2 us  [beside(): off = lax.ppermute(half, ('shot', 'sub'), pairs)]
  transfers between devices with their start and end apart: 34 -> 34, of which waited for: 10 -> 16; matrix products, arithmetic and copies ran while one was open for 2% -> 1% of each run, Pallas kernels for 35% -> 25%
where the time goes in v2:
time: 122 us
  waiting for transfers between devices  44.6 us (37%)
  Pallas kernels  41.2 us (34%)
  starting transfers between devices  31.2 us (26%)
  local copies, waits for them, and re-layouts  2.3 us (2%)
  other arithmetic  1.88 us (2%)
    pallas_call x30, Pallas kernels, call(): pl.pallas_call(kernel, out_shape=outs, in_specs=list(specs), out_specs=tu...  41.2 us
    ppermute x16, waiting for transfers between devices, swap_over(): return lax.ppermute(value, axis, [(i, i ^ bit) for i in range(count)])  23.3 us
    ppermute x9, waiting for transfers between devices, beside(): off = lax.ppermute(half, ('shot', 'sub'), pairs)  21.2 us
    ppermute x16, starting transfers between devices, swap_over(): return lax.ppermute(value, axis, [(i, i ^ bit) for i in range(count)])  18.7 us
    ppermute x9, starting transfers between devices, beside(): off = lax.ppermute(half, ('shot', 'sub'), pairs)  10.2 us
  transfers between devices with their start and end apart: 34, of which 16 were waited for; matrix products, arithmetic and copies ran while one was open for 1% of the time, Pallas kernels for 25%

profile of v2, /device:TPU:0, one launch (start us, length us, event | category | flops | bytes accessed | tf_op | source)
XLA Modules:
  0.0 122.2 jit_solution(3826190886201110971)
XLA Ops:
  1.7 3.0 %collective-permute-start.2 = (bf16[2,320,128]{2,1,0:T(8,128)(2,1)S(1)}, bf16[2,320,128]{2,1,0:T(8,128)(2,1)S(1)}, u32[]{:S(2)}, u32[]{:S(2)}) collective-permute-start(bf16[2,320,128]{2,1,0:T(8,128)(2,1)S(1)} %get-tuple-element.151.refs_1_), channel_id=1, source_target_pairs={{0,8},{8,0},{16,24},{24,16},{1,9},{9,1},{17,25},{25,17},{2,10},{10... | collective-permute-start | bytes 491528 | tf_op jit(solution)/shard_map/ppermute | solution.py:371
  4.7 1.5 %collective-permute-start.3 = (bf16[2,320,128]{2,1,0:T(8,128)(2,1)S(1)}, bf16[2,320,128]{2,1,0:T(8,128)(2,1)S(1)}, u32[]{:S(2)}, u32[]{:S(2)}) collective-permute-start(bf16[2,320,128]{2,1,0:T(8,128)(2,1)S(1)} %get-tuple-element.150.refs_3_.refs_4_), channel_id=1, source_target_pairs={{0,16},{8,24},{16,0},{24,8},{1,17},{9,25},{17,1},{25,9},{2,18},{10... | collective-permute-start | bytes 491528 | tf_op jit(solution)/shard_map/ppermute | solution.py:371
  7.0 2.7 %collective-permute-done.2.refs_2_ = bf16[2,320,128]{2,1,0:T(8,128)(2,1)S(1)} collective-permute-done((bf16[2,320,128]{2,1,0:T(8,128)(2,1)S(1)}, bf16[2,320,128]{2,1,0:T(8,128)(2,1)S(1)}, u32[]{:S(2)}, u32[]{:S(2)}) %collective-permute-start.2) | collective-permute-done | bytes 163872 | tf_op jit(solution)/shard_map/ppermute | solution.py:371
  9.6 2.2 %collective-permute-done.3.refs_4_.refs_5_ = bf16[2,320,128]{2,1,0:T(8,128)(2,1)S(1)} collective-permute-done((bf16[2,320,128]{2,1,0:T(8,128)(2,1)S(1)}, bf16[2,320,128]{2,1,0:T(8,128)(2,1)S(1)}, u32[]{:S(2)}, u32[]{:S(2)}) %collective-permute-start.3) | collective-permute-done | bytes 163872 | tf_op jit(solution)/shard_map/ppermute | solution.py:371
  12.4 1.6 %collective-permute-start.4 = (bf16[2,320,128]{2,1,0:T(8,128)(2,1)S(1)}, bf16[2,320,128]{2,1,0:T(8,128)(2,1)S(1)}, u32[]{:S(2)}, u32[]{:S(2)}) collective-permute-start(bf16[2,320,128]{2,1,0:T(8,128)(2,1)S(1)} %get-tuple-element.76), channel_id=1, source_target_pairs={{0,16},{8,24},{16,0},{24,8},{1,17},{9,25},{17,1},{25,9},{2,18},{10... | collective-permute-start | bytes 491528 | tf_op jit(solution)/shard_map/ppermute | solution.py:371
  16.0 1.6 %collective-permute-start.10 = (bf16[2,320,128]{2,1,0:T(8,128)(2,1)S(1)}, bf16[2,320,128]{2,1,0:T(8,128)(2,1)S(1)}, u32[]{:S(2)}, u32[]{:S(2)}) collective-permute-start(bf16[2,320,128]{2,1,0:T(8,128)(2,1)S(1)} %get-tuple-element.82), channel_id=1, source_target_pairs={{0,16},{8,24},{16,0},{24,8},{1,17},{9,25},{17,1},{25,9},{2,18},{10... | collective-permute-start | bytes 491528 | tf_op jit(solution)/shard_map/ppermute | solution.py:371
  17.6 1.9 %collective-permute-done.4.refs_3_ = bf16[2,320,128]{2,1,0:T(8,128)(2,1)S(1)} collective-permute-done((bf16[2,320,128]{2,1,0:T(8,128)(2,1)S(1)}, bf16[2,320,128]{2,1,0:T(8,128)(2,1)S(1)}, u32[]{:S(2)}, u32[]{:S(2)}) %collective-permute-start.4) | collective-permute-done | bytes 163872 | tf_op jit(solution)/shard_map/ppermute | solution.py:371
  21.6 1.2 %collective-permute-start = (bf16[4,320,128]{2,1,0:T(8,128)(2,1)S(1)}, bf16[4,320,128]{2,1,0:T(8,128)(2,1)S(1)}, u32[]{:S(2)}, u32[]{:S(2)}) collective-permute-start(bf16[4,320,128]{2,1,0:T(8,128)(2,1)S(1)} %get-tuple-element.75), channel_id=1, source_target_pairs={{0,1},{1,0},{2,3},{3,2},{4,5},{5,4},{6,7},{7,6},{8,9},{9,8},{10,11... | collective-permute-start | bytes 983048 | tf_op jit(solution)/shard_map/ppermute | solution.py:376
  23.3 1.6 %collective-permute-start.11 = (bf16[2,320,128]{2,1,0:T(8,128)(2,1)S(1)}, bf16[2,320,128]{2,1,0:T(8,128)(2,1)S(1)}, u32[]{:S(2)}, u32[]{:S(2)}) collective-permute-start(bf16[2,320,128]{2,1,0:T(8,128)(2,1)S(1)} %get-tuple-element.83), channel_id=1, source_target_pairs={{0,8},{8,0},{16,24},{24,16},{1,9},{9,1},{17,25},{25,17},{2,10},{10... | collective-permute-start | bytes 491528 | tf_op jit(solution)/shard_map/ppermute | solution.py:371
  24.9 6.6 %shard_map.114.refs_2_.refs_1_ = s32[1033]{0:T(1024)S(1)} custom-call(s32[1,512]{1,0:T(1,128)S(1)} %copy-done.7), custom_call_target="tpu_custom_call" | custom-call | bytes 6180 | tf_op jit(solution)/shard_map/pallas_call | solution.py:27
  31.6 1.3 %shard_map.117 = (f32[4,336,128]{2,1,0:T(8,128)S(1)}, f32[4,320,128]{2,1,0:T(8,128)S(1)}, f32[4,320,128]{2,1,0:T(8,128)S(1)}) custom-call(bf16[4,320,128]{2,1,0:T(8,128)(2,1)S(1)} %shard_map.116.den_ref.dmodel_ref, bf16[384,256]{1,0:T(8,128)(2,1)S(1)} %copy-done), custom_call_target="tpu_custom_call" | custom-call | bytes 2523136 | tf_op jit(solution)/shard_map/pallas_call | solution.py:27
  32.9 1.5 %shard_map.118 = (f32[4,320,128]{2,1,0:T(8,128)S(1)}, f32[4,320,128]{2,1,0:T(8,128)S(1)}, f32[4,320,128]{2,1,0:T(8,128)S(1)}) custom-call(f32[4,336,128]{2,1,0:T(8,128)S(1)} %get-tuple-element.74.f_ref.before_ref, f32[4,320,128]{2,1,0:T(8,128)S(1)} %get-tuple-element.78.s2_ref.refs_1_, f32[4,320,128]{2,1,0:T(8,128)S(1)} %get-tuple-element.79.s3_ref.refs_2_, ...), custom_call_target="tpu_custom_call" | custom-call | bytes 4161536 | tf_op jit(solution)/shard_map/pallas_call | solution.py:27
  37.2 1.4 %collective-permute-start.13 = (bf16[4,320,128]{2,1,0:T(8,128)(2,1)S(1)}, bf16[4,320,128]{2,1,0:T(8,128)(2,1)S(1)}, u32[]{:S(2)}, u32[]{:S(2)}) collective-permute-start(bf16[4,320,128]{2,1,0:T(8,128)(2,1)S(1)} %get-tuple-element.87), channel_id=1, source_target_pairs={{1,2},{2,1},{3,4},{4,3},{5,6},{6,5},{0,8},{7,15},{9,10},{10,9},{11... | collective-permute-start | bytes 983048 | tf_op jit(solution)/shard_map/ppermute | solution.py:384
  38.6 1.5 %shard_map.123 = (f32[4,320,128]{2,1,0:T(8,128)S(1)}, f32[4,320,128]{2,1,0:T(8,128)S(1)}, f32[4,320,128]{2,1,0:T(8,128)S(1)}) custom-call(f32[4,336,128]{2,1,0:T(8,128)S(1)} %get-tuple-element.86.f_ref.before_ref, f32[4,320,128]{2,1,0:T(8,128)S(1)} %get-tuple-element.78.s2_ref.refs_1_, f32[4,320,128]{2,1,0:T(8,128)S(1)} %get-tuple-element.79.s3_ref.refs_2_, ...), custom_call_target="tpu_custom_call" | custom-call | bytes 4161536 | tf_op jit(solution)/shard_map/pallas_call | solution.py:27
  40.1 4.3 %collective-permute-done.13.off_ref = bf16[4,320,128]{2,1,0:T(8,128)(2,1)S(1)} collective-permute-done((bf16[4,320,128]{2,1,0:T(8,128)(2,1)S(1)}, bf16[4,320,128]{2,1,0:T(8,128)(2,1)S(1)}, u32[]{:S(2)}, u32[]{:S(2)}) %collective-permute-start.13) | collective-permute-done | bytes 327712 | tf_op jit(solution)/shard_map/ppermute | solution.py:384
  45.5 1.3 %collective-permute-start.15 = (bf16[4,320,128]{2,1,0:T(8,128)(2,1)S(1)}, bf16[4,320,128]{2,1,0:T(8,128)(2,1)S(1)}, u32[]{:S(2)}, u32[]{:S(2)}) collective-permute-start(bf16[4,320,128]{2,1,0:T(8,128)(2,1)S(1)} %get-tuple-element.90), channel_id=1, source_target_pairs={{1,2},{2,1},{3,4},{4,3},{5,6},{6,5},{0,8},{7,15},{9,10},{10,9},{11... | collective-permute-start | bytes 983048 | tf_op jit(solution)/shard_map/ppermute | solution.py:384
  46.8 1.5 %shard_map.125 = (f32[4,320,128]{2,1,0:T(8,128)S(1)}, f32[4,320,128]{2,1,0:T(8,128)S(1)}, f32[4,320,128]{2,1,0:T(8,128)S(1)}) custom-call(f32[4,336,128]{2,1,0:T(8,128)S(1)} %get-tuple-element.89.f_ref.before_ref, f32[4,320,128]{2,1,0:T(8,128)S(1)} %get-tuple-element.78.s2_ref.refs_1_, f32[4,320,128]{2,1,0:T(8,128)S(1)} %get-tuple-element.79.s3_ref.refs_2_, ...), custom_call_target="tpu_custom_call" | custom-call | bytes 4161536 | tf_op jit(solution)/shard_map/pallas_call | solution.py:27
  48.3 4.3 %collective-permute-done.15.off_ref = bf16[4,320,128]{2,1,0:T(8,128)(2,1)S(1)} collective-permute-done((bf16[4,320,128]{2,1,0:T(8,128)(2,1)S(1)}, bf16[4,320,128]{2,1,0:T(8,128)(2,1)S(1)}, u32[]{:S(2)}, u32[]{:S(2)}) %collective-permute-start.15) | collective-permute-done | bytes 327712 | tf_op jit(solution)/shard_map/ppermute | solution.py:384
  53.7 1.3 %collective-permute-start.17 = (bf16[4,320,128]{2,1,0:T(8,128)(2,1)S(1)}, bf16[4,320,128]{2,1,0:T(8,128)(2,1)S(1)}, u32[]{:S(2)}, u32[]{:S(2)}) collective-permute-start(bf16[4,320,128]{2,1,0:T(8,128)(2,1)S(1)} %get-tuple-element.93), channel_id=1, source_target_pairs={{1,2},{2,1},{3,4},{4,3},{5,6},{6,5},{0,8},{7,15},{9,10},{10,9},{11... | collective-permute-start | bytes 983048 | tf_op jit(solution)/shard_map/ppermute | solution.py:384
  55.0 1.5 %shard_map.127 = (f32[4,320,128]{2,1,0:T(8,128)S(1)}, f32[4,320,128]{2,1,0:T(8,128)S(1)}, f32[4,320,128]{2,1,0:T(8,128)S(1)}) custom-call(f32[4,336,128]{2,1,0:T(8,128)S(1)} %get-tuple-element.92.f_ref, f32[4,320,128]{2,1,0:T(8,128)S(1)} %get-tuple-element.78.s2_ref.refs_1_, f32[4,320,128]{2,1,0:T(8,128)S(1)} %get-tuple-element.79.s3_ref.refs_2_, ...), custom_call_target="tpu_custom_call" | custom-call | bytes 4161536 | tf_op jit(solution)/shard_map/pallas_call | solution.py:27
  56.5 4.3 %collective-permute-done.17.off_ref = bf16[4,320,128]{2,1,0:T(8,128)(2,1)S(1)} collective-permute-done((bf16[4,320,128]{2,1,0:T(8,128)(2,1)S(1)}, bf16[4,320,128]{2,1,0:T(8,128)(2,1)S(1)}, u32[]{:S(2)}, u32[]{:S(2)}) %collective-permute-start.17) | collective-permute-done | bytes 327712 | tf_op jit(solution)/shard_map/ppermute | solution.py:384
  60.8 1.7 %shard_map.128 = (f32[4,320,128]{2,1,0:T(8,128)S(1)}, f32[4,320,128]{2,1,0:T(8,128)S(1)}, f32[4,336,128]{2,1,0:T(8,128)S(1)}, bf16[4,320,128]{2,1,0:T(8,128)(2,1)}) custom-call(f32[4,336,128]{2,1,0:T(8,128)S(1)} %get-tuple-element.92.f_ref, bf16[4,320,128]{2,1,0:T(8,128)(2,1)S(1)} %collective-permute-done.16.on_ref, ...), custom_call_target="tpu_custom_call" | custom-call | bytes 6324224 | tf_op jit(solution)/shard_map/pallas_call | solution.py:27
  63.2 1.5 %shard_map.129 = (f32[1344,128]{1,0:T(8,128)S(1)}, bf16[4,320,128]{2,1,0:T(8,128)(2,1)S(1)}) custom-call(f32[1344,128]{1,0:T(8,128)S(1)} %bitcast.35, f32[1344,128]{1,0:T(8,128)S(1)} %bitcast.29, s32[1033]{0:T(1024)S(1)} %shard_map.114.refs_2_.refs_1_, f32[4,512]{1,0:T(4,128)S(1)} %bitcast.40), custom_call_target="tpu_custom_call" | custom-call | bytes 2404388 | tf_op jit(solution)/shard_map/pallas_call | solution.py:27
  64.9 1.3 %collective-permute-start.19 = (bf16[4,320,128]{2,1,0:T(8,128)(2,1)S(1)}, bf16[4,320,128]{2,1,0:T(8,128)(2,1)S(1)}, u32[]{:S(2)}, u32[]{:S(2)}) collective-permute-start(bf16[4,320,128]{2,1,0:T(8,128)(2,1)S(1)} %get-tuple-element.99), channel_id=1, source_target_pairs={{1,2},{2,1},{3,4},{4,3},{5,6},{6,5},{0,8},{7,15},{9,10},{10,9},{11... | collective-permute-start | bytes 983048 | tf_op jit(solution)/shard_map/ppermute | solution.py:384
  66.2 1.3 %shard_map.131 = f32[1344,128]{1,0:T(8,128)S(1)} custom-call(f32[1344,128]{1,0:T(8,128)S(1)} %bitcast.28, s32[1033]{0:T(1024)S(1)} %shard_map.114.refs_2_.refs_1_, f32[4,512]{1,0:T(4,128)S(1)} %bitcast.41), custom_call_target="tpu_custom_call" | custom-call | bytes 1388580 | tf_op jit(solution)/shard_map/pallas_call | solution.py:27
  67.6 1.6 %shard_map.130 = (f32[4,320,128]{2,1,0:T(8,128)S(1)}, f32[4,320,128]{2,1,0:T(8,128)S(1)}, f32[4,320,128]{2,1,0:T(8,128)S(1)}) custom-call(f32[4,336,128]{2,1,0:T(8,128)S(1)} %bitcast.33, f32[4,320,128]{2,1,0:T(8,128)S(1)} %get-tuple-element.78.s2_ref.refs_1_, f32[4,320,128]{2,1,0:T(8,128)S(1)} %get-tuple-element.79.s3_ref.refs_2_, ...), custom_call_target="tpu_custom_call" | custom-call | bytes 6127616 | tf_op jit(solution)/shard_map/pallas_call | solution.py:27
  69.1 2.8 %collective-permute-done.19.refs_2_ = bf16[4,320,128]{2,1,0:T(8,128)(2,1)S(1)} collective-permute-done((bf16[4,320,128]{2,1,0:T(8,128)(2,1)S(1)}, bf16[4,320,128]{2,1,0:T(8,128)(2,1)S(1)}, u32[]{:S(2)}, u32[]{:S(2)}) %collective-permute-start.19) | collective-permute-done | bytes 327712 | tf_op jit(solution)/shard_map/ppermute | solution.py:384
  73.2 1.3 %collective-permute-start.21 = (bf16[4,320,128]{2,1,0:T(8,128)(2,1)S(1)}, bf16[4,320,128]{2,1,0:T(8,128)(2,1)S(1)}, u32[]{:S(2)}, u32[]{:S(2)}) collective-permute-start(bf16[4,320,128]{2,1,0:T(8,128)(2,1)S(1)} %get-tuple-element.107), channel_id=1, source_target_pairs={{1,2},{2,1},{3,4},{4,3},{5,6},{6,5},{0,8},{7,15},{9,10},{10,9},{11... | collective-permute-start | bytes 983048 | tf_op jit(solution)/shard_map/ppermute | solution.py:384
  74.5 1.3 %shard_map.134 = f32[1344,128]{1,0:T(8,128)S(1)} custom-call(f32[1344,128]{1,0:T(8,128)S(1)} %bitcast.27, s32[1033]{0:T(1024)S(1)} %shard_map.114.refs_2_.refs_1_, f32[4,512]{1,0:T(4,128)S(1)} %bitcast.42), custom_call_target="tpu_custom_call" | custom-call | bytes 1388580 | tf_op jit(solution)/shard_map/pallas_call | solution.py:27
  75.9 1.7 %shard_map.133 = (f32[4,320,128]{2,1,0:T(8,128)S(1)}, f32[4,320,128]{2,1,0:T(8,128)S(1)}, f32[4,320,128]{2,1,0:T(8,128)S(1)}) custom-call(f32[4,336,128]{2,1,0:T(8,128)S(1)} %get-tuple-element.106.refs_0_, f32[4,320,128]{2,1,0:T(8,128)S(1)} %get-tuple-element.78.s2_ref.refs_1_, f32[4,320,128]{2,1,0:T(8,128)S(1)} %get-tuple-element.79.s3_ref.refs_2_, ...), custom_call_target="tpu_custom_call" | custom-call | bytes 7438336 | tf_op jit(solution)/shard_map/pallas_call | solution.py:27
  77.5 2.8 %collective-permute-done.21.refs_2_ = bf16[4,320,128]{2,1,0:T(8,128)(2,1)S(1)} collective-permute-done((bf16[4,320,128]{2,1,0:T(8,128)(2,1)S(1)}, bf16[4,320,128]{2,1,0:T(8,128)(2,1)S(1)}, u32[]{:S(2)}, u32[]{:S(2)}) %collective-permute-start.21) | collective-permute-done | bytes 327712 | tf_op jit(solution)/shard_map/ppermute | solution.py:384
  80.3 1.9 %shard_map.135 = (f32[4,320,128]{2,1,0:T(8,128)}, f32[4,336,128]{2,1,0:T(8,128)S(1)}, bf16[4,320,128]{2,1,0:T(8,128)(2,1)S(1)}, f32[4,320,128]{2,1,0:T(8,128)S(1)}) custom-call(f32[4,336,128]{2,1,0:T(8,128)S(1)} %get-tuple-element.106.refs_0_, bf16[4,320,128]{2,1,0:T(8,128)(2,1)S(1)} %collective-permute-done.20.refs_1_, ...), custom_call_target="tpu_custom_call" | custom-call | bytes 8323072 | tf_op jit(solution)/shard_map/pallas_call | solution.py:27
  82.3 1.3 %collective-permute-start.23 = (bf16[4,320,128]{2,1,0:T(8,128)(2,1)S(1)}, bf16[4,320,128]{2,1,0:T(8,128)(2,1)S(1)}, u32[]{:S(2)}, u32[]{:S(2)}) collective-permute-start(bf16[4,320,128]{2,1,0:T(8,128)(2,1)S(1)} %get-tuple-element.117), channel_id=1, source_target_pairs={{1,2},{2,1},{3,4},{4,3},{5,6},{6,5},{0,8},{7,15},{9,10},{10,9},{11... | collective-permute-start | bytes 983048 | tf_op jit(solution)/shard_map/ppermute | solution.py:384
  83.6 1.3 %shard_map.137 = f32[1344,128]{1,0:T(8,128)S(1)} custom-call(f32[1344,128]{1,0:T(8,128)S(1)} %bitcast.26, s32[1033]{0:T(1024)S(1)} %shard_map.114.refs_2_.refs_1_, f32[4,512]{1,0:T(4,128)S(1)} %bitcast.43), custom_call_target="tpu_custom_call" | custom-call | bytes 1388580 | tf_op jit(solution)/shard_map/pallas_call | solution.py:27
  84.9 1.7 %shard_map.136 = (f32[4,320,128]{2,1,0:T(8,128)S(1)}, f32[4,320,128]{2,1,0:T(8,128)S(1)}, f32[4,320,128]{2,1,0:T(8,128)S(1)}) custom-call(f32[4,336,128]{2,1,0:T(8,128)S(1)} %get-tuple-element.116.refs_0_, f32[4,320,128]{2,1,0:T(8,128)S(1)} %get-tuple-element.78.s2_ref.refs_1_, f32[4,320,128]{2,1,0:T(8,128)S(1)} %get-tuple-element.79.s3_ref.refs_2_, ...), custom_call_target="tpu_custom_call" | custom-call | bytes 7438336 | tf_op jit(solution)/shard_map/pallas_call | solution.py:27
  86.6 2.8 %collective-permute-done.23.refs_2_ = bf16[4,320,128]{2,1,0:T(8,128)(2,1)S(1)} collective-permute-done((bf16[4,320,128]{2,1,0:T(8,128)(2,1)S(1)}, bf16[4,320,128]{2,1,0:T(8,128)(2,1)S(1)}, u32[]{:S(2)}, u32[]{:S(2)}) %collective-permute-start.23) | collective-permute-done | bytes 327712 | tf_op jit(solution)/shard_map/ppermute | solution.py:384
  89.4 1.8 %shard_map.138 = (f32[8,128]{1,0:T(8,128)}, f32[4,336,128]{2,1,0:T(8,128)S(1)}, bf16[4,320,128]{2,1,0:T(8,128)(2,1)S(1)}, f32[4,320,128]{2,1,0:T(8,128)S(1)}, bf16[4,320,128]{2,1,0:T(8,128)(2,1)S(1)}) custom-call(f32[4,336,128]{2,1,0:T(8,128)S(1)} %get-tuple-element.116.refs_0_, bf16[4,320,128]{2,1,0:T(8,128)(2,1)S(1)} %collective-permute-done.22.refs_1_, ...), custom_call_target="tpu_custom_call" | custom-call | bytes 9605120 | tf_op jit(solution)/shard_map/pallas_call | solution.py:27
  91.3 1.3 %collective-permute-start.29 = (bf16[4,320,128]{2,1,0:T(8,128)(2,1)S(1)}, bf16[4,320,128]{2,1,0:T(8,128)(2,1)S(1)}, u32[]{:S(2)}, u32[]{:S(2)}) collective-permute-start(bf16[4,320,128]{2,1,0:T(8,128)(2,1)S(1)} %get-tuple-element.135), channel_id=1, source_target_pairs={{1,2},{2,1},{3,4},{4,3},{5,6},{6,5},{0,8},{7,15},{9,10},{10,9},{11... | collective-permute-start | bytes 983048 | tf_op jit(solution)/shard_map/ppermute | solution.py:384
  93.4 1.5 %collective-permute-start.25 = (bf16[2,320,128]{2,1,0:T(8,128)(2,1)S(1)}, bf16[2,320,128]{2,1,0:T(8,128)(2,1)S(1)}, u32[]{:S(2)}, u32[]{:S(2)}) collective-permute-start(bf16[2,320,128]{2,1,0:T(8,128)(2,1)S(1)} %get-tuple-element.146), channel_id=1, source_target_pairs={{0,16},{8,24},{16,0},{24,8},{1,17},{9,25},{17,1},{25,9},{2,18},{10... | collective-permute-start | bytes 491528 | tf_op jit(solution)/shard_map/ppermute | solution.py:371
  95.0 1.2 %shard_map.140.den_in = f32[4,320,128]{2,1,0:T(8,128)S(1)} custom-call(f32[4,336,128]{2,1,0:T(8,128)S(1)} %get-tuple-element.134.f_ref, bf16[384,256]{1,0:T(8,128)(2,1)S(1)} %copy-done, f32[4,320,128]{2,1,0:T(8,128)S(1)} %get-tuple-element.137.fdy_ref, f32[4,320,128]{2,1,0:T(8,128)S(1)} %get-tuple-element.138.fdz_ref, ...), custom_call_target="tpu_custom_call" | custom-call | bytes 3506176 | tf_op jit(solution)/shard_map/pallas_call | solution.py:27
  96.2 5.2 %collective-permute-done.24.refs_2_ = bf16[2,320,128]{2,1,0:T(8,128)(2,1)S(1)} collective-permute-done((bf16[2,320,128]{2,1,0:T(8,128)(2,1)S(1)}, bf16[2,320,128]{2,1,0:T(8,128)(2,1)S(1)}, u32[]{:S(2)}, u32[]{:S(2)}) %collective-permute-start.24) | collective-permute-done | bytes 163872 | tf_op jit(solution)/shard_map/ppermute | solution.py:371
  102.2 1.8 %collective-permute-start.26 = (bf16[2,320,128]{2,1,0:T(8,128)(2,1)S(1)}, bf16[2,320,128]{2,1,0:T(8,128)(2,1)S(1)}, u32[]{:S(2)}, u32[]{:S(2)}) collective-permute-start(bf16[2,320,128]{2,1,0:T(8,128)(2,1)S(1)} %get-tuple-element.131), channel_id=1, source_target_pairs={{0,16},{8,24},{16,0},{24,8},{1,17},{9,25},{17,1},{25,9},{2,18},{10... | collective-permute-start | bytes 491528 | tf_op jit(solution)/shard_map/ppermute | solution.py:371
  104.1 1.3 %collective-permute-start.27 = (bf16[2,320,128]{2,1,0:T(8,128)(2,1)S(1)}, bf16[2,320,128]{2,1,0:T(8,128)(2,1)S(1)}, u32[]{:S(2)}, u32[]{:S(2)}) collective-permute-start(bf16[2,320,128]{2,1,0:T(8,128)(2,1)S(1)} %get-tuple-element.133), channel_id=1, source_target_pairs={{0,8},{8,0},{16,24},{24,16},{1,9},{9,1},{17,25},{25,17},{2,10},{10... | collective-permute-start | bytes 491528 | tf_op jit(solution)/shard_map/ppermute | solution.py:371
  108.1 3.6 %collective-permute-done.30.refs_2_ = bf16[2,320,128]{2,1,0:T(8,128)(2,1)S(1)} collective-permute-done((bf16[2,320,128]{2,1,0:T(8,128)(2,1)S(1)}, bf16[2,320,128]{2,1,0:T(8,128)(2,1)S(1)}, u32[]{:S(2)}, u32[]{:S(2)}) %collective-permute-start.30) | collective-permute-done | bytes 163872 | tf_op jit(solution)/shard_map/ppermute | solution.py:371
  111.7 2.2 %collective-permute-done.31.refs_3_ = bf16[2,320,128]{2,1,0:T(8,128)(2,1)S(1)} collective-permute-done((bf16[2,320,128]{2,1,0:T(8,128)(2,1)S(1)}, bf16[2,320,128]{2,1,0:T(8,128)(2,1)S(1)}, u32[]{:S(2)}, u32[]{:S(2)}) %collective-permute-start.31) | collective-permute-done | bytes 163872 | tf_op jit(solution)/shard_map/ppermute | solution.py:371
  116.0 1.3 %collective-permute-start.33 = (bf16[2,320,128]{2,1,0:T(8,128)(2,1)S(1)}, bf16[2,320,128]{2,1,0:T(8,128)(2,1)S(1)}, u32[]{:S(2)}, u32[]{:S(2)}) collective-permute-start(bf16[2,320,128]{2,1,0:T(8,128)(2,1)S(1)} %get-tuple-element.143), channel_id=1, source_target_pairs={{0,8},{8,0},{16,24},{24,16},{1,9},{9,1},{17,25},{25,17},{2,10},{10... | collective-permute-start | bytes 491528 | tf_op jit(solution)/shard_map/ppermute | solution.py:371
  117.3 2.8 %collective-permute-done.32 = bf16[2,320,128]{2,1,0:T(8,128)(2,1)S(1)} collective-permute-done((bf16[2,320,128]{2,1,0:T(8,128)(2,1)S(1)}, bf16[2,320,128]{2,1,0:T(8,128)(2,1)S(1)}, u32[]{:S(2)}, u32[]{:S(2)}) %collective-permute-start.32) | collective-permute-done | bytes 163872 | tf_op jit(solution)/shard_map/ppermute | solution.py:371
  120.1 1.2 collective-permute-done.33
  (78 shorter events, 21.8 us)
Async XLA Ops:
  0.6 5.6 %copy-start.8 = (bf16[1,4,320,128]{3,2,1,0:T(8,128)(2,1)S(1)}, bf16[1,4,320,128]{3,2,1,0:T(8,128)(2,1)}, u32[]{:S(2)}) copy-start(bf16[1,4,320,128]{3,2,1,0:T(8,128)(2,1)} %param.10) | copy-start | bytes 983044
  1.7 7.9 %collective-permute-start.2 = (bf16[2,320,128]{2,1,0:T(8,128)(2,1)S(1)}, bf16[2,320,128]{2,1,0:T(8,128)(2,1)S(1)}, u32[]{:S(2)}, u32[]{:S(2)}) collective-permute-start(bf16[2,320,128]{2,1,0:T(8,128)(2,1)S(1)} %get-tuple-element.151.refs_1_), channel_id=1, source_target_pairs={{0,8},{8,0},{16,24},{24,16},{1,9},{9,1},{17,25},{25,17},{2,10},{10... | collective-permute-start | bytes 491528 | tf_op jit(solution)/shard_map/ppermute | solution.py:371
  4.7 7.1 %collective-permute-start.3 = (bf16[2,320,128]{2,1,0:T(8,128)(2,1)S(1)}, bf16[2,320,128]{2,1,0:T(8,128)(2,1)S(1)}, u32[]{:S(2)}, u32[]{:S(2)}) collective-permute-start(bf16[2,320,128]{2,1,0:T(8,128)(2,1)S(1)} %get-tuple-element.150.refs_3_.refs_4_), channel_id=1, source_target_pairs={{0,16},{8,24},{16,0},{24,8},{1,17},{9,25},{17,1},{25,9},{2,18},{10... | collective-permute-start | bytes 491528 | tf_op jit(solution)/shard_map/ppermute | solution.py:371
  6.3 5.5 %copy-start.6 = (s32[4,8]{1,0:T(4,128)S(1)}, s32[4,8]{1,0:T(4,128)}, u32[]{:S(2)}) copy-start(s32[4,8]{1,0:T(4,128)} %refs_0_.11) | copy-start | bytes 388
  6.3 8.3 %collective-permute-start.8 = (bf16[2,320,128]{2,1,0:T(8,128)(2,1)S(1)}, bf16[2,320,128]{2,1,0:T(8,128)(2,1)S(1)}, u32[]{:S(2)}, u32[]{:S(2)}) collective-permute-start(bf16[2,320,128]{2,1,0:T(8,128)(2,1)S(1)} %get-tuple-element.149.refs_1_), channel_id=1, source_target_pairs={{0,8},{8,0},{16,24},{24,16},{1,9},{9,1},{17,25},{25,17},{2,10},{10... | collective-permute-start | bytes 491528 | tf_op jit(solution)/shard_map/ppermute | solution.py:371
  6.9 8.4 %collective-permute-start.9 = (bf16[2,320,128]{2,1,0:T(8,128)(2,1)S(1)}, bf16[2,320,128]{2,1,0:T(8,128)(2,1)S(1)}, u32[]{:S(2)}, u32[]{:S(2)}) collective-permute-start(bf16[2,320,128]{2,1,0:T(8,128)(2,1)S(1)} %get-tuple-element.148.refs_3_.refs_4_), channel_id=1, source_target_pairs={{0,16},{8,24},{16,0},{24,8},{1,17},{9,25},{17,1},{25,9},{2,18},{10... | collective-permute-start | bytes 491528 | tf_op jit(solution)/shard_map/ppermute | solution.py:371
  12.4 7.0 %collective-permute-start.4 = (bf16[2,320,128]{2,1,0:T(8,128)(2,1)S(1)}, bf16[2,320,128]{2,1,0:T(8,128)(2,1)S(1)}, u32[]{:S(2)}, u32[]{:S(2)}) collective-permute-start(bf16[2,320,128]{2,1,0:T(8,128)(2,1)S(1)} %get-tuple-element.76), channel_id=1, source_target_pairs={{0,16},{8,24},{16,0},{24,8},{1,17},{9,25},{17,1},{25,9},{2,18},{10... | collective-permute-start | bytes 491528 | tf_op jit(solution)/shard_map/ppermute | solution.py:371
  14.0 5.4 %collective-permute-start.5 = (bf16[2,320,128]{2,1,0:T(8,128)(2,1)S(1)}, bf16[2,320,128]{2,1,0:T(8,128)(2,1)S(1)}, u32[]{:S(2)}, u32[]{:S(2)}) collective-permute-start(bf16[2,320,128]{2,1,0:T(8,128)(2,1)S(1)} %get-tuple-element.77), channel_id=1, source_target_pairs={{0,8},{8,0},{16,24},{24,16},{1,9},{9,1},{17,25},{25,17},{2,10},{10... | collective-permute-start | bytes 491528 | tf_op jit(solution)/shard_map/ppermute | solution.py:371
  15.9 4.7 %copy-start.2 = (f32[1,4,320,128]{3,2,1,0:T(8,128)S(1)}, f32[1,4,320,128]{3,2,1,0:T(8,128)}, u32[]{:S(2)}) copy-start(f32[1,4,320,128]{3,2,1,0:T(8,128)} %param.15) | copy-start | bytes 1966084
  16.0 4.7 %copy-start.3 = (f32[1,4,320,128]{3,2,1,0:T(8,128)S(1)}, f32[1,4,320,128]{3,2,1,0:T(8,128)}, u32[]{:S(2)}) copy-start(f32[1,4,320,128]{3,2,1,0:T(8,128)} %param.17) | copy-start | bytes 1966084
  16.0 7.4 %collective-permute-start.10 = (bf16[2,320,128]{2,1,0:T(8,128)(2,1)S(1)}, bf16[2,320,128]{2,1,0:T(8,128)(2,1)S(1)}, u32[]{:S(2)}, u32[]{:S(2)}) collective-permute-start(bf16[2,320,128]{2,1,0:T(8,128)(2,1)S(1)} %get-tuple-element.82), channel_id=1, source_target_pairs={{0,16},{8,24},{16,0},{24,8},{1,17},{9,25},{17,1},{25,9},{2,18},{10... | collective-permute-start | bytes 491528 | tf_op jit(solution)/shard_map/ppermute | solution.py:371
  20.1 15.0 %collective-permute-start.6 = (bf16[4,320,128]{2,1,0:T(8,128)(2,1)S(1)}, bf16[4,320,128]{2,1,0:T(8,128)(2,1)S(1)}, u32[]{:S(2)}, u32[]{:S(2)}) collective-permute-start(bf16[4,320,128]{2,1,0:T(8,128)(2,1)S(1)} %shard_map.116.den_ref.dmodel_ref), channel_id=1, source_target_pairs={{0,1},{1,0},{2,3},{3,2},{4,5},{5,4},{6,7},{7,6},{8,9},{9,8},{10,11... | collective-permute-start | bytes 983048 | tf_op jit(solution)/shard_map/ppermute | solution.py:376
  20.1 14.9 %collective-permute-start.7 = (bf16[4,320,128]{2,1,0:T(8,128)(2,1)S(1)}, bf16[4,320,128]{2,1,0:T(8,128)(2,1)S(1)}, u32[]{:S(2)}, u32[]{:S(2)}) collective-permute-start(bf16[4,320,128]{2,1,0:T(8,128)(2,1)S(1)} %shard_map.116.den_ref.dmodel_ref), channel_id=1, source_target_pairs={{1,2},{2,1},{3,4},{4,3},{5,6},{6,5},{0,8},{7,15},{9,10},{10,9},{11... | collective-permute-start | bytes 983048 | tf_op jit(solution)/shard_map/ppermute | solution.py:384
  20.7 10.9 %copy-start = (bf16[384,256]{1,0:T(8,128)(2,1)S(1)}, bf16[384,256]{1,0:T(8,128)(2,1)}, u32[]{:S(2)}) copy-start(bf16[384,256]{1,0:T(8,128)(2,1)} %constant.2.clone.matrix_ref.refs_3_) | copy-start | bytes 589828
  21.6 3.3 %copy-start.7 = (s32[1,512]{1,0:T(1,128)S(1)}, s32[1,512]{1,0:T(1,128)}, u32[]{:S(2)}) copy-start(s32[1,512]{1,0:T(1,128)} %rec.1) | copy-start | bytes 6148
  21.6 14.1 %collective-permute-start = (bf16[4,320,128]{2,1,0:T(8,128)(2,1)S(1)}, bf16[4,320,128]{2,1,0:T(8,128)(2,1)S(1)}, u32[]{:S(2)}, u32[]{:S(2)}) collective-permute-start(bf16[4,320,128]{2,1,0:T(8,128)(2,1)S(1)} %get-tuple-element.75), channel_id=1, source_target_pairs={{0,1},{1,0},{2,3},{3,2},{4,5},{5,4},{6,7},{7,6},{8,9},{9,8},{10,11... | collective-permute-start | bytes 983048 | tf_op jit(solution)/shard_map/ppermute | solution.py:376
  22.9 12.8 %collective-permute-start.1 = (bf16[4,320,128]{2,1,0:T(8,128)(2,1)S(1)}, bf16[4,320,128]{2,1,0:T(8,128)(2,1)S(1)}, u32[]{:S(2)}, u32[]{:S(2)}) collective-permute-start(bf16[4,320,128]{2,1,0:T(8,128)(2,1)S(1)} %get-tuple-element.75), channel_id=1, source_target_pairs={{1,2},{2,1},{3,4},{4,3},{5,6},{6,5},{0,8},{7,15},{9,10},{10,9},{11... | collective-permute-start | bytes 983048 | tf_op jit(solution)/shard_map/ppermute | solution.py:384
  23.3 11.1 %collective-permute-start.11 = (bf16[2,320,128]{2,1,0:T(8,128)(2,1)S(1)}, bf16[2,320,128]{2,1,0:T(8,128)(2,1)S(1)}, u32[]{:S(2)}, u32[]{:S(2)}) collective-permute-start(bf16[2,320,128]{2,1,0:T(8,128)(2,1)S(1)} %get-tuple-element.83), channel_id=1, source_target_pairs={{0,8},{8,0},{16,24},{24,16},{1,9},{9,1},{17,25},{25,17},{2,10},{10... | collective-permute-start | bytes 491528 | tf_op jit(solution)/shard_map/ppermute | solution.py:371
  35.0 1.1 copy-start.4
  37.1 2.9 %collective-permute-start.12 = (bf16[4,320,128]{2,1,0:T(8,128)(2,1)S(1)}, bf16[4,320,128]{2,1,0:T(8,128)(2,1)S(1)}, u32[]{:S(2)}, u32[]{:S(2)}) collective-permute-start(bf16[4,320,128]{2,1,0:T(8,128)(2,1)S(1)} %get-tuple-element.87), channel_id=1, source_target_pairs={{0,1},{1,0},{2,3},{3,2},{4,5},{5,4},{6,7},{7,6},{8,9},{9,8},{10,11... | collective-permute-start | bytes 983048 | tf_op jit(solution)/shard_map/ppermute | solution.py:376
  37.2 7.1 %collective-permute-start.13 = (bf16[4,320,128]{2,1,0:T(8,128)(2,1)S(1)}, bf16[4,320,128]{2,1,0:T(8,128)(2,1)S(1)}, u32[]{:S(2)}, u32[]{:S(2)}) collective-permute-start(bf16[4,320,128]{2,1,0:T(8,128)(2,1)S(1)} %get-tuple-element.87), channel_id=1, source_target_pairs={{1,2},{2,1},{3,4},{4,3},{5,6},{6,5},{0,8},{7,15},{9,10},{10,9},{11... | collective-permute-start | bytes 983048 | tf_op jit(solution)/shard_map/ppermute | solution.py:384
  45.3 2.9 %collective-permute-start.14 = (bf16[4,320,128]{2,1,0:T(8,128)(2,1)S(1)}, bf16[4,320,128]{2,1,0:T(8,128)(2,1)S(1)}, u32[]{:S(2)}, u32[]{:S(2)}) collective-permute-start(bf16[4,320,128]{2,1,0:T(8,128)(2,1)S(1)} %get-tuple-element.90), channel_id=1, source_target_pairs={{0,1},{1,0},{2,3},{3,2},{4,5},{5,4},{6,7},{7,6},{8,9},{9,8},{10,11... | collective-permute-start | bytes 983048 | tf_op jit(solution)/shard_map/ppermute | solution.py:376
  45.5 7.1 %collective-permute-start.15 = (bf16[4,320,128]{2,1,0:T(8,128)(2,1)S(1)}, bf16[4,320,128]{2,1,0:T(8,128)(2,1)S(1)}, u32[]{:S(2)}, u32[]{:S(2)}) collective-permute-start(bf16[4,320,128]{2,1,0:T(8,128)(2,1)S(1)} %get-tuple-element.90), channel_id=1, source_target_pairs={{1,2},{2,1},{3,4},{4,3},{5,6},{6,5},{0,8},{7,15},{9,10},{10,9},{11... | collective-permute-start | bytes 983048 | tf_op jit(solution)/shard_map/ppermute | solution.py:384
  53.6 3.0 %collective-permute-start.16 = (bf16[4,320,128]{2,1,0:T(8,128)(2,1)S(1)}, bf16[4,320,128]{2,1,0:T(8,128)(2,1)S(1)}, u32[]{:S(2)}, u32[]{:S(2)}) collective-permute-start(bf16[4,320,128]{2,1,0:T(8,128)(2,1)S(1)} %get-tuple-element.93), channel_id=1, source_target_pairs={{0,1},{1,0},{2,3},{3,2},{4,5},{5,4},{6,7},{7,6},{8,9},{9,8},{10,11... | collective-permute-start | bytes 983048 | tf_op jit(solution)/shard_map/ppermute | solution.py:376
  53.7 7.1 %collective-permute-start.17 = (bf16[4,320,128]{2,1,0:T(8,128)(2,1)S(1)}, bf16[4,320,128]{2,1,0:T(8,128)(2,1)S(1)}, u32[]{:S(2)}, u32[]{:S(2)}) collective-permute-start(bf16[4,320,128]{2,1,0:T(8,128)(2,1)S(1)} %get-tuple-element.93), channel_id=1, source_target_pairs={{1,2},{2,1},{3,4},{4,3},{5,6},{6,5},{0,8},{7,15},{9,10},{10,9},{11... | collective-permute-start | bytes 983048 | tf_op jit(solution)/shard_map/ppermute | solution.py:384
  62.5 0.7 copy-start.5
  64.7 4.4 %collective-permute-start.18 = (bf16[4,320,128]{2,1,0:T(8,128)(2,1)S(1)}, bf16[4,320,128]{2,1,0:T(8,128)(2,1)S(1)}, u32[]{:S(2)}, u32[]{:S(2)}) collective-permute-start(bf16[4,320,128]{2,1,0:T(8,128)(2,1)S(1)} %get-tuple-element.99), channel_id=1, source_target_pairs={{0,1},{1,0},{2,3},{3,2},{4,5},{5,4},{6,7},{7,6},{8,9},{9,8},{10,11... | collective-permute-start | bytes 983048 | tf_op jit(solution)/shard_map/ppermute | solution.py:376
  64.9 7.1 %collective-permute-start.19 = (bf16[4,320,128]{2,1,0:T(8,128)(2,1)S(1)}, bf16[4,320,128]{2,1,0:T(8,128)(2,1)S(1)}, u32[]{:S(2)}, u32[]{:S(2)}) collective-permute-start(bf16[4,320,128]{2,1,0:T(8,128)(2,1)S(1)} %get-tuple-element.99), channel_id=1, source_target_pairs={{1,2},{2,1},{3,4},{4,3},{5,6},{6,5},{0,8},{7,15},{9,10},{10,9},{11... | collective-permute-start | bytes 983048 | tf_op jit(solution)/shard_map/ppermute | solution.py:384
  67.5 4.4 %copy-start.1 = (f32[1,4,320,128]{3,2,1,0:T(8,128)S(1)}, f32[1,4,320,128]{3,2,1,0:T(8,128)}, u32[]{:S(2)}) copy-start(f32[1,4,320,128]{3,2,1,0:T(8,128)} %param.18) | copy-start | bytes 1966084
  73.0 4.5 %collective-permute-start.20 = (bf16[4,320,128]{2,1,0:T(8,128)(2,1)S(1)}, bf16[4,320,128]{2,1,0:T(8,128)(2,1)S(1)}, u32[]{:S(2)}, u32[]{:S(2)}) collective-permute-start(bf16[4,320,128]{2,1,0:T(8,128)(2,1)S(1)} %get-tuple-element.107), channel_id=1, source_target_pairs={{0,1},{1,0},{2,3},{3,2},{4,5},{5,4},{6,7},{7,6},{8,9},{9,8},{10,11... | collective-permute-start | bytes 983048 | tf_op jit(solution)/shard_map/ppermute | solution.py:376
  73.2 7.1 %collective-permute-start.21 = (bf16[4,320,128]{2,1,0:T(8,128)(2,1)S(1)}, bf16[4,320,128]{2,1,0:T(8,128)(2,1)S(1)}, u32[]{:S(2)}, u32[]{:S(2)}) collective-permute-start(bf16[4,320,128]{2,1,0:T(8,128)(2,1)S(1)} %get-tuple-element.107), channel_id=1, source_target_pairs={{1,2},{2,1},{3,4},{4,3},{5,6},{6,5},{0,8},{7,15},{9,10},{10,9},{11... | collective-permute-start | bytes 983048 | tf_op jit(solution)/shard_map/ppermute | solution.py:384
  82.2 4.4 %collective-permute-start.22 = (bf16[4,320,128]{2,1,0:T(8,128)(2,1)S(1)}, bf16[4,320,128]{2,1,0:T(8,128)(2,1)S(1)}, u32[]{:S(2)}, u32[]{:S(2)}) collective-permute-start(bf16[4,320,128]{2,1,0:T(8,128)(2,1)S(1)} %get-tuple-element.117), channel_id=1, source_target_pairs={{0,1},{1,0},{2,3},{3,2},{4,5},{5,4},{6,7},{7,6},{8,9},{9,8},{10,11... | collective-permute-start | bytes 983048 | tf_op jit(solution)/shard_map/ppermute | solution.py:376
  82.3 7.1 %collective-permute-start.23 = (bf16[4,320,128]{2,1,0:T(8,128)(2,1)S(1)}, bf16[4,320,128]{2,1,0:T(8,128)(2,1)S(1)}, u32[]{:S(2)}, u32[]{:S(2)}) collective-permute-start(bf16[4,320,128]{2,1,0:T(8,128)(2,1)S(1)} %get-tuple-element.117), channel_id=1, source_target_pairs={{1,2},{2,1},{3,4},{4,3},{5,6},{6,5},{0,8},{7,15},{9,10},{10,9},{11... | collective-permute-start | bytes 983048 | tf_op jit(solution)/shard_map/ppermute | solution.py:384
  91.2 14.2 %collective-permute-start.28 = (bf16[4,320,128]{2,1,0:T(8,128)(2,1)S(1)}, bf16[4,320,128]{2,1,0:T(8,128)(2,1)S(1)}, u32[]{:S(2)}, u32[]{:S(2)}) collective-permute-start(bf16[4,320,128]{2,1,0:T(8,128)(2,1)S(1)} %get-tuple-element.135), channel_id=1, source_target_pairs={{0,1},{1,0},{2,3},{3,2},{4,5},{5,4},{6,7},{7,6},{8,9},{9,8},{10,11... | collective-permute-start | bytes 983048 | tf_op jit(solution)/shard_map/ppermute | solution.py:376
  91.3 14.1 %collective-permute-start.29 = (bf16[4,320,128]{2,1,0:T(8,128)(2,1)S(1)}, bf16[4,320,128]{2,1,0:T(8,128)(2,1)S(1)}, u32[]{:S(2)}, u32[]{:S(2)}) collective-permute-start(bf16[4,320,128]{2,1,0:T(8,128)(2,1)S(1)} %get-tuple-element.135), channel_id=1, source_target_pairs={{1,2},{2,1},{3,4},{4,3},{5,6},{6,5},{0,8},{7,15},{9,10},{10,9},{11... | collective-permute-start | bytes 983048 | tf_op jit(solution)/shard_map/ppermute | solution.py:384
  92.6 8.8 %collective-permute-start.24 = (bf16[2,320,128]{2,1,0:T(8,128)(2,1)S(1)}, bf16[2,320,128]{2,1,0:T(8,128)(2,1)S(1)}, u32[]{:S(2)}, u32[]{:S(2)}) collective-permute-start(bf16[2,320,128]{2,1,0:T(8,128)(2,1)S(1)} %get-tuple-element.147), channel_id=1, source_target_pairs={{0,8},{8,0},{16,24},{24,16},{1,9},{9,1},{17,25},{25,17},{2,10},{10... | collective-permute-start | bytes 491528 | tf_op jit(solution)/shard_map/ppermute | solution.py:371
  93.4 8.0 %collective-permute-start.25 = (bf16[2,320,128]{2,1,0:T(8,128)(2,1)S(1)}, bf16[2,320,128]{2,1,0:T(8,128)(2,1)S(1)}, u32[]{:S(2)}, u32[]{:S(2)}) collective-permute-start(bf16[2,320,128]{2,1,0:T(8,128)(2,1)S(1)} %get-tuple-element.146), channel_id=1, source_target_pairs={{0,16},{8,24},{16,0},{24,8},{1,17},{9,25},{17,1},{25,9},{2,18},{10... | collective-permute-start | bytes 491528 | tf_op jit(solution)/shard_map/ppermute | solution.py:371
  102.2 5.8 %collective-permute-start.26 = (bf16[2,320,128]{2,1,0:T(8,128)(2,1)S(1)}, bf16[2,320,128]{2,1,0:T(8,128)(2,1)S(1)}, u32[]{:S(2)}, u32[]{:S(2)}) collective-permute-start(bf16[2,320,128]{2,1,0:T(8,128)(2,1)S(1)} %get-tuple-element.131), channel_id=1, source_target_pairs={{0,16},{8,24},{16,0},{24,8},{1,17},{9,25},{17,1},{25,9},{2,18},{10... | collective-permute-start | bytes 491528 | tf_op jit(solution)/shard_map/ppermute | solution.py:371
  104.1 11.0 %collective-permute-start.27 = (bf16[2,320,128]{2,1,0:T(8,128)(2,1)S(1)}, bf16[2,320,128]{2,1,0:T(8,128)(2,1)S(1)}, u32[]{:S(2)}, u32[]{:S(2)}) collective-permute-start(bf16[2,320,128]{2,1,0:T(8,128)(2,1)S(1)} %get-tuple-element.133), channel_id=1, source_target_pairs={{0,8},{8,0},{16,24},{24,16},{1,9},{9,1},{17,25},{25,17},{2,10},{10... | collective-permute-start | bytes 491528 | tf_op jit(solution)/shard_map/ppermute | solution.py:371
  106.1 5.6 %collective-permute-start.30 = (bf16[2,320,128]{2,1,0:T(8,128)(2,1)S(1)}, bf16[2,320,128]{2,1,0:T(8,128)(2,1)S(1)}, u32[]{:S(2)}, u32[]{:S(2)}) collective-permute-start(bf16[2,320,128]{2,1,0:T(8,128)(2,1)S(1)} %get-tuple-element.145), channel_id=1, source_target_pairs={{0,8},{8,0},{16,24},{24,16},{1,9},{9,1},{17,25},{25,17},{2,10},{10... | collective-permute-start | bytes 491528 | tf_op jit(solution)/shard_map/ppermute | solution.py:371
  106.9 7.0 %collective-permute-start.31 = (bf16[2,320,128]{2,1,0:T(8,128)(2,1)S(1)}, bf16[2,320,128]{2,1,0:T(8,128)(2,1)S(1)}, u32[]{:S(2)}, u32[]{:S(2)}) collective-permute-start(bf16[2,320,128]{2,1,0:T(8,128)(2,1)S(1)} %get-tuple-element.144), channel_id=1, source_target_pairs={{0,16},{8,24},{16,0},{24,8},{1,17},{9,25},{17,1},{25,9},{2,18},{10... | collective-permute-start | bytes 491528 | tf_op jit(solution)/shard_map/ppermute | solution.py:371
  114.7 5.4 %collective-permute-start.32 = (bf16[2,320,128]{2,1,0:T(8,128)(2,1)S(1)}, bf16[2,320,128]{2,1,0:T(8,128)(2,1)S(1)}, u32[]{:S(2)}, u32[]{:S(2)}) collective-permute-start(bf16[2,320,128]{2,1,0:T(8,128)(2,1)S(1)} %get-tuple-element.141), channel_id=1, source_target_pairs={{0,16},{8,24},{16,0},{24,8},{1,17},{9,25},{17,1},{25,9},{2,18},{10... | collective-permute-start | bytes 491528 | tf_op jit(solution)/shard_map/ppermute | solution.py:371
  116.0 5.3 %collective-permute-start.33 = (bf16[2,320,128]{2,1,0:T(8,128)(2,1)S(1)}, bf16[2,320,128]{2,1,0:T(8,128)(2,1)S(1)}, u32[]{:S(2)}, u32[]{:S(2)}) collective-permute-start(bf16[2,320,128]{2,1,0:T(8,128)(2,1)S(1)} %get-tuple-element.143), channel_id=1, source_target_pairs={{0,8},{8,0},{16,24},{24,16},{1,9},{9,1},{17,25},{25,17},{2,10},{10... | collective-permute-start | bytes 491528 | tf_op jit(solution)/shard_map/ppermute | solution.py:371

commit v3 on v2

--- a/solution.py
+++ b/solution.py
@@ -13,6 +13,7 @@
 FIRST = (4.0 / 5.0, -1.0 / 5.0, 4.0 / 105.0, -1.0 / 280.0)
 SPEED = 0.15
 PAD = 8
+PARTS = 2
 UNROLL = 4
 F32, BF16 = jnp.float32, jnp.bfloat16
 VMEM_LIMIT = 4 << 20
@@ -21,15 +22,16 @@
 SM = pl.BlockSpec(memory_space=pltpu.SMEM)
 
 
-def call(kernel, outs, ins, specs, out_specs=None, scratch=(), flops=0):
+def call(kernel, outs, ins, specs=None, out_specs=None, scratch=(), flops=0, aliases=None):
     outs = tuple(jax.ShapeDtypeStruct(shape, dtype) for shape, dtype in outs)
     moved_bytes = sum(math.prod(x.shape) * x.dtype.itemsize for x in (*ins, *outs))
     return pl.pallas_call(
         kernel,
         out_shape=outs,
-        in_specs=list(specs),
+        in_specs=list(specs or [VM] * len(ins)),
         out_specs=tuple(out_specs or [VM] * len(outs)),
         scratch_shapes=list(scratch),
+        input_output_aliases=aliases or {},
         cost_estimate=pl.CostEstimate(flops=flops, bytes_accessed=moved_bytes, transcendentals=0),
         compiler_params=pltpu.CompilerParams(vmem_limit_bytes=VMEM_LIMIT),
     )(*ins)
@@ -82,14 +84,26 @@
     return even, valid
 
 
-def x_values(own, on_ref, off_ref, rows):
+def x_values(own, on_ref, off_ref, rows, off_rows):
     even, valid = where_am_i()
     count = len(own)
     on = [on_ref[l, rows, :].astype(F32) for l in range(count)]
-    off = [jnp.where(valid, off_ref[l, rows, :].astype(F32), 0.0) for l in range(count)]
+    off = [jnp.where(valid, off_ref[l, off_rows, :].astype(F32), 0.0) for l in range(count)]
     low = [jnp.where(even, b, a) for a, b in zip(on, off)]
     high = [jnp.where(even, a, b) for a, b in zip(on, off)]
     return low[count - 4 :] + own + high[:4]
+
+
+def part_rows(part, width, off_ref, body):
+    size = width // PARTS
+    first = part * size
+    back = first if off_ref.shape[1] == size else 0
+
+    @pl.loop(0, size // 16)
+    def _(j):
+        at = pl.multiple_of(first + 16 * j, 16)
+        off_at = pl.multiple_of(first - back + 16 * j, 16)
+        body(pl.ds(at, 16), pl.ds(off_at, 16), pl.ds(at + PAD, 16), pl.ds(pl.multiple_of(16 * j, 16), 16))
 
 
 def x_pairs(values, layer):
@@ -104,18 +118,18 @@
         ref[l, pl.ds(tall - PAD, PAD), :] = zeros
 
 
-def prepare_kernel(p_ref, q_ref, pw_ref, qw_ref, ph_ref, qh_ref):
+def prepare_kernel(p_ref, pw_ref, *half_refs):
     layers, width, _ = p_ref.shape
-    for src, wide, half in ((p_ref, pw_ref, ph_ref), (q_ref, qw_ref, qh_ref)):
-        zero_pads(wide)
-
-        @pl.loop(0, width // 16)
-        def _(j, src=src, wide=wide, half=half):
-            at = pl.multiple_of(16 * j, 16)
-            for l in range(layers):
-                v = src[l, pl.ds(at, 16), :]
-                wide[l, pl.ds(at + PAD, 16), :] = v
-                half[l, pl.ds(at, 16), :] = v.astype(BF16)
+    zero_pads(pw_ref)
+
+    @pl.loop(0, width // 16)
+    def _(j):
+        at = pl.multiple_of(16 * j, 16)
+        for l in range(layers):
+            v = p_ref[l, pl.ds(at, 16), :]
+            pw_ref[l, pl.ds(at + PAD, 16), :] = v
+            for half_ref in half_refs:
+                half_ref[l, pl.ds(at, 16), :] = v.astype(BF16)
 
 
 def list_kernel(rec_ref, layers, width, depth, list_ref):
@@ -125,15 +139,22 @@
 
     def step(i, count):
         local = rec_ref[0, i] - first
-        inside = jnp.logical_and(local >= 0, local < cells)
+        list_ref[count] = i
+        inside = jnp.bitwise_or(local, cells - 1 - local) >= 0
+        return count + jnp.where(inside, 1, 0)
+
+    count = lax.fori_loop(0, total, step, jnp.int32(0), unroll=8)
+
+    @pl.loop(0, count)
+    def _(c):
+        i = list_ref[c]
+        local = rec_ref[0, i] - first
         skip = jnp.int32(PAD * depth)
         for l in range(1, layers):
             skip += jnp.where(local >= l * width * depth, 2 * PAD * depth, 0)
-        list_ref[count] = local + skip
-        list_ref[total + UNROLL + count] = i
-        return count + jnp.where(inside, 1, 0)
-
-    count = lax.fori_loop(0, total, step, jnp.int32(0))
+        list_ref[c] = local + skip
+        list_ref[total + UNROLL + c] = i
+
     for n in range(UNROLL):
         list_ref[count + n] = -1
         list_ref[total + UNROLL + count + n] = 0
@@ -166,18 +187,23 @@
     add_receivers(n, field_ref, source_ref, list_ref, observed_ref)
 
 
-def first_adjoint_kernel(n, p_ref, q_ref, list_ref, observed_ref, a_ref, half_ref):
+def first_adjoint_kernel(n, p_ref, q_ref, list_ref, observed_ref, a_ref, half_ref, *part_refs):
     a_ref[...] = q_ref[...]
     add_receivers(n, p_ref, a_ref, list_ref, observed_ref)
     layers, width, _ = half_ref.shape
     tall = width + 2 * PAD
 
-    @pl.loop(0, width // 16)
-    def _(j):
-        at = pl.multiple_of(16 * j, 16)
-        for l in range(layers):
-            from_row = pl.multiple_of(at + l * tall + PAD, 8)
-            half_ref[l, pl.ds(at, 16), :] = a_ref[pl.ds(from_row, 16), :].astype(BF16)
+    for n, part_ref in enumerate(part_refs):
+        size = part_ref.shape[1]
+
+        @pl.loop(0, size // 16)
+        def _(j, n=n, size=size, part_ref=part_ref):
+            at = pl.multiple_of(16 * j, 16)
+            for l in range(layers):
+                from_row = pl.multiple_of(at + n * size + l * tall + PAD, 8)
+                value = a_ref[pl.ds(from_row, 16), :].astype(BF16)
+                half_ref[l, pl.ds(pl.multiple_of(at + n * size, 16), 16), :] = value
+                part_ref[l, pl.ds(at, 16), :] = value
 
 
 def log_kernel(den_ref, matrix_ref, log_ref, s2_ref, s3_ref, z_ref):
@@ -245,21 +271,16 @@
             dz_ref[l, rows, :] = d_z
 
 
-def forward_x_kernel(
-    f_ref, on_ref, off_ref, part_ref, s1_ref, scale_ref, before_ref,
-    dx_ref, applied_ref, next_ref, half_ref,
-):
+def forward_x_kernel(part, f_ref, on_ref, off_ref, part_ref, s1_ref, scale_ref, before_ref, *refs):
+    dx_ref, applied_ref, next_ref, half_ref, send_ref = refs[-5:]
     layers, width, _ = part_ref.shape
-    zero_pads(next_ref)
     shift = before_ref.shape[1] != width
-
-    @pl.loop(0, width // 16)
-    def _(j):
-        at = pl.multiple_of(16 * j, 16)
-        rows = pl.ds(at, 16)
-        wide = pl.ds(at + PAD, 16)
+    if part == 0:
+        zero_pads(next_ref)
+
+    def body(rows, off_rows, wide, send_rows):
         own = [f_ref[l, wide, :] for l in range(layers)]
-        values = x_values(own, on_ref, off_ref, rows)
+        values = x_values(own, on_ref, off_ref, rows, off_rows)
         for l in range(layers):
             lap, d_x = weighted(x_pairs(values, l))
             applied = part_ref[l, rows, :] + (lap - s1_ref[l, rows, :] * d_x)
@@ -268,7 +289,11 @@
             dx_ref[l, rows, :] = d_x
             applied_ref[l, rows, :] = applied
             next_ref[l, wide, :] = later
-            half_ref[l, rows, :] = later.astype(BF16)
+            narrow = later.astype(BF16)
+            half_ref[l, rows, :] = narrow
+            send_ref[l, send_rows, :] = narrow
+
+    part_rows(part, width, off_ref, body)
 
 
 def adjoint_yz_kernel(
@@ -298,24 +323,22 @@
 
 
 def adjoint_x_kernel(
-    last, f_ref, on_ref, off_ref, part_ref, s1_ref, scale_ref, before_ref,
+    part, last, f_ref, on_ref, off_ref, part_ref, s1_ref, scale_ref, before_ref,
     source_ref, fdx_ref, den_in, *refs,
 ):
     if last:
-        vel_in, fapplied_ref, vmodel_ref, q_ref, a_ref, half_ref, den_ref, shot_ref = refs
+        vel_in, fapplied_ref, vmodel_ref = refs[:3]
+        a_ref, half_ref, den_ref, send_ref, shot_ref = refs[-5:]
     else:
-        q_ref, a_ref, half_ref, den_ref = refs
+        a_ref, half_ref, den_ref, q_ref, send_ref = refs[-5:]
     layers, width, _ = part_ref.shape
-    zero_pads(a_ref)
     shift = before_ref.shape[1] != width
-
-    @pl.loop(0, width // 16)
-    def _(j):
-        at = pl.multiple_of(16 * j, 16)
-        rows = pl.ds(at, 16)
-        wide = pl.ds(at + PAD, 16)
+    if part == 0:
+        zero_pads(a_ref)
+
+    def body(rows, off_rows, wide, send_rows):
         own = [f_ref[l, wide, :] for l in range(layers)]
-        values = x_values(own, on_ref, off_ref, rows)
+        values = x_values(own, on_ref, off_ref, rows, off_rows)
         for l in range(layers):
             lap, d_x = weighted(x_pairs(values, l))
             applied = part_ref[l, rows, :] + (lap - s1_ref[l, rows, :] * d_x)
@@ -325,14 +348,16 @@
                 q_ref[l, rows, :] = later
             adjoint = later + source_ref[l, wide, :]
             a_ref[l, wide, :] = adjoint
-            half_ref[l, rows, :] = adjoint.astype(BF16)
+            narrow = adjoint.astype(BF16)
+            half_ref[l, rows, :] = narrow
+            send_ref[l, send_rows, :] = narrow
             den_ref[l, rows, :] = den_in[l, rows, :] + d_x * fdx_ref[l, rows, :]
             if last:
                 total = vel_in[l, rows, :] + adjoint * fapplied_ref[l, rows, :]
                 v = vmodel_ref[l, rows, :].astype(F32)
-                shot_ref[l, rows, :] = ((2.0 * SPEED) * v * total).astype(BF16)
-    if last:
-        q_ref[...] = jnp.zeros(q_ref.shape, F32)
+                shot_ref[l, send_rows, :] = ((2.0 * SPEED) * v * total).astype(BF16)
+
+    part_rows(part, width, off_ref, body)
 
 
 def last_yz_kernel(f_ref, matrix_ref, fdy_ref, fdz_ref, den_in, den_ref, z_ref):
@@ -351,38 +376,40 @@
             )
 
 
-def last_x_kernel(f_ref, on_ref, off_ref, fdx_ref, den_in, scale_ref, dmodel_ref, shot_ref):
-    layers, width, _ = shot_ref.shape
-
-    @pl.loop(0, width // 16)
-    def _(j):
-        at = pl.multiple_of(16 * j, 16)
-        rows = pl.ds(at, 16)
-        own = [f_ref[l, pl.ds(at + PAD, 16), :] for l in range(layers)]
-        values = x_values(own, on_ref, off_ref, rows)
+def last_x_kernel(part, f_ref, on_ref, off_ref, fdx_ref, den_in, scale_ref, dmodel_ref, shot_ref):
+    layers, width, _ = den_in.shape
+
+    def body(rows, off_rows, wide, send_rows):
+        own = [f_ref[l, wide, :] for l in range(layers)]
+        values = x_values(own, on_ref, off_ref, rows, off_rows)
         for l in range(layers):
             d_x = weighted(x_pairs(values, l))[1]
             total = den_in[l, rows, :] + d_x * fdx_ref[l, rows, :]
             density = dmodel_ref[l, rows, :].astype(F32)
-            shot_ref[l, rows, :] = (scale_ref[l, rows, :] / density * total).astype(BF16)
+            shot_ref[l, send_rows, :] = (scale_ref[l, rows, :] / density * total).astype(BF16)
+
+    part_rows(part, width, off_ref, body)
 
 
 def swap_over(axis, count, bit, value):
     return lax.ppermute(value, axis, [(i, i ^ bit) for i in range(count)])
 
 
-def beside(half):
+def paired(half):
+    count = lax.axis_size("sub")
+    return lax.ppermute(half, "sub", [(i, i ^ 1) for i in range(count)])
+
+
+def across(half, fill=True):
     groups, count = lax.axis_size("shot"), lax.axis_size("sub")
-    on = lax.ppermute(half, "sub", [(i, i ^ 1) for i in range(count)])
     pairs = []
     for s in range(groups):
         for i in range(1, count - 1, 2):
             pairs += [(s * count + i, s * count + i + 1), (s * count + i + 1, s * count + i)]
-        if groups % 2 == 0:
+        if fill and groups % 2 == 0:
             for i in (0, count - 1):
                 pairs.append((s * count + i, (s ^ 1) * count + i))
-    off = lax.ppermute(half, ("shot", "sub"), pairs)
-    return on, off
+    return lax.ppermute(half, ("shot", "sub"), pairs)
 
 
 def bits_of(groups):
@@ -425,7 +452,7 @@
             out_ref[spot, :, :] = far[...]
 
 
-def fetch(tile, cover):
+def fetch(tile, cover, tie=lambda x: x, tie_last=lambda x: x):
     groups = cover.shape[0]
     layers = tile.shape[0] // 2
     small = (layers, *tile.shape[1:])
@@ -444,11 +471,13 @@
             offsets[way] = offsets[way] + [o ^ bit for o in offsets[way]]
     last = [way[-1] for way in ways]
     count = len(held[0])
+    held = tie(held)
     sends = call(
         lambda *refs: pick_kernel(offsets, last, *refs),
         [(small, BF16)] * 2, [cover, *held[0], *held[1]], [SM] + [VM] * (2 * count),
     )
     far = [swap_over("shot", groups, last[way], sends[way]) for way in range(2)]
+    far = tie_last(far)
     (out,) = call(
         lambda *refs: gather_kernel(offsets, last, *refs),
         [(tile.shape, BF16)], [cover, *held[0], far[0], *held[1], far[1]],
@@ -457,14 +486,13 @@
     return out
 
 
-def bucket_kernel(offsets, bits, cover_ref, tile_ref, *refs):
+def bucket_kernel(offsets, bits, cover_ref, *refs):
     me, column = lax.axis_index("shot"), lax.axis_index("sub")
-    layers = tile_ref.shape[0] // 2
-    got, outs = refs[:2], refs[2:]
+    own, got, outs = refs[:1], refs[1:2], refs[2:]
     mine = cover_ref[me, column]
-    for way in range(2):
+    for way in range(1):
         theirs = cover_ref[me ^ bits[way], column]
-        own_ref = tile_ref.at[pl.ds(way * layers, layers)]
+        own_ref = own[way]
         for n, offset in enumerate(offsets[way]):
             out = outs[way * len(offsets[way]) + n]
             a = jnp.where(mine == (me ^ offset), own_ref[...].astype(F32), 0.0)
@@ -472,40 +500,29 @@
             out[...] = (a + b).astype(out.dtype)
 
 
-def give_back(tile, cover):
+def give_back(part, way, cover):
     groups = cover.shape[0]
-    layers = tile.shape[0] // 2
-    small = (layers, *tile.shape[1:])
-    ways = [bits_of(groups), bits_of(groups)[::-1]]
-    got = [
-        swap_over("shot", groups, ways[way][0], tile[way * layers : (way + 1) * layers])
-        for way in range(2)
-    ]
-    offsets, types = [], []
-    for way in ways:
-        own = [0]
-        for b in reversed(way[1:]):
-            own = own + [o ^ b for o in own]
-        offsets.append(own)
-        types += [BF16 if o & way[1] else F32 for o in own]
+    layers = part.shape[0]
+    bits = bits_of(groups)[:: 1 if way == 0 else -1]
+    got = swap_over("shot", groups, bits[0], part)
+    offsets = [0]
+    for b in reversed(bits[1:]):
+        offsets = offsets + [o ^ b for o in offsets]
+    types = [BF16 if o & bits[1] else F32 for o in offsets]
     sums = call(
-        lambda *refs: bucket_kernel(offsets, [way[0] for way in ways], *refs),
-        [(small, kind) for kind in types], [cover, tile, *got], [SM] + [VM] * 3,
+        lambda *refs: bucket_kernel([offsets], [bits[0]], *refs),
+        [(part.shape, kind) for kind in types], [cover, part, got], [SM, VM, VM],
     )
-    parts = []
-    for way in range(2):
-        count = len(offsets[way])
-        left = dict(zip(offsets[way], sums[way * count : (way + 1) * count]))
-        for b in ways[way][1:]:
-            away = [o for o in left if o & b]
-            block = jnp.concatenate([left[o].astype(BF16) for o in away], axis=0)
-            came = swap_over("shot", groups, b, block)
-            left = {
-                o ^ b: left[o ^ b] + came[n * layers : (n + 1) * layers].astype(F32)
-                for n, o in enumerate(away)
-            }
-        parts.append(left[0])
-    return jnp.concatenate(parts, axis=0)
+    left = dict(zip(offsets, sums))
+    for b in bits[1:]:
+        away = [o for o in left if o & b]
+        block = jnp.concatenate([left[o].astype(BF16) for o in away], axis=0)
+        came = swap_over("shot", groups, b, block)
+        left = {
+            o ^ b: left[o ^ b] + came[n * layers : (n + 1) * layers].astype(F32)
+            for n, o in enumerate(away)
+        }
+    return left[0]
 
 
 def body(vel_model, den_model, cover, receivers, observed, p_now, p_before, q_now, q_before):
@@ -517,78 +534,109 @@
     matrix = z_matrix(depth)
     seen = observed[0]
 
-    den = fetch(den_model[0], cover)
-    vel = fetch(vel_model[0], cover)
-
-    p, q, p_half, q_half = call(prepare_kernel, [padded, padded, half, half], [p_now[0], q_now[0]], [VM] * 2)
+    size = width // PARTS
+    part_half = ((layers, size, depth), BF16)
+    parts = range(PARTS)
+
+    p, p_half = call(prepare_kernel, [padded, half], [p_now[0]])
     n_rec = receivers.shape[1]
     (lists,) = call(
         lambda rec, out: list_kernel(rec, layers, width, depth, out),
         [((2 * (n_rec + UNROLL) + 1,), jnp.int32)], [receivers], [SM], [SM],
     )
-    p, lists = lax.optimization_barrier((p, lists))
-
-    log_den, s2, s3 = call(log_kernel, [padded, narrow, narrow], [den, matrix], [VM] * 2, scratch=z_scratch)
-    den_on, den_off = beside(den)
-    s1, scale = call(slope_x_kernel, [narrow, narrow], [log_den, den_on, den_off, vel], [VM] * 4)
+    on, off = paired(p_half), across(p_half, fill=False)
+    kept = {}
+
+    def tie(held):
+        held, kept["p"] = lax.optimization_barrier((held, p))
+        return held
+
+    def tie_last(far):
+        far, kept["lists"], kept["on"], kept["off"] = lax.optimization_barrier((far, lists, on, off))
+        return far
+
+    den = fetch(den_model[0], cover, tie, tie_last)
+    vel = fetch(vel_model[0], cover)
+    p, lists, on, offs = kept["p"], kept["lists"], kept["on"], [kept["off"]] * PARTS
+
+    log_den, s2, s3 = call(log_kernel, [padded, narrow, narrow], [den, matrix], scratch=z_scratch)
+    s1, scale = call(slope_x_kernel, [narrow, narrow], [log_den, paired(den), across(den), vel])
 
     stored, sources = [], []
     before = p_before[0]
     for step in range(ITERS):
-        on, off = beside(p_half)
-        part, d_y, d_z = call(
-            forward_yz_kernel, [narrow] * 3, [p, s2, s3, matrix], [VM] * 4, scratch=z_scratch
-        )
+        part, d_y, d_z = call(forward_yz_kernel, [narrow] * 3, [p, s2, s3, matrix], scratch=z_scratch)
         if step > 0:
             (source,) = call(
                 lambda *refs, n=step - 1: receivers_kernel(n, *refs),
                 [flat], [p.reshape(flat[0]), lists, seen], [VM, SM, SM],
             )
             sources.append(source.reshape(padded[0]))
-        d_x, applied, later, p_half = call(
-            forward_x_kernel, [narrow, narrow, padded, half],
-            [p, on, off, part, s1, scale, before], [VM] * 7,
-        )
+        made, sends = (), []
+        for k in parts:
+            ins = [p, on, offs[k], part, s1, scale, before]
+            *made, send = call(
+                lambda *refs, k=k: forward_x_kernel(k, *refs),
+                [narrow, narrow, padded, half, part_half], [*ins, *made],
+                aliases={len(ins) + n: n for n in range(len(made))},
+            )
+            if step < ITERS - 1:
+                sends.append(across(send))
+        d_x, applied, later, p_half = made
+        if step < ITERS - 1:
+            on, offs = paired(p_half), sends
         stored.append((applied, d_x, d_y, d_z))
         before, p = p, later
 
-    a, a_half = call(
+    (q,) = call(prepare_kernel, [padded], [q_now[0]])
+    a, a_half, *sends = call(
         lambda *refs: first_adjoint_kernel(ITERS - 1, *refs),
-        [flat, half], [p.reshape(flat[0]), q.reshape(flat[0]), lists, seen], [VM, VM, SM, SM],
+        [flat, half] + [part_half] * PARTS, [p.reshape(flat[0]), q.reshape(flat[0]), lists, seen],
+        [VM, VM, SM, SM],
     )
+    offs = [across(send) for send in sends]
+    on = paired(a_half)
     a = a.reshape(padded[0])
     before, current = q_before[0], q
     sums = ()
     for step in range(ITERS - 1):
         f_applied, f_dx, f_dy, f_dz = stored[ITERS - 1 - step]
         last = step == ITERS - 2
-        on, off = beside(a_half)
         part, sum_vel, sum_den = call(
             lambda *refs, first=step == 0: adjoint_yz_kernel(first, *refs),
-            [narrow] * 3, [a, s2, s3, matrix, f_dy, f_dz, f_applied, *sums], [VM] * (7 + len(sums)),
-            scratch=z_scratch,
+            [narrow] * 3, [a, s2, s3, matrix, f_dy, f_dz, f_applied, *sums], scratch=z_scratch,
         )
         extra = [sum_vel, stored[0][0], vel] if last else []
-        later, a, a_half, sum_den, *shot = call(
-            lambda *refs, last=last: adjoint_x_kernel(last, *refs),
-            [((8, 128), F32) if last else narrow, padded, half, narrow] + ([half] if last else []),
-            [a, on, off, part, s1, scale, before, sources[ITERS - 2 - step], f_dx, sum_den, *extra],
-            [VM] * (10 + len(extra)),
+        made, sends, shot_vel = (), [], []
+        for k in parts:
+            ins = [
+                a, on, offs[k], part, s1, scale, before, sources[ITERS - 2 - step], f_dx, sum_den, *extra,
+            ]
+            kinds = [padded, half, narrow] + ([] if last else [narrow])
+            outs = call(
+                lambda *refs, k=k, last=last: adjoint_x_kernel(k, last, *refs),
+                kinds + [part_half] * (2 if last else 1), [*ins, *made],
+                aliases={len(ins) + n: n for n in range(len(made))},
+            )
+            made = outs[: len(kinds)]
+            sends.append(across(outs[len(kinds)]))
+            shot_vel += outs[len(kinds) + 1 :]
+        a, a_half, sum_den, *later = made
+        on, offs = paired(a_half), sends
+        if not last:
+            before, current = current, later[0]
+        sums = (sum_vel, sum_den)
+    _, f_dx, f_dy, f_dz = stored[0]
+    grad_vel = [give_back(shot_vel[k], k, cover) for k in parts]
+    (sum_den,) = call(last_yz_kernel, [narrow], [a, matrix, f_dy, f_dz, sum_den], scratch=z_scratch)
+    grad_den = []
+    for k in parts:
+        (shot_den,) = call(
+            lambda *refs, k=k: last_x_kernel(k, *refs),
+            [part_half], [a, on, offs[k], f_dx, sum_den, scale, den],
         )
-        before, current = current, later
-        sums = (sum_vel, sum_den)
-    shot_vel = shot[0]
-    _, f_dx, f_dy, f_dz = stored[0]
-    on, off = beside(a_half)
-    grad_vel = give_back(shot_vel, cover)
-    (sum_den,) = call(
-        last_yz_kernel, [narrow], [a, matrix, f_dy, f_dz, sum_den], [VM] * 5, scratch=z_scratch
-    )
-    (shot_den,) = call(
-        last_x_kernel, [half], [a, on, off, f_dx, sum_den, scale, den], [VM] * 7
-    )
-    grad_den = give_back(shot_den, cover)
-    return grad_vel[None], grad_den[None]
+        grad_den.append(give_back(shot_den, k, cover))
+    return jnp.concatenate(grad_vel, axis=1)[None], jnp.concatenate(grad_den, axis=1)[None]
 
 
 def solution(mesh):

time: 122 us -> 110 us (0.902)
  waiting for transfers between devices: 44.6 us -> 28.9 us
  starting transfers between devices: 31.2 us -> 39.2 us
  Pallas kernels: 41.2 us -> 37.6 us
    ppermute x18 -> x25, starting transfers between devices: 12.5 us -> 21 us  [the longest x16 16.4 us: across(): return lax.ppermute(half, ('shot', 'sub'), pairs)]
    ppermute x18 -> x25, waiting for transfers between devices: 21.2 us -> 13.3 us  [the longest x16 13.3 us: across(): return lax.ppermute(half, ('shot', 'sub'), pairs)]
    ppermute x16, waiting for transfers between devices: 23.3 us -> 15.6 us  [swap_over(): return lax.ppermute(value, axis, [(i, i ^ bit) for i in range(count)])]
    pallas_call x30 -> x41, Pallas kernels: 41.2 us -> 37.6 us  [call(): pl.pallas_call(kernel, out_shape=outs, in_specs=list(specs or [VM] * len(...]
  transfers between devices with their start and end apart: 34 -> 41, of which waited for: 16 -> 21; matrix products, arithmetic and copies ran while one was open for 1% -> 1% of each run, Pallas kernels for 25% -> 28%
where the time goes in v3:
time: 110 us
  starting transfers between devices  39.2 us (36%)
  Pallas kernels  37.6 us (34%)
  waiting for transfers between devices  28.9 us (26%)
  other arithmetic  1.9 us (2%)
  local copies, waits for them, and re-layouts  1.6 us (1%)
    pallas_call x41, Pallas kernels, call(): pl.pallas_call(kernel, out_shape=outs, in_specs=list(specs or [VM] * len(...  37.6 us
    ppermute x16, starting transfers between devices, swap_over(): return lax.ppermute(value, axis, [(i, i ^ bit) for i in range(count)])  18.2 us
    ppermute x16, starting transfers between devices, across(): return lax.ppermute(half, ('shot', 'sub'), pairs)  16.4 us
    ppermute x16, waiting for transfers between devices, swap_over(): return lax.ppermute(value, axis, [(i, i ^ bit) for i in range(count)])  15.6 us
    ppermute x16, waiting for transfers between devices, across(): return lax.ppermute(half, ('shot', 'sub'), pairs)  13.3 us
    ppermute x9, starting transfers between devices, paired(): return lax.ppermute(half, 'sub', [(i, i ^ 1) for i in range(count)])  4.51 us
  transfers between devices with their start and end apart: 41, of which 21 were waited for; matrix products, arithmetic and copies ran while one was open for 1% of the time, Pallas kernels for 28%

profile of v3, /device:TPU:0, one launch (start us, length us, event | category | flops | bytes accessed | tf_op | source)
XLA Modules:
  0.0 110.1 jit_solution(1082464169809498326)
XLA Ops:
  0.6 1.1 slice_bitcast_fusion.2
  1.7 3.1 %collective-permute-start.1 = (bf16[2,320,128]{2,1,0:T(8,128)(2,1)S(1)}, bf16[2,320,128]{2,1,0:T(8,128)(2,1)S(1)}, u32[]{:S(2)}, u32[]{:S(2)}) collective-permute-start(bf16[2,320,128]{2,1,0:T(8,128)(2,1)S(1)} %get-tuple-element.126.refs_3_.refs_4_), channel_id=1, source_target_pairs={{0,16},{8,24},{16,0},{24,8},{1,17},{9,25},{17,1},{25,9},{2,18},{10... | collective-permute-start | bytes 491528 | tf_op jit(solution)/shard_map/ppermute | solution.py:395
  4.8 1.5 %collective-permute-start = (bf16[2,320,128]{2,1,0:T(8,128)(2,1)S(1)}, bf16[2,320,128]{2,1,0:T(8,128)(2,1)S(1)}, u32[]{:S(2)}, u32[]{:S(2)}) collective-permute-start(bf16[2,320,128]{2,1,0:T(8,128)(2,1)S(1)} %get-tuple-element.124.refs_1_), channel_id=1, source_target_pairs={{0,8},{8,0},{16,24},{24,16},{1,9},{9,1},{17,25},{25,17},{2,10},{10... | collective-permute-start | bytes 491528 | tf_op jit(solution)/shard_map/ppermute | solution.py:395
  7.1 3.0 %collective-permute-start.4 = (bf16[4,320,128]{2,1,0:T(8,128)(2,1)S(1)}, bf16[4,320,128]{2,1,0:T(8,128)(2,1)S(1)}, u32[]{:S(2)}, u32[]{:S(2)}) collective-permute-start(bf16[4,320,128]{2,1,0:T(8,128)(2,1)S(1)} %get-tuple-element.130), channel_id=1, source_target_pairs={{0,1},{1,0},{2,3},{3,2},{4,5},{5,4},{6,7},{7,6},{8,9},{9,8},{10,11... | collective-permute-start | bytes 983048 | tf_op jit(solution)/shard_map/ppermute | solution.py:400
  11.5 1.6 %collective-permute-start.3 = (bf16[2,320,128]{2,1,0:T(8,128)(2,1)S(1)}, bf16[2,320,128]{2,1,0:T(8,128)(2,1)S(1)}, u32[]{:S(2)}, u32[]{:S(2)}) collective-permute-start(bf16[2,320,128]{2,1,0:T(8,128)(2,1)S(1)} %get-tuple-element.129), channel_id=1, source_target_pairs={{0,8},{8,0},{16,24},{24,16},{1,9},{9,1},{17,25},{25,17},{2,10},{10... | collective-permute-start | bytes 491528 | tf_op jit(solution)/shard_map/ppermute | solution.py:395
  13.2 1.6 %collective-permute-start.9 = (bf16[2,320,128]{2,1,0:T(8,128)(2,1)S(1)}, bf16[2,320,128]{2,1,0:T(8,128)(2,1)S(1)}, u32[]{:S(2)}, u32[]{:S(2)}) collective-permute-start(bf16[2,320,128]{2,1,0:T(8,128)(2,1)S(1)} %get-tuple-element.242.refs_3_.refs_4_), channel_id=1, source_target_pairs={{0,16},{8,24},{16,0},{24,8},{1,17},{9,25},{17,1},{25,9},{2,18},{10... | collective-permute-start | bytes 491528 | tf_op jit(solution)/shard_map/ppermute | solution.py:395
  14.8 3.8 %shard_map.115.refs_2_.refs_1_ = s32[1033]{0:T(1024)S(1)} custom-call(s32[1,512]{1,0:T(1,128)S(1)} %copy-done.7), custom_call_target="tpu_custom_call" | custom-call | bytes 6180 | tf_op jit(solution)/shard_map/pallas_call | solution.py:28
  19.9 1.5 %collective-permute-start.7 = (bf16[4,320,128]{2,1,0:T(8,128)(2,1)S(1)}, bf16[4,320,128]{2,1,0:T(8,128)(2,1)S(1)}, u32[]{:S(2)}, u32[]{:S(2)}) collective-permute-start(bf16[4,320,128]{2,1,0:T(8,128)(2,1)S(1)} %shard_map.116.den_ref.refs_6_), channel_id=1, source_target_pairs={{1,2},{2,1},{3,4},{4,3},{5,6},{6,5},{0,8},{7,15},{9,10},{10,9},{11... | collective-permute-start | bytes 983048 | tf_op jit(solution)/shard_map/ppermute | solution.py:412
  21.8 2.2 %collective-permute-done.8.refs_2_ = bf16[2,320,128]{2,1,0:T(8,128)(2,1)S(1)} collective-permute-done((bf16[2,320,128]{2,1,0:T(8,128)(2,1)S(1)}, bf16[2,320,128]{2,1,0:T(8,128)(2,1)S(1)}, u32[]{:S(2)}, u32[]{:S(2)}) %collective-permute-start.8) | collective-permute-done | bytes 163872 | tf_op jit(solution)/shard_map/ppermute | solution.py:395
  25.9 1.3 %shard_map.117 = (f32[4,336,128]{2,1,0:T(8,128)S(1)}, f32[4,320,128]{2,1,0:T(8,128)S(1)}, f32[4,320,128]{2,1,0:T(8,128)S(1)}) custom-call(bf16[4,320,128]{2,1,0:T(8,128)(2,1)S(1)} %shard_map.116.den_ref.refs_6_, bf16[384,256]{1,0:T(8,128)(2,1)S(1)} %copy-done), custom_call_target="tpu_custom_call" | custom-call | bytes 2523136 | tf_op jit(solution)/shard_map/pallas_call | solution.py:28
  27.2 1.4 %shard_map.118 = (f32[4,320,128]{2,1,0:T(8,128)S(1)}, f32[4,320,128]{2,1,0:T(8,128)S(1)}, f32[4,320,128]{2,1,0:T(8,128)S(1)}) custom-call(f32[4,336,128]{2,1,0:T(8,128)S(1)} %get-tuple-element.123.f_ref.refs_0_.refs_6_, f32[4,320,128]{2,1,0:T(8,128)S(1)} %get-tuple-element.135.s2_ref.refs_1_, f32[4,320,128]{2,1,0:T(8,128)S(1)} %get-tuple-element.136.s3_ref.refs_2_, ...), custom_call_target="tpu_custom_call" | custom-call | bytes 4161536 | tf_op jit(solution)/shard_map/pallas_call | solution.py:28
  28.6 1.3 %collective-permute-done.10.refs_3_ = bf16[2,320,128]{2,1,0:T(8,128)(2,1)S(1)} collective-permute-done((bf16[2,320,128]{2,1,0:T(8,128)(2,1)S(1)}, bf16[2,320,128]{2,1,0:T(8,128)(2,1)S(1)}, u32[]{:S(2)}, u32[]{:S(2)}) %collective-permute-start.10) | collective-permute-done | bytes 163872 | tf_op jit(solution)/shard_map/ppermute | solution.py:395
  33.8 1.1 collective-permute-start.14
  34.9 1.0 collective-permute-start.13
  35.9 1.4 %shard_map.124 = (f32[4,320,128]{2,1,0:T(8,128)S(1)}, f32[4,320,128]{2,1,0:T(8,128)S(1)}, f32[4,320,128]{2,1,0:T(8,128)S(1)}) custom-call(f32[4,336,128]{2,1,0:T(8,128)S(1)} %get-tuple-element.147.f_ref.refs_0_.refs_6_, f32[4,320,128]{2,1,0:T(8,128)S(1)} %get-tuple-element.135.s2_ref.refs_1_, f32[4,320,128]{2,1,0:T(8,128)S(1)} %get-tuple-element.136.s3_ref.refs_2_, ...), custom_call_target="tpu_custom_call" | custom-call | bytes 4161536 | tf_op jit(solution)/shard_map/pallas_call | solution.py:28
  37.3 1.9 %collective-permute-done.14.refs_2_ = bf16[4,160,128]{2,1,0:T(8,128)(2,1)S(1)} collective-permute-done((bf16[4,160,128]{2,1,0:T(8,128)(2,1)S(1)}, bf16[4,160,128]{2,1,0:T(8,128)(2,1)S(1)}, u32[]{:S(2)}, u32[]{:S(2)}) %collective-permute-start.14) | collective-permute-done | bytes 163872 | tf_op jit(solution)/shard_map/ppermute | solution.py:412
  39.7 1.3 %collective-permute-done.13.refs_2_ = bf16[4,160,128]{2,1,0:T(8,128)(2,1)S(1)} collective-permute-done((bf16[4,160,128]{2,1,0:T(8,128)(2,1)S(1)}, bf16[4,160,128]{2,1,0:T(8,128)(2,1)S(1)}, u32[]{:S(2)}, u32[]{:S(2)}) %collective-permute-start.13) | collective-permute-done | bytes 163872 | tf_op jit(solution)/shard_map/ppermute | solution.py:412
  43.6 1.4 %shard_map.127 = (f32[4,320,128]{2,1,0:T(8,128)S(1)}, f32[4,320,128]{2,1,0:T(8,128)S(1)}, f32[4,320,128]{2,1,0:T(8,128)S(1)}) custom-call(f32[4,336,128]{2,1,0:T(8,128)S(1)} %get-tuple-element.156.f_ref.refs_0_.refs_6_, f32[4,320,128]{2,1,0:T(8,128)S(1)} %get-tuple-element.135.s2_ref.refs_1_, f32[4,320,128]{2,1,0:T(8,128)S(1)} %get-tuple-element.136.s3_ref.refs_2_, ...), custom_call_target="tpu_custom_call" | custom-call | bytes 4161536 | tf_op jit(solution)/shard_map/pallas_call | solution.py:28
  45.1 1.9 %collective-permute-done.17.refs_2_ = bf16[4,160,128]{2,1,0:T(8,128)(2,1)S(1)} collective-permute-done((bf16[4,160,128]{2,1,0:T(8,128)(2,1)S(1)}, bf16[4,160,128]{2,1,0:T(8,128)(2,1)S(1)}, u32[]{:S(2)}, u32[]{:S(2)}) %collective-permute-start.17) | collective-permute-done | bytes 163872 | tf_op jit(solution)/shard_map/ppermute | solution.py:412
  47.4 1.3 %collective-permute-done.16.refs_2_ = bf16[4,160,128]{2,1,0:T(8,128)(2,1)S(1)} collective-permute-done((bf16[4,160,128]{2,1,0:T(8,128)(2,1)S(1)}, bf16[4,160,128]{2,1,0:T(8,128)(2,1)S(1)}, u32[]{:S(2)}, u32[]{:S(2)}) %collective-permute-start.16) | collective-permute-done | bytes 163872 | tf_op jit(solution)/shard_map/ppermute | solution.py:412
  50.4 1.0 collective-permute-start.19
  51.5 1.4 %shard_map.130 = (f32[4,320,128]{2,1,0:T(8,128)S(1)}, f32[4,320,128]{2,1,0:T(8,128)S(1)}, f32[4,320,128]{2,1,0:T(8,128)S(1)}) custom-call(f32[4,336,128]{2,1,0:T(8,128)S(1)} %get-tuple-element.165.f_ref.refs_0_, f32[4,320,128]{2,1,0:T(8,128)S(1)} %get-tuple-element.135.s2_ref.refs_1_, f32[4,320,128]{2,1,0:T(8,128)S(1)} %get-tuple-element.136.s3_ref.refs_2_, ...), custom_call_target="tpu_custom_call" | custom-call | bytes 4161536 | tf_op jit(solution)/shard_map/pallas_call | solution.py:28
  52.9 1.7 %collective-permute-done.20.refs_2_ = bf16[4,160,128]{2,1,0:T(8,128)(2,1)S(1)} collective-permute-done((bf16[4,160,128]{2,1,0:T(8,128)(2,1)S(1)}, bf16[4,160,128]{2,1,0:T(8,128)(2,1)S(1)}, u32[]{:S(2)}, u32[]{:S(2)}) %collective-permute-start.20) | collective-permute-done | bytes 163872 | tf_op jit(solution)/shard_map/ppermute | solution.py:412
  54.7 1.1 %shard_map.131 = (f32[4,320,128]{2,1,0:T(8,128)S(1)}, f32[4,320,128]{2,1,0:T(8,128)S(1)}, f32[4,336,128]{2,1,0:T(8,128)S(1)}, bf16[4,320,128]{2,1,0:T(8,128)(2,1)S(1)}, bf16[4,160,128]{2,1,0:T(8,128)(2,1)}) custom-call(f32[4,336,128]{2,1,0:T(8,128)S(1)} %get-tuple-element.165.f_ref.refs_0_, bf16[4,320,128]{2,1,0:T(8,128)(2,1)S(1)} %collective-permute-done.18.refs_1_, ...), custom_call_target="tpu_custom_call" | custom-call | bytes 6324224 | tf_op jit(solution)/shard_map/pallas_call | solution.py:28
  56.4 1.1 %shard_map.132 = (f32[4,320,128]{2,1,0:T(8,128)S(1)}, f32[4,320,128]{2,1,0:T(8,128)S(1)}, f32[4,336,128]{2,1,0:T(8,128)S(1)}, bf16[4,320,128]{2,1,0:T(8,128)(2,1)S(1)}, bf16[4,160,128]{2,1,0:T(8,128)(2,1)}) custom-call(f32[4,336,128]{2,1,0:T(8,128)S(1)} %get-tuple-element.165.f_ref.refs_0_, ...), custom_call_target="tpu_custom_call", output_to_operand_aliasing={{0}: (7, {}), {1}: (8, {}), {2}: (9, {}), {3}: (10, {})} | custom-call | bytes 8650752 | tf_op jit(solution)/shard_map/pallas_call | solution.py:28
  57.6 1.4 %shard_map.134 = (f32[1344,128]{1,0:T(8,128)S(1)}, bf16[4,320,128]{2,1,0:T(8,128)(2,1)S(1)}, bf16[4,160,128]{2,1,0:T(8,128)(2,1)S(1)}, bf16[4,160,128]{2,1,0:T(8,128)(2,1)S(1)}) custom-call(f32[1344,128]{1,0:T(8,128)S(1)} %bitcast.39, f32[1344,128]{1,0:T(8,128)S(1)} %bitcast.29, s32[1033]{0:T(1024)S(1)} %shard_map.115.refs_2_.refs_1_, f32[4,512]{1,0:T(4,128)S(1)} %bitcast.46), custom_call_target="tpu_custom_call" | custom-call | bytes 2732068 | tf_op jit(solution)/shard_map/pallas_call | solution.py:28
  60.2 1.1 collective-permute-start.22
  61.3 1.3 %shard_map.136 = f32[1344,128]{1,0:T(8,128)S(1)} custom-call(f32[1344,128]{1,0:T(8,128)S(1)} %bitcast.28, s32[1033]{0:T(1024)S(1)} %shard_map.115.refs_2_.refs_1_, f32[4,512]{1,0:T(4,128)S(1)} %bitcast.47), custom_call_target="tpu_custom_call" | custom-call | bytes 1388580 | tf_op jit(solution)/shard_map/pallas_call | solution.py:28
  62.6 1.5 %shard_map.135 = (f32[4,320,128]{2,1,0:T(8,128)S(1)}, f32[4,320,128]{2,1,0:T(8,128)S(1)}, f32[4,320,128]{2,1,0:T(8,128)S(1)}) custom-call(f32[4,336,128]{2,1,0:T(8,128)S(1)} %bitcast.36, f32[4,320,128]{2,1,0:T(8,128)S(1)} %get-tuple-element.135.s2_ref.refs_1_, f32[4,320,128]{2,1,0:T(8,128)S(1)} %get-tuple-element.136.s3_ref.refs_2_, ...), custom_call_target="tpu_custom_call" | custom-call | bytes 6127616 | tf_op jit(solution)/shard_map/pallas_call | solution.py:28
  65.1 1.2 %collective-permute-done.22.refs_2_ = bf16[4,160,128]{2,1,0:T(8,128)(2,1)S(1)} collective-permute-done((bf16[4,160,128]{2,1,0:T(8,128)(2,1)S(1)}, bf16[4,160,128]{2,1,0:T(8,128)(2,1)S(1)}, u32[]{:S(2)}, u32[]{:S(2)}) %collective-permute-start.22) | collective-permute-done | bytes 163872 | tf_op jit(solution)/shard_map/ppermute | solution.py:412
  68.0 1.1 collective-permute-start.25
  69.0 1.3 %shard_map.140 = f32[1344,128]{1,0:T(8,128)S(1)} custom-call(f32[1344,128]{1,0:T(8,128)S(1)} %bitcast.26, s32[1033]{0:T(1024)S(1)} %shard_map.115.refs_2_.refs_1_, f32[4,512]{1,0:T(4,128)S(1)} %bitcast.48), custom_call_target="tpu_custom_call" | custom-call | bytes 1388580 | tf_op jit(solution)/shard_map/pallas_call | solution.py:28
  70.3 1.6 %shard_map.139 = (f32[4,320,128]{2,1,0:T(8,128)S(1)}, f32[4,320,128]{2,1,0:T(8,128)S(1)}, f32[4,320,128]{2,1,0:T(8,128)S(1)}) custom-call(f32[4,336,128]{2,1,0:T(8,128)S(1)} %get-tuple-element.190.refs_0_, f32[4,320,128]{2,1,0:T(8,128)S(1)} %get-tuple-element.135.s2_ref.refs_1_, f32[4,320,128]{2,1,0:T(8,128)S(1)} %get-tuple-element.136.s3_ref.refs_2_, ...), custom_call_target="tpu_custom_call" | custom-call | bytes 7438336 | tf_op jit(solution)/shard_map/pallas_call | solution.py:28
  72.9 1.2 %collective-permute-done.25.refs_2_ = bf16[4,160,128]{2,1,0:T(8,128)(2,1)S(1)} collective-permute-done((bf16[4,160,128]{2,1,0:T(8,128)(2,1)S(1)}, bf16[4,160,128]{2,1,0:T(8,128)(2,1)S(1)}, u32[]{:S(2)}, u32[]{:S(2)}) %collective-permute-start.25) | collective-permute-done | bytes 163872 | tf_op jit(solution)/shard_map/ppermute | solution.py:412
  75.8 1.1 collective-permute-start.31
  76.8 1.3 %shard_map.144 = f32[1344,128]{1,0:T(8,128)S(1)} custom-call(f32[1344,128]{1,0:T(8,128)S(1)} %bitcast.27, s32[1033]{0:T(1024)S(1)} %shard_map.115.refs_2_.refs_1_, f32[4,512]{1,0:T(4,128)S(1)} %bitcast.49), custom_call_target="tpu_custom_call" | custom-call | bytes 1388580 | tf_op jit(solution)/shard_map/pallas_call | solution.py:28
  78.1 1.6 %shard_map.143 = (f32[4,320,128]{2,1,0:T(8,128)S(1)}, f32[4,320,128]{2,1,0:T(8,128)S(1)}, f32[4,320,128]{2,1,0:T(8,128)S(1)}) custom-call(f32[4,336,128]{2,1,0:T(8,128)S(1)} %get-tuple-element.206.refs_0_, f32[4,320,128]{2,1,0:T(8,128)S(1)} %get-tuple-element.135.s2_ref.refs_1_, f32[4,320,128]{2,1,0:T(8,128)S(1)} %get-tuple-element.136.s3_ref.refs_2_, ...), custom_call_target="tpu_custom_call" | custom-call | bytes 7438336 | tf_op jit(solution)/shard_map/pallas_call | solution.py:28
  80.7 1.1 %collective-permute-done.31.refs_2_ = bf16[4,160,128]{2,1,0:T(8,128)(2,1)S(1)} collective-permute-done((bf16[4,160,128]{2,1,0:T(8,128)(2,1)S(1)}, bf16[4,160,128]{2,1,0:T(8,128)(2,1)S(1)}, u32[]{:S(2)}, u32[]{:S(2)}) %collective-permute-start.31) | collective-permute-done | bytes 163872 | tf_op jit(solution)/shard_map/ppermute | solution.py:412
  84.3 1.4 %collective-permute-start.35 = (bf16[4,160,128]{2,1,0:T(8,128)(2,1)S(1)}, bf16[4,160,128]{2,1,0:T(8,128)(2,1)S(1)}, u32[]{:S(2)}, u32[]{:S(2)}) collective-permute-start(bf16[4,160,128]{2,1,0:T(8,128)(2,1)S(1)} %get-tuple-element.232), channel_id=1, source_target_pairs={{1,2},{2,1},{3,4},{4,3},{5,6},{6,5},{0,8},{7,15},{9,10},{10,9},{11... | collective-permute-start | bytes 491528 | tf_op jit(solution)/shard_map/ppermute | solution.py:412
  86.3 2.8 %collective-permute-done.32.refs_2_ = bf16[4,160,128]{2,1,0:T(8,128)(2,1)S(1)} collective-permute-done((bf16[4,160,128]{2,1,0:T(8,128)(2,1)S(1)}, bf16[4,160,128]{2,1,0:T(8,128)(2,1)S(1)}, u32[]{:S(2)}, u32[]{:S(2)}) %collective-permute-start.32) | collective-permute-done | bytes 163872 | tf_op jit(solution)/shard_map/ppermute | solution.py:395
  90.9 1.2 %shard_map.149.refs_4_ = f32[4,320,128]{2,1,0:T(8,128)S(1)} custom-call(f32[4,336,128]{2,1,0:T(8,128)S(1)} %get-tuple-element.230.f_ref.refs_0_, bf16[384,256]{1,0:T(8,128)(2,1)S(1)} %copy-done, f32[4,320,128]{2,1,0:T(8,128)S(1)} %get-tuple-element.234.fdy_ref, f32[4,320,128]{2,1,0:T(8,128)S(1)} %get-tuple-element.235.fdz_ref, ...), custom_call_target="tpu_custom_call" | custom-call | bytes 3506176 | tf_op jit(solution)/shard_map/pallas_call | solution.py:28
  93.9 1.4 %collective-permute-start.36 = (bf16[4,160,128]{2,1,0:T(8,128)(2,1)S(1)}, bf16[4,160,128]{2,1,0:T(8,128)(2,1)S(1)}, u32[]{:S(2)}, u32[]{:S(2)}) collective-permute-start(bf16[4,160,128]{2,1,0:T(8,128)(2,1)S(1)} %shard_map.150.refs_1_), channel_id=1, source_target_pairs={{0,8},{8,0},{16,24},{24,16},{1,9},{9,1},{17,25},{25,17},{2,10},{10... | collective-permute-start | bytes 491528 | tf_op jit(solution)/shard_map/ppermute | solution.py:395
  95.7 1.1 %collective-permute-start.39 = (bf16[4,160,128]{2,1,0:T(8,128)(2,1)S(1)}, bf16[4,160,128]{2,1,0:T(8,128)(2,1)S(1)}, u32[]{:S(2)}, u32[]{:S(2)}) collective-permute-start(bf16[4,160,128]{2,1,0:T(8,128)(2,1)S(1)} %shard_map.152.refs_1_), channel_id=1, source_target_pairs={{0,16},{8,24},{16,0},{24,8},{1,17},{9,25},{17,1},{25,9},{2,18},{10... | collective-permute-start | bytes 491528 | tf_op jit(solution)/shard_map/ppermute | solution.py:395
  96.9 1.3 %collective-permute-done.33 = bf16[4,160,128]{2,1,0:T(8,128)(2,1)S(1)} collective-permute-done((bf16[4,160,128]{2,1,0:T(8,128)(2,1)S(1)}, bf16[4,160,128]{2,1,0:T(8,128)(2,1)S(1)}, u32[]{:S(2)}, u32[]{:S(2)}) %collective-permute-start.33) | collective-permute-done | bytes 163872 | tf_op jit(solution)/shard_map/ppermute | solution.py:395
  98.2 2.2 %collective-permute-done.36.refs_2_ = bf16[4,160,128]{2,1,0:T(8,128)(2,1)S(1)} collective-permute-done((bf16[4,160,128]{2,1,0:T(8,128)(2,1)S(1)}, bf16[4,160,128]{2,1,0:T(8,128)(2,1)S(1)}, u32[]{:S(2)}, u32[]{:S(2)}) %collective-permute-start.36) | collective-permute-done | bytes 163872 | tf_op jit(solution)/shard_map/ppermute | solution.py:395
  101.1 1.1 %collective-permute-start.37 = (bf16[4,160,128]{2,1,0:T(8,128)(2,1)S(1)}, bf16[4,160,128]{2,1,0:T(8,128)(2,1)S(1)}, u32[]{:S(2)}, u32[]{:S(2)}) collective-permute-start(bf16[4,160,128]{2,1,0:T(8,128)(2,1)S(1)} %get-tuple-element.238), channel_id=1, source_target_pairs={{0,16},{8,24},{16,0},{24,8},{1,17},{9,25},{17,1},{25,9},{2,18},{10... | collective-permute-start | bytes 491528 | tf_op jit(solution)/shard_map/ppermute | solution.py:395
  104.9 1.6 %collective-permute-done.37 = bf16[4,160,128]{2,1,0:T(8,128)(2,1)S(1)} collective-permute-done((bf16[4,160,128]{2,1,0:T(8,128)(2,1)S(1)}, bf16[4,160,128]{2,1,0:T(8,128)(2,1)S(1)}, u32[]{:S(2)}, u32[]{:S(2)}) %collective-permute-start.37) | collective-permute-done | bytes 163872 | tf_op jit(solution)/shard_map/ppermute | solution.py:395
  106.5 2.7 %collective-permute-done.40 = bf16[4,160,128]{2,1,0:T(8,128)(2,1)S(1)} collective-permute-done((bf16[4,160,128]{2,1,0:T(8,128)(2,1)S(1)}, bf16[4,160,128]{2,1,0:T(8,128)(2,1)S(1)}, u32[]{:S(2)}, u32[]{:S(2)}) %collective-permute-start.40) | collective-permute-done | bytes 163872 | tf_op jit(solution)/shard_map/ppermute | solution.py:395
  (101 shorter events, 34.2 us)
Async XLA Ops:
  0.6 5.7 %copy-start.3 = (f32[1,4,320,128]{3,2,1,0:T(8,128)S(1)}, f32[1,4,320,128]{3,2,1,0:T(8,128)}, u32[]{:S(2)}) copy-start(f32[1,4,320,128]{3,2,1,0:T(8,128)} %param.15) | copy-start | bytes 1966084
  1.7 8.4 %collective-permute-start.1 = (bf16[2,320,128]{2,1,0:T(8,128)(2,1)S(1)}, bf16[2,320,128]{2,1,0:T(8,128)(2,1)S(1)}, u32[]{:S(2)}, u32[]{:S(2)}) collective-permute-start(bf16[2,320,128]{2,1,0:T(8,128)(2,1)S(1)} %get-tuple-element.126.refs_3_.refs_4_), channel_id=1, source_target_pairs={{0,16},{8,24},{16,0},{24,8},{1,17},{9,25},{17,1},{25,9},{2,18},{10... | collective-permute-start | bytes 491528 | tf_op jit(solution)/shard_map/ppermute | solution.py:395
  4.8 5.7 %collective-permute-start = (bf16[2,320,128]{2,1,0:T(8,128)(2,1)S(1)}, bf16[2,320,128]{2,1,0:T(8,128)(2,1)S(1)}, u32[]{:S(2)}, u32[]{:S(2)}) collective-permute-start(bf16[2,320,128]{2,1,0:T(8,128)(2,1)S(1)} %get-tuple-element.124.refs_1_), channel_id=1, source_target_pairs={{0,8},{8,0},{16,24},{24,16},{1,9},{9,1},{17,25},{25,17},{2,10},{10... | collective-permute-start | bytes 491528 | tf_op jit(solution)/shard_map/ppermute | solution.py:395
  6.4 4.0 %copy-start.6 = (s32[4,8]{1,0:T(4,128)S(1)}, s32[4,8]{1,0:T(4,128)}, u32[]{:S(2)}) copy-start(s32[4,8]{1,0:T(4,128)} %refs_0_.15) | copy-start | bytes 388
  6.4 12.8 %collective-permute-start.5 = (bf16[4,320,128]{2,1,0:T(8,128)(2,1)S(1)}, bf16[4,320,128]{2,1,0:T(8,128)(2,1)S(1)}, u32[]{:S(2)}, u32[]{:S(2)}) collective-permute-start(bf16[4,320,128]{2,1,0:T(8,128)(2,1)S(1)} %get-tuple-element.130), channel_id=1, source_target_pairs={{1,2},{2,1},{3,4},{4,3},{5,6},{6,5},{9,10},{10,9},{11,12},{12,11},... | collective-permute-start | bytes 983048 | tf_op jit(solution)/shard_map/ppermute | solution.py:412
  7.1 12.1 %collective-permute-start.4 = (bf16[4,320,128]{2,1,0:T(8,128)(2,1)S(1)}, bf16[4,320,128]{2,1,0:T(8,128)(2,1)S(1)}, u32[]{:S(2)}, u32[]{:S(2)}) collective-permute-start(bf16[4,320,128]{2,1,0:T(8,128)(2,1)S(1)} %get-tuple-element.130), channel_id=1, source_target_pairs={{0,1},{1,0},{2,3},{3,2},{4,5},{5,4},{6,7},{7,6},{8,9},{9,8},{10,11... | collective-permute-start | bytes 983048 | tf_op jit(solution)/shard_map/ppermute | solution.py:400
  10.4 2.7 %copy-start.8 = (bf16[1,4,320,128]{3,2,1,0:T(8,128)(2,1)S(1)}, bf16[1,4,320,128]{3,2,1,0:T(8,128)(2,1)}, u32[]{:S(2)}) copy-start(bf16[1,4,320,128]{3,2,1,0:T(8,128)(2,1)} %param.10) | copy-start | bytes 983044
  11.1 7.5 %collective-permute-start.2 = (bf16[2,320,128]{2,1,0:T(8,128)(2,1)S(1)}, bf16[2,320,128]{2,1,0:T(8,128)(2,1)S(1)}, u32[]{:S(2)}, u32[]{:S(2)}) collective-permute-start(bf16[2,320,128]{2,1,0:T(8,128)(2,1)S(1)} %get-tuple-element.128), channel_id=1, source_target_pairs={{0,16},{8,24},{16,0},{24,8},{1,17},{9,25},{17,1},{25,9},{2,18},{10... | collective-permute-start | bytes 491528 | tf_op jit(solution)/shard_map/ppermute | solution.py:395
  11.5 7.7 %collective-permute-start.3 = (bf16[2,320,128]{2,1,0:T(8,128)(2,1)S(1)}, bf16[2,320,128]{2,1,0:T(8,128)(2,1)S(1)}, u32[]{:S(2)}, u32[]{:S(2)}) collective-permute-start(bf16[2,320,128]{2,1,0:T(8,128)(2,1)S(1)} %get-tuple-element.129), channel_id=1, source_target_pairs={{0,8},{8,0},{16,24},{24,16},{1,9},{9,1},{17,25},{25,17},{2,10},{10... | collective-permute-start | bytes 491528 | tf_op jit(solution)/shard_map/ppermute | solution.py:395
  13.1 1.6 %copy-start.7 = (s32[1,512]{1,0:T(1,128)S(1)}, s32[1,512]{1,0:T(1,128)}, u32[]{:S(2)}) copy-start(s32[1,512]{1,0:T(1,128)} %rec.1) | copy-start | bytes 6148
  13.2 8.6 %collective-permute-start.9 = (bf16[2,320,128]{2,1,0:T(8,128)(2,1)S(1)}, bf16[2,320,128]{2,1,0:T(8,128)(2,1)S(1)}, u32[]{:S(2)}, u32[]{:S(2)}) collective-permute-start(bf16[2,320,128]{2,1,0:T(8,128)(2,1)S(1)} %get-tuple-element.242.refs_3_.refs_4_), channel_id=1, source_target_pairs={{0,16},{8,24},{16,0},{24,8},{1,17},{9,25},{17,1},{25,9},{2,18},{10... | collective-permute-start | bytes 491528 | tf_op jit(solution)/shard_map/ppermute | solution.py:395
  18.6 5.4 %collective-permute-start.8 = (bf16[2,320,128]{2,1,0:T(8,128)(2,1)S(1)}, bf16[2,320,128]{2,1,0:T(8,128)(2,1)S(1)}, u32[]{:S(2)}, u32[]{:S(2)}) collective-permute-start(bf16[2,320,128]{2,1,0:T(8,128)(2,1)S(1)} %get-tuple-element.243.refs_1_), channel_id=1, source_target_pairs={{0,8},{8,0},{16,24},{24,16},{1,9},{9,1},{17,25},{25,17},{2,10},{10... | collective-permute-start | bytes 491528 | tf_op jit(solution)/shard_map/ppermute | solution.py:395
  19.9 6.0 %copy-start = (bf16[384,256]{1,0:T(8,128)(2,1)S(1)}, bf16[384,256]{1,0:T(8,128)(2,1)}, u32[]{:S(2)}) copy-start(bf16[384,256]{1,0:T(8,128)(2,1)} %constant.2.clone.matrix_ref.refs_3_) | copy-start | bytes 589828
  19.9 11.7 %collective-permute-start.7 = (bf16[4,320,128]{2,1,0:T(8,128)(2,1)S(1)}, bf16[4,320,128]{2,1,0:T(8,128)(2,1)S(1)}, u32[]{:S(2)}, u32[]{:S(2)}) collective-permute-start(bf16[4,320,128]{2,1,0:T(8,128)(2,1)S(1)} %shard_map.116.den_ref.refs_6_), channel_id=1, source_target_pairs={{1,2},{2,1},{3,4},{4,3},{5,6},{6,5},{0,8},{7,15},{9,10},{10,9},{11... | collective-permute-start | bytes 983048 | tf_op jit(solution)/shard_map/ppermute | solution.py:412
  21.4 10.2 %collective-permute-start.6 = (bf16[4,320,128]{2,1,0:T(8,128)(2,1)S(1)}, bf16[4,320,128]{2,1,0:T(8,128)(2,1)S(1)}, u32[]{:S(2)}, u32[]{:S(2)}) collective-permute-start(bf16[4,320,128]{2,1,0:T(8,128)(2,1)S(1)} %shard_map.116.den_ref.refs_6_), channel_id=1, source_target_pairs={{0,1},{1,0},{2,3},{3,2},{4,5},{5,4},{6,7},{7,6},{8,9},{9,8},{10,11... | collective-permute-start | bytes 983048 | tf_op jit(solution)/shard_map/ppermute | solution.py:400
  24.6 5.4 %collective-permute-start.10 = (bf16[2,320,128]{2,1,0:T(8,128)(2,1)S(1)}, bf16[2,320,128]{2,1,0:T(8,128)(2,1)S(1)}, u32[]{:S(2)}, u32[]{:S(2)}) collective-permute-start(bf16[2,320,128]{2,1,0:T(8,128)(2,1)S(1)} %get-tuple-element.139), channel_id=1, source_target_pairs={{0,16},{8,24},{16,0},{24,8},{1,17},{9,25},{17,1},{25,9},{2,18},{10... | collective-permute-start | bytes 491528 | tf_op jit(solution)/shard_map/ppermute | solution.py:395
  25.3 5.7 %collective-permute-start.11 = (bf16[2,320,128]{2,1,0:T(8,128)(2,1)S(1)}, bf16[2,320,128]{2,1,0:T(8,128)(2,1)S(1)}, u32[]{:S(2)}, u32[]{:S(2)}) collective-permute-start(bf16[2,320,128]{2,1,0:T(8,128)(2,1)S(1)} %get-tuple-element.140), channel_id=1, source_target_pairs={{0,8},{8,0},{16,24},{24,16},{1,9},{9,1},{17,25},{25,17},{2,10},{10... | collective-permute-start | bytes 491528 | tf_op jit(solution)/shard_map/ppermute | solution.py:395
  33.7 5.5 %collective-permute-start.12 = (bf16[4,320,128]{2,1,0:T(8,128)(2,1)S(1)}, bf16[4,320,128]{2,1,0:T(8,128)(2,1)S(1)}, u32[]{:S(2)}, u32[]{:S(2)}) collective-permute-start(bf16[4,320,128]{2,1,0:T(8,128)(2,1)S(1)} %get-tuple-element.148), channel_id=1, source_target_pairs={{0,1},{1,0},{2,3},{3,2},{4,5},{5,4},{6,7},{7,6},{8,9},{9,8},{10,11... | collective-permute-start | bytes 983048 | tf_op jit(solution)/shard_map/ppermute | solution.py:400
  33.8 5.4 %collective-permute-start.14 = (bf16[4,160,128]{2,1,0:T(8,128)(2,1)S(1)}, bf16[4,160,128]{2,1,0:T(8,128)(2,1)S(1)}, u32[]{:S(2)}, u32[]{:S(2)}) collective-permute-start(bf16[4,160,128]{2,1,0:T(8,128)(2,1)S(1)} %get-tuple-element.151), channel_id=1, source_target_pairs={{1,2},{2,1},{3,4},{4,3},{5,6},{6,5},{0,8},{7,15},{9,10},{10,9},{11... | collective-permute-start | bytes 491528 | tf_op jit(solution)/shard_map/ppermute | solution.py:412
  34.9 6.1 %collective-permute-start.13 = (bf16[4,160,128]{2,1,0:T(8,128)(2,1)S(1)}, bf16[4,160,128]{2,1,0:T(8,128)(2,1)S(1)}, u32[]{:S(2)}, u32[]{:S(2)}) collective-permute-start(bf16[4,160,128]{2,1,0:T(8,128)(2,1)S(1)} %get-tuple-element.149), channel_id=1, source_target_pairs={{1,2},{2,1},{3,4},{4,3},{5,6},{6,5},{0,8},{7,15},{9,10},{10,9},{11... | collective-permute-start | bytes 491528 | tf_op jit(solution)/shard_map/ppermute | solution.py:412
  41.4 5.5 %collective-permute-start.15 = (bf16[4,320,128]{2,1,0:T(8,128)(2,1)S(1)}, bf16[4,320,128]{2,1,0:T(8,128)(2,1)S(1)}, u32[]{:S(2)}, u32[]{:S(2)}) collective-permute-start(bf16[4,320,128]{2,1,0:T(8,128)(2,1)S(1)} %get-tuple-element.157), channel_id=1, source_target_pairs={{0,1},{1,0},{2,3},{3,2},{4,5},{5,4},{6,7},{7,6},{8,9},{9,8},{10,11... | collective-permute-start | bytes 983048 | tf_op jit(solution)/shard_map/ppermute | solution.py:400
  41.6 5.3 %collective-permute-start.17 = (bf16[4,160,128]{2,1,0:T(8,128)(2,1)S(1)}, bf16[4,160,128]{2,1,0:T(8,128)(2,1)S(1)}, u32[]{:S(2)}, u32[]{:S(2)}) collective-permute-start(bf16[4,160,128]{2,1,0:T(8,128)(2,1)S(1)} %get-tuple-element.160), channel_id=1, source_target_pairs={{1,2},{2,1},{3,4},{4,3},{5,6},{6,5},{0,8},{7,15},{9,10},{10,9},{11... | collective-permute-start | bytes 491528 | tf_op jit(solution)/shard_map/ppermute | solution.py:412
  42.6 6.1 %collective-permute-start.16 = (bf16[4,160,128]{2,1,0:T(8,128)(2,1)S(1)}, bf16[4,160,128]{2,1,0:T(8,128)(2,1)S(1)}, u32[]{:S(2)}, u32[]{:S(2)}) collective-permute-start(bf16[4,160,128]{2,1,0:T(8,128)(2,1)S(1)} %get-tuple-element.158), channel_id=1, source_target_pairs={{1,2},{2,1},{3,4},{4,3},{5,6},{6,5},{0,8},{7,15},{9,10},{10,9},{11... | collective-permute-start | bytes 491528 | tf_op jit(solution)/shard_map/ppermute | solution.py:412
  48.7 2.7 %copy-start.4 = (f32[1,4,320,128]{3,2,1,0:T(8,128)S(1)}, f32[1,4,320,128]{3,2,1,0:T(8,128)}, u32[]{:S(2)}) copy-start(f32[1,4,320,128]{3,2,1,0:T(8,128)} %param.17) | copy-start | bytes 1966084
  49.2 5.5 %collective-permute-start.18 = (bf16[4,320,128]{2,1,0:T(8,128)(2,1)S(1)}, bf16[4,320,128]{2,1,0:T(8,128)(2,1)S(1)}, u32[]{:S(2)}, u32[]{:S(2)}) collective-permute-start(bf16[4,320,128]{2,1,0:T(8,128)(2,1)S(1)} %get-tuple-element.166), channel_id=1, source_target_pairs={{0,1},{1,0},{2,3},{3,2},{4,5},{5,4},{6,7},{7,6},{8,9},{9,8},{10,11... | collective-permute-start | bytes 983048 | tf_op jit(solution)/shard_map/ppermute | solution.py:400
  49.4 5.3 %collective-permute-start.20 = (bf16[4,160,128]{2,1,0:T(8,128)(2,1)S(1)}, bf16[4,160,128]{2,1,0:T(8,128)(2,1)S(1)}, u32[]{:S(2)}, u32[]{:S(2)}) collective-permute-start(bf16[4,160,128]{2,1,0:T(8,128)(2,1)S(1)} %get-tuple-element.169), channel_id=1, source_target_pairs={{1,2},{2,1},{3,4},{4,3},{5,6},{6,5},{0,8},{7,15},{9,10},{10,9},{11... | collective-permute-start | bytes 491528 | tf_op jit(solution)/shard_map/ppermute | solution.py:412
  50.4 6.1 %collective-permute-start.19 = (bf16[4,160,128]{2,1,0:T(8,128)(2,1)S(1)}, bf16[4,160,128]{2,1,0:T(8,128)(2,1)S(1)}, u32[]{:S(2)}, u32[]{:S(2)}) collective-permute-start(bf16[4,160,128]{2,1,0:T(8,128)(2,1)S(1)} %get-tuple-element.167), channel_id=1, source_target_pairs={{1,2},{2,1},{3,4},{4,3},{5,6},{6,5},{0,8},{7,15},{9,10},{10,9},{11... | collective-permute-start | bytes 491528 | tf_op jit(solution)/shard_map/ppermute | solution.py:412
  59.0 5.5 %collective-permute-start.21 = (bf16[4,320,128]{2,1,0:T(8,128)(2,1)S(1)}, bf16[4,320,128]{2,1,0:T(8,128)(2,1)S(1)}, u32[]{:S(2)}, u32[]{:S(2)}) collective-permute-start(bf16[4,320,128]{2,1,0:T(8,128)(2,1)S(1)} %get-tuple-element.177), channel_id=1, source_target_pairs={{0,1},{1,0},{2,3},{3,2},{4,5},{5,4},{6,7},{7,6},{8,9},{9,8},{10,11... | collective-permute-start | bytes 983048 | tf_op jit(solution)/shard_map/ppermute | solution.py:400
  59.2 5.3 %collective-permute-start.23 = (bf16[4,160,128]{2,1,0:T(8,128)(2,1)S(1)}, bf16[4,160,128]{2,1,0:T(8,128)(2,1)S(1)}, u32[]{:S(2)}, u32[]{:S(2)}) collective-permute-start(bf16[4,160,128]{2,1,0:T(8,128)(2,1)S(1)} %get-tuple-element.185), channel_id=1, source_target_pairs={{1,2},{2,1},{3,4},{4,3},{5,6},{6,5},{0,8},{7,15},{9,10},{10,9},{11... | collective-permute-start | bytes 491528 | tf_op jit(solution)/shard_map/ppermute | solution.py:412
  60.2 6.1 %collective-permute-start.22 = (bf16[4,160,128]{2,1,0:T(8,128)(2,1)S(1)}, bf16[4,160,128]{2,1,0:T(8,128)(2,1)S(1)}, u32[]{:S(2)}, u32[]{:S(2)}) collective-permute-start(bf16[4,160,128]{2,1,0:T(8,128)(2,1)S(1)} %get-tuple-element.178), channel_id=1, source_target_pairs={{1,2},{2,1},{3,4},{4,3},{5,6},{6,5},{0,8},{7,15},{9,10},{10,9},{11... | collective-permute-start | bytes 491528 | tf_op jit(solution)/shard_map/ppermute | solution.py:412
  62.6 2.0 %copy-start.2 = (f32[1,4,320,128]{3,2,1,0:T(8,128)S(1)}, f32[1,4,320,128]{3,2,1,0:T(8,128)}, u32[]{:S(2)}) copy-start(f32[1,4,320,128]{3,2,1,0:T(8,128)} %param.18) | copy-start | bytes 1966084
  66.9 5.5 %collective-permute-start.24 = (bf16[4,320,128]{2,1,0:T(8,128)(2,1)S(1)}, bf16[4,320,128]{2,1,0:T(8,128)(2,1)S(1)}, u32[]{:S(2)}, u32[]{:S(2)}) collective-permute-start(bf16[4,320,128]{2,1,0:T(8,128)(2,1)S(1)} %get-tuple-element.191), channel_id=1, source_target_pairs={{0,1},{1,0},{2,3},{3,2},{4,5},{5,4},{6,7},{7,6},{8,9},{9,8},{10,11... | collective-permute-start | bytes 983048 | tf_op jit(solution)/shard_map/ppermute | solution.py:400
  67.0 5.3 %collective-permute-start.26 = (bf16[4,160,128]{2,1,0:T(8,128)(2,1)S(1)}, bf16[4,160,128]{2,1,0:T(8,128)(2,1)S(1)}, u32[]{:S(2)}, u32[]{:S(2)}) collective-permute-start(bf16[4,160,128]{2,1,0:T(8,128)(2,1)S(1)} %get-tuple-element.201), channel_id=1, source_target_pairs={{1,2},{2,1},{3,4},{4,3},{5,6},{6,5},{0,8},{7,15},{9,10},{10,9},{11... | collective-permute-start | bytes 491528 | tf_op jit(solution)/shard_map/ppermute | solution.py:412
  68.0 6.1 %collective-permute-start.25 = (bf16[4,160,128]{2,1,0:T(8,128)(2,1)S(1)}, bf16[4,160,128]{2,1,0:T(8,128)(2,1)S(1)}, u32[]{:S(2)}, u32[]{:S(2)}) collective-permute-start(bf16[4,160,128]{2,1,0:T(8,128)(2,1)S(1)} %get-tuple-element.192), channel_id=1, source_target_pairs={{1,2},{2,1},{3,4},{4,3},{5,6},{6,5},{0,8},{7,15},{9,10},{10,9},{11... | collective-permute-start | bytes 491528 | tf_op jit(solution)/shard_map/ppermute | solution.py:412
  74.6 5.5 %collective-permute-start.27 = (bf16[4,320,128]{2,1,0:T(8,128)(2,1)S(1)}, bf16[4,320,128]{2,1,0:T(8,128)(2,1)S(1)}, u32[]{:S(2)}, u32[]{:S(2)}) collective-permute-start(bf16[4,320,128]{2,1,0:T(8,128)(2,1)S(1)} %get-tuple-element.207), channel_id=1, source_target_pairs={{0,1},{1,0},{2,3},{3,2},{4,5},{5,4},{6,7},{7,6},{8,9},{9,8},{10,11... | collective-permute-start | bytes 983048 | tf_op jit(solution)/shard_map/ppermute | solution.py:400
  74.8 5.3 %collective-permute-start.28 = (bf16[4,160,128]{2,1,0:T(8,128)(2,1)S(1)}, bf16[4,160,128]{2,1,0:T(8,128)(2,1)S(1)}, u32[]{:S(2)}, u32[]{:S(2)}) collective-permute-start(bf16[4,160,128]{2,1,0:T(8,128)(2,1)S(1)} %get-tuple-element.208), channel_id=1, source_target_pairs={{1,2},{2,1},{3,4},{4,3},{5,6},{6,5},{0,8},{7,15},{9,10},{10,9},{11... | collective-permute-start | bytes 491528 | tf_op jit(solution)/shard_map/ppermute | solution.py:412
  75.8 6.1 %collective-permute-start.31 = (bf16[4,160,128]{2,1,0:T(8,128)(2,1)S(1)}, bf16[4,160,128]{2,1,0:T(8,128)(2,1)S(1)}, u32[]{:S(2)}, u32[]{:S(2)}) collective-permute-start(bf16[4,160,128]{2,1,0:T(8,128)(2,1)S(1)} %get-tuple-element.223), channel_id=1, source_target_pairs={{1,2},{2,1},{3,4},{4,3},{5,6},{6,5},{0,8},{7,15},{9,10},{10,9},{11... | collective-permute-start | bytes 491528 | tf_op jit(solution)/shard_map/ppermute | solution.py:412
  82.5 11.1 %collective-permute-start.34 = (bf16[4,320,128]{2,1,0:T(8,128)(2,1)S(1)}, bf16[4,320,128]{2,1,0:T(8,128)(2,1)S(1)}, u32[]{:S(2)}, u32[]{:S(2)}) collective-permute-start(bf16[4,320,128]{2,1,0:T(8,128)(2,1)S(1)} %get-tuple-element.231), channel_id=1, source_target_pairs={{0,1},{1,0},{2,3},{3,2},{4,5},{5,4},{6,7},{7,6},{8,9},{9,8},{10,11... | collective-permute-start | bytes 983048 | tf_op jit(solution)/shard_map/ppermute | solution.py:400
  82.7 6.5 %collective-permute-start.32 = (bf16[4,160,128]{2,1,0:T(8,128)(2,1)S(1)}, bf16[4,160,128]{2,1,0:T(8,128)(2,1)S(1)}, u32[]{:S(2)}, u32[]{:S(2)}) collective-permute-start(bf16[4,160,128]{2,1,0:T(8,128)(2,1)S(1)} %get-tuple-element.227.refs_1_), channel_id=1, source_target_pairs={{0,16},{8,24},{16,0},{24,8},{1,17},{9,25},{17,1},{25,9},{2,18},{10... | collective-permute-start | bytes 491528 | tf_op jit(solution)/shard_map/ppermute | solution.py:395
  83.6 8.5 %collective-permute-start.29 = (bf16[4,160,128]{2,1,0:T(8,128)(2,1)S(1)}, bf16[4,160,128]{2,1,0:T(8,128)(2,1)S(1)}, u32[]{:S(2)}, u32[]{:S(2)}) collective-permute-start(bf16[4,160,128]{2,1,0:T(8,128)(2,1)S(1)} %get-tuple-element.220.refs_1_), channel_id=1, source_target_pairs={{0,8},{8,0},{16,24},{24,16},{1,9},{9,1},{17,25},{25,17},{2,10},{10... | collective-permute-start | bytes 491528 | tf_op jit(solution)/shard_map/ppermute | solution.py:395
  84.3 9.3 %collective-permute-start.35 = (bf16[4,160,128]{2,1,0:T(8,128)(2,1)S(1)}, bf16[4,160,128]{2,1,0:T(8,128)(2,1)S(1)}, u32[]{:S(2)}, u32[]{:S(2)}) collective-permute-start(bf16[4,160,128]{2,1,0:T(8,128)(2,1)S(1)} %get-tuple-element.232), channel_id=1, source_target_pairs={{1,2},{2,1},{3,4},{4,3},{5,6},{6,5},{0,8},{7,15},{9,10},{10,9},{11... | collective-permute-start | bytes 491528 | tf_op jit(solution)/shard_map/ppermute | solution.py:412
  85.7 9.7 %collective-permute-start.38 = (bf16[4,160,128]{2,1,0:T(8,128)(2,1)S(1)}, bf16[4,160,128]{2,1,0:T(8,128)(2,1)S(1)}, u32[]{:S(2)}, u32[]{:S(2)}) collective-permute-start(bf16[4,160,128]{2,1,0:T(8,128)(2,1)S(1)} %get-tuple-element.239), channel_id=1, source_target_pairs={{1,2},{2,1},{3,4},{4,3},{5,6},{6,5},{0,8},{7,15},{9,10},{10,9},{11... | collective-permute-start | bytes 491528 | tf_op jit(solution)/shard_map/ppermute | solution.py:412
  89.9 8.3 %collective-permute-start.33 = (bf16[4,160,128]{2,1,0:T(8,128)(2,1)S(1)}, bf16[4,160,128]{2,1,0:T(8,128)(2,1)S(1)}, u32[]{:S(2)}, u32[]{:S(2)}) collective-permute-start(bf16[4,160,128]{2,1,0:T(8,128)(2,1)S(1)} %get-tuple-element.229), channel_id=1, source_target_pairs={{0,8},{8,0},{16,24},{24,16},{1,9},{9,1},{17,25},{25,17},{2,10},{10... | collective-permute-start | bytes 491528 | tf_op jit(solution)/shard_map/ppermute | solution.py:395
  92.8 9.4 %collective-permute-start.30 = (bf16[4,160,128]{2,1,0:T(8,128)(2,1)S(1)}, bf16[4,160,128]{2,1,0:T(8,128)(2,1)S(1)}, u32[]{:S(2)}, u32[]{:S(2)}) collective-permute-start(bf16[4,160,128]{2,1,0:T(8,128)(2,1)S(1)} %get-tuple-element.222), channel_id=1, source_target_pairs={{0,16},{8,24},{16,0},{24,8},{1,17},{9,25},{17,1},{25,9},{2,18},{10... | collective-permute-start | bytes 491528 | tf_op jit(solution)/shard_map/ppermute | solution.py:395
  93.9 6.4 %collective-permute-start.36 = (bf16[4,160,128]{2,1,0:T(8,128)(2,1)S(1)}, bf16[4,160,128]{2,1,0:T(8,128)(2,1)S(1)}, u32[]{:S(2)}, u32[]{:S(2)}) collective-permute-start(bf16[4,160,128]{2,1,0:T(8,128)(2,1)S(1)} %shard_map.150.refs_1_), channel_id=1, source_target_pairs={{0,8},{8,0},{16,24},{24,16},{1,9},{9,1},{17,25},{25,17},{2,10},{10... | collective-permute-start | bytes 491528 | tf_op jit(solution)/shard_map/ppermute | solution.py:395
  95.7 7.4 %collective-permute-start.39 = (bf16[4,160,128]{2,1,0:T(8,128)(2,1)S(1)}, bf16[4,160,128]{2,1,0:T(8,128)(2,1)S(1)}, u32[]{:S(2)}, u32[]{:S(2)}) collective-permute-start(bf16[4,160,128]{2,1,0:T(8,128)(2,1)S(1)} %shard_map.152.refs_1_), channel_id=1, source_target_pairs={{0,16},{8,24},{16,0},{24,8},{1,17},{9,25},{17,1},{25,9},{2,18},{10... | collective-permute-start | bytes 491528 | tf_op jit(solution)/shard_map/ppermute | solution.py:395
  101.1 5.4 %collective-permute-start.37 = (bf16[4,160,128]{2,1,0:T(8,128)(2,1)S(1)}, bf16[4,160,128]{2,1,0:T(8,128)(2,1)S(1)}, u32[]{:S(2)}, u32[]{:S(2)}) collective-permute-start(bf16[4,160,128]{2,1,0:T(8,128)(2,1)S(1)} %get-tuple-element.238), channel_id=1, source_target_pairs={{0,16},{8,24},{16,0},{24,8},{1,17},{9,25},{17,1},{25,9},{2,18},{10... | collective-permute-start | bytes 491528 | tf_op jit(solution)/shard_map/ppermute | solution.py:395
  103.8 5.4 %collective-permute-start.40 = (bf16[4,160,128]{2,1,0:T(8,128)(2,1)S(1)}, bf16[4,160,128]{2,1,0:T(8,128)(2,1)S(1)}, u32[]{:S(2)}, u32[]{:S(2)}) collective-permute-start(bf16[4,160,128]{2,1,0:T(8,128)(2,1)S(1)} %get-tuple-element.241), channel_id=1, source_target_pairs={{0,8},{8,0},{16,24},{24,16},{1,9},{9,1},{17,25},{25,17},{2,10},{10... | collective-permute-start | bytes 491528 | tf_op jit(solution)/shard_map/ppermute | solution.py:395
  (2 other events, 2.2 us)

commit v4 on v3

--- a/solution.py
+++ b/solution.py
@@ -7,6 +7,7 @@
 from jax.experimental import pallas as pl
 from jax.experimental.pallas import tpu as pltpu
 from jax.sharding import PartitionSpec as P
+
 
 ITERS = 4
 SECOND = (-205.0 / 72.0, 8.0 / 5.0, -1.0 / 5.0, 8.0 / 315.0, -1.0 / 560.0)
@@ -135,56 +136,61 @@
 def list_kernel(rec_ref, layers, width, depth, list_ref):
     total = rec_ref.shape[1]
     cells = layers * width * depth
-    first = lax.axis_index("sub") * cells
-
-    def step(i, count):
-        local = rec_ref[0, i] - first
-        list_ref[count] = i
-        inside = jnp.bitwise_or(local, cells - 1 - local) >= 0
-        return count + jnp.where(inside, 1, 0)
-
-    count = lax.fori_loop(0, total, step, jnp.int32(0), unroll=8)
-
-    @pl.loop(0, count)
-    def _(c):
-        i = list_ref[c]
-        local = rec_ref[0, i] - first
-        skip = jnp.int32(PAD * depth)
-        for l in range(1, layers):
-            skip += jnp.where(local >= l * width * depth, 2 * PAD * depth, 0)
-        list_ref[c] = local + skip
-        list_ref[total + UNROLL + c] = i
-
-    for n in range(UNROLL):
-        list_ref[count + n] = -1
-        list_ref[total + UNROLL + count + n] = 0
-    list_ref[2 * (total + UNROLL)] = count
+    local = rec_ref[...] - lax.axis_index("sub") * cells
+    inside = jnp.logical_and(local >= 0, local < cells)
+    line = lax.shift_right_arithmetic(local, depth.bit_length() - 1)
+    row = line + PAD
+    for l in range(1, layers):
+        row += jnp.where(line >= l * width, 2 * PAD, 0)
+    number = lax.broadcasted_iota(jnp.int32, (1, total), 1)
+    down = lax.broadcasted_iota(jnp.int32, (total, total), 0)
+    across_ = lax.broadcasted_iota(jnp.int32, (total, total), 1)
+    earlier = jnp.where(down < across_, 1.0, 0.0).astype(BF16)
+    counted = jnp.broadcast_to(jnp.where(inside, 1.0, 0.0), (8, total))
+    place = jnp.dot(counted.astype(BF16), earlier, preferred_element_type=F32)[:1]
+    place = jnp.where(inside, place.astype(jnp.int32), -1)
+    spots = jnp.where(down == place, 1.0, 0.0).astype(BF16)
+    pieces = [local & (depth - 1), row & 255, row >> 8, number & 255, number >> 8]
+    kind = lax.broadcasted_iota(jnp.int32, (8, total), 0)
+    values = jnp.zeros((8, total), jnp.int32)
+    for n, piece in enumerate(pieces):
+        values = jnp.where(kind == n, piece, values)
+    listed = lax.dot_general(
+        values.astype(F32).astype(BF16), spots, (((1,), (1,)), ((), ())), preferred_element_type=F32
+    ).astype(jnp.int32)
+    count = jnp.sum(counted[:1], axis=1, keepdims=True).astype(jnp.int32)
+    code = (listed[2:3] * 256 + listed[1:2]) * (2 * depth) + listed[0:1]
+    list_ref[0:1, :] = jnp.where(number < count, code, depth)
+    list_ref[1:2, :] = listed[3:4] + 256 * listed[4:5]
+    list_ref[2:3, :] = jnp.broadcast_to(count, (1, total))
+    list_ref[3:4, :] = jnp.zeros((1, total), jnp.int32)
 
 
 def add_receivers(n, field_ref, into_ref, list_ref, observed_ref):
     depth = field_ref.shape[1]
     lane = lax.broadcasted_iota(jnp.int32, (1, depth), 1)
-    start = (list_ref.shape[0] - 1) // 2
-    count = list_ref[2 * start]
+    count = list_ref[2, 0]
 
     @pl.loop(0, (count + UNROLL - 1) // UNROLL)
     def _(c):
         rows, terms = [], []
         for k in range(UNROLL):
-            at = list_ref[c * UNROLL + k]
-            real = at >= 0
-            row = jnp.where(real, lax.div(at, depth), 0)
-            spot = jnp.where(real, lax.rem(at, depth), depth)
-            seen = observed_ref[n, list_ref[start + c * UNROLL + k]]
+            code = list_ref[0, c * UNROLL + k]
+            row = lax.div(code, 2 * depth)
+            spot = code - row * (2 * depth)
+            seen = observed_ref[n, list_ref[1, c * UNROLL + k]]
             rows.append(row)
             terms.append(jnp.where(lane == spot, field_ref[pl.ds(row, 1), :] - seen, 0.0))
         for row, term in zip(rows, terms):
             into_ref[pl.ds(row, 1), :] += term
 
 
-def receivers_kernel(n, field_ref, list_ref, observed_ref, source_ref):
-    source_ref[...] = jnp.zeros(source_ref.shape, F32)
-    add_receivers(n, field_ref, source_ref, list_ref, observed_ref)
+def receivers_kernel(*refs):
+    count = (len(refs) - 2) // 2
+    fields, (list_ref, observed_ref), outs = refs[:count], refs[count : count + 2], refs[count + 2 :]
+    for n, (field_ref, source_ref) in enumerate(zip(fields, outs)):
+        source_ref[...] = jnp.zeros(source_ref.shape, F32)
+        add_receivers(n, field_ref, source_ref, list_ref, observed_ref)
 
 
 def first_adjoint_kernel(n, p_ref, q_ref, list_ref, observed_ref, a_ref, half_ref, *part_refs):
@@ -206,7 +212,7 @@
                 part_ref[l, pl.ds(at, 16), :] = value
 
 
-def log_kernel(den_ref, matrix_ref, log_ref, s2_ref, s3_ref, z_ref):
+def log_kernel(den_ref, matrix_ref, before_ref, log_ref, s2_ref, s3_ref, z_ref):
     layers, width, depth = den_ref.shape
     zero_pads(log_ref)
 
@@ -257,7 +263,7 @@
 
 
 def forward_yz_kernel(f_ref, s2_ref, s3_ref, matrix_ref, part_ref, dy_ref, dz_ref, z_ref):
-    layers, width, depth = part_ref.shape
+    layers, width, _ = part_ref.shape
     z_terms(f_ref, matrix_ref, z_ref)
 
     @pl.loop(0, width // 8)
@@ -265,14 +271,18 @@
         at = pl.multiple_of(8 * j, 8)
         rows = pl.ds(at, 8)
         for l in range(layers):
-            f, part, d_y, d_z = yz_terms(f_ref, s2_ref, s3_ref, z_ref, l, at)
+            _, part, d_y, d_z = yz_terms(f_ref, s2_ref, s3_ref, z_ref, l, at)
             part_ref[l, rows, :] = part
             dy_ref[l, rows, :] = d_y
             dz_ref[l, rows, :] = d_z
 
 
-def forward_x_kernel(part, f_ref, on_ref, off_ref, part_ref, s1_ref, scale_ref, before_ref, *refs):
-    dx_ref, applied_ref, next_ref, half_ref, send_ref = refs[-5:]
+def forward_x_kernel(part, send, f_ref, on_ref, off_ref, part_ref, s1_ref, scale_ref, before_ref, *refs):
+    sending = send
+    if sending:
+        dx_ref, applied_ref, next_ref, half_ref, send_ref = refs[-5:]
+    else:
+        dx_ref, applied_ref, next_ref = refs[-3:]
     layers, width, _ = part_ref.shape
     shift = before_ref.shape[1] != width
     if part == 0:
@@ -289,9 +299,10 @@
             dx_ref[l, rows, :] = d_x
             applied_ref[l, rows, :] = applied
             next_ref[l, wide, :] = later
-            narrow = later.astype(BF16)
-            half_ref[l, rows, :] = narrow
-            send_ref[l, send_rows, :] = narrow
+            if sending:
+                narrow = later.astype(BF16)
+                half_ref[l, rows, :] = narrow
+                send_ref[l, send_rows, :] = narrow
 
     part_rows(part, width, off_ref, body)
 
@@ -303,7 +314,7 @@
         part_ref, vel_ref, den_ref, z_ref = refs
     else:
         vel_in, den_in, part_ref, vel_ref, den_ref, z_ref = refs
-    layers, width, depth = part_ref.shape
+    layers, width, _ = part_ref.shape
     z_terms(f_ref, matrix_ref, z_ref)
 
     @pl.loop(0, width // 8)
@@ -416,44 +427,51 @@
     return [1 << k for k in range(groups.bit_length() - 1)]
 
 
-def pick_into(out_ref, spot, held, me, row):
-    for offset, ref in held:
-
-        @pl.when(row == (me ^ offset))
-        def _(ref=ref):
-            if spot is None:
-                out_ref[...] = ref[...]
-            else:
-                out_ref[spot, :, :] = ref[...]
-
-
-def pick_kernel(offsets, bits, cover_ref, *refs):
-    me, column = lax.axis_index("shot"), lax.axis_index("sub")
+def routes_kernel(cover_ref, out_ref):
+    column = lax.axis_index("sub")
+    for g in range(out_ref.shape[0]):
+        out_ref[g, :, :] = jnp.full(out_ref.shape[1:], cover_ref[g, column], jnp.int32)
+
+
+def masked_sum(out_ref, first, terms):
+    layers, width, _ = terms[0][1].shape
+
+    @pl.loop(0, width // 16)
+    def _(j):
+        rows = pl.ds(pl.multiple_of(16 * j, 16), 16)
+        for l in range(layers):
+            total = None
+            for mask, ref in terms:
+                term = jnp.where(mask, ref[l, rows, :].astype(F32), 0.0)
+                total = term if total is None else total + term
+            out_ref[first + l, rows, :] = total.astype(out_ref.dtype)
+
+
+def pick_kernel(offsets, bits, route_ref, *refs):
+    me = lax.axis_index("shot")
     outs = refs[-2:]
     count = len(refs) // 2 - 1
     for way in range(2):
-        held = list(zip(offsets[way], refs[way * count : (way + 1) * count]))
-        pick_into(outs[way], None, held, me, cover_ref[me ^ bits[way], column])
-
-
-def gather_kernel(offsets, bits, cover_ref, *refs):
-    me, column = lax.axis_index("shot"), lax.axis_index("sub")
+        row = route_ref[me ^ bits[way]]
+        held = refs[way * count : (way + 1) * count]
+        masked_sum(outs[way], 0, [(row == (me ^ o), ref) for o, ref in zip(offsets[way], held)])
+
+
+def gather_kernel(offsets, bits, route_ref, *refs):
+    me = lax.axis_index("shot")
     out_ref = refs[-1]
     count = (len(refs) - 1) // 2
-    mine = cover_ref[me, column]
+    mine = route_ref[me]
     layers = out_ref.shape[0] // 2
     for way in range(2):
         *near, far = refs[way * count : (way + 1) * count]
-        spot = pl.ds(way * layers, layers)
-        pick_into(out_ref, spot, list(zip(offsets[way], near)), me, mine)
-
-        @pl.when((mine & bits[way]) != (me & bits[way]))
-        def _(far=far, spot=spot):
-            out_ref[spot, :, :] = far[...]
-
-
-def fetch(tile, cover, tie=lambda x: x, tie_last=lambda x: x):
-    groups = cover.shape[0]
+        terms = [(mine == (me ^ o), ref) for o, ref in zip(offsets[way], near)]
+        terms.append(((mine & bits[way]) != (me & bits[way]), far))
+        masked_sum(out_ref, way * layers, terms)
+
+
+def fetch(tile, route, tie=lambda x: x):
+    groups = route.shape[0]
     layers = tile.shape[0] // 2
     small = (layers, *tile.shape[1:])
     ways = [bits_of(groups), bits_of(groups)[::-1]]
@@ -470,38 +488,29 @@
             ]
             offsets[way] = offsets[way] + [o ^ bit for o in offsets[way]]
     last = [way[-1] for way in ways]
-    count = len(held[0])
     held = tie(held)
     sends = call(
         lambda *refs: pick_kernel(offsets, last, *refs),
-        [(small, BF16)] * 2, [cover, *held[0], *held[1]], [SM] + [VM] * (2 * count),
+        [(small, BF16)] * 2, [route, *held[0], *held[1]],
     )
     far = [swap_over("shot", groups, last[way], sends[way]) for way in range(2)]
-    far = tie_last(far)
     (out,) = call(
         lambda *refs: gather_kernel(offsets, last, *refs),
-        [(tile.shape, BF16)], [cover, *held[0], far[0], *held[1], far[1]],
-        [SM] + [VM] * (2 * count + 2),
+        [(tile.shape, BF16)], [route, *held[0], far[0], *held[1], far[1]],
     )
     return out
 
 
-def bucket_kernel(offsets, bits, cover_ref, *refs):
-    me, column = lax.axis_index("shot"), lax.axis_index("sub")
-    own, got, outs = refs[:1], refs[1:2], refs[2:]
-    mine = cover_ref[me, column]
-    for way in range(1):
-        theirs = cover_ref[me ^ bits[way], column]
-        own_ref = own[way]
-        for n, offset in enumerate(offsets[way]):
-            out = outs[way * len(offsets[way]) + n]
-            a = jnp.where(mine == (me ^ offset), own_ref[...].astype(F32), 0.0)
-            b = jnp.where(theirs == (me ^ offset), got[way][...].astype(F32), 0.0)
-            out[...] = (a + b).astype(out.dtype)
-
-
-def give_back(part, way, cover):
-    groups = cover.shape[0]
+def bucket_kernel(offsets, bit, route_ref, own_ref, got_ref, *outs):
+    me = lax.axis_index("shot")
+    mine, theirs = route_ref[me], route_ref[me ^ bit]
+    for offset, out in zip(offsets, outs):
+        row = me ^ offset
+        masked_sum(out, 0, [(mine == row, own_ref), (theirs == row, got_ref)])
+
+
+def give_back(part, way, route):
+    groups = route.shape[0]
     layers = part.shape[0]
     bits = bits_of(groups)[:: 1 if way == 0 else -1]
     got = swap_over("shot", groups, bits[0], part)
@@ -510,8 +519,8 @@
         offsets = offsets + [o ^ b for o in offsets]
     types = [BF16 if o & bits[1] else F32 for o in offsets]
     sums = call(
-        lambda *refs: bucket_kernel([offsets], [bits[0]], *refs),
-        [(part.shape, kind) for kind in types], [cover, part, got], [SM, VM, VM],
+        lambda *refs: bucket_kernel(offsets, bits[0], *refs),
+        [(part.shape, kind) for kind in types], [route, part, got],
     )
     left = dict(zip(offsets, sums))
     for b in bits[1:]:
@@ -525,7 +534,7 @@
     return left[0]
 
 
-def body(vel_model, den_model, cover, receivers, observed, p_now, p_before, q_now, q_before):
+def inner(vel_model, den_model, cover, receivers, observed, p_now, p_before, q_now, q_before):
     layers, width, depth = p_now.shape[1:]
     tall = width + 2 * PAD
     narrow, padded = ((layers, width, depth), F32), ((layers, tall, depth), F32)
@@ -538,53 +547,50 @@
     part_half = ((layers, size, depth), BF16)
     parts = range(PARTS)
 
+    groups = cover.shape[0]
+    (route,) = call(routes_kernel, [((groups, 16, depth), jnp.int32)], [cover], [SM])
+
     p, p_half = call(prepare_kernel, [padded, half], [p_now[0]])
     n_rec = receivers.shape[1]
     (lists,) = call(
         lambda rec, out: list_kernel(rec, layers, width, depth, out),
-        [((2 * (n_rec + UNROLL) + 1,), jnp.int32)], [receivers], [SM], [SM],
+        [((4, n_rec), jnp.int32)], [receivers],
     )
-    on, off = paired(p_half), across(p_half, fill=False)
+    on, off = paired(p_half), across(p_half)
     kept = {}
 
     def tie(held):
         held, kept["p"] = lax.optimization_barrier((held, p))
         return held
 
-    def tie_last(far):
-        far, kept["lists"], kept["on"], kept["off"] = lax.optimization_barrier((far, lists, on, off))
-        return far
-
-    den = fetch(den_model[0], cover, tie, tie_last)
-    vel = fetch(vel_model[0], cover)
-    p, lists, on, offs = kept["p"], kept["lists"], kept["on"], [kept["off"]] * PARTS
-
-    log_den, s2, s3 = call(log_kernel, [padded, narrow, narrow], [den, matrix], scratch=z_scratch)
+    den = fetch(den_model[0], route, tie)
+    vel = fetch(vel_model[0], route)
+    p, offs = kept["p"], [off] * PARTS
+
+    before = p_before[0]
+    log_den, s2, s3 = call(log_kernel, [padded, narrow, narrow], [den, matrix, before], scratch=z_scratch)
     s1, scale = call(slope_x_kernel, [narrow, narrow], [log_den, paired(den), across(den), vel])
 
-    stored, sources = [], []
-    before = p_before[0]
+    stored, fields = [], []
     for step in range(ITERS):
         part, d_y, d_z = call(forward_yz_kernel, [narrow] * 3, [p, s2, s3, matrix], scratch=z_scratch)
         if step > 0:
-            (source,) = call(
-                lambda *refs, n=step - 1: receivers_kernel(n, *refs),
-                [flat], [p.reshape(flat[0]), lists, seen], [VM, SM, SM],
-            )
-            sources.append(source.reshape(padded[0]))
+            fields.append(p.reshape(flat[0]))
+        sending = step < ITERS - 1
         made, sends = (), []
         for k in parts:
             ins = [p, on, offs[k], part, s1, scale, before]
-            *made, send = call(
-                lambda *refs, k=k: forward_x_kernel(k, *refs),
-                [narrow, narrow, padded, half, part_half], [*ins, *made],
+            outs = call(
+                lambda *refs, k=k, sending=sending: forward_x_kernel(k, sending, *refs),
+                [narrow, narrow, padded] + ([half, part_half] if sending else []), [*ins, *made],
                 aliases={len(ins) + n: n for n in range(len(made))},
             )
-            if step < ITERS - 1:
-                sends.append(across(send))
-        d_x, applied, later, p_half = made
-        if step < ITERS - 1:
-            on, offs = paired(p_half), sends
+            made = outs[: 4 if sending else 3]
+            if sending:
+                sends.append(across(outs[4]))
+        d_x, applied, later = made[:3]
+        if sending:
+            on, offs = paired(made[3]), sends
         stored.append((applied, d_x, d_y, d_z))
         before, p = p, later
 
@@ -597,6 +603,11 @@
     offs = [across(send) for send in sends]
     on = paired(a_half)
     a = a.reshape(padded[0])
+    sources = call(
+        receivers_kernel, [flat] * len(fields), [*fields, lists, seen],
+        [VM] * len(fields) + [SM, SM],
+    )
+    sources = [source.reshape(padded[0]) for source in sources]
     before, current = q_before[0], q
     sums = ()
     for step in range(ITERS - 1):
@@ -627,7 +638,7 @@
             before, current = current, later[0]
         sums = (sum_vel, sum_den)
     _, f_dx, f_dy, f_dz = stored[0]
-    grad_vel = [give_back(shot_vel[k], k, cover) for k in parts]
+    grad_vel = [give_back(shot_vel[k], k, route) for k in parts]
     (sum_den,) = call(last_yz_kernel, [narrow], [a, matrix, f_dy, f_dz, sum_den], scratch=z_scratch)
     grad_den = []
     for k in parts:
@@ -635,25 +646,16 @@
             lambda *refs, k=k: last_x_kernel(k, *refs),
             [part_half], [a, on, offs[k], f_dx, sum_den, scale, den],
         )
-        grad_den.append(give_back(shot_den, k, cover))
+        grad_den.append(give_back(shot_den, k, route))
     return jnp.concatenate(grad_vel, axis=1)[None], jnp.concatenate(grad_den, axis=1)[None]
 
 
 def solution(mesh):
+    spec = P("shot", "sub", None, None)
     return jax.shard_map(
-        body,
+        inner,
         mesh=mesh,
-        in_specs=(
-            P("shot", "sub", None, None),
-            P("shot", "sub", None, None),
-            P(),
-            P("shot", None),
-            P("shot", None, None),
-            P("shot", "sub", None, None),
-            P("shot", "sub", None, None),
-            P("shot", "sub", None, None),
-            P("shot", "sub", None, None),
-        ),
-        out_specs=(P("shot", "sub", None, None), P("shot", "sub", None, None)),
+        in_specs=(spec, spec, P(), P("shot", None), P("shot", None, None), spec, spec, spec, spec),
+        out_specs=(spec, spec),
         check_vma=False,
     )

time: 110 us -> 111 us (level)
  waiting for transfers between devices: 28.9 us -> 38.8 us
  Pallas kernels: 37.6 us -> 29.8 us
  starting transfers between devices: 39.2 us -> 38 us
    ppermute x16, waiting for transfers between devices: 15.6 us -> 24.2 us  [swap_over(): return lax.ppermute(value, axis, [(i, i ^ bit) for i in range(count)])]
    pallas_call x41 -> x40, Pallas kernels: 37.6 us -> 29.8 us  [call(): pl.pallas_call(kernel, out_shape=outs, in_specs=list(specs or [VM] * len(...]
    ppermute x9, starting transfers between devices: 4.51 us -> 1.38 us  [paired(): return lax.ppermute(half, 'sub', [(i, i ^ 1) for i in range(count)])]
    ppermute x16, waiting for transfers between devices: 13.3 us -> 14.6 us  [across(): return lax.ppermute(half, ('shot', 'sub'), pairs)]
  transfers between devices with their start and end apart: 41 -> 41, of which waited for: 21 -> 21; matrix products, arithmetic and copies ran while one was open for 1% -> 1% of each run, Pallas kernels for 28% -> 22%
where the time goes in v4:
time: 111 us
  waiting for transfers between devices  38.8 us (35%)
  starting transfers between devices  38 us (34%)
  Pallas kernels  29.8 us (27%)
  other arithmetic  1.89 us (2%)
  local copies, waits for them, and re-layouts  1.37 us (1%)
  between operations  1.13 us (1%)
    pallas_call x40, Pallas kernels, call(): pl.pallas_call(kernel, out_shape=outs, in_specs=list(specs or [VM] * len(...  29.8 us
    ppermute x16, waiting for transfers between devices, swap_over(): return lax.ppermute(value, axis, [(i, i ^ bit) for i in range(count)])  24.2 us
    ppermute x16, starting transfers between devices, swap_over(): return lax.ppermute(value, axis, [(i, i ^ bit) for i in range(count)])  19.3 us
    ppermute x16, starting transfers between devices, across(): return lax.ppermute(half, ('shot', 'sub'), pairs)  17.4 us
    ppermute x16, waiting for transfers between devices, across(): return lax.ppermute(half, ('shot', 'sub'), pairs)  14.6 us
  transfers between devices with their start and end apart: 41, of which 21 were waited for; matrix products, arithmetic and copies ran while one was open for 1% of the time, Pallas kernels for 22%

profile of v4, /device:TPU:0, one launch (start us, length us, event | category | flops | bytes accessed | tf_op | source)
XLA Modules:
  0.0 111.1 jit_solution(12194081265171097839)
XLA Ops:
  0.6 1.1 slice_bitcast_fusion.2
  1.8 3.1 %collective-permute-start.1 = (bf16[2,320,128]{2,1,0:T(8,128)(2,1)S(1)}, bf16[2,320,128]{2,1,0:T(8,128)(2,1)S(1)}, u32[]{:S(2)}, u32[]{:S(2)}) collective-permute-start(bf16[2,320,128]{2,1,0:T(8,128)(2,1)S(1)} %get-tuple-element.124.refs_3_.refs_4_), channel_id=1, source_target_pairs={{0,16},{8,24},{16,0},{24,8},{1,17},{9,25},{17,1},{25,9},{2,18},{10... | collective-permute-start | bytes 491528 | tf_op jit(solution)/shard_map/ppermute | solution.py:406
  4.8 1.5 %collective-permute-start = (bf16[2,320,128]{2,1,0:T(8,128)(2,1)S(1)}, bf16[2,320,128]{2,1,0:T(8,128)(2,1)S(1)}, u32[]{:S(2)}, u32[]{:S(2)}) collective-permute-start(bf16[2,320,128]{2,1,0:T(8,128)(2,1)S(1)} %get-tuple-element.122.refs_1_), channel_id=1, source_target_pairs={{0,8},{8,0},{16,24},{24,16},{1,9},{9,1},{17,25},{25,17},{2,10},{10... | collective-permute-start | bytes 491528 | tf_op jit(solution)/shard_map/ppermute | solution.py:406
  7.8 2.0 %collective-permute-done.1.refs_4_.refs_5_ = bf16[2,320,128]{2,1,0:T(8,128)(2,1)S(1)} collective-permute-done((bf16[2,320,128]{2,1,0:T(8,128)(2,1)S(1)}, bf16[2,320,128]{2,1,0:T(8,128)(2,1)S(1)}, u32[]{:S(2)}, u32[]{:S(2)}) %collective-permute-start.1) | collective-permute-done | bytes 163872 | tf_op jit(solution)/shard_map/ppermute | solution.py:406
  9.7 2.1 %collective-permute-done.refs_2_ = bf16[2,320,128]{2,1,0:T(8,128)(2,1)S(1)} collective-permute-done((bf16[2,320,128]{2,1,0:T(8,128)(2,1)S(1)}, bf16[2,320,128]{2,1,0:T(8,128)(2,1)S(1)}, u32[]{:S(2)}, u32[]{:S(2)}) %collective-permute-start) | collective-permute-done | bytes 163872 | tf_op jit(solution)/shard_map/ppermute | solution.py:406
  12.3 2.0 %collective-permute-start.5 = (bf16[2,320,128]{2,1,0:T(8,128)(2,1)S(1)}, bf16[2,320,128]{2,1,0:T(8,128)(2,1)S(1)}, u32[]{:S(2)}, u32[]{:S(2)}) collective-permute-start(bf16[2,320,128]{2,1,0:T(8,128)(2,1)S(1)} %get-tuple-element.127), channel_id=1, source_target_pairs={{0,8},{8,0},{16,24},{24,16},{1,9},{9,1},{17,25},{25,17},{2,10},{10... | collective-permute-start | bytes 491528 | tf_op jit(solution)/shard_map/ppermute | solution.py:406
  14.3 1.1 collective-permute-done.8.refs_2_
  16.3 3.0 %collective-permute-done.4.refs_3_ = bf16[2,320,128]{2,1,0:T(8,128)(2,1)S(1)} collective-permute-done((bf16[2,320,128]{2,1,0:T(8,128)(2,1)S(1)}, bf16[2,320,128]{2,1,0:T(8,128)(2,1)S(1)}, u32[]{:S(2)}, u32[]{:S(2)}) %collective-permute-start.4) | collective-permute-done | bytes 163872 | tf_op jit(solution)/shard_map/ppermute | solution.py:406
  19.7 1.6 %collective-permute-start.7 = (bf16[4,320,128]{2,1,0:T(8,128)(2,1)S(1)}, bf16[4,320,128]{2,1,0:T(8,128)(2,1)S(1)}, u32[]{:S(2)}, u32[]{:S(2)}) collective-permute-start(bf16[4,320,128]{2,1,0:T(8,128)(2,1)S(1)} %shard_map.116.den_ref.refs_6_), channel_id=1, source_target_pairs={{1,2},{2,1},{3,4},{4,3},{5,6},{6,5},{0,8},{7,15},{9,10},{10,9},{11... | collective-permute-start | bytes 983048 | tf_op jit(solution)/shard_map/ppermute | solution.py:423
  21.4 1.5 %collective-permute-start.3 = (bf16[4,320,128]{2,1,0:T(8,128)(2,1)S(1)}, bf16[4,320,128]{2,1,0:T(8,128)(2,1)S(1)}, u32[]{:S(2)}, u32[]{:S(2)}) collective-permute-start(bf16[4,320,128]{2,1,0:T(8,128)(2,1)S(1)} %get-tuple-element.121), channel_id=1, source_target_pairs={{1,2},{2,1},{3,4},{4,3},{5,6},{6,5},{0,8},{7,15},{9,10},{10,9},{11... | collective-permute-start | bytes 983048 | tf_op jit(solution)/shard_map/ppermute | solution.py:423
  23.1 1.5 %collective-permute-start.11 = (bf16[2,320,128]{2,1,0:T(8,128)(2,1)S(1)}, bf16[2,320,128]{2,1,0:T(8,128)(2,1)S(1)}, u32[]{:S(2)}, u32[]{:S(2)}) collective-permute-start(bf16[2,320,128]{2,1,0:T(8,128)(2,1)S(1)} %get-tuple-element.133), channel_id=1, source_target_pairs={{0,8},{8,0},{16,24},{24,16},{1,9},{9,1},{17,25},{25,17},{2,10},{10... | collective-permute-start | bytes 491528 | tf_op jit(solution)/shard_map/ppermute | solution.py:406
  24.6 1.3 %shard_map.117 = (f32[4,336,128]{2,1,0:T(8,128)S(1)}, f32[4,320,128]{2,1,0:T(8,128)S(1)}, f32[4,320,128]{2,1,0:T(8,128)S(1)}) custom-call(bf16[4,320,128]{2,1,0:T(8,128)(2,1)S(1)} %shard_map.116.den_ref.refs_6_, bf16[384,256]{1,0:T(8,128)(2,1)S(1)} %copy-done, f32[4,320,128]{2,1,0:T(8,128)S(1)} %bitcast.33), custom_call_target="tpu_custom_call" | custom-call | bytes 3178496 | tf_op jit(solution)/shard_map/pallas_call | solution.py:29
  26.0 1.4 %shard_map.118 = (f32[4,320,128]{2,1,0:T(8,128)S(1)}, f32[4,320,128]{2,1,0:T(8,128)S(1)}, f32[4,320,128]{2,1,0:T(8,128)S(1)}) custom-call(f32[4,336,128]{2,1,0:T(8,128)S(1)} %get-tuple-element.120.f_ref.refs_0_.refs_6_, f32[4,320,128]{2,1,0:T(8,128)S(1)} %get-tuple-element.128.s2_ref.refs_1_, f32[4,320,128]{2,1,0:T(8,128)S(1)} %get-tuple-element.129.s3_ref.refs_2_, ...), custom_call_target="tpu_custom_call" | custom-call | bytes 4161536 | tf_op jit(solution)/shard_map/pallas_call | solution.py:29
  27.4 6.4 %collective-permute-done.11.refs_6_ = bf16[2,320,128]{2,1,0:T(8,128)(2,1)S(1)} collective-permute-done((bf16[2,320,128]{2,1,0:T(8,128)(2,1)S(1)}, bf16[2,320,128]{2,1,0:T(8,128)(2,1)S(1)}, u32[]{:S(2)}, u32[]{:S(2)}) %collective-permute-start.11) | collective-permute-done | bytes 163872 | tf_op jit(solution)/shard_map/ppermute | solution.py:406
  36.0 1.6 %collective-permute-start.14 = (bf16[4,160,128]{2,1,0:T(8,128)(2,1)S(1)}, bf16[4,160,128]{2,1,0:T(8,128)(2,1)S(1)}, u32[]{:S(2)}, u32[]{:S(2)}) collective-permute-start(bf16[4,160,128]{2,1,0:T(8,128)(2,1)S(1)} %get-tuple-element.144), channel_id=1, source_target_pairs={{1,2},{2,1},{3,4},{4,3},{5,6},{6,5},{0,8},{7,15},{9,10},{10,9},{11... | collective-permute-start | bytes 491528 | tf_op jit(solution)/shard_map/ppermute | solution.py:423
  38.1 1.4 %shard_map.124 = (f32[4,320,128]{2,1,0:T(8,128)S(1)}, f32[4,320,128]{2,1,0:T(8,128)S(1)}, f32[4,320,128]{2,1,0:T(8,128)S(1)}) custom-call(f32[4,336,128]{2,1,0:T(8,128)S(1)} %get-tuple-element.140.f_ref.refs_0_.refs_6_, f32[4,320,128]{2,1,0:T(8,128)S(1)} %get-tuple-element.128.s2_ref.refs_1_, f32[4,320,128]{2,1,0:T(8,128)S(1)} %get-tuple-element.129.s3_ref.refs_2_, ...), custom_call_target="tpu_custom_call" | custom-call | bytes 4161536 | tf_op jit(solution)/shard_map/pallas_call | solution.py:29
  39.5 1.9 %collective-permute-done.14.refs_2_ = bf16[4,160,128]{2,1,0:T(8,128)(2,1)S(1)} collective-permute-done((bf16[4,160,128]{2,1,0:T(8,128)(2,1)S(1)}, bf16[4,160,128]{2,1,0:T(8,128)(2,1)S(1)}, u32[]{:S(2)}, u32[]{:S(2)}) %collective-permute-start.14) | collective-permute-done | bytes 163872 | tf_op jit(solution)/shard_map/ppermute | solution.py:423
  41.9 1.3 %collective-permute-done.13.refs_2_ = bf16[4,160,128]{2,1,0:T(8,128)(2,1)S(1)} collective-permute-done((bf16[4,160,128]{2,1,0:T(8,128)(2,1)S(1)}, bf16[4,160,128]{2,1,0:T(8,128)(2,1)S(1)}, u32[]{:S(2)}, u32[]{:S(2)}) %collective-permute-start.13) | collective-permute-done | bytes 163872 | tf_op jit(solution)/shard_map/ppermute | solution.py:423
  43.8 1.5 %collective-permute-start.17 = (bf16[4,160,128]{2,1,0:T(8,128)(2,1)S(1)}, bf16[4,160,128]{2,1,0:T(8,128)(2,1)S(1)}, u32[]{:S(2)}, u32[]{:S(2)}) collective-permute-start(bf16[4,160,128]{2,1,0:T(8,128)(2,1)S(1)} %get-tuple-element.153), channel_id=1, source_target_pairs={{1,2},{2,1},{3,4},{4,3},{5,6},{6,5},{0,8},{7,15},{9,10},{10,9},{11... | collective-permute-start | bytes 491528 | tf_op jit(solution)/shard_map/ppermute | solution.py:423
  45.9 1.4 %shard_map.127 = (f32[4,320,128]{2,1,0:T(8,128)S(1)}, f32[4,320,128]{2,1,0:T(8,128)S(1)}, f32[4,320,128]{2,1,0:T(8,128)S(1)}) custom-call(f32[4,336,128]{2,1,0:T(8,128)S(1)} %get-tuple-element.149.f_ref.refs_0_.refs_6_, f32[4,320,128]{2,1,0:T(8,128)S(1)} %get-tuple-element.128.s2_ref.refs_1_, f32[4,320,128]{2,1,0:T(8,128)S(1)} %get-tuple-element.129.s3_ref.refs_2_, ...), custom_call_target="tpu_custom_call" | custom-call | bytes 4161536 | tf_op jit(solution)/shard_map/pallas_call | solution.py:29
  47.3 1.9 %collective-permute-done.17.refs_2_ = bf16[4,160,128]{2,1,0:T(8,128)(2,1)S(1)} collective-permute-done((bf16[4,160,128]{2,1,0:T(8,128)(2,1)S(1)}, bf16[4,160,128]{2,1,0:T(8,128)(2,1)S(1)}, u32[]{:S(2)}, u32[]{:S(2)}) %collective-permute-start.17) | collective-permute-done | bytes 163872 | tf_op jit(solution)/shard_map/ppermute | solution.py:423
  49.6 1.3 %collective-permute-done.16.refs_2_ = bf16[4,160,128]{2,1,0:T(8,128)(2,1)S(1)} collective-permute-done((bf16[4,160,128]{2,1,0:T(8,128)(2,1)S(1)}, bf16[4,160,128]{2,1,0:T(8,128)(2,1)S(1)}, u32[]{:S(2)}, u32[]{:S(2)}) %collective-permute-start.16) | collective-permute-done | bytes 163872 | tf_op jit(solution)/shard_map/ppermute | solution.py:423
  51.6 1.5 %collective-permute-start.20 = (bf16[4,160,128]{2,1,0:T(8,128)(2,1)S(1)}, bf16[4,160,128]{2,1,0:T(8,128)(2,1)S(1)}, u32[]{:S(2)}, u32[]{:S(2)}) collective-permute-start(bf16[4,160,128]{2,1,0:T(8,128)(2,1)S(1)} %get-tuple-element.162), channel_id=1, source_target_pairs={{1,2},{2,1},{3,4},{4,3},{5,6},{6,5},{0,8},{7,15},{9,10},{10,9},{11... | collective-permute-start | bytes 491528 | tf_op jit(solution)/shard_map/ppermute | solution.py:423
  54.2 1.4 %shard_map.130 = (f32[4,320,128]{2,1,0:T(8,128)S(1)}, f32[4,320,128]{2,1,0:T(8,128)S(1)}, f32[4,320,128]{2,1,0:T(8,128)S(1)}) custom-call(f32[4,336,128]{2,1,0:T(8,128)S(1)} %get-tuple-element.158.f_ref.refs_0_, f32[4,320,128]{2,1,0:T(8,128)S(1)} %get-tuple-element.128.s2_ref.refs_1_, f32[4,320,128]{2,1,0:T(8,128)S(1)} %get-tuple-element.129.s3_ref.refs_2_, ...), custom_call_target="tpu_custom_call" | custom-call | bytes 4161536 | tf_op jit(solution)/shard_map/pallas_call | solution.py:29
  55.6 1.3 %collective-permute-done.20.refs_2_ = bf16[4,160,128]{2,1,0:T(8,128)(2,1)S(1)} collective-permute-done((bf16[4,160,128]{2,1,0:T(8,128)(2,1)S(1)}, bf16[4,160,128]{2,1,0:T(8,128)(2,1)S(1)}, u32[]{:S(2)}, u32[]{:S(2)}) %collective-permute-start.20) | collective-permute-done | bytes 163872 | tf_op jit(solution)/shard_map/ppermute | solution.py:423
  57.4 1.3 %collective-permute-done.19.refs_2_ = bf16[4,160,128]{2,1,0:T(8,128)(2,1)S(1)} collective-permute-done((bf16[4,160,128]{2,1,0:T(8,128)(2,1)S(1)}, bf16[4,160,128]{2,1,0:T(8,128)(2,1)S(1)}, u32[]{:S(2)}, u32[]{:S(2)}) %collective-permute-start.19) | collective-permute-done | bytes 163872 | tf_op jit(solution)/shard_map/ppermute | solution.py:423
  59.4 1.7 %shard_map.135 = (f32[1344,128]{1,0:T(8,128)S(1)}, bf16[4,320,128]{2,1,0:T(8,128)(2,1)S(1)}, bf16[4,160,128]{2,1,0:T(8,128)(2,1)S(1)}, bf16[4,160,128]{2,1,0:T(8,128)(2,1)S(1)}) custom-call(f32[1344,128]{1,0:T(8,128)S(1)} %bitcast.38, f32[1344,128]{1,0:T(8,128)S(1)} %bitcast.29, s32[4,512]{1,0:T(4,128)S(1)} %shard_map.134.refs_2_.refs_3_, f32[4,512]{1,0:T(4,128)S(1)} %bitcast.47), custom_call_target="tpu_custom_call" | custom-call | bytes 2736128 | tf_op jit(solution)/shard_map/pallas_call | solution.py:29
  61.1 1.6 %collective-permute-start.23 = (bf16[4,160,128]{2,1,0:T(8,128)(2,1)S(1)}, bf16[4,160,128]{2,1,0:T(8,128)(2,1)S(1)}, u32[]{:S(2)}, u32[]{:S(2)}) collective-permute-start(bf16[4,160,128]{2,1,0:T(8,128)(2,1)S(1)} %get-tuple-element.177), channel_id=1, source_target_pairs={{1,2},{2,1},{3,4},{4,3},{5,6},{6,5},{0,8},{7,15},{9,10},{10,9},{11... | collective-permute-start | bytes 491528 | tf_op jit(solution)/shard_map/ppermute | solution.py:423
  63.2 3.0 %shard_map.137 = (f32[1344,128]{1,0:T(8,128)S(1)}, f32[1344,128]{1,0:T(8,128)S(1)}, f32[1344,128]{1,0:T(8,128)S(1)}) custom-call(f32[1344,128]{1,0:T(8,128)S(1)} %bitcast.26, f32[1344,128]{1,0:T(8,128)S(1)} %bitcast.27, f32[1344,128]{1,0:T(8,128)S(1)} %bitcast.28, s32[4,512]{1,0:T(4,128)S(1)} %shard_map.134.refs_2_.refs_3_, f32[4,512]{1,0:T(4,128)S(1)} %bitcast.48), custom_call_target="tpu_custom_call" | custom-call | bytes 4145152 | tf_op jit(solution)/shard_map/pallas_call | solution.py:29
  66.2 1.5 %shard_map.136 = (f32[4,320,128]{2,1,0:T(8,128)S(1)}, f32[4,320,128]{2,1,0:T(8,128)S(1)}, f32[4,320,128]{2,1,0:T(8,128)S(1)}) custom-call(f32[4,336,128]{2,1,0:T(8,128)S(1)} %bitcast.30, f32[4,320,128]{2,1,0:T(8,128)S(1)} %get-tuple-element.128.s2_ref.refs_1_, f32[4,320,128]{2,1,0:T(8,128)S(1)} %get-tuple-element.129.s3_ref.refs_2_, ...), custom_call_target="tpu_custom_call" | custom-call | bytes 6127616 | tf_op jit(solution)/shard_map/pallas_call | solution.py:29
  68.9 1.5 %collective-permute-start.26 = (bf16[4,160,128]{2,1,0:T(8,128)(2,1)S(1)}, bf16[4,160,128]{2,1,0:T(8,128)(2,1)S(1)}, u32[]{:S(2)}, u32[]{:S(2)}) collective-permute-start(bf16[4,160,128]{2,1,0:T(8,128)(2,1)S(1)} %get-tuple-element.194), channel_id=1, source_target_pairs={{1,2},{2,1},{3,4},{4,3},{5,6},{6,5},{0,8},{7,15},{9,10},{10,9},{11... | collective-permute-start | bytes 491528 | tf_op jit(solution)/shard_map/ppermute | solution.py:423
  71.0 1.6 %shard_map.140 = (f32[4,320,128]{2,1,0:T(8,128)S(1)}, f32[4,320,128]{2,1,0:T(8,128)S(1)}, f32[4,320,128]{2,1,0:T(8,128)S(1)}) custom-call(f32[4,336,128]{2,1,0:T(8,128)S(1)} %get-tuple-element.182.refs_0_, f32[4,320,128]{2,1,0:T(8,128)S(1)} %get-tuple-element.128.s2_ref.refs_1_, f32[4,320,128]{2,1,0:T(8,128)S(1)} %get-tuple-element.129.s3_ref.refs_2_, ...), custom_call_target="tpu_custom_call" | custom-call | bytes 7438336 | tf_op jit(solution)/shard_map/pallas_call | solution.py:29
  72.6 1.7 %collective-permute-done.26.refs_2_ = bf16[4,160,128]{2,1,0:T(8,128)(2,1)S(1)} collective-permute-done((bf16[4,160,128]{2,1,0:T(8,128)(2,1)S(1)}, bf16[4,160,128]{2,1,0:T(8,128)(2,1)S(1)}, u32[]{:S(2)}, u32[]{:S(2)}) %collective-permute-start.26) | collective-permute-done | bytes 163872 | tf_op jit(solution)/shard_map/ppermute | solution.py:423
  74.8 1.2 %collective-permute-done.25.refs_2_ = bf16[4,160,128]{2,1,0:T(8,128)(2,1)S(1)} collective-permute-done((bf16[4,160,128]{2,1,0:T(8,128)(2,1)S(1)}, bf16[4,160,128]{2,1,0:T(8,128)(2,1)S(1)}, u32[]{:S(2)}, u32[]{:S(2)}) %collective-permute-start.25) | collective-permute-done | bytes 163872 | tf_op jit(solution)/shard_map/ppermute | solution.py:423
  76.8 1.4 %collective-permute-start.28 = (bf16[4,160,128]{2,1,0:T(8,128)(2,1)S(1)}, bf16[4,160,128]{2,1,0:T(8,128)(2,1)S(1)}, u32[]{:S(2)}, u32[]{:S(2)}) collective-permute-start(bf16[4,160,128]{2,1,0:T(8,128)(2,1)S(1)} %get-tuple-element.201), channel_id=1, source_target_pairs={{1,2},{2,1},{3,4},{4,3},{5,6},{6,5},{0,8},{7,15},{9,10},{10,9},{11... | collective-permute-start | bytes 491528 | tf_op jit(solution)/shard_map/ppermute | solution.py:423
  78.8 1.6 %shard_map.143 = (f32[4,320,128]{2,1,0:T(8,128)S(1)}, f32[4,320,128]{2,1,0:T(8,128)S(1)}, f32[4,320,128]{2,1,0:T(8,128)S(1)}) custom-call(f32[4,336,128]{2,1,0:T(8,128)S(1)} %get-tuple-element.199.refs_0_, f32[4,320,128]{2,1,0:T(8,128)S(1)} %get-tuple-element.128.s2_ref.refs_1_, f32[4,320,128]{2,1,0:T(8,128)S(1)} %get-tuple-element.129.s3_ref.refs_2_, ...), custom_call_target="tpu_custom_call" | custom-call | bytes 7438336 | tf_op jit(solution)/shard_map/pallas_call | solution.py:29
  80.4 1.7 %collective-permute-done.28.refs_2_ = bf16[4,160,128]{2,1,0:T(8,128)(2,1)S(1)} collective-permute-done((bf16[4,160,128]{2,1,0:T(8,128)(2,1)S(1)}, bf16[4,160,128]{2,1,0:T(8,128)(2,1)S(1)}, u32[]{:S(2)}, u32[]{:S(2)}) %collective-permute-start.28) | collective-permute-done | bytes 163872 | tf_op jit(solution)/shard_map/ppermute | solution.py:423
  82.7 1.1 %collective-permute-done.31.refs_2_ = bf16[4,160,128]{2,1,0:T(8,128)(2,1)S(1)} collective-permute-done((bf16[4,160,128]{2,1,0:T(8,128)(2,1)S(1)}, bf16[4,160,128]{2,1,0:T(8,128)(2,1)S(1)}, u32[]{:S(2)}, u32[]{:S(2)}) %collective-permute-start.31) | collective-permute-done | bytes 163872 | tf_op jit(solution)/shard_map/ppermute | solution.py:423
  85.0 1.5 %collective-permute-start.29 = (bf16[4,160,128]{2,1,0:T(8,128)(2,1)S(1)}, bf16[4,160,128]{2,1,0:T(8,128)(2,1)S(1)}, u32[]{:S(2)}, u32[]{:S(2)}) collective-permute-start(bf16[4,160,128]{2,1,0:T(8,128)(2,1)S(1)} %get-tuple-element.214.refs_1_), channel_id=1, source_target_pairs={{0,8},{8,0},{16,24},{24,16},{1,9},{9,1},{17,25},{25,17},{2,10},{10... | collective-permute-start | bytes 491528 | tf_op jit(solution)/shard_map/ppermute | solution.py:406
  87.0 1.5 %collective-permute-start.38 = (bf16[4,160,128]{2,1,0:T(8,128)(2,1)S(1)}, bf16[4,160,128]{2,1,0:T(8,128)(2,1)S(1)}, u32[]{:S(2)}, u32[]{:S(2)}) collective-permute-start(bf16[4,160,128]{2,1,0:T(8,128)(2,1)S(1)} %get-tuple-element.233), channel_id=1, source_target_pairs={{1,2},{2,1},{3,4},{4,3},{5,6},{6,5},{0,8},{7,15},{9,10},{10,9},{11... | collective-permute-start | bytes 491528 | tf_op jit(solution)/shard_map/ppermute | solution.py:423
  88.6 2.5 %collective-permute-done.32.refs_2_ = bf16[4,160,128]{2,1,0:T(8,128)(2,1)S(1)} collective-permute-done((bf16[4,160,128]{2,1,0:T(8,128)(2,1)S(1)}, bf16[4,160,128]{2,1,0:T(8,128)(2,1)S(1)}, u32[]{:S(2)}, u32[]{:S(2)}) %collective-permute-start.32) | collective-permute-done | bytes 163872 | tf_op jit(solution)/shard_map/ppermute | solution.py:406
  91.3 1.5 %collective-permute-start.33 = (bf16[4,160,128]{2,1,0:T(8,128)(2,1)S(1)}, bf16[4,160,128]{2,1,0:T(8,128)(2,1)S(1)}, u32[]{:S(2)}, u32[]{:S(2)}) collective-permute-start(bf16[4,160,128]{2,1,0:T(8,128)(2,1)S(1)} %get-tuple-element.223), channel_id=1, source_target_pairs={{0,8},{8,0},{16,24},{24,16},{1,9},{9,1},{17,25},{25,17},{2,10},{10... | collective-permute-start | bytes 491528 | tf_op jit(solution)/shard_map/ppermute | solution.py:406
  92.8 1.2 %shard_map.148.refs_4_ = f32[4,320,128]{2,1,0:T(8,128)S(1)} custom-call(f32[4,336,128]{2,1,0:T(8,128)S(1)} %get-tuple-element.224.f_ref.refs_0_, bf16[384,256]{1,0:T(8,128)(2,1)S(1)} %copy-done, f32[4,320,128]{2,1,0:T(8,128)S(1)} %get-tuple-element.228.fdy_ref, f32[4,320,128]{2,1,0:T(8,128)S(1)} %get-tuple-element.229.fdz_ref, ...), custom_call_target="tpu_custom_call" | custom-call | bytes 3506176 | tf_op jit(solution)/shard_map/pallas_call | solution.py:29
  96.3 2.3 %collective-permute-start.39 = (bf16[4,160,128]{2,1,0:T(8,128)(2,1)S(1)}, bf16[4,160,128]{2,1,0:T(8,128)(2,1)S(1)}, u32[]{:S(2)}, u32[]{:S(2)}) collective-permute-start(bf16[4,160,128]{2,1,0:T(8,128)(2,1)S(1)} %shard_map.151.refs_1_), channel_id=1, source_target_pairs={{0,16},{8,24},{16,0},{24,8},{1,17},{9,25},{17,1},{25,9},{2,18},{10... | collective-permute-start | bytes 491528 | tf_op jit(solution)/shard_map/ppermute | solution.py:406
  99.5 2.3 %collective-permute-done.36.refs_2_ = bf16[4,160,128]{2,1,0:T(8,128)(2,1)S(1)} collective-permute-done((bf16[4,160,128]{2,1,0:T(8,128)(2,1)S(1)}, bf16[4,160,128]{2,1,0:T(8,128)(2,1)S(1)}, u32[]{:S(2)}, u32[]{:S(2)}) %collective-permute-start.36) | collective-permute-done | bytes 163872 | tf_op jit(solution)/shard_map/ppermute | solution.py:406
  102.0 1.7 %collective-permute-start.37 = (bf16[4,160,128]{2,1,0:T(8,128)(2,1)S(1)}, bf16[4,160,128]{2,1,0:T(8,128)(2,1)S(1)}, u32[]{:S(2)}, u32[]{:S(2)}) collective-permute-start(bf16[4,160,128]{2,1,0:T(8,128)(2,1)S(1)} %get-tuple-element.232), channel_id=1, source_target_pairs={{0,16},{8,24},{16,0},{24,8},{1,17},{9,25},{17,1},{25,9},{2,18},{10... | collective-permute-start | bytes 491528 | tf_op jit(solution)/shard_map/ppermute | solution.py:406
  104.8 1.5 %collective-permute-start.40 = (bf16[4,160,128]{2,1,0:T(8,128)(2,1)S(1)}, bf16[4,160,128]{2,1,0:T(8,128)(2,1)S(1)}, u32[]{:S(2)}, u32[]{:S(2)}) collective-permute-start(bf16[4,160,128]{2,1,0:T(8,128)(2,1)S(1)} %get-tuple-element.235), channel_id=1, source_target_pairs={{0,8},{8,0},{16,24},{24,16},{1,9},{9,1},{17,25},{25,17},{2,10},{10... | collective-permute-start | bytes 491528 | tf_op jit(solution)/shard_map/ppermute | solution.py:406
  107.4 2.8 %collective-permute-done.40 = bf16[4,160,128]{2,1,0:T(8,128)(2,1)S(1)} collective-permute-done((bf16[4,160,128]{2,1,0:T(8,128)(2,1)S(1)}, bf16[4,160,128]{2,1,0:T(8,128)(2,1)S(1)}, u32[]{:S(2)}, u32[]{:S(2)}) %collective-permute-start.40) | collective-permute-done | bytes 163872 | tf_op jit(solution)/shard_map/ppermute | solution.py:406
  (100 shorter events, 24.4 us)
Async XLA Ops:
  0.6 5.7 %copy-start.8 = (bf16[1,4,320,128]{3,2,1,0:T(8,128)(2,1)S(1)}, bf16[1,4,320,128]{3,2,1,0:T(8,128)(2,1)}, u32[]{:S(2)}) copy-start(bf16[1,4,320,128]{3,2,1,0:T(8,128)(2,1)} %param.10) | copy-start | bytes 983044
  0.6 7.0 %copy-start.3 = (f32[1,4,320,128]{3,2,1,0:T(8,128)S(1)}, f32[1,4,320,128]{3,2,1,0:T(8,128)}, u32[]{:S(2)}) copy-start(f32[1,4,320,128]{3,2,1,0:T(8,128)} %param.15) | copy-start | bytes 1966084
  1.8 8.0 %collective-permute-start.1 = (bf16[2,320,128]{2,1,0:T(8,128)(2,1)S(1)}, bf16[2,320,128]{2,1,0:T(8,128)(2,1)S(1)}, u32[]{:S(2)}, u32[]{:S(2)}) collective-permute-start(bf16[2,320,128]{2,1,0:T(8,128)(2,1)S(1)} %get-tuple-element.124.refs_3_.refs_4_), channel_id=1, source_target_pairs={{0,16},{8,24},{16,0},{24,8},{1,17},{9,25},{17,1},{25,9},{2,18},{10... | collective-permute-start | bytes 491528 | tf_op jit(solution)/shard_map/ppermute | solution.py:406
  4.8 7.1 %collective-permute-start = (bf16[2,320,128]{2,1,0:T(8,128)(2,1)S(1)}, bf16[2,320,128]{2,1,0:T(8,128)(2,1)S(1)}, u32[]{:S(2)}, u32[]{:S(2)}) collective-permute-start(bf16[2,320,128]{2,1,0:T(8,128)(2,1)S(1)} %get-tuple-element.122.refs_1_), channel_id=1, source_target_pairs={{0,8},{8,0},{16,24},{24,16},{1,9},{9,1},{17,25},{25,17},{2,10},{10... | collective-permute-start | bytes 491528 | tf_op jit(solution)/shard_map/ppermute | solution.py:406
  6.3 8.0 %collective-permute-start.9 = (bf16[2,320,128]{2,1,0:T(8,128)(2,1)S(1)}, bf16[2,320,128]{2,1,0:T(8,128)(2,1)S(1)}, u32[]{:S(2)}, u32[]{:S(2)}) collective-permute-start(bf16[2,320,128]{2,1,0:T(8,128)(2,1)S(1)} %get-tuple-element.236.refs_3_.refs_4_), channel_id=1, source_target_pairs={{0,16},{8,24},{16,0},{24,8},{1,17},{9,25},{17,1},{25,9},{2,18},{10... | collective-permute-start | bytes 491528 | tf_op jit(solution)/shard_map/ppermute | solution.py:406
  6.9 8.5 %collective-permute-start.8 = (bf16[2,320,128]{2,1,0:T(8,128)(2,1)S(1)}, bf16[2,320,128]{2,1,0:T(8,128)(2,1)S(1)}, u32[]{:S(2)}, u32[]{:S(2)}) collective-permute-start(bf16[2,320,128]{2,1,0:T(8,128)(2,1)S(1)} %get-tuple-element.237.refs_1_), channel_id=1, source_target_pairs={{0,8},{8,0},{16,24},{24,16},{1,9},{9,1},{17,25},{25,17},{2,10},{10... | collective-permute-start | bytes 491528 | tf_op jit(solution)/shard_map/ppermute | solution.py:406
  12.2 7.0 %collective-permute-start.4 = (bf16[2,320,128]{2,1,0:T(8,128)(2,1)S(1)}, bf16[2,320,128]{2,1,0:T(8,128)(2,1)S(1)}, u32[]{:S(2)}, u32[]{:S(2)}) collective-permute-start(bf16[2,320,128]{2,1,0:T(8,128)(2,1)S(1)} %get-tuple-element.126), channel_id=1, source_target_pairs={{0,16},{8,24},{16,0},{24,8},{1,17},{9,25},{17,1},{25,9},{2,18},{10... | collective-permute-start | bytes 491528 | tf_op jit(solution)/shard_map/ppermute | solution.py:406
  12.3 6.9 %collective-permute-start.5 = (bf16[2,320,128]{2,1,0:T(8,128)(2,1)S(1)}, bf16[2,320,128]{2,1,0:T(8,128)(2,1)S(1)}, u32[]{:S(2)}, u32[]{:S(2)}) collective-permute-start(bf16[2,320,128]{2,1,0:T(8,128)(2,1)S(1)} %get-tuple-element.127), channel_id=1, source_target_pairs={{0,8},{8,0},{16,24},{24,16},{1,9},{9,1},{17,25},{25,17},{2,10},{10... | collective-permute-start | bytes 491528 | tf_op jit(solution)/shard_map/ppermute | solution.py:406
  15.7 8.9 %copy-start = (bf16[384,256]{1,0:T(8,128)(2,1)S(1)}, bf16[384,256]{1,0:T(8,128)(2,1)}, u32[]{:S(2)}) copy-start(bf16[384,256]{1,0:T(8,128)(2,1)} %constant.2.clone.matrix_ref.refs_3_) | copy-start | bytes 589828
  15.8 8.9 %copy-start.1 = (f32[1,4,320,128]{3,2,1,0:T(8,128)S(1)}, f32[1,4,320,128]{3,2,1,0:T(8,128)}, u32[]{:S(2)}) copy-start(f32[1,4,320,128]{3,2,1,0:T(8,128)} %param.16) | copy-start | bytes 1966084
  15.8 7.4 %collective-permute-start.10 = (bf16[2,320,128]{2,1,0:T(8,128)(2,1)S(1)}, bf16[2,320,128]{2,1,0:T(8,128)(2,1)S(1)}, u32[]{:S(2)}, u32[]{:S(2)}) collective-permute-start(bf16[2,320,128]{2,1,0:T(8,128)(2,1)S(1)} %get-tuple-element.132), channel_id=1, source_target_pairs={{0,16},{8,24},{16,0},{24,8},{1,17},{9,25},{17,1},{25,9},{2,18},{10... | collective-permute-start | bytes 491528 | tf_op jit(solution)/shard_map/ppermute | solution.py:406
  19.7 14.6 %collective-permute-start.7 = (bf16[4,320,128]{2,1,0:T(8,128)(2,1)S(1)}, bf16[4,320,128]{2,1,0:T(8,128)(2,1)S(1)}, u32[]{:S(2)}, u32[]{:S(2)}) collective-permute-start(bf16[4,320,128]{2,1,0:T(8,128)(2,1)S(1)} %shard_map.116.den_ref.refs_6_), channel_id=1, source_target_pairs={{1,2},{2,1},{3,4},{4,3},{5,6},{6,5},{0,8},{7,15},{9,10},{10,9},{11... | collective-permute-start | bytes 983048 | tf_op jit(solution)/shard_map/ppermute | solution.py:423
  21.2 13.1 %collective-permute-start.6 = (bf16[4,320,128]{2,1,0:T(8,128)(2,1)S(1)}, bf16[4,320,128]{2,1,0:T(8,128)(2,1)S(1)}, u32[]{:S(2)}, u32[]{:S(2)}) collective-permute-start(bf16[4,320,128]{2,1,0:T(8,128)(2,1)S(1)} %shard_map.116.den_ref.refs_6_), channel_id=1, source_target_pairs={{0,1},{1,0},{2,3},{3,2},{4,5},{5,4},{6,7},{7,6},{8,9},{9,8},{10,11... | collective-permute-start | bytes 983048 | tf_op jit(solution)/shard_map/ppermute | solution.py:411
  21.4 13.5 %collective-permute-start.3 = (bf16[4,320,128]{2,1,0:T(8,128)(2,1)S(1)}, bf16[4,320,128]{2,1,0:T(8,128)(2,1)S(1)}, u32[]{:S(2)}, u32[]{:S(2)}) collective-permute-start(bf16[4,320,128]{2,1,0:T(8,128)(2,1)S(1)} %get-tuple-element.121), channel_id=1, source_target_pairs={{1,2},{2,1},{3,4},{4,3},{5,6},{6,5},{0,8},{7,15},{9,10},{10,9},{11... | collective-permute-start | bytes 983048 | tf_op jit(solution)/shard_map/ppermute | solution.py:423
  22.9 12.0 %collective-permute-start.2 = (bf16[4,320,128]{2,1,0:T(8,128)(2,1)S(1)}, bf16[4,320,128]{2,1,0:T(8,128)(2,1)S(1)}, u32[]{:S(2)}, u32[]{:S(2)}) collective-permute-start(bf16[4,320,128]{2,1,0:T(8,128)(2,1)S(1)} %get-tuple-element.121), channel_id=1, source_target_pairs={{0,1},{1,0},{2,3},{3,2},{4,5},{5,4},{6,7},{7,6},{8,9},{9,8},{10,11... | collective-permute-start | bytes 983048 | tf_op jit(solution)/shard_map/ppermute | solution.py:411
  23.1 10.7 %collective-permute-start.11 = (bf16[2,320,128]{2,1,0:T(8,128)(2,1)S(1)}, bf16[2,320,128]{2,1,0:T(8,128)(2,1)S(1)}, u32[]{:S(2)}, u32[]{:S(2)}) collective-permute-start(bf16[2,320,128]{2,1,0:T(8,128)(2,1)S(1)} %get-tuple-element.133), channel_id=1, source_target_pairs={{0,8},{8,0},{16,24},{24,16},{1,9},{9,1},{17,25},{25,17},{2,10},{10... | collective-permute-start | bytes 491528 | tf_op jit(solution)/shard_map/ppermute | solution.py:406
  35.9 5.5 %collective-permute-start.12 = (bf16[4,320,128]{2,1,0:T(8,128)(2,1)S(1)}, bf16[4,320,128]{2,1,0:T(8,128)(2,1)S(1)}, u32[]{:S(2)}, u32[]{:S(2)}) collective-permute-start(bf16[4,320,128]{2,1,0:T(8,128)(2,1)S(1)} %get-tuple-element.141), channel_id=1, source_target_pairs={{0,1},{1,0},{2,3},{3,2},{4,5},{5,4},{6,7},{7,6},{8,9},{9,8},{10,11... | collective-permute-start | bytes 983048 | tf_op jit(solution)/shard_map/ppermute | solution.py:411
  36.0 5.4 %collective-permute-start.14 = (bf16[4,160,128]{2,1,0:T(8,128)(2,1)S(1)}, bf16[4,160,128]{2,1,0:T(8,128)(2,1)S(1)}, u32[]{:S(2)}, u32[]{:S(2)}) collective-permute-start(bf16[4,160,128]{2,1,0:T(8,128)(2,1)S(1)} %get-tuple-element.144), channel_id=1, source_target_pairs={{1,2},{2,1},{3,4},{4,3},{5,6},{6,5},{0,8},{7,15},{9,10},{10,9},{11... | collective-permute-start | bytes 491528 | tf_op jit(solution)/shard_map/ppermute | solution.py:423
  37.6 5.6 %collective-permute-start.13 = (bf16[4,160,128]{2,1,0:T(8,128)(2,1)S(1)}, bf16[4,160,128]{2,1,0:T(8,128)(2,1)S(1)}, u32[]{:S(2)}, u32[]{:S(2)}) collective-permute-start(bf16[4,160,128]{2,1,0:T(8,128)(2,1)S(1)} %get-tuple-element.142), channel_id=1, source_target_pairs={{1,2},{2,1},{3,4},{4,3},{5,6},{6,5},{0,8},{7,15},{9,10},{10,9},{11... | collective-permute-start | bytes 491528 | tf_op jit(solution)/shard_map/ppermute | solution.py:423
  43.6 5.5 %collective-permute-start.15 = (bf16[4,320,128]{2,1,0:T(8,128)(2,1)S(1)}, bf16[4,320,128]{2,1,0:T(8,128)(2,1)S(1)}, u32[]{:S(2)}, u32[]{:S(2)}) collective-permute-start(bf16[4,320,128]{2,1,0:T(8,128)(2,1)S(1)} %get-tuple-element.150), channel_id=1, source_target_pairs={{0,1},{1,0},{2,3},{3,2},{4,5},{5,4},{6,7},{7,6},{8,9},{9,8},{10,11... | collective-permute-start | bytes 983048 | tf_op jit(solution)/shard_map/ppermute | solution.py:411
  43.8 5.3 %collective-permute-start.17 = (bf16[4,160,128]{2,1,0:T(8,128)(2,1)S(1)}, bf16[4,160,128]{2,1,0:T(8,128)(2,1)S(1)}, u32[]{:S(2)}, u32[]{:S(2)}) collective-permute-start(bf16[4,160,128]{2,1,0:T(8,128)(2,1)S(1)} %get-tuple-element.153), channel_id=1, source_target_pairs={{1,2},{2,1},{3,4},{4,3},{5,6},{6,5},{0,8},{7,15},{9,10},{10,9},{11... | collective-permute-start | bytes 491528 | tf_op jit(solution)/shard_map/ppermute | solution.py:423
  45.3 5.6 %collective-permute-start.16 = (bf16[4,160,128]{2,1,0:T(8,128)(2,1)S(1)}, bf16[4,160,128]{2,1,0:T(8,128)(2,1)S(1)}, u32[]{:S(2)}, u32[]{:S(2)}) collective-permute-start(bf16[4,160,128]{2,1,0:T(8,128)(2,1)S(1)} %get-tuple-element.151), channel_id=1, source_target_pairs={{1,2},{2,1},{3,4},{4,3},{5,6},{6,5},{0,8},{7,15},{9,10},{10,9},{11... | collective-permute-start | bytes 491528 | tf_op jit(solution)/shard_map/ppermute | solution.py:423
  50.9 3.2 %copy-start.4 = (f32[1,4,320,128]{3,2,1,0:T(8,128)S(1)}, f32[1,4,320,128]{3,2,1,0:T(8,128)}, u32[]{:S(2)}) copy-start(f32[1,4,320,128]{3,2,1,0:T(8,128)} %param.17) | copy-start | bytes 1966084
  51.4 2.2 %copy-start.7 = (s32[1,512]{1,0:T(1,128)S(1)}, s32[1,512]{1,0:T(1,128)}, u32[]{:S(2)}) copy-start(s32[1,512]{1,0:T(1,128)} %rec.1) | copy-start | bytes 6148
  51.4 5.5 %collective-permute-start.18 = (bf16[4,320,128]{2,1,0:T(8,128)(2,1)S(1)}, bf16[4,320,128]{2,1,0:T(8,128)(2,1)S(1)}, u32[]{:S(2)}, u32[]{:S(2)}) collective-permute-start(bf16[4,320,128]{2,1,0:T(8,128)(2,1)S(1)} %get-tuple-element.159), channel_id=1, source_target_pairs={{0,1},{1,0},{2,3},{3,2},{4,5},{5,4},{6,7},{7,6},{8,9},{9,8},{10,11... | collective-permute-start | bytes 983048 | tf_op jit(solution)/shard_map/ppermute | solution.py:411
  51.6 5.3 %collective-permute-start.20 = (bf16[4,160,128]{2,1,0:T(8,128)(2,1)S(1)}, bf16[4,160,128]{2,1,0:T(8,128)(2,1)S(1)}, u32[]{:S(2)}, u32[]{:S(2)}) collective-permute-start(bf16[4,160,128]{2,1,0:T(8,128)(2,1)S(1)} %get-tuple-element.162), channel_id=1, source_target_pairs={{1,2},{2,1},{3,4},{4,3},{5,6},{6,5},{0,8},{7,15},{9,10},{10,9},{11... | collective-permute-start | bytes 491528 | tf_op jit(solution)/shard_map/ppermute | solution.py:423
  53.1 5.6 %collective-permute-start.19 = (bf16[4,160,128]{2,1,0:T(8,128)(2,1)S(1)}, bf16[4,160,128]{2,1,0:T(8,128)(2,1)S(1)}, u32[]{:S(2)}, u32[]{:S(2)}) collective-permute-start(bf16[4,160,128]{2,1,0:T(8,128)(2,1)S(1)} %get-tuple-element.160), channel_id=1, source_target_pairs={{1,2},{2,1},{3,4},{4,3},{5,6},{6,5},{0,8},{7,15},{9,10},{10,9},{11... | collective-permute-start | bytes 491528 | tf_op jit(solution)/shard_map/ppermute | solution.py:423
  61.0 6.7 %collective-permute-start.21 = (bf16[4,320,128]{2,1,0:T(8,128)(2,1)S(1)}, bf16[4,320,128]{2,1,0:T(8,128)(2,1)S(1)}, u32[]{:S(2)}, u32[]{:S(2)}) collective-permute-start(bf16[4,320,128]{2,1,0:T(8,128)(2,1)S(1)} %get-tuple-element.168), channel_id=1, source_target_pairs={{0,1},{1,0},{2,3},{3,2},{4,5},{5,4},{6,7},{7,6},{8,9},{9,8},{10,11... | collective-permute-start | bytes 983048 | tf_op jit(solution)/shard_map/ppermute | solution.py:411
  61.1 6.6 %collective-permute-start.23 = (bf16[4,160,128]{2,1,0:T(8,128)(2,1)S(1)}, bf16[4,160,128]{2,1,0:T(8,128)(2,1)S(1)}, u32[]{:S(2)}, u32[]{:S(2)}) collective-permute-start(bf16[4,160,128]{2,1,0:T(8,128)(2,1)S(1)} %get-tuple-element.177), channel_id=1, source_target_pairs={{1,2},{2,1},{3,4},{4,3},{5,6},{6,5},{0,8},{7,15},{9,10},{10,9},{11... | collective-permute-start | bytes 491528 | tf_op jit(solution)/shard_map/ppermute | solution.py:423
  62.7 5.6 %collective-permute-start.22 = (bf16[4,160,128]{2,1,0:T(8,128)(2,1)S(1)}, bf16[4,160,128]{2,1,0:T(8,128)(2,1)S(1)}, u32[]{:S(2)}, u32[]{:S(2)}) collective-permute-start(bf16[4,160,128]{2,1,0:T(8,128)(2,1)S(1)} %get-tuple-element.169), channel_id=1, source_target_pairs={{1,2},{2,1},{3,4},{4,3},{5,6},{6,5},{0,8},{7,15},{9,10},{10,9},{11... | collective-permute-start | bytes 491528 | tf_op jit(solution)/shard_map/ppermute | solution.py:423
  66.2 1.6 %copy-start.2 = (f32[1,4,320,128]{3,2,1,0:T(8,128)S(1)}, f32[1,4,320,128]{3,2,1,0:T(8,128)}, u32[]{:S(2)}) copy-start(f32[1,4,320,128]{3,2,1,0:T(8,128)} %param.18) | copy-start | bytes 1966084
  68.8 5.5 %collective-permute-start.24 = (bf16[4,320,128]{2,1,0:T(8,128)(2,1)S(1)}, bf16[4,320,128]{2,1,0:T(8,128)(2,1)S(1)}, u32[]{:S(2)}, u32[]{:S(2)}) collective-permute-start(bf16[4,320,128]{2,1,0:T(8,128)(2,1)S(1)} %get-tuple-element.183), channel_id=1, source_target_pairs={{0,1},{1,0},{2,3},{3,2},{4,5},{5,4},{6,7},{7,6},{8,9},{9,8},{10,11... | collective-permute-start | bytes 983048 | tf_op jit(solution)/shard_map/ppermute | solution.py:411
  68.9 5.3 %collective-permute-start.26 = (bf16[4,160,128]{2,1,0:T(8,128)(2,1)S(1)}, bf16[4,160,128]{2,1,0:T(8,128)(2,1)S(1)}, u32[]{:S(2)}, u32[]{:S(2)}) collective-permute-start(bf16[4,160,128]{2,1,0:T(8,128)(2,1)S(1)} %get-tuple-element.194), channel_id=1, source_target_pairs={{1,2},{2,1},{3,4},{4,3},{5,6},{6,5},{0,8},{7,15},{9,10},{10,9},{11... | collective-permute-start | bytes 491528 | tf_op jit(solution)/shard_map/ppermute | solution.py:423
  70.4 5.6 %collective-permute-start.25 = (bf16[4,160,128]{2,1,0:T(8,128)(2,1)S(1)}, bf16[4,160,128]{2,1,0:T(8,128)(2,1)S(1)}, u32[]{:S(2)}, u32[]{:S(2)}) collective-permute-start(bf16[4,160,128]{2,1,0:T(8,128)(2,1)S(1)} %get-tuple-element.184), channel_id=1, source_target_pairs={{1,2},{2,1},{3,4},{4,3},{5,6},{6,5},{0,8},{7,15},{9,10},{10,9},{11... | collective-permute-start | bytes 491528 | tf_op jit(solution)/shard_map/ppermute | solution.py:423
  76.6 5.5 %collective-permute-start.27 = (bf16[4,320,128]{2,1,0:T(8,128)(2,1)S(1)}, bf16[4,320,128]{2,1,0:T(8,128)(2,1)S(1)}, u32[]{:S(2)}, u32[]{:S(2)}) collective-permute-start(bf16[4,320,128]{2,1,0:T(8,128)(2,1)S(1)} %get-tuple-element.200), channel_id=1, source_target_pairs={{0,1},{1,0},{2,3},{3,2},{4,5},{5,4},{6,7},{7,6},{8,9},{9,8},{10,11... | collective-permute-start | bytes 983048 | tf_op jit(solution)/shard_map/ppermute | solution.py:411
  76.8 5.3 %collective-permute-start.28 = (bf16[4,160,128]{2,1,0:T(8,128)(2,1)S(1)}, bf16[4,160,128]{2,1,0:T(8,128)(2,1)S(1)}, u32[]{:S(2)}, u32[]{:S(2)}) collective-permute-start(bf16[4,160,128]{2,1,0:T(8,128)(2,1)S(1)} %get-tuple-element.201), channel_id=1, source_target_pairs={{1,2},{2,1},{3,4},{4,3},{5,6},{6,5},{0,8},{7,15},{9,10},{10,9},{11... | collective-permute-start | bytes 491528 | tf_op jit(solution)/shard_map/ppermute | solution.py:423
  78.2 5.6 %collective-permute-start.31 = (bf16[4,160,128]{2,1,0:T(8,128)(2,1)S(1)}, bf16[4,160,128]{2,1,0:T(8,128)(2,1)S(1)}, u32[]{:S(2)}, u32[]{:S(2)}) collective-permute-start(bf16[4,160,128]{2,1,0:T(8,128)(2,1)S(1)} %get-tuple-element.217), channel_id=1, source_target_pairs={{1,2},{2,1},{3,4},{4,3},{5,6},{6,5},{0,8},{7,15},{9,10},{10,9},{11... | collective-permute-start | bytes 491528 | tf_op jit(solution)/shard_map/ppermute | solution.py:423
  84.4 10.4 %collective-permute-start.34 = (bf16[4,320,128]{2,1,0:T(8,128)(2,1)S(1)}, bf16[4,320,128]{2,1,0:T(8,128)(2,1)S(1)}, u32[]{:S(2)}, u32[]{:S(2)}) collective-permute-start(bf16[4,320,128]{2,1,0:T(8,128)(2,1)S(1)} %get-tuple-element.225), channel_id=1, source_target_pairs={{0,1},{1,0},{2,3},{3,2},{4,5},{5,4},{6,7},{7,6},{8,9},{9,8},{10,11... | collective-permute-start | bytes 983048 | tf_op jit(solution)/shard_map/ppermute | solution.py:411
  84.6 6.5 %collective-permute-start.32 = (bf16[4,160,128]{2,1,0:T(8,128)(2,1)S(1)}, bf16[4,160,128]{2,1,0:T(8,128)(2,1)S(1)}, u32[]{:S(2)}, u32[]{:S(2)}) collective-permute-start(bf16[4,160,128]{2,1,0:T(8,128)(2,1)S(1)} %get-tuple-element.221.refs_1_), channel_id=1, source_target_pairs={{0,16},{8,24},{16,0},{24,8},{1,17},{9,25},{17,1},{25,9},{2,18},{10... | collective-permute-start | bytes 491528 | tf_op jit(solution)/shard_map/ppermute | solution.py:406
  85.0 9.1 %collective-permute-start.29 = (bf16[4,160,128]{2,1,0:T(8,128)(2,1)S(1)}, bf16[4,160,128]{2,1,0:T(8,128)(2,1)S(1)}, u32[]{:S(2)}, u32[]{:S(2)}) collective-permute-start(bf16[4,160,128]{2,1,0:T(8,128)(2,1)S(1)} %get-tuple-element.214.refs_1_), channel_id=1, source_target_pairs={{0,8},{8,0},{16,24},{24,16},{1,9},{9,1},{17,25},{25,17},{2,10},{10... | collective-permute-start | bytes 491528 | tf_op jit(solution)/shard_map/ppermute | solution.py:406
  86.6 8.3 %collective-permute-start.35 = (bf16[4,160,128]{2,1,0:T(8,128)(2,1)S(1)}, bf16[4,160,128]{2,1,0:T(8,128)(2,1)S(1)}, u32[]{:S(2)}, u32[]{:S(2)}) collective-permute-start(bf16[4,160,128]{2,1,0:T(8,128)(2,1)S(1)} %get-tuple-element.226), channel_id=1, source_target_pairs={{1,2},{2,1},{3,4},{4,3},{5,6},{6,5},{0,8},{7,15},{9,10},{10,9},{11... | collective-permute-start | bytes 491528 | tf_op jit(solution)/shard_map/ppermute | solution.py:423
  87.0 8.9 %collective-permute-start.38 = (bf16[4,160,128]{2,1,0:T(8,128)(2,1)S(1)}, bf16[4,160,128]{2,1,0:T(8,128)(2,1)S(1)}, u32[]{:S(2)}, u32[]{:S(2)}) collective-permute-start(bf16[4,160,128]{2,1,0:T(8,128)(2,1)S(1)} %get-tuple-element.233), channel_id=1, source_target_pairs={{1,2},{2,1},{3,4},{4,3},{5,6},{6,5},{0,8},{7,15},{9,10},{10,9},{11... | collective-permute-start | bytes 491528 | tf_op jit(solution)/shard_map/ppermute | solution.py:423
  91.3 8.1 %collective-permute-start.33 = (bf16[4,160,128]{2,1,0:T(8,128)(2,1)S(1)}, bf16[4,160,128]{2,1,0:T(8,128)(2,1)S(1)}, u32[]{:S(2)}, u32[]{:S(2)}) collective-permute-start(bf16[4,160,128]{2,1,0:T(8,128)(2,1)S(1)} %get-tuple-element.223), channel_id=1, source_target_pairs={{0,8},{8,0},{16,24},{24,16},{1,9},{9,1},{17,25},{25,17},{2,10},{10... | collective-permute-start | bytes 491528 | tf_op jit(solution)/shard_map/ppermute | solution.py:406
  94.3 9.4 %collective-permute-start.30 = (bf16[4,160,128]{2,1,0:T(8,128)(2,1)S(1)}, bf16[4,160,128]{2,1,0:T(8,128)(2,1)S(1)}, u32[]{:S(2)}, u32[]{:S(2)}) collective-permute-start(bf16[4,160,128]{2,1,0:T(8,128)(2,1)S(1)} %get-tuple-element.216), channel_id=1, source_target_pairs={{0,16},{8,24},{16,0},{24,8},{1,17},{9,25},{17,1},{25,9},{2,18},{10... | collective-permute-start | bytes 491528 | tf_op jit(solution)/shard_map/ppermute | solution.py:406
  95.2 6.5 %collective-permute-start.36 = (bf16[4,160,128]{2,1,0:T(8,128)(2,1)S(1)}, bf16[4,160,128]{2,1,0:T(8,128)(2,1)S(1)}, u32[]{:S(2)}, u32[]{:S(2)}) collective-permute-start(bf16[4,160,128]{2,1,0:T(8,128)(2,1)S(1)} %shard_map.149.refs_1_), channel_id=1, source_target_pairs={{0,8},{8,0},{16,24},{24,16},{1,9},{9,1},{17,25},{25,17},{2,10},{10... | collective-permute-start | bytes 491528 | tf_op jit(solution)/shard_map/ppermute | solution.py:406
  96.3 8.3 %collective-permute-start.39 = (bf16[4,160,128]{2,1,0:T(8,128)(2,1)S(1)}, bf16[4,160,128]{2,1,0:T(8,128)(2,1)S(1)}, u32[]{:S(2)}, u32[]{:S(2)}) collective-permute-start(bf16[4,160,128]{2,1,0:T(8,128)(2,1)S(1)} %shard_map.151.refs_1_), channel_id=1, source_target_pairs={{0,16},{8,24},{16,0},{24,8},{1,17},{9,25},{17,1},{25,9},{2,18},{10... | collective-permute-start | bytes 491528 | tf_op jit(solution)/shard_map/ppermute | solution.py:406
  102.0 5.4 %collective-permute-start.37 = (bf16[4,160,128]{2,1,0:T(8,128)(2,1)S(1)}, bf16[4,160,128]{2,1,0:T(8,128)(2,1)S(1)}, u32[]{:S(2)}, u32[]{:S(2)}) collective-permute-start(bf16[4,160,128]{2,1,0:T(8,128)(2,1)S(1)} %get-tuple-element.232), channel_id=1, source_target_pairs={{0,16},{8,24},{16,0},{24,8},{1,17},{9,25},{17,1},{25,9},{2,18},{10... | collective-permute-start | bytes 491528 | tf_op jit(solution)/shard_map/ppermute | solution.py:406
  104.8 5.4 %collective-permute-start.40 = (bf16[4,160,128]{2,1,0:T(8,128)(2,1)S(1)}, bf16[4,160,128]{2,1,0:T(8,128)(2,1)S(1)}, u32[]{:S(2)}, u32[]{:S(2)}) collective-permute-start(bf16[4,160,128]{2,1,0:T(8,128)(2,1)S(1)} %get-tuple-element.235), channel_id=1, source_target_pairs={{0,8},{8,0},{16,24},{24,16},{1,9},{9,1},{17,25},{25,17},{2,10},{10... | collective-permute-start | bytes 491528 | tf_op jit(solution)/shard_map/ppermute | solution.py:406
  (2 other events, 1.4 us)

commit v5 on v4

--- a/solution.py
+++ b/solution.py
@@ -159,11 +159,10 @@
         values.astype(F32).astype(BF16), spots, (((1,), (1,)), ((), ())), preferred_element_type=F32
     ).astype(jnp.int32)
     count = jnp.sum(counted[:1], axis=1, keepdims=True).astype(jnp.int32)
-    code = (listed[2:3] * 256 + listed[1:2]) * (2 * depth) + listed[0:1]
-    list_ref[0:1, :] = jnp.where(number < count, code, depth)
+    list_ref[0:1, :] = listed[2:3] * 256 + listed[1:2]
     list_ref[1:2, :] = listed[3:4] + 256 * listed[4:5]
     list_ref[2:3, :] = jnp.broadcast_to(count, (1, total))
-    list_ref[3:4, :] = jnp.zeros((1, total), jnp.int32)
+    list_ref[3:4, :] = jnp.where(number < count, listed[0:1], depth)
 
 
 def add_receivers(n, field_ref, into_ref, list_ref, observed_ref):
@@ -175,9 +174,8 @@
     def _(c):
         rows, terms = [], []
         for k in range(UNROLL):
-            code = list_ref[0, c * UNROLL + k]
-            row = lax.div(code, 2 * depth)
-            spot = code - row * (2 * depth)
+            row = list_ref[0, c * UNROLL + k]
+            spot = list_ref[3, c * UNROLL + k]
             seen = observed_ref[n, list_ref[1, c * UNROLL + k]]
             rows.append(row)
             terms.append(jnp.where(lane == spot, field_ref[pl.ds(row, 1), :] - seen, 0.0))
@@ -185,12 +183,12 @@
             into_ref[pl.ds(row, 1), :] += term
 
 
-def receivers_kernel(*refs):
+def receivers_kernel(first, *refs):
     count = (len(refs) - 2) // 2
     fields, (list_ref, observed_ref), outs = refs[:count], refs[count : count + 2], refs[count + 2 :]
     for n, (field_ref, source_ref) in enumerate(zip(fields, outs)):
         source_ref[...] = jnp.zeros(source_ref.shape, F32)
-        add_receivers(n, field_ref, source_ref, list_ref, observed_ref)
+        add_receivers(first + n, field_ref, source_ref, list_ref, observed_ref)
 
 
 def first_adjoint_kernel(n, p_ref, q_ref, list_ref, observed_ref, a_ref, half_ref, *part_refs):
@@ -232,17 +230,15 @@
             s3_ref[l, pl.ds(at, 8), :] = z_ref[l, pl.ds(at, 8), pl.ds(depth, depth)]
 
 
-def slope_x_kernel(log_ref, on_ref, off_ref, vel_ref, s1_ref, scale_ref):
+def slope_x_kernel(part, log_ref, on_ref, off_ref, vel_ref, *refs):
+    s1_ref, scale_ref = refs[-2:]
     layers, width, _ = s1_ref.shape
     even, valid = where_am_i()
 
-    @pl.loop(0, width // 16)
-    def _(j):
-        at = pl.multiple_of(16 * j, 16)
-        rows = pl.ds(at, 16)
-        own = [log_ref[l, pl.ds(at + PAD, 16), :] for l in range(layers)]
+    def body(rows, off_rows, wide, send_rows):
+        own = [log_ref[l, wide, :] for l in range(layers)]
         on = [jnp.log(on_ref[l, rows, :].astype(F32)) for l in range(layers)]
-        off = [jnp.log(jnp.where(valid, off_ref[l, rows, :].astype(F32), 1.0)) for l in range(layers)]
+        off = [jnp.log(jnp.where(valid, off_ref[l, off_rows, :].astype(F32), 1.0)) for l in range(layers)]
         low = [jnp.where(even, b, a) for a, b in zip(on, off)]
         high = [jnp.where(even, a, b) for a, b in zip(on, off)]
         values = low[layers - 4 :] + own + high[:4]
@@ -250,6 +246,8 @@
             s1_ref[l, rows, :] = weighted(x_pairs(values, l))[1]
             v = vel_ref[l, rows, :].astype(F32)
             scale_ref[l, rows, :] = SPEED * v * v
+
+    part_rows(part, width, off_ref, body)
 
 
 def yz_terms(f_ref, s2_ref, s3_ref, z_ref, l, at):
@@ -457,8 +455,10 @@
         masked_sum(outs[way], 0, [(row == (me ^ o), ref) for o, ref in zip(offsets[way], held)])
 
 
-def gather_kernel(offsets, bits, route_ref, *refs):
+def gather_kernel(offsets, bits, parts, route_ref, *refs):
     me = lax.axis_index("shot")
+    part_refs = refs[len(refs) - parts :]
+    refs = refs[: len(refs) - parts]
     out_ref = refs[-1]
     count = (len(refs) - 1) // 2
     mine = route_ref[me]
@@ -468,9 +468,12 @@
         terms = [(mine == (me ^ o), ref) for o, ref in zip(offsets[way], near)]
         terms.append(((mine & bits[way]) != (me & bits[way]), far))
         masked_sum(out_ref, way * layers, terms)
-
-
-def fetch(tile, route, tie=lambda x: x):
+    for n, part_ref in enumerate(part_refs):
+        size = part_ref.shape[1]
+        part_ref[...] = out_ref[:, n * size : (n + 1) * size, :]
+
+
+def fetch(tile, route, parts=0, tie=lambda x: x):
     groups = route.shape[0]
     layers = tile.shape[0] // 2
     small = (layers, *tile.shape[1:])
@@ -494,11 +497,11 @@
         [(small, BF16)] * 2, [route, *held[0], *held[1]],
     )
     far = [swap_over("shot", groups, last[way], sends[way]) for way in range(2)]
-    (out,) = call(
-        lambda *refs: gather_kernel(offsets, last, *refs),
-        [(tile.shape, BF16)], [route, *held[0], far[0], *held[1], far[1]],
+    part_shape = (tile.shape[0], tile.shape[1] // PARTS, tile.shape[2])
+    return call(
+        lambda *refs: gather_kernel(offsets, last, parts, *refs),
+        [(tile.shape, BF16)] + [(part_shape, BF16)] * parts, [route, *held[0], far[0], *held[1], far[1]],
     )
-    return out
 
 
 def bucket_kernel(offsets, bit, route_ref, own_ref, got_ref, *outs):
@@ -563,13 +566,24 @@
         held, kept["p"] = lax.optimization_barrier((held, p))
         return held
 
-    den = fetch(den_model[0], route, tie)
-    vel = fetch(vel_model[0], route)
+    den, *den_parts = fetch(den_model[0], route, PARTS, tie)
+    (vel,) = fetch(vel_model[0], route)
     p, offs = kept["p"], [off] * PARTS
 
     before = p_before[0]
     log_den, s2, s3 = call(log_kernel, [padded, narrow, narrow], [den, matrix, before], scratch=z_scratch)
-    s1, scale = call(slope_x_kernel, [narrow, narrow], [log_den, paired(den), across(den), vel])
+    on_den = paired(den)
+    off_den = [across(den_part) for den_part in den_parts]
+    slopes = [()]
+    for k in parts:
+        ins = [log_den, on_den, off_den[k], vel]
+        slopes.append(
+            call(
+                lambda *refs, k=k: slope_x_kernel(k, *refs),
+                [narrow, narrow], [*ins, *slopes[-1]],
+                aliases={len(ins) + n: n for n in range(len(slopes[-1]))},
+            )
+        )
 
     stored, fields = [], []
     for step in range(ITERS):
@@ -579,6 +593,7 @@
         sending = step < ITERS - 1
         made, sends = (), []
         for k in parts:
+            s1, scale = slopes[1 + k] if step == 0 else slopes[-1]
             ins = [p, on, offs[k], part, s1, scale, before]
             outs = call(
                 lambda *refs, k=k, sending=sending: forward_x_kernel(k, sending, *refs),
@@ -603,10 +618,12 @@
     offs = [across(send) for send in sends]
     on = paired(a_half)
     a = a.reshape(padded[0])
-    sources = call(
-        receivers_kernel, [flat] * len(fields), [*fields, lists, seen],
-        [VM] * len(fields) + [SM, SM],
-    )
+    sources = []
+    for first, some in ((0, fields[:-1]), (len(fields) - 1, fields[-1:])):
+        sources += call(
+            lambda *refs, first=first: receivers_kernel(first, *refs),
+            [flat] * len(some), [*some, lists, seen], [VM] * len(some) + [SM, SM],
+        )
     sources = [source.reshape(padded[0]) for source in sources]
     before, current = q_before[0], q
     sums = ()

time: 111 us -> 112 us (level)
    ppermute x16, waiting for transfers between devices: 24.2 us -> 25.3 us  [swap_over(): return lax.ppermute(value, axis, [(i, i ^ bit) for i in range(count)])]
    pallas_call x40 -> x42, Pallas kernels: 29.8 us -> 30.4 us  [call(): pl.pallas_call(kernel, out_shape=outs, in_specs=list(specs or [VM] * len(...]
    ppermute x16 -> x17, starting transfers between devices: 17.4 us -> 17.9 us  [across(): return lax.ppermute(half, ('shot', 'sub'), pairs)]
    ppermute x16 -> x17, waiting for transfers between devices: 14.6 us -> 14.2 us  [across(): return lax.ppermute(half, ('shot', 'sub'), pairs)]
  transfers between devices with their start and end apart: 41 -> 42, of which waited for: 21 -> 22; matrix products, arithmetic and copies ran while one was open for 1% -> 1% of each run, Pallas kernels for 22% -> 22%
where the time goes in v5:
time: 112 us
  waiting for transfers between devices  39.6 us (35%)
  starting transfers between devices  37.6 us (34%)
  Pallas kernels  30.4 us (27%)
  other arithmetic  1.9 us (2%)
  local copies, waits for them, and re-layouts  1.37 us (1%)
  between operations  1.14 us (1%)
    pallas_call x42, Pallas kernels, call(): pl.pallas_call(kernel, out_shape=outs, in_specs=list(specs or [VM] * len(...  30.4 us
    ppermute x16, waiting for transfers between devices, swap_over(): return lax.ppermute(value, axis, [(i, i ^ bit) for i in range(count)])  25.3 us
    ppermute x16, starting transfers between devices, swap_over(): return lax.ppermute(value, axis, [(i, i ^ bit) for i in range(count)])  18.4 us
    ppermute x17, starting transfers between devices, across(): return lax.ppermute(half, ('shot', 'sub'), pairs)  17.9 us
    ppermute x17, waiting for transfers between devices, across(): return lax.ppermute(half, ('shot', 'sub'), pairs)  14.2 us
  transfers between devices with their start and end apart: 42, of which 22 were waited for; matrix products, arithmetic and copies ran while one was open for 1% of the time, Pallas kernels for 22%

profile of v5, /device:TPU:0, one launch (start us, length us, event | category | flops | bytes accessed | tf_op | source)
XLA Modules:
  0.0 111.9 jit_solution(7195150703342902405)
XLA Ops:
  1.8 3.1 %collective-permute-start.1 = (bf16[2,320,128]{2,1,0:T(8,128)(2,1)S(1)}, bf16[2,320,128]{2,1,0:T(8,128)(2,1)S(1)}, u32[]{:S(2)}, u32[]{:S(2)}) collective-permute-start(bf16[2,320,128]{2,1,0:T(8,128)(2,1)S(1)} %get-tuple-element.128.refs_3_.refs_4_), channel_id=1, source_target_pairs={{0,16},{8,24},{16,0},{24,8},{1,17},{9,25},{17,1},{25,9},{2,18},{10... | collective-permute-start | bytes 491528 | tf_op jit(solution)/shard_map/ppermute | solution.py:404
  4.8 1.5 %collective-permute-start = (bf16[2,320,128]{2,1,0:T(8,128)(2,1)S(1)}, bf16[2,320,128]{2,1,0:T(8,128)(2,1)S(1)}, u32[]{:S(2)}, u32[]{:S(2)}) collective-permute-start(bf16[2,320,128]{2,1,0:T(8,128)(2,1)S(1)} %get-tuple-element.126.refs_1_), channel_id=1, source_target_pairs={{0,8},{8,0},{16,24},{24,16},{1,9},{9,1},{17,25},{25,17},{2,10},{10... | collective-permute-start | bytes 491528 | tf_op jit(solution)/shard_map/ppermute | solution.py:404
  7.8 2.0 %collective-permute-done.1.refs_4_.refs_5_ = bf16[2,320,128]{2,1,0:T(8,128)(2,1)S(1)} collective-permute-done((bf16[2,320,128]{2,1,0:T(8,128)(2,1)S(1)}, bf16[2,320,128]{2,1,0:T(8,128)(2,1)S(1)}, u32[]{:S(2)}, u32[]{:S(2)}) %collective-permute-start.1) | collective-permute-done | bytes 163872 | tf_op jit(solution)/shard_map/ppermute | solution.py:404
  9.7 2.1 %collective-permute-done.refs_2_ = bf16[2,320,128]{2,1,0:T(8,128)(2,1)S(1)} collective-permute-done((bf16[2,320,128]{2,1,0:T(8,128)(2,1)S(1)}, bf16[2,320,128]{2,1,0:T(8,128)(2,1)S(1)}, u32[]{:S(2)}, u32[]{:S(2)}) %collective-permute-start) | collective-permute-done | bytes 163872 | tf_op jit(solution)/shard_map/ppermute | solution.py:404
  12.3 2.0 %collective-permute-start.5 = (bf16[2,320,128]{2,1,0:T(8,128)(2,1)S(1)}, bf16[2,320,128]{2,1,0:T(8,128)(2,1)S(1)}, u32[]{:S(2)}, u32[]{:S(2)}) collective-permute-start(bf16[2,320,128]{2,1,0:T(8,128)(2,1)S(1)} %get-tuple-element.131), channel_id=1, source_target_pairs={{0,8},{8,0},{16,24},{24,16},{1,9},{9,1},{17,25},{25,17},{2,10},{10... | collective-permute-start | bytes 491528 | tf_op jit(solution)/shard_map/ppermute | solution.py:404
  16.3 3.0 %collective-permute-done.4.refs_3_ = bf16[2,320,128]{2,1,0:T(8,128)(2,1)S(1)} collective-permute-done((bf16[2,320,128]{2,1,0:T(8,128)(2,1)S(1)}, bf16[2,320,128]{2,1,0:T(8,128)(2,1)S(1)}, u32[]{:S(2)}, u32[]{:S(2)}) %collective-permute-start.4) | collective-permute-done | bytes 163872 | tf_op jit(solution)/shard_map/ppermute | solution.py:404
  19.8 1.6 %collective-permute-start.3 = (bf16[4,320,128]{2,1,0:T(8,128)(2,1)S(1)}, bf16[4,320,128]{2,1,0:T(8,128)(2,1)S(1)}, u32[]{:S(2)}, u32[]{:S(2)}) collective-permute-start(bf16[4,320,128]{2,1,0:T(8,128)(2,1)S(1)} %get-tuple-element.125), channel_id=1, source_target_pairs={{1,2},{2,1},{3,4},{4,3},{5,6},{6,5},{0,8},{7,15},{9,10},{10,9},{11... | collective-permute-start | bytes 983048 | tf_op jit(solution)/shard_map/ppermute | solution.py:421
  21.5 1.5 %collective-permute-start.11 = (bf16[2,320,128]{2,1,0:T(8,128)(2,1)S(1)}, bf16[2,320,128]{2,1,0:T(8,128)(2,1)S(1)}, u32[]{:S(2)}, u32[]{:S(2)}) collective-permute-start(bf16[2,320,128]{2,1,0:T(8,128)(2,1)S(1)} %get-tuple-element.139), channel_id=1, source_target_pairs={{0,8},{8,0},{16,24},{24,16},{1,9},{9,1},{17,25},{25,17},{2,10},{10... | collective-permute-start | bytes 491528 | tf_op jit(solution)/shard_map/ppermute | solution.py:404
  23.6 6.9 %collective-permute-done.11.refs_6_ = bf16[2,320,128]{2,1,0:T(8,128)(2,1)S(1)} collective-permute-done((bf16[2,320,128]{2,1,0:T(8,128)(2,1)S(1)}, bf16[2,320,128]{2,1,0:T(8,128)(2,1)S(1)}, u32[]{:S(2)}, u32[]{:S(2)}) %collective-permute-start.11) | collective-permute-done | bytes 163872 | tf_op jit(solution)/shard_map/ppermute | solution.py:404
  30.4 1.5 %collective-permute-start.7 = (bf16[4,160,128]{2,1,0:T(8,128)(2,1)S(1)}, bf16[4,160,128]{2,1,0:T(8,128)(2,1)S(1)}, u32[]{:S(2)}, u32[]{:S(2)}) collective-permute-start(bf16[4,160,128]{2,1,0:T(8,128)(2,1)S(1)} %get-tuple-element.137), channel_id=1, source_target_pairs={{1,2},{2,1},{3,4},{4,3},{5,6},{6,5},{0,8},{7,15},{9,10},{10,9},{11... | collective-permute-start | bytes 491528 | tf_op jit(solution)/shard_map/ppermute | solution.py:421
  31.9 1.3 %shard_map.117 = (f32[4,336,128]{2,1,0:T(8,128)S(1)}, f32[4,320,128]{2,1,0:T(8,128)S(1)}, f32[4,320,128]{2,1,0:T(8,128)S(1)}) custom-call(bf16[4,320,128]{2,1,0:T(8,128)(2,1)S(1)} %get-tuple-element.132.den_ref.refs_6_, bf16[384,256]{1,0:T(8,128)(2,1)S(1)} %copy-done, f32[4,320,128]{2,1,0:T(8,128)S(1)} %bitcast.35), custom_call_target="tpu_custom_call" | custom-call | bytes 3178496 | tf_op jit(solution)/shard_map/pallas_call | solution.py:29
  33.3 1.4 %shard_map.118 = (f32[4,320,128]{2,1,0:T(8,128)S(1)}, f32[4,320,128]{2,1,0:T(8,128)S(1)}, f32[4,320,128]{2,1,0:T(8,128)S(1)}) custom-call(f32[4,336,128]{2,1,0:T(8,128)S(1)} %get-tuple-element.124.f_ref.refs_0_.refs_6_, f32[4,320,128]{2,1,0:T(8,128)S(1)} %get-tuple-element.133.s2_ref.refs_1_, f32[4,320,128]{2,1,0:T(8,128)S(1)} %get-tuple-element.134.s3_ref.refs_2_, ...), custom_call_target="tpu_custom_call" | custom-call | bytes 4161536 | tf_op jit(solution)/shard_map/pallas_call | solution.py:29
  36.9 1.3 %collective-permute-start.15 = (bf16[4,160,128]{2,1,0:T(8,128)(2,1)S(1)}, bf16[4,160,128]{2,1,0:T(8,128)(2,1)S(1)}, u32[]{:S(2)}, u32[]{:S(2)}) collective-permute-start(bf16[4,160,128]{2,1,0:T(8,128)(2,1)S(1)} %get-tuple-element.153), channel_id=1, source_target_pairs={{1,2},{2,1},{3,4},{4,3},{5,6},{6,5},{0,8},{7,15},{9,10},{10,9},{11... | collective-permute-start | bytes 491528 | tf_op jit(solution)/shard_map/ppermute | solution.py:421
  39.0 1.4 %shard_map.125 = (f32[4,320,128]{2,1,0:T(8,128)S(1)}, f32[4,320,128]{2,1,0:T(8,128)S(1)}, f32[4,320,128]{2,1,0:T(8,128)S(1)}) custom-call(f32[4,336,128]{2,1,0:T(8,128)S(1)} %get-tuple-element.149.f_ref.refs_0_.refs_6_, f32[4,320,128]{2,1,0:T(8,128)S(1)} %get-tuple-element.133.s2_ref.refs_1_, f32[4,320,128]{2,1,0:T(8,128)S(1)} %get-tuple-element.134.s3_ref.refs_2_, ...), custom_call_target="tpu_custom_call" | custom-call | bytes 4161536 | tf_op jit(solution)/shard_map/pallas_call | solution.py:29
  40.5 1.9 %collective-permute-done.15.refs_2_ = bf16[4,160,128]{2,1,0:T(8,128)(2,1)S(1)} collective-permute-done((bf16[4,160,128]{2,1,0:T(8,128)(2,1)S(1)}, bf16[4,160,128]{2,1,0:T(8,128)(2,1)S(1)}, u32[]{:S(2)}, u32[]{:S(2)}) %collective-permute-start.15) | collective-permute-done | bytes 163872 | tf_op jit(solution)/shard_map/ppermute | solution.py:421
  42.8 1.3 %collective-permute-done.14.refs_2_ = bf16[4,160,128]{2,1,0:T(8,128)(2,1)S(1)} collective-permute-done((bf16[4,160,128]{2,1,0:T(8,128)(2,1)S(1)}, bf16[4,160,128]{2,1,0:T(8,128)(2,1)S(1)}, u32[]{:S(2)}, u32[]{:S(2)}) %collective-permute-start.14) | collective-permute-done | bytes 163872 | tf_op jit(solution)/shard_map/ppermute | solution.py:421
  44.7 1.2 %collective-permute-start.18 = (bf16[4,160,128]{2,1,0:T(8,128)(2,1)S(1)}, bf16[4,160,128]{2,1,0:T(8,128)(2,1)S(1)}, u32[]{:S(2)}, u32[]{:S(2)}) collective-permute-start(bf16[4,160,128]{2,1,0:T(8,128)(2,1)S(1)} %get-tuple-element.162), channel_id=1, source_target_pairs={{1,2},{2,1},{3,4},{4,3},{5,6},{6,5},{0,8},{7,15},{9,10},{10,9},{11... | collective-permute-start | bytes 491528 | tf_op jit(solution)/shard_map/ppermute | solution.py:421
  46.8 1.4 %shard_map.128 = (f32[4,320,128]{2,1,0:T(8,128)S(1)}, f32[4,320,128]{2,1,0:T(8,128)S(1)}, f32[4,320,128]{2,1,0:T(8,128)S(1)}) custom-call(f32[4,336,128]{2,1,0:T(8,128)S(1)} %get-tuple-element.158.f_ref.refs_0_.refs_6_, f32[4,320,128]{2,1,0:T(8,128)S(1)} %get-tuple-element.133.s2_ref.refs_1_, f32[4,320,128]{2,1,0:T(8,128)S(1)} %get-tuple-element.134.s3_ref.refs_2_, ...), custom_call_target="tpu_custom_call" | custom-call | bytes 4161536 | tf_op jit(solution)/shard_map/pallas_call | solution.py:29
  48.2 1.9 %collective-permute-done.18.refs_2_ = bf16[4,160,128]{2,1,0:T(8,128)(2,1)S(1)} collective-permute-done((bf16[4,160,128]{2,1,0:T(8,128)(2,1)S(1)}, bf16[4,160,128]{2,1,0:T(8,128)(2,1)S(1)}, u32[]{:S(2)}, u32[]{:S(2)}) %collective-permute-start.18) | collective-permute-done | bytes 163872 | tf_op jit(solution)/shard_map/ppermute | solution.py:421
  50.6 1.3 %collective-permute-done.17.refs_2_ = bf16[4,160,128]{2,1,0:T(8,128)(2,1)S(1)} collective-permute-done((bf16[4,160,128]{2,1,0:T(8,128)(2,1)S(1)}, bf16[4,160,128]{2,1,0:T(8,128)(2,1)S(1)}, u32[]{:S(2)}, u32[]{:S(2)}) %collective-permute-start.17) | collective-permute-done | bytes 163872 | tf_op jit(solution)/shard_map/ppermute | solution.py:421
  52.5 1.2 %collective-permute-start.21 = (bf16[4,160,128]{2,1,0:T(8,128)(2,1)S(1)}, bf16[4,160,128]{2,1,0:T(8,128)(2,1)S(1)}, u32[]{:S(2)}, u32[]{:S(2)}) collective-permute-start(bf16[4,160,128]{2,1,0:T(8,128)(2,1)S(1)} %get-tuple-element.171), channel_id=1, source_target_pairs={{1,2},{2,1},{3,4},{4,3},{5,6},{6,5},{0,8},{7,15},{9,10},{10,9},{11... | collective-permute-start | bytes 491528 | tf_op jit(solution)/shard_map/ppermute | solution.py:421
  55.1 1.4 %shard_map.131 = (f32[4,320,128]{2,1,0:T(8,128)S(1)}, f32[4,320,128]{2,1,0:T(8,128)S(1)}, f32[4,320,128]{2,1,0:T(8,128)S(1)}) custom-call(f32[4,336,128]{2,1,0:T(8,128)S(1)} %get-tuple-element.167.f_ref.refs_0_, f32[4,320,128]{2,1,0:T(8,128)S(1)} %get-tuple-element.133.s2_ref.refs_1_, f32[4,320,128]{2,1,0:T(8,128)S(1)} %get-tuple-element.134.s3_ref.refs_2_, ...), custom_call_target="tpu_custom_call" | custom-call | bytes 4161536 | tf_op jit(solution)/shard_map/pallas_call | solution.py:29
  56.6 1.3 %collective-permute-done.21.refs_2_ = bf16[4,160,128]{2,1,0:T(8,128)(2,1)S(1)} collective-permute-done((bf16[4,160,128]{2,1,0:T(8,128)(2,1)S(1)}, bf16[4,160,128]{2,1,0:T(8,128)(2,1)S(1)}, u32[]{:S(2)}, u32[]{:S(2)}) %collective-permute-start.21) | collective-permute-done | bytes 163872 | tf_op jit(solution)/shard_map/ppermute | solution.py:421
  58.3 1.3 %collective-permute-done.20.refs_2_ = bf16[4,160,128]{2,1,0:T(8,128)(2,1)S(1)} collective-permute-done((bf16[4,160,128]{2,1,0:T(8,128)(2,1)S(1)}, bf16[4,160,128]{2,1,0:T(8,128)(2,1)S(1)}, u32[]{:S(2)}, u32[]{:S(2)}) %collective-permute-start.20) | collective-permute-done | bytes 163872 | tf_op jit(solution)/shard_map/ppermute | solution.py:421
  60.3 1.6 %shard_map.136 = (f32[1344,128]{1,0:T(8,128)S(1)}, bf16[4,320,128]{2,1,0:T(8,128)(2,1)S(1)}, bf16[4,160,128]{2,1,0:T(8,128)(2,1)S(1)}, bf16[4,160,128]{2,1,0:T(8,128)(2,1)S(1)}) custom-call(f32[1344,128]{1,0:T(8,128)S(1)} %bitcast.40, f32[1344,128]{1,0:T(8,128)S(1)} %bitcast.29, s32[4,512]{1,0:T(4,128)S(1)} %shard_map.135.refs_2_.refs_1_, f32[4,512]{1,0:T(4,128)S(1)} %bitcast.47), custom_call_target="tpu_custom_call" | custom-call | bytes 2736128 | tf_op jit(solution)/shard_map/pallas_call | solution.py:29
  61.9 1.3 %collective-permute-start.24 = (bf16[4,160,128]{2,1,0:T(8,128)(2,1)S(1)}, bf16[4,160,128]{2,1,0:T(8,128)(2,1)S(1)}, u32[]{:S(2)}, u32[]{:S(2)}) collective-permute-start(bf16[4,160,128]{2,1,0:T(8,128)(2,1)S(1)} %get-tuple-element.185), channel_id=1, source_target_pairs={{1,2},{2,1},{3,4},{4,3},{5,6},{6,5},{0,8},{7,15},{9,10},{10,9},{11... | collective-permute-start | bytes 491528 | tf_op jit(solution)/shard_map/ppermute | solution.py:421
  64.0 1.4 %shard_map.138 = f32[1344,128]{1,0:T(8,128)S(1)} custom-call(f32[1344,128]{1,0:T(8,128)S(1)} %bitcast.28, s32[4,512]{1,0:T(4,128)S(1)} %shard_map.135.refs_2_.refs_1_, f32[4,512]{1,0:T(4,128)S(1)} %bitcast.48), custom_call_target="tpu_custom_call" | custom-call | bytes 1392640 | tf_op jit(solution)/shard_map/pallas_call | solution.py:29
  65.5 1.5 %shard_map.137 = (f32[4,320,128]{2,1,0:T(8,128)S(1)}, f32[4,320,128]{2,1,0:T(8,128)S(1)}, f32[4,320,128]{2,1,0:T(8,128)S(1)}) custom-call(f32[4,336,128]{2,1,0:T(8,128)S(1)} %bitcast.32, f32[4,320,128]{2,1,0:T(8,128)S(1)} %get-tuple-element.133.s2_ref.refs_1_, f32[4,320,128]{2,1,0:T(8,128)S(1)} %get-tuple-element.134.s3_ref.refs_2_, ...), custom_call_target="tpu_custom_call" | custom-call | bytes 6127616 | tf_op jit(solution)/shard_map/pallas_call | solution.py:29
  67.9 1.2 %collective-permute-done.23.refs_2_ = bf16[4,160,128]{2,1,0:T(8,128)(2,1)S(1)} collective-permute-done((bf16[4,160,128]{2,1,0:T(8,128)(2,1)S(1)}, bf16[4,160,128]{2,1,0:T(8,128)(2,1)S(1)}, u32[]{:S(2)}, u32[]{:S(2)}) %collective-permute-start.23) | collective-permute-done | bytes 163872 | tf_op jit(solution)/shard_map/ppermute | solution.py:421
  69.8 1.2 %collective-permute-start.27 = (bf16[4,160,128]{2,1,0:T(8,128)(2,1)S(1)}, bf16[4,160,128]{2,1,0:T(8,128)(2,1)S(1)}, u32[]{:S(2)}, u32[]{:S(2)}) collective-permute-start(bf16[4,160,128]{2,1,0:T(8,128)(2,1)S(1)} %get-tuple-element.202), channel_id=1, source_target_pairs={{1,2},{2,1},{3,4},{4,3},{5,6},{6,5},{0,8},{7,15},{9,10},{10,9},{11... | collective-permute-start | bytes 491528 | tf_op jit(solution)/shard_map/ppermute | solution.py:421
  71.8 2.1 %shard_map.142 = (f32[1344,128]{1,0:T(8,128)S(1)}, f32[1344,128]{1,0:T(8,128)S(1)}) custom-call(f32[1344,128]{1,0:T(8,128)S(1)} %bitcast.26, f32[1344,128]{1,0:T(8,128)S(1)} %bitcast.27, s32[4,512]{1,0:T(4,128)S(1)} %shard_map.135.refs_2_.refs_1_, f32[4,512]{1,0:T(4,128)S(1)} %bitcast.49), custom_call_target="tpu_custom_call" | custom-call | bytes 2768896 | tf_op jit(solution)/shard_map/pallas_call | solution.py:29
  73.9 1.6 %shard_map.141 = (f32[4,320,128]{2,1,0:T(8,128)S(1)}, f32[4,320,128]{2,1,0:T(8,128)S(1)}, f32[4,320,128]{2,1,0:T(8,128)S(1)}) custom-call(f32[4,336,128]{2,1,0:T(8,128)S(1)} %get-tuple-element.190.refs_0_, f32[4,320,128]{2,1,0:T(8,128)S(1)} %get-tuple-element.133.s2_ref.refs_1_, f32[4,320,128]{2,1,0:T(8,128)S(1)} %get-tuple-element.134.s3_ref.refs_2_, ...), custom_call_target="tpu_custom_call" | custom-call | bytes 7438336 | tf_op jit(solution)/shard_map/pallas_call | solution.py:29
  77.6 1.2 %collective-permute-start.29 = (bf16[4,160,128]{2,1,0:T(8,128)(2,1)S(1)}, bf16[4,160,128]{2,1,0:T(8,128)(2,1)S(1)}, u32[]{:S(2)}, u32[]{:S(2)}) collective-permute-start(bf16[4,160,128]{2,1,0:T(8,128)(2,1)S(1)} %get-tuple-element.209), channel_id=1, source_target_pairs={{1,2},{2,1},{3,4},{4,3},{5,6},{6,5},{0,8},{7,15},{9,10},{10,9},{11... | collective-permute-start | bytes 491528 | tf_op jit(solution)/shard_map/ppermute | solution.py:421
  79.6 1.6 %shard_map.145 = (f32[4,320,128]{2,1,0:T(8,128)S(1)}, f32[4,320,128]{2,1,0:T(8,128)S(1)}, f32[4,320,128]{2,1,0:T(8,128)S(1)}) custom-call(f32[4,336,128]{2,1,0:T(8,128)S(1)} %get-tuple-element.207.refs_0_, f32[4,320,128]{2,1,0:T(8,128)S(1)} %get-tuple-element.133.s2_ref.refs_1_, f32[4,320,128]{2,1,0:T(8,128)S(1)} %get-tuple-element.134.s3_ref.refs_2_, ...), custom_call_target="tpu_custom_call" | custom-call | bytes 7438336 | tf_op jit(solution)/shard_map/pallas_call | solution.py:29
  81.2 1.7 %collective-permute-done.29.refs_2_ = bf16[4,160,128]{2,1,0:T(8,128)(2,1)S(1)} collective-permute-done((bf16[4,160,128]{2,1,0:T(8,128)(2,1)S(1)}, bf16[4,160,128]{2,1,0:T(8,128)(2,1)S(1)}, u32[]{:S(2)}, u32[]{:S(2)}) %collective-permute-start.29) | collective-permute-done | bytes 163872 | tf_op jit(solution)/shard_map/ppermute | solution.py:421
  83.5 1.1 %collective-permute-done.32.refs_2_ = bf16[4,160,128]{2,1,0:T(8,128)(2,1)S(1)} collective-permute-done((bf16[4,160,128]{2,1,0:T(8,128)(2,1)S(1)}, bf16[4,160,128]{2,1,0:T(8,128)(2,1)S(1)}, u32[]{:S(2)}, u32[]{:S(2)}) %collective-permute-start.32) | collective-permute-done | bytes 163872 | tf_op jit(solution)/shard_map/ppermute | solution.py:421
  86.0 1.1 collective-permute-start.30
  88.0 1.1 collective-permute-start.39
  89.1 2.8 %collective-permute-done.33.refs_2_ = bf16[4,160,128]{2,1,0:T(8,128)(2,1)S(1)} collective-permute-done((bf16[4,160,128]{2,1,0:T(8,128)(2,1)S(1)}, bf16[4,160,128]{2,1,0:T(8,128)(2,1)S(1)}, u32[]{:S(2)}, u32[]{:S(2)}) %collective-permute-start.33) | collective-permute-done | bytes 163872 | tf_op jit(solution)/shard_map/ppermute | solution.py:404
  92.1 1.2 %collective-permute-start.34 = (bf16[4,160,128]{2,1,0:T(8,128)(2,1)S(1)}, bf16[4,160,128]{2,1,0:T(8,128)(2,1)S(1)}, u32[]{:S(2)}, u32[]{:S(2)}) collective-permute-start(bf16[4,160,128]{2,1,0:T(8,128)(2,1)S(1)} %get-tuple-element.231), channel_id=1, source_target_pairs={{0,8},{8,0},{16,24},{24,16},{1,9},{9,1},{17,25},{25,17},{2,10},{10... | collective-permute-start | bytes 491528 | tf_op jit(solution)/shard_map/ppermute | solution.py:404
  93.4 1.2 %shard_map.150.refs_4_ = f32[4,320,128]{2,1,0:T(8,128)S(1)} custom-call(f32[4,336,128]{2,1,0:T(8,128)S(1)} %get-tuple-element.232.f_ref.refs_0_, bf16[384,256]{1,0:T(8,128)(2,1)S(1)} %copy-done, f32[4,320,128]{2,1,0:T(8,128)S(1)} %get-tuple-element.236.fdy_ref, f32[4,320,128]{2,1,0:T(8,128)S(1)} %get-tuple-element.237.fdz_ref, ...), custom_call_target="tpu_custom_call" | custom-call | bytes 3506176 | tf_op jit(solution)/shard_map/pallas_call | solution.py:29
  97.5 1.9 %collective-permute-start.40 = (bf16[4,160,128]{2,1,0:T(8,128)(2,1)S(1)}, bf16[4,160,128]{2,1,0:T(8,128)(2,1)S(1)}, u32[]{:S(2)}, u32[]{:S(2)}) collective-permute-start(bf16[4,160,128]{2,1,0:T(8,128)(2,1)S(1)} %shard_map.153.refs_1_), channel_id=1, source_target_pairs={{0,16},{8,24},{16,0},{24,8},{1,17},{9,25},{17,1},{25,9},{2,18},{10... | collective-permute-start | bytes 491528 | tf_op jit(solution)/shard_map/ppermute | solution.py:404
  99.4 1.3 %collective-permute-done.34 = bf16[4,160,128]{2,1,0:T(8,128)(2,1)S(1)} collective-permute-done((bf16[4,160,128]{2,1,0:T(8,128)(2,1)S(1)}, bf16[4,160,128]{2,1,0:T(8,128)(2,1)S(1)}, u32[]{:S(2)}, u32[]{:S(2)}) %collective-permute-start.34) | collective-permute-done | bytes 163872 | tf_op jit(solution)/shard_map/ppermute | solution.py:404
  100.7 2.1 %collective-permute-done.37.refs_2_ = bf16[4,160,128]{2,1,0:T(8,128)(2,1)S(1)} collective-permute-done((bf16[4,160,128]{2,1,0:T(8,128)(2,1)S(1)}, bf16[4,160,128]{2,1,0:T(8,128)(2,1)S(1)}, u32[]{:S(2)}, u32[]{:S(2)}) %collective-permute-start.37) | collective-permute-done | bytes 163872 | tf_op jit(solution)/shard_map/ppermute | solution.py:404
  103.0 1.5 %collective-permute-start.38 = (bf16[4,160,128]{2,1,0:T(8,128)(2,1)S(1)}, bf16[4,160,128]{2,1,0:T(8,128)(2,1)S(1)}, u32[]{:S(2)}, u32[]{:S(2)}) collective-permute-start(bf16[4,160,128]{2,1,0:T(8,128)(2,1)S(1)} %get-tuple-element.240), channel_id=1, source_target_pairs={{0,16},{8,24},{16,0},{24,8},{1,17},{9,25},{17,1},{25,9},{2,18},{10... | collective-permute-start | bytes 491528 | tf_op jit(solution)/shard_map/ppermute | solution.py:404
  105.6 1.2 %collective-permute-start.41 = (bf16[4,160,128]{2,1,0:T(8,128)(2,1)S(1)}, bf16[4,160,128]{2,1,0:T(8,128)(2,1)S(1)}, u32[]{:S(2)}, u32[]{:S(2)}) collective-permute-start(bf16[4,160,128]{2,1,0:T(8,128)(2,1)S(1)} %get-tuple-element.243), channel_id=1, source_target_pairs={{0,8},{8,0},{16,24},{24,16},{1,9},{9,1},{17,25},{25,17},{2,10},{10... | collective-permute-start | bytes 491528 | tf_op jit(solution)/shard_map/ppermute | solution.py:404
  106.9 1.5 %collective-permute-done.38 = bf16[4,160,128]{2,1,0:T(8,128)(2,1)S(1)} collective-permute-done((bf16[4,160,128]{2,1,0:T(8,128)(2,1)S(1)}, bf16[4,160,128]{2,1,0:T(8,128)(2,1)S(1)}, u32[]{:S(2)}, u32[]{:S(2)}) %collective-permute-start.38) | collective-permute-done | bytes 163872 | tf_op jit(solution)/shard_map/ppermute | solution.py:404
  108.4 2.6 %collective-permute-done.41 = bf16[4,160,128]{2,1,0:T(8,128)(2,1)S(1)} collective-permute-done((bf16[4,160,128]{2,1,0:T(8,128)(2,1)S(1)}, bf16[4,160,128]{2,1,0:T(8,128)(2,1)S(1)}, u32[]{:S(2)}, u32[]{:S(2)}) %collective-permute-start.41) | collective-permute-done | bytes 163872 | tf_op jit(solution)/shard_map/ppermute | solution.py:404
  (104 shorter events, 29.3 us)
Async XLA Ops:
  0.6 5.7 %copy-start.8 = (bf16[1,4,320,128]{3,2,1,0:T(8,128)(2,1)S(1)}, bf16[1,4,320,128]{3,2,1,0:T(8,128)(2,1)}, u32[]{:S(2)}) copy-start(bf16[1,4,320,128]{3,2,1,0:T(8,128)(2,1)} %param.10) | copy-start | bytes 983044
  0.6 7.0 %copy-start.3 = (f32[1,4,320,128]{3,2,1,0:T(8,128)S(1)}, f32[1,4,320,128]{3,2,1,0:T(8,128)}, u32[]{:S(2)}) copy-start(f32[1,4,320,128]{3,2,1,0:T(8,128)} %param.15) | copy-start | bytes 1966084
  1.8 8.0 %collective-permute-start.1 = (bf16[2,320,128]{2,1,0:T(8,128)(2,1)S(1)}, bf16[2,320,128]{2,1,0:T(8,128)(2,1)S(1)}, u32[]{:S(2)}, u32[]{:S(2)}) collective-permute-start(bf16[2,320,128]{2,1,0:T(8,128)(2,1)S(1)} %get-tuple-element.128.refs_3_.refs_4_), channel_id=1, source_target_pairs={{0,16},{8,24},{16,0},{24,8},{1,17},{9,25},{17,1},{25,9},{2,18},{10... | collective-permute-start | bytes 491528 | tf_op jit(solution)/shard_map/ppermute | solution.py:404
  4.8 7.1 %collective-permute-start = (bf16[2,320,128]{2,1,0:T(8,128)(2,1)S(1)}, bf16[2,320,128]{2,1,0:T(8,128)(2,1)S(1)}, u32[]{:S(2)}, u32[]{:S(2)}) collective-permute-start(bf16[2,320,128]{2,1,0:T(8,128)(2,1)S(1)} %get-tuple-element.126.refs_1_), channel_id=1, source_target_pairs={{0,8},{8,0},{16,24},{24,16},{1,9},{9,1},{17,25},{25,17},{2,10},{10... | collective-permute-start | bytes 491528 | tf_op jit(solution)/shard_map/ppermute | solution.py:404
  6.3 8.0 %collective-permute-start.9 = (bf16[2,320,128]{2,1,0:T(8,128)(2,1)S(1)}, bf16[2,320,128]{2,1,0:T(8,128)(2,1)S(1)}, u32[]{:S(2)}, u32[]{:S(2)}) collective-permute-start(bf16[2,320,128]{2,1,0:T(8,128)(2,1)S(1)} %get-tuple-element.244.refs_3_.refs_4_), channel_id=1, source_target_pairs={{0,16},{8,24},{16,0},{24,8},{1,17},{9,25},{17,1},{25,9},{2,18},{10... | collective-permute-start | bytes 491528 | tf_op jit(solution)/shard_map/ppermute | solution.py:404
  6.9 8.5 %collective-permute-start.8 = (bf16[2,320,128]{2,1,0:T(8,128)(2,1)S(1)}, bf16[2,320,128]{2,1,0:T(8,128)(2,1)S(1)}, u32[]{:S(2)}, u32[]{:S(2)}) collective-permute-start(bf16[2,320,128]{2,1,0:T(8,128)(2,1)S(1)} %get-tuple-element.245.refs_1_), channel_id=1, source_target_pairs={{0,8},{8,0},{16,24},{24,16},{1,9},{9,1},{17,25},{25,17},{2,10},{10... | collective-permute-start | bytes 491528 | tf_op jit(solution)/shard_map/ppermute | solution.py:404
  12.2 7.0 %collective-permute-start.4 = (bf16[2,320,128]{2,1,0:T(8,128)(2,1)S(1)}, bf16[2,320,128]{2,1,0:T(8,128)(2,1)S(1)}, u32[]{:S(2)}, u32[]{:S(2)}) collective-permute-start(bf16[2,320,128]{2,1,0:T(8,128)(2,1)S(1)} %get-tuple-element.130), channel_id=1, source_target_pairs={{0,16},{8,24},{16,0},{24,8},{1,17},{9,25},{17,1},{25,9},{2,18},{10... | collective-permute-start | bytes 491528 | tf_op jit(solution)/shard_map/ppermute | solution.py:404
  12.3 6.9 %collective-permute-start.5 = (bf16[2,320,128]{2,1,0:T(8,128)(2,1)S(1)}, bf16[2,320,128]{2,1,0:T(8,128)(2,1)S(1)}, u32[]{:S(2)}, u32[]{:S(2)}) collective-permute-start(bf16[2,320,128]{2,1,0:T(8,128)(2,1)S(1)} %get-tuple-element.131), channel_id=1, source_target_pairs={{0,8},{8,0},{16,24},{24,16},{1,9},{9,1},{17,25},{25,17},{2,10},{10... | collective-permute-start | bytes 491528 | tf_op jit(solution)/shard_map/ppermute | solution.py:404
  15.7 16.2 %copy-start.1 = (f32[1,4,320,128]{3,2,1,0:T(8,128)S(1)}, f32[1,4,320,128]{3,2,1,0:T(8,128)}, u32[]{:S(2)}) copy-start(f32[1,4,320,128]{3,2,1,0:T(8,128)} %param.16) | copy-start | bytes 1966084
  15.8 16.2 %copy-start = (bf16[384,256]{1,0:T(8,128)(2,1)S(1)}, bf16[384,256]{1,0:T(8,128)(2,1)}, u32[]{:S(2)}) copy-start(bf16[384,256]{1,0:T(8,128)(2,1)} %constant.2.clone.matrix_ref.refs_3_) | copy-start | bytes 589828
  15.8 7.3 %collective-permute-start.10 = (bf16[2,320,128]{2,1,0:T(8,128)(2,1)S(1)}, bf16[2,320,128]{2,1,0:T(8,128)(2,1)S(1)}, u32[]{:S(2)}, u32[]{:S(2)}) collective-permute-start(bf16[2,320,128]{2,1,0:T(8,128)(2,1)S(1)} %get-tuple-element.138), channel_id=1, source_target_pairs={{0,16},{8,24},{16,0},{24,8},{1,17},{9,25},{17,1},{25,9},{2,18},{10... | collective-permute-start | bytes 491528 | tf_op jit(solution)/shard_map/ppermute | solution.py:404
  19.7 15.5 %collective-permute-start.6 = (bf16[4,320,128]{2,1,0:T(8,128)(2,1)S(1)}, bf16[4,320,128]{2,1,0:T(8,128)(2,1)S(1)}, u32[]{:S(2)}, u32[]{:S(2)}) collective-permute-start(bf16[4,320,128]{2,1,0:T(8,128)(2,1)S(1)} %get-tuple-element.132.den_ref.refs_6_), channel_id=1, source_target_pairs={{0,1},{1,0},{2,3},{3,2},{4,5},{5,4},{6,7},{7,6},{8,9},{9,8},{10,11... | collective-permute-start | bytes 983048 | tf_op jit(solution)/shard_map/ppermute | solution.py:409
  19.8 15.7 %collective-permute-start.3 = (bf16[4,320,128]{2,1,0:T(8,128)(2,1)S(1)}, bf16[4,320,128]{2,1,0:T(8,128)(2,1)S(1)}, u32[]{:S(2)}, u32[]{:S(2)}) collective-permute-start(bf16[4,320,128]{2,1,0:T(8,128)(2,1)S(1)} %get-tuple-element.125), channel_id=1, source_target_pairs={{1,2},{2,1},{3,4},{4,3},{5,6},{6,5},{0,8},{7,15},{9,10},{10,9},{11... | collective-permute-start | bytes 983048 | tf_op jit(solution)/shard_map/ppermute | solution.py:421
  21.3 14.2 %collective-permute-start.2 = (bf16[4,320,128]{2,1,0:T(8,128)(2,1)S(1)}, bf16[4,320,128]{2,1,0:T(8,128)(2,1)S(1)}, u32[]{:S(2)}, u32[]{:S(2)}) collective-permute-start(bf16[4,320,128]{2,1,0:T(8,128)(2,1)S(1)} %get-tuple-element.125), channel_id=1, source_target_pairs={{0,1},{1,0},{2,3},{3,2},{4,5},{5,4},{6,7},{7,6},{8,9},{9,8},{10,11... | collective-permute-start | bytes 983048 | tf_op jit(solution)/shard_map/ppermute | solution.py:409
  21.5 8.9 %collective-permute-start.11 = (bf16[2,320,128]{2,1,0:T(8,128)(2,1)S(1)}, bf16[2,320,128]{2,1,0:T(8,128)(2,1)S(1)}, u32[]{:S(2)}, u32[]{:S(2)}) collective-permute-start(bf16[2,320,128]{2,1,0:T(8,128)(2,1)S(1)} %get-tuple-element.139), channel_id=1, source_target_pairs={{0,8},{8,0},{16,24},{24,16},{1,9},{9,1},{17,25},{25,17},{2,10},{10... | collective-permute-start | bytes 491528 | tf_op jit(solution)/shard_map/ppermute | solution.py:404
  23.0 12.1 %collective-permute-start.12 = (bf16[4,160,128]{2,1,0:T(8,128)(2,1)S(1)}, bf16[4,160,128]{2,1,0:T(8,128)(2,1)S(1)}, u32[]{:S(2)}, u32[]{:S(2)}) collective-permute-start(bf16[4,160,128]{2,1,0:T(8,128)(2,1)S(1)} %get-tuple-element.140), channel_id=1, source_target_pairs={{1,2},{2,1},{3,4},{4,3},{5,6},{6,5},{0,8},{7,15},{9,10},{10,9},{11... | collective-permute-start | bytes 491528 | tf_op jit(solution)/shard_map/ppermute | solution.py:421
  30.4 5.6 %collective-permute-start.7 = (bf16[4,160,128]{2,1,0:T(8,128)(2,1)S(1)}, bf16[4,160,128]{2,1,0:T(8,128)(2,1)S(1)}, u32[]{:S(2)}, u32[]{:S(2)}) collective-permute-start(bf16[4,160,128]{2,1,0:T(8,128)(2,1)S(1)} %get-tuple-element.137), channel_id=1, source_target_pairs={{1,2},{2,1},{3,4},{4,3},{5,6},{6,5},{0,8},{7,15},{9,10},{10,9},{11... | collective-permute-start | bytes 491528 | tf_op jit(solution)/shard_map/ppermute | solution.py:421
  36.9 5.5 %collective-permute-start.13 = (bf16[4,320,128]{2,1,0:T(8,128)(2,1)S(1)}, bf16[4,320,128]{2,1,0:T(8,128)(2,1)S(1)}, u32[]{:S(2)}, u32[]{:S(2)}) collective-permute-start(bf16[4,320,128]{2,1,0:T(8,128)(2,1)S(1)} %get-tuple-element.150), channel_id=1, source_target_pairs={{0,1},{1,0},{2,3},{3,2},{4,5},{5,4},{6,7},{7,6},{8,9},{9,8},{10,11... | collective-permute-start | bytes 983048 | tf_op jit(solution)/shard_map/ppermute | solution.py:409
  36.9 5.4 %collective-permute-start.15 = (bf16[4,160,128]{2,1,0:T(8,128)(2,1)S(1)}, bf16[4,160,128]{2,1,0:T(8,128)(2,1)S(1)}, u32[]{:S(2)}, u32[]{:S(2)}) collective-permute-start(bf16[4,160,128]{2,1,0:T(8,128)(2,1)S(1)} %get-tuple-element.153), channel_id=1, source_target_pairs={{1,2},{2,1},{3,4},{4,3},{5,6},{6,5},{0,8},{7,15},{9,10},{10,9},{11... | collective-permute-start | bytes 491528 | tf_op jit(solution)/shard_map/ppermute | solution.py:421
  38.2 5.9 %collective-permute-start.14 = (bf16[4,160,128]{2,1,0:T(8,128)(2,1)S(1)}, bf16[4,160,128]{2,1,0:T(8,128)(2,1)S(1)}, u32[]{:S(2)}, u32[]{:S(2)}) collective-permute-start(bf16[4,160,128]{2,1,0:T(8,128)(2,1)S(1)} %get-tuple-element.151), channel_id=1, source_target_pairs={{1,2},{2,1},{3,4},{4,3},{5,6},{6,5},{0,8},{7,15},{9,10},{10,9},{11... | collective-permute-start | bytes 491528 | tf_op jit(solution)/shard_map/ppermute | solution.py:421
  44.6 5.5 %collective-permute-start.16 = (bf16[4,320,128]{2,1,0:T(8,128)(2,1)S(1)}, bf16[4,320,128]{2,1,0:T(8,128)(2,1)S(1)}, u32[]{:S(2)}, u32[]{:S(2)}) collective-permute-start(bf16[4,320,128]{2,1,0:T(8,128)(2,1)S(1)} %get-tuple-element.159), channel_id=1, source_target_pairs={{0,1},{1,0},{2,3},{3,2},{4,5},{5,4},{6,7},{7,6},{8,9},{9,8},{10,11... | collective-permute-start | bytes 983048 | tf_op jit(solution)/shard_map/ppermute | solution.py:409
  44.7 5.3 %collective-permute-start.18 = (bf16[4,160,128]{2,1,0:T(8,128)(2,1)S(1)}, bf16[4,160,128]{2,1,0:T(8,128)(2,1)S(1)}, u32[]{:S(2)}, u32[]{:S(2)}) collective-permute-start(bf16[4,160,128]{2,1,0:T(8,128)(2,1)S(1)} %get-tuple-element.162), channel_id=1, source_target_pairs={{1,2},{2,1},{3,4},{4,3},{5,6},{6,5},{0,8},{7,15},{9,10},{10,9},{11... | collective-permute-start | bytes 491528 | tf_op jit(solution)/shard_map/ppermute | solution.py:421
  45.9 5.9 %collective-permute-start.17 = (bf16[4,160,128]{2,1,0:T(8,128)(2,1)S(1)}, bf16[4,160,128]{2,1,0:T(8,128)(2,1)S(1)}, u32[]{:S(2)}, u32[]{:S(2)}) collective-permute-start(bf16[4,160,128]{2,1,0:T(8,128)(2,1)S(1)} %get-tuple-element.160), channel_id=1, source_target_pairs={{1,2},{2,1},{3,4},{4,3},{5,6},{6,5},{0,8},{7,15},{9,10},{10,9},{11... | collective-permute-start | bytes 491528 | tf_op jit(solution)/shard_map/ppermute | solution.py:421
  51.8 3.2 %copy-start.4 = (f32[1,4,320,128]{3,2,1,0:T(8,128)S(1)}, f32[1,4,320,128]{3,2,1,0:T(8,128)}, u32[]{:S(2)}) copy-start(f32[1,4,320,128]{3,2,1,0:T(8,128)} %param.17) | copy-start | bytes 1966084
  52.3 2.2 %copy-start.7 = (s32[1,512]{1,0:T(1,128)S(1)}, s32[1,512]{1,0:T(1,128)}, u32[]{:S(2)}) copy-start(s32[1,512]{1,0:T(1,128)} %rec.1) | copy-start | bytes 6148
  52.3 5.5 %collective-permute-start.19 = (bf16[4,320,128]{2,1,0:T(8,128)(2,1)S(1)}, bf16[4,320,128]{2,1,0:T(8,128)(2,1)S(1)}, u32[]{:S(2)}, u32[]{:S(2)}) collective-permute-start(bf16[4,320,128]{2,1,0:T(8,128)(2,1)S(1)} %get-tuple-element.168), channel_id=1, source_target_pairs={{0,1},{1,0},{2,3},{3,2},{4,5},{5,4},{6,7},{7,6},{8,9},{9,8},{10,11... | collective-permute-start | bytes 983048 | tf_op jit(solution)/shard_map/ppermute | solution.py:409
  52.5 5.3 %collective-permute-start.21 = (bf16[4,160,128]{2,1,0:T(8,128)(2,1)S(1)}, bf16[4,160,128]{2,1,0:T(8,128)(2,1)S(1)}, u32[]{:S(2)}, u32[]{:S(2)}) collective-permute-start(bf16[4,160,128]{2,1,0:T(8,128)(2,1)S(1)} %get-tuple-element.171), channel_id=1, source_target_pairs={{1,2},{2,1},{3,4},{4,3},{5,6},{6,5},{0,8},{7,15},{9,10},{10,9},{11... | collective-permute-start | bytes 491528 | tf_op jit(solution)/shard_map/ppermute | solution.py:421
  53.7 5.9 %collective-permute-start.20 = (bf16[4,160,128]{2,1,0:T(8,128)(2,1)S(1)}, bf16[4,160,128]{2,1,0:T(8,128)(2,1)S(1)}, u32[]{:S(2)}, u32[]{:S(2)}) collective-permute-start(bf16[4,160,128]{2,1,0:T(8,128)(2,1)S(1)} %get-tuple-element.169), channel_id=1, source_target_pairs={{1,2},{2,1},{3,4},{4,3},{5,6},{6,5},{0,8},{7,15},{9,10},{10,9},{11... | collective-permute-start | bytes 491528 | tf_op jit(solution)/shard_map/ppermute | solution.py:421
  61.9 5.5 %collective-permute-start.22 = (bf16[4,320,128]{2,1,0:T(8,128)(2,1)S(1)}, bf16[4,320,128]{2,1,0:T(8,128)(2,1)S(1)}, u32[]{:S(2)}, u32[]{:S(2)}) collective-permute-start(bf16[4,320,128]{2,1,0:T(8,128)(2,1)S(1)} %get-tuple-element.177), channel_id=1, source_target_pairs={{0,1},{1,0},{2,3},{3,2},{4,5},{5,4},{6,7},{7,6},{8,9},{9,8},{10,11... | collective-permute-start | bytes 983048 | tf_op jit(solution)/shard_map/ppermute | solution.py:409
  61.9 5.4 %collective-permute-start.24 = (bf16[4,160,128]{2,1,0:T(8,128)(2,1)S(1)}, bf16[4,160,128]{2,1,0:T(8,128)(2,1)S(1)}, u32[]{:S(2)}, u32[]{:S(2)}) collective-permute-start(bf16[4,160,128]{2,1,0:T(8,128)(2,1)S(1)} %get-tuple-element.185), channel_id=1, source_target_pairs={{1,2},{2,1},{3,4},{4,3},{5,6},{6,5},{0,8},{7,15},{9,10},{10,9},{11... | collective-permute-start | bytes 491528 | tf_op jit(solution)/shard_map/ppermute | solution.py:421
  63.2 5.9 %collective-permute-start.23 = (bf16[4,160,128]{2,1,0:T(8,128)(2,1)S(1)}, bf16[4,160,128]{2,1,0:T(8,128)(2,1)S(1)}, u32[]{:S(2)}, u32[]{:S(2)}) collective-permute-start(bf16[4,160,128]{2,1,0:T(8,128)(2,1)S(1)} %get-tuple-element.178), channel_id=1, source_target_pairs={{1,2},{2,1},{3,4},{4,3},{5,6},{6,5},{0,8},{7,15},{9,10},{10,9},{11... | collective-permute-start | bytes 491528 | tf_op jit(solution)/shard_map/ppermute | solution.py:421
  69.6 5.9 %collective-permute-start.25 = (bf16[4,320,128]{2,1,0:T(8,128)(2,1)S(1)}, bf16[4,320,128]{2,1,0:T(8,128)(2,1)S(1)}, u32[]{:S(2)}, u32[]{:S(2)}) collective-permute-start(bf16[4,320,128]{2,1,0:T(8,128)(2,1)S(1)} %get-tuple-element.191), channel_id=1, source_target_pairs={{0,1},{1,0},{2,3},{3,2},{4,5},{5,4},{6,7},{7,6},{8,9},{9,8},{10,11... | collective-permute-start | bytes 983048 | tf_op jit(solution)/shard_map/ppermute | solution.py:409
  69.8 5.7 %collective-permute-start.27 = (bf16[4,160,128]{2,1,0:T(8,128)(2,1)S(1)}, bf16[4,160,128]{2,1,0:T(8,128)(2,1)S(1)}, u32[]{:S(2)}, u32[]{:S(2)}) collective-permute-start(bf16[4,160,128]{2,1,0:T(8,128)(2,1)S(1)} %get-tuple-element.202), channel_id=1, source_target_pairs={{1,2},{2,1},{3,4},{4,3},{5,6},{6,5},{0,8},{7,15},{9,10},{10,9},{11... | collective-permute-start | bytes 491528 | tf_op jit(solution)/shard_map/ppermute | solution.py:421
  71.0 5.9 %collective-permute-start.26 = (bf16[4,160,128]{2,1,0:T(8,128)(2,1)S(1)}, bf16[4,160,128]{2,1,0:T(8,128)(2,1)S(1)}, u32[]{:S(2)}, u32[]{:S(2)}) collective-permute-start(bf16[4,160,128]{2,1,0:T(8,128)(2,1)S(1)} %get-tuple-element.192), channel_id=1, source_target_pairs={{1,2},{2,1},{3,4},{4,3},{5,6},{6,5},{0,8},{7,15},{9,10},{10,9},{11... | collective-permute-start | bytes 491528 | tf_op jit(solution)/shard_map/ppermute | solution.py:421
  77.4 5.5 %collective-permute-start.28 = (bf16[4,320,128]{2,1,0:T(8,128)(2,1)S(1)}, bf16[4,320,128]{2,1,0:T(8,128)(2,1)S(1)}, u32[]{:S(2)}, u32[]{:S(2)}) collective-permute-start(bf16[4,320,128]{2,1,0:T(8,128)(2,1)S(1)} %get-tuple-element.208), channel_id=1, source_target_pairs={{0,1},{1,0},{2,3},{3,2},{4,5},{5,4},{6,7},{7,6},{8,9},{9,8},{10,11... | collective-permute-start | bytes 983048 | tf_op jit(solution)/shard_map/ppermute | solution.py:409
  77.6 5.3 %collective-permute-start.29 = (bf16[4,160,128]{2,1,0:T(8,128)(2,1)S(1)}, bf16[4,160,128]{2,1,0:T(8,128)(2,1)S(1)}, u32[]{:S(2)}, u32[]{:S(2)}) collective-permute-start(bf16[4,160,128]{2,1,0:T(8,128)(2,1)S(1)} %get-tuple-element.209), channel_id=1, source_target_pairs={{1,2},{2,1},{3,4},{4,3},{5,6},{6,5},{0,8},{7,15},{9,10},{10,9},{11... | collective-permute-start | bytes 491528 | tf_op jit(solution)/shard_map/ppermute | solution.py:421
  78.7 5.9 %collective-permute-start.32 = (bf16[4,160,128]{2,1,0:T(8,128)(2,1)S(1)}, bf16[4,160,128]{2,1,0:T(8,128)(2,1)S(1)}, u32[]{:S(2)}, u32[]{:S(2)}) collective-permute-start(bf16[4,160,128]{2,1,0:T(8,128)(2,1)S(1)} %get-tuple-element.225), channel_id=1, source_target_pairs={{1,2},{2,1},{3,4},{4,3},{5,6},{6,5},{0,8},{7,15},{9,10},{10,9},{11... | collective-permute-start | bytes 491528 | tf_op jit(solution)/shard_map/ppermute | solution.py:421
  85.3 10.2 %collective-permute-start.35 = (bf16[4,320,128]{2,1,0:T(8,128)(2,1)S(1)}, bf16[4,320,128]{2,1,0:T(8,128)(2,1)S(1)}, u32[]{:S(2)}, u32[]{:S(2)}) collective-permute-start(bf16[4,320,128]{2,1,0:T(8,128)(2,1)S(1)} %get-tuple-element.233), channel_id=1, source_target_pairs={{0,1},{1,0},{2,3},{3,2},{4,5},{5,4},{6,7},{7,6},{8,9},{9,8},{10,11... | collective-permute-start | bytes 983048 | tf_op jit(solution)/shard_map/ppermute | solution.py:409
  85.4 6.5 %collective-permute-start.33 = (bf16[4,160,128]{2,1,0:T(8,128)(2,1)S(1)}, bf16[4,160,128]{2,1,0:T(8,128)(2,1)S(1)}, u32[]{:S(2)}, u32[]{:S(2)}) collective-permute-start(bf16[4,160,128]{2,1,0:T(8,128)(2,1)S(1)} %get-tuple-element.229.refs_1_), channel_id=1, source_target_pairs={{0,16},{8,24},{16,0},{24,8},{1,17},{9,25},{17,1},{25,9},{2,18},{10... | collective-permute-start | bytes 491528 | tf_op jit(solution)/shard_map/ppermute | solution.py:404
  86.0 8.6 %collective-permute-start.30 = (bf16[4,160,128]{2,1,0:T(8,128)(2,1)S(1)}, bf16[4,160,128]{2,1,0:T(8,128)(2,1)S(1)}, u32[]{:S(2)}, u32[]{:S(2)}) collective-permute-start(bf16[4,160,128]{2,1,0:T(8,128)(2,1)S(1)} %get-tuple-element.222.refs_1_), channel_id=1, source_target_pairs={{0,8},{8,0},{16,24},{24,16},{1,9},{9,1},{17,25},{25,17},{2,10},{10... | collective-permute-start | bytes 491528 | tf_op jit(solution)/shard_map/ppermute | solution.py:404
  87.1 8.3 %collective-permute-start.36 = (bf16[4,160,128]{2,1,0:T(8,128)(2,1)S(1)}, bf16[4,160,128]{2,1,0:T(8,128)(2,1)S(1)}, u32[]{:S(2)}, u32[]{:S(2)}) collective-permute-start(bf16[4,160,128]{2,1,0:T(8,128)(2,1)S(1)} %get-tuple-element.234), channel_id=1, source_target_pairs={{1,2},{2,1},{3,4},{4,3},{5,6},{6,5},{0,8},{7,15},{9,10},{10,9},{11... | collective-permute-start | bytes 491528 | tf_op jit(solution)/shard_map/ppermute | solution.py:421
  88.0 9.1 %collective-permute-start.39 = (bf16[4,160,128]{2,1,0:T(8,128)(2,1)S(1)}, bf16[4,160,128]{2,1,0:T(8,128)(2,1)S(1)}, u32[]{:S(2)}, u32[]{:S(2)}) collective-permute-start(bf16[4,160,128]{2,1,0:T(8,128)(2,1)S(1)} %get-tuple-element.241), channel_id=1, source_target_pairs={{1,2},{2,1},{3,4},{4,3},{5,6},{6,5},{0,8},{7,15},{9,10},{10,9},{11... | collective-permute-start | bytes 491528 | tf_op jit(solution)/shard_map/ppermute | solution.py:421
  92.1 8.5 %collective-permute-start.34 = (bf16[4,160,128]{2,1,0:T(8,128)(2,1)S(1)}, bf16[4,160,128]{2,1,0:T(8,128)(2,1)S(1)}, u32[]{:S(2)}, u32[]{:S(2)}) collective-permute-start(bf16[4,160,128]{2,1,0:T(8,128)(2,1)S(1)} %get-tuple-element.231), channel_id=1, source_target_pairs={{0,8},{8,0},{16,24},{24,16},{1,9},{9,1},{17,25},{25,17},{2,10},{10... | collective-permute-start | bytes 491528 | tf_op jit(solution)/shard_map/ppermute | solution.py:404
  94.9 9.6 %collective-permute-start.31 = (bf16[4,160,128]{2,1,0:T(8,128)(2,1)S(1)}, bf16[4,160,128]{2,1,0:T(8,128)(2,1)S(1)}, u32[]{:S(2)}, u32[]{:S(2)}) collective-permute-start(bf16[4,160,128]{2,1,0:T(8,128)(2,1)S(1)} %get-tuple-element.224), channel_id=1, source_target_pairs={{0,16},{8,24},{16,0},{24,8},{1,17},{9,25},{17,1},{25,9},{2,18},{10... | collective-permute-start | bytes 491528 | tf_op jit(solution)/shard_map/ppermute | solution.py:404
  95.8 7.0 %collective-permute-start.37 = (bf16[4,160,128]{2,1,0:T(8,128)(2,1)S(1)}, bf16[4,160,128]{2,1,0:T(8,128)(2,1)S(1)}, u32[]{:S(2)}, u32[]{:S(2)}) collective-permute-start(bf16[4,160,128]{2,1,0:T(8,128)(2,1)S(1)} %shard_map.151.refs_1_), channel_id=1, source_target_pairs={{0,8},{8,0},{16,24},{24,16},{1,9},{9,1},{17,25},{25,17},{2,10},{10... | collective-permute-start | bytes 491528 | tf_op jit(solution)/shard_map/ppermute | solution.py:404
  97.5 7.9 %collective-permute-start.40 = (bf16[4,160,128]{2,1,0:T(8,128)(2,1)S(1)}, bf16[4,160,128]{2,1,0:T(8,128)(2,1)S(1)}, u32[]{:S(2)}, u32[]{:S(2)}) collective-permute-start(bf16[4,160,128]{2,1,0:T(8,128)(2,1)S(1)} %shard_map.153.refs_1_), channel_id=1, source_target_pairs={{0,16},{8,24},{16,0},{24,8},{1,17},{9,25},{17,1},{25,9},{2,18},{10... | collective-permute-start | bytes 491528 | tf_op jit(solution)/shard_map/ppermute | solution.py:404
  103.0 5.4 %collective-permute-start.38 = (bf16[4,160,128]{2,1,0:T(8,128)(2,1)S(1)}, bf16[4,160,128]{2,1,0:T(8,128)(2,1)S(1)}, u32[]{:S(2)}, u32[]{:S(2)}) collective-permute-start(bf16[4,160,128]{2,1,0:T(8,128)(2,1)S(1)} %get-tuple-element.240), channel_id=1, source_target_pairs={{0,16},{8,24},{16,0},{24,8},{1,17},{9,25},{17,1},{25,9},{2,18},{10... | collective-permute-start | bytes 491528 | tf_op jit(solution)/shard_map/ppermute | solution.py:404
  105.6 5.4 %collective-permute-start.41 = (bf16[4,160,128]{2,1,0:T(8,128)(2,1)S(1)}, bf16[4,160,128]{2,1,0:T(8,128)(2,1)S(1)}, u32[]{:S(2)}, u32[]{:S(2)}) collective-permute-start(bf16[4,160,128]{2,1,0:T(8,128)(2,1)S(1)} %get-tuple-element.243), channel_id=1, source_target_pairs={{0,8},{8,0},{16,24},{24,16},{1,9},{9,1},{17,25},{25,17},{2,10},{10... | collective-permute-start | bytes 491528 | tf_op jit(solution)/shard_map/ppermute | solution.py:404
  (3 other events, 3.2 us)

commit v6 on v5

--- a/solution.py
+++ b/solution.py
@@ -275,7 +275,27 @@
             dz_ref[l, rows, :] = d_z
 
 
-def forward_x_kernel(part, send, f_ref, on_ref, off_ref, part_ref, s1_ref, scale_ref, before_ref, *refs):
+def plain_yz_kernel(f_ref, matrix_ref, part_ref, dy_ref, dz_ref, z_ref):
+    layers, width, depth = part_ref.shape
+    z_terms(f_ref, matrix_ref, z_ref)
+
+    @pl.loop(0, width // 8)
+    def _(j):
+        at = pl.multiple_of(8 * j, 8)
+        rows = pl.ds(at, 8)
+        for l in range(layers):
+            lap_y, d_y = weighted(y_pairs(f_ref, l, at + PAD, 8))
+            f = f_ref[l, pl.ds(at + PAD, 8), :]
+            part_ref[l, rows, :] = (3.0 * SECOND[0]) * f + lap_y + z_ref[l, rows, pl.ds(0, depth)]
+            dy_ref[l, rows, :] = d_y
+            dz_ref[l, rows, :] = z_ref[l, rows, pl.ds(depth, depth)]
+
+
+def forward_x_kernel(
+    part, send, plain, f_ref, on_ref, off_ref, part_ref, s1_ref, scale_ref, before_ref, *refs
+):
+    if plain:
+        s2_ref, s3_ref, dy_ref, dz_ref = refs[:4]
     sending = send
     if sending:
         dx_ref, applied_ref, next_ref, half_ref, send_ref = refs[-5:]
@@ -292,6 +312,10 @@
         for l in range(layers):
             lap, d_x = weighted(x_pairs(values, l))
             applied = part_ref[l, rows, :] + (lap - s1_ref[l, rows, :] * d_x)
+            if plain:
+                applied = applied - (
+                    s2_ref[l, rows, :] * dy_ref[l, rows, :] + s3_ref[l, rows, :] * dz_ref[l, rows, :]
+                )
             before = before_ref[l, wide if shift else rows, :]
             later = 2.0 * own[l] - before + scale_ref[l, rows, :] * applied
             dx_ref[l, rows, :] = d_x
@@ -409,13 +433,15 @@
     return lax.ppermute(half, "sub", [(i, i ^ 1) for i in range(count)])
 
 
-def across(half, fill=True):
+def across(half, ring=False):
     groups, count = lax.axis_size("shot"), lax.axis_size("sub")
     pairs = []
     for s in range(groups):
         for i in range(1, count - 1, 2):
             pairs += [(s * count + i, s * count + i + 1), (s * count + i + 1, s * count + i)]
-        if fill and groups % 2 == 0:
+        if ring:
+            pairs += [(s * count, s * count + count - 1), (s * count + count - 1, s * count)]
+        elif groups % 2 == 0:
             for i in (0, count - 1):
                 pairs.append((s * count + i, (s ^ 1) * count + i))
     return lax.ppermute(half, ("shot", "sub"), pairs)
@@ -559,7 +585,7 @@
         lambda rec, out: list_kernel(rec, layers, width, depth, out),
         [((4, n_rec), jnp.int32)], [receivers],
     )
-    on, off = paired(p_half), across(p_half)
+    on, off = paired(p_half), across(p_half, ring=True)
     kept = {}
 
     def tie(held):
@@ -587,16 +613,20 @@
 
     stored, fields = [], []
     for step in range(ITERS):
-        part, d_y, d_z = call(forward_yz_kernel, [narrow] * 3, [p, s2, s3, matrix], scratch=z_scratch)
+        plain = step == 0
+        part, d_y, d_z = call(
+            plain_yz_kernel if plain else forward_yz_kernel, [narrow] * 3,
+            [p, matrix] if plain else [p, s2, s3, matrix], scratch=z_scratch,
+        )
         if step > 0:
             fields.append(p.reshape(flat[0]))
         sending = step < ITERS - 1
         made, sends = (), []
         for k in parts:
             s1, scale = slopes[1 + k] if step == 0 else slopes[-1]
-            ins = [p, on, offs[k], part, s1, scale, before]
+            ins = [p, on, offs[k], part, s1, scale, before] + ([s2, s3, d_y, d_z] if plain else [])
             outs = call(
-                lambda *refs, k=k, sending=sending: forward_x_kernel(k, sending, *refs),
+                lambda *refs, k=k, sending=sending, plain=plain: forward_x_kernel(k, sending, plain, *refs),
                 [narrow, narrow, padded] + ([half, part_half] if sending else []), [*ins, *made],
                 aliases={len(ins) + n: n for n in range(len(made))},
             )
@@ -619,7 +649,7 @@
     on = paired(a_half)
     a = a.reshape(padded[0])
     sources = []
-    for first, some in ((0, fields[:-1]), (len(fields) - 1, fields[-1:])):
+    for first, some in ((0, fields[:1]), (1, fields[1:])):
         sources += call(
             lambda *refs, first=first: receivers_kernel(first, *refs),
             [flat] * len(some), [*some, lists, seen], [VM] * len(some) + [SM, SM],

time: 112 us -> 112 us (level)
  waiting for transfers between devices: 39.6 us -> 37.2 us
  starting transfers between devices: 37.6 us -> 39.6 us
    ppermute x16, waiting for transfers between devices: 25.3 us -> 22.9 us  [swap_over(): return lax.ppermute(value, axis, [(i, i ^ bit) for i in range(count)])]
    ppermute x17, starting transfers between devices: 17.9 us -> 20 us  [across(): return lax.ppermute(half, ('shot', 'sub'), pairs)]
where the time goes in v6:
time: 112 us
  starting transfers between devices  39.6 us (35%)
  waiting for transfers between devices  37.2 us (33%)
  Pallas kernels  30.4 us (27%)
  other arithmetic  1.88 us (2%)
  local copies, waits for them, and re-layouts  1.37 us (1%)
  between operations  1.16 us (1%)
    pallas_call x42, Pallas kernels, call(): pl.pallas_call(kernel, out_shape=outs, in_specs=list(specs or [VM] * len(...  30.4 us
    ppermute x16, waiting for transfers between devices, swap_over(): return lax.ppermute(value, axis, [(i, i ^ bit) for i in range(count)])  22.9 us
    ppermute x17, starting transfers between devices, across(): return lax.ppermute(half, ('shot', 'sub'), pairs)  20 us
    ppermute x16, starting transfers between devices, swap_over(): return lax.ppermute(value, axis, [(i, i ^ bit) for i in range(count)])  18.5 us
    ppermute x17, waiting for transfers between devices, across(): return lax.ppermute(half, ('shot', 'sub'), pairs)  14.2 us
  transfers between devices with their start and end apart: 42, of which 22 were waited for; matrix products, arithmetic and copies ran while one was open for 1% of the time, Pallas kernels for 22%

profile of v6, /device:TPU:0, one launch (start us, length us, event | category | flops | bytes accessed | tf_op | source)
XLA Modules:
  0.0 111.6 jit_solution(9316138821608471649)
XLA Ops:
  1.8 3.1 %collective-permute-start.1 = (bf16[2,320,128]{2,1,0:T(8,128)(2,1)S(1)}, bf16[2,320,128]{2,1,0:T(8,128)(2,1)S(1)}, u32[]{:S(2)}, u32[]{:S(2)}) collective-permute-start(bf16[2,320,128]{2,1,0:T(8,128)(2,1)S(1)} %get-tuple-element.129.refs_3_.refs_4_), channel_id=1, source_target_pairs={{0,16},{8,24},{16,0},{24,8},{1,17},{9,25},{17,1},{25,9},{2,18},{10... | collective-permute-start | bytes 491528 | tf_op jit(solution)/shard_map/ppermute | solution.py:428
  4.8 1.5 %collective-permute-start = (bf16[2,320,128]{2,1,0:T(8,128)(2,1)S(1)}, bf16[2,320,128]{2,1,0:T(8,128)(2,1)S(1)}, u32[]{:S(2)}, u32[]{:S(2)}) collective-permute-start(bf16[2,320,128]{2,1,0:T(8,128)(2,1)S(1)} %get-tuple-element.127.refs_1_), channel_id=1, source_target_pairs={{0,8},{8,0},{16,24},{24,16},{1,9},{9,1},{17,25},{25,17},{2,10},{10... | collective-permute-start | bytes 491528 | tf_op jit(solution)/shard_map/ppermute | solution.py:428
  7.8 2.0 %collective-permute-done.1.refs_4_.refs_5_ = bf16[2,320,128]{2,1,0:T(8,128)(2,1)S(1)} collective-permute-done((bf16[2,320,128]{2,1,0:T(8,128)(2,1)S(1)}, bf16[2,320,128]{2,1,0:T(8,128)(2,1)S(1)}, u32[]{:S(2)}, u32[]{:S(2)}) %collective-permute-start.1) | collective-permute-done | bytes 163872 | tf_op jit(solution)/shard_map/ppermute | solution.py:428
  9.7 2.1 %collective-permute-done.refs_2_ = bf16[2,320,128]{2,1,0:T(8,128)(2,1)S(1)} collective-permute-done((bf16[2,320,128]{2,1,0:T(8,128)(2,1)S(1)}, bf16[2,320,128]{2,1,0:T(8,128)(2,1)S(1)}, u32[]{:S(2)}, u32[]{:S(2)}) %collective-permute-start) | collective-permute-done | bytes 163872 | tf_op jit(solution)/shard_map/ppermute | solution.py:428
  12.3 2.0 %collective-permute-start.5 = (bf16[2,320,128]{2,1,0:T(8,128)(2,1)S(1)}, bf16[2,320,128]{2,1,0:T(8,128)(2,1)S(1)}, u32[]{:S(2)}, u32[]{:S(2)}) collective-permute-start(bf16[2,320,128]{2,1,0:T(8,128)(2,1)S(1)} %get-tuple-element.132), channel_id=1, source_target_pairs={{0,8},{8,0},{16,24},{24,16},{1,9},{9,1},{17,25},{25,17},{2,10},{10... | collective-permute-start | bytes 491528 | tf_op jit(solution)/shard_map/ppermute | solution.py:428
  16.3 3.0 %collective-permute-done.4.refs_3_ = bf16[2,320,128]{2,1,0:T(8,128)(2,1)S(1)} collective-permute-done((bf16[2,320,128]{2,1,0:T(8,128)(2,1)S(1)}, bf16[2,320,128]{2,1,0:T(8,128)(2,1)S(1)}, u32[]{:S(2)}, u32[]{:S(2)}) %collective-permute-start.4) | collective-permute-done | bytes 163872 | tf_op jit(solution)/shard_map/ppermute | solution.py:428
  19.8 3.7 %collective-permute-start.3 = (bf16[4,320,128]{2,1,0:T(8,128)(2,1)S(1)}, bf16[4,320,128]{2,1,0:T(8,128)(2,1)S(1)}, u32[]{:S(2)}, u32[]{:S(2)}) collective-permute-start(bf16[4,320,128]{2,1,0:T(8,128)(2,1)S(1)} %get-tuple-element.125), channel_id=1, source_target_pairs={{1,2},{2,1},{3,4},{4,3},{5,6},{6,5},{0,7},{7,0},{9,10},{10,9},{11,... | collective-permute-start | bytes 983048 | tf_op jit(solution)/shard_map/ppermute | solution.py:447
  23.5 1.5 %collective-permute-start.11 = (bf16[2,320,128]{2,1,0:T(8,128)(2,1)S(1)}, bf16[2,320,128]{2,1,0:T(8,128)(2,1)S(1)}, u32[]{:S(2)}, u32[]{:S(2)}) collective-permute-start(bf16[2,320,128]{2,1,0:T(8,128)(2,1)S(1)} %get-tuple-element.137), channel_id=1, source_target_pairs={{0,8},{8,0},{16,24},{24,16},{1,9},{9,1},{17,25},{25,17},{2,10},{10... | collective-permute-start | bytes 491528 | tf_op jit(solution)/shard_map/ppermute | solution.py:428
  25.5 4.6 %collective-permute-done.11.refs_6_ = bf16[2,320,128]{2,1,0:T(8,128)(2,1)S(1)} collective-permute-done((bf16[2,320,128]{2,1,0:T(8,128)(2,1)S(1)}, bf16[2,320,128]{2,1,0:T(8,128)(2,1)S(1)}, u32[]{:S(2)}, u32[]{:S(2)}) %collective-permute-start.11) | collective-permute-done | bytes 163872 | tf_op jit(solution)/shard_map/ppermute | solution.py:428
  30.1 1.5 %collective-permute-start.7 = (bf16[4,160,128]{2,1,0:T(8,128)(2,1)S(1)}, bf16[4,160,128]{2,1,0:T(8,128)(2,1)S(1)}, u32[]{:S(2)}, u32[]{:S(2)}) collective-permute-start(bf16[4,160,128]{2,1,0:T(8,128)(2,1)S(1)} %get-tuple-element.135), channel_id=1, source_target_pairs={{1,2},{2,1},{3,4},{4,3},{5,6},{6,5},{0,8},{7,15},{9,10},{10,9},{11... | collective-permute-start | bytes 491528 | tf_op jit(solution)/shard_map/ppermute | solution.py:447
  31.6 1.3 %shard_map.115 = (f32[4,320,128]{2,1,0:T(8,128)S(1)}, f32[4,320,128]{2,1,0:T(8,128)S(1)}, f32[4,320,128]{2,1,0:T(8,128)S(1)}) custom-call(f32[4,336,128]{2,1,0:T(8,128)S(1)} %get-tuple-element.124.f_ref.refs_0_.refs_6_, bf16[384,256]{1,0:T(8,128)(2,1)S(1)} %copy-done), custom_call_target="tpu_custom_call" | custom-call | bytes 2850816 | tf_op jit(solution)/shard_map/pallas_call | solution.py:29
  32.9 1.3 %shard_map.118 = (f32[4,336,128]{2,1,0:T(8,128)S(1)}, f32[4,320,128]{2,1,0:T(8,128)S(1)}, f32[4,320,128]{2,1,0:T(8,128)S(1)}) custom-call(bf16[4,320,128]{2,1,0:T(8,128)(2,1)S(1)} %get-tuple-element.133.den_ref.refs_6_, bf16[384,256]{1,0:T(8,128)(2,1)S(1)} %copy-done, f32[4,320,128]{2,1,0:T(8,128)S(1)} %bitcast.35), custom_call_target="tpu_custom_call" | custom-call | bytes 3178496 | tf_op jit(solution)/shard_map/pallas_call | solution.py:29
  36.6 1.3 %collective-permute-start.15 = (bf16[4,160,128]{2,1,0:T(8,128)(2,1)S(1)}, bf16[4,160,128]{2,1,0:T(8,128)(2,1)S(1)}, u32[]{:S(2)}, u32[]{:S(2)}) collective-permute-start(bf16[4,160,128]{2,1,0:T(8,128)(2,1)S(1)} %get-tuple-element.155), channel_id=1, source_target_pairs={{1,2},{2,1},{3,4},{4,3},{5,6},{6,5},{0,8},{7,15},{9,10},{10,9},{11... | collective-permute-start | bytes 491528 | tf_op jit(solution)/shard_map/ppermute | solution.py:447
  38.7 1.4 %shard_map.125 = (f32[4,320,128]{2,1,0:T(8,128)S(1)}, f32[4,320,128]{2,1,0:T(8,128)S(1)}, f32[4,320,128]{2,1,0:T(8,128)S(1)}) custom-call(f32[4,336,128]{2,1,0:T(8,128)S(1)} %get-tuple-element.151.f_ref.refs_0_.refs_6_, f32[4,320,128]{2,1,0:T(8,128)S(1)} %get-tuple-element.143.refs_7_.s2_ref.refs_1_, ...), custom_call_target="tpu_custom_call" | custom-call | bytes 4161536 | tf_op jit(solution)/shard_map/pallas_call | solution.py:29
  40.2 1.9 %collective-permute-done.15.refs_2_ = bf16[4,160,128]{2,1,0:T(8,128)(2,1)S(1)} collective-permute-done((bf16[4,160,128]{2,1,0:T(8,128)(2,1)S(1)}, bf16[4,160,128]{2,1,0:T(8,128)(2,1)S(1)}, u32[]{:S(2)}, u32[]{:S(2)}) %collective-permute-start.15) | collective-permute-done | bytes 163872 | tf_op jit(solution)/shard_map/ppermute | solution.py:447
  42.5 1.3 %collective-permute-done.14.refs_2_ = bf16[4,160,128]{2,1,0:T(8,128)(2,1)S(1)} collective-permute-done((bf16[4,160,128]{2,1,0:T(8,128)(2,1)S(1)}, bf16[4,160,128]{2,1,0:T(8,128)(2,1)S(1)}, u32[]{:S(2)}, u32[]{:S(2)}) %collective-permute-start.14) | collective-permute-done | bytes 163872 | tf_op jit(solution)/shard_map/ppermute | solution.py:447
  44.4 1.2 %collective-permute-start.18 = (bf16[4,160,128]{2,1,0:T(8,128)(2,1)S(1)}, bf16[4,160,128]{2,1,0:T(8,128)(2,1)S(1)}, u32[]{:S(2)}, u32[]{:S(2)}) collective-permute-start(bf16[4,160,128]{2,1,0:T(8,128)(2,1)S(1)} %get-tuple-element.164), channel_id=1, source_target_pairs={{1,2},{2,1},{3,4},{4,3},{5,6},{6,5},{0,8},{7,15},{9,10},{10,9},{11... | collective-permute-start | bytes 491528 | tf_op jit(solution)/shard_map/ppermute | solution.py:447
  46.5 1.4 %shard_map.128 = (f32[4,320,128]{2,1,0:T(8,128)S(1)}, f32[4,320,128]{2,1,0:T(8,128)S(1)}, f32[4,320,128]{2,1,0:T(8,128)S(1)}) custom-call(f32[4,336,128]{2,1,0:T(8,128)S(1)} %get-tuple-element.160.f_ref.refs_0_.refs_6_, f32[4,320,128]{2,1,0:T(8,128)S(1)} %get-tuple-element.143.refs_7_.s2_ref.refs_1_, ...), custom_call_target="tpu_custom_call" | custom-call | bytes 4161536 | tf_op jit(solution)/shard_map/pallas_call | solution.py:29
  47.9 1.9 %collective-permute-done.18.refs_2_ = bf16[4,160,128]{2,1,0:T(8,128)(2,1)S(1)} collective-permute-done((bf16[4,160,128]{2,1,0:T(8,128)(2,1)S(1)}, bf16[4,160,128]{2,1,0:T(8,128)(2,1)S(1)}, u32[]{:S(2)}, u32[]{:S(2)}) %collective-permute-start.18) | collective-permute-done | bytes 163872 | tf_op jit(solution)/shard_map/ppermute | solution.py:447
  50.3 1.3 %collective-permute-done.17.refs_2_ = bf16[4,160,128]{2,1,0:T(8,128)(2,1)S(1)} collective-permute-done((bf16[4,160,128]{2,1,0:T(8,128)(2,1)S(1)}, bf16[4,160,128]{2,1,0:T(8,128)(2,1)S(1)}, u32[]{:S(2)}, u32[]{:S(2)}) %collective-permute-start.17) | collective-permute-done | bytes 163872 | tf_op jit(solution)/shard_map/ppermute | solution.py:447
  52.2 1.2 %collective-permute-start.21 = (bf16[4,160,128]{2,1,0:T(8,128)(2,1)S(1)}, bf16[4,160,128]{2,1,0:T(8,128)(2,1)S(1)}, u32[]{:S(2)}, u32[]{:S(2)}) collective-permute-start(bf16[4,160,128]{2,1,0:T(8,128)(2,1)S(1)} %get-tuple-element.173), channel_id=1, source_target_pairs={{1,2},{2,1},{3,4},{4,3},{5,6},{6,5},{0,8},{7,15},{9,10},{10,9},{11... | collective-permute-start | bytes 491528 | tf_op jit(solution)/shard_map/ppermute | solution.py:447
  54.8 1.4 %shard_map.131 = (f32[4,320,128]{2,1,0:T(8,128)S(1)}, f32[4,320,128]{2,1,0:T(8,128)S(1)}, f32[4,320,128]{2,1,0:T(8,128)S(1)}) custom-call(f32[4,336,128]{2,1,0:T(8,128)S(1)} %get-tuple-element.169.f_ref.refs_0_, f32[4,320,128]{2,1,0:T(8,128)S(1)} %get-tuple-element.143.refs_7_.s2_ref.refs_1_, f32[4,320,128]{2,1,0:T(8,128)S(1)} %get-tuple-element.144.refs_8_.s3_ref.refs_2_, ...), custom_call_target="tpu_custom_call" | custom-call | bytes 4161536 | tf_op jit(solution)/shard_map/pallas_call | solution.py:29
  56.3 1.3 %collective-permute-done.21.refs_2_ = bf16[4,160,128]{2,1,0:T(8,128)(2,1)S(1)} collective-permute-done((bf16[4,160,128]{2,1,0:T(8,128)(2,1)S(1)}, bf16[4,160,128]{2,1,0:T(8,128)(2,1)S(1)}, u32[]{:S(2)}, u32[]{:S(2)}) %collective-permute-start.21) | collective-permute-done | bytes 163872 | tf_op jit(solution)/shard_map/ppermute | solution.py:447
  58.0 1.3 %collective-permute-done.20.refs_2_ = bf16[4,160,128]{2,1,0:T(8,128)(2,1)S(1)} collective-permute-done((bf16[4,160,128]{2,1,0:T(8,128)(2,1)S(1)}, bf16[4,160,128]{2,1,0:T(8,128)(2,1)S(1)}, u32[]{:S(2)}, u32[]{:S(2)}) %collective-permute-start.20) | collective-permute-done | bytes 163872 | tf_op jit(solution)/shard_map/ppermute | solution.py:447
  60.0 1.6 %shard_map.136 = (f32[1344,128]{1,0:T(8,128)S(1)}, bf16[4,320,128]{2,1,0:T(8,128)(2,1)S(1)}, bf16[4,160,128]{2,1,0:T(8,128)(2,1)S(1)}, bf16[4,160,128]{2,1,0:T(8,128)(2,1)S(1)}) custom-call(f32[1344,128]{1,0:T(8,128)S(1)} %bitcast.38, f32[1344,128]{1,0:T(8,128)S(1)} %bitcast.29, s32[4,512]{1,0:T(4,128)S(1)} %shard_map.135.refs_2_.refs_1_, f32[4,512]{1,0:T(4,128)S(1)} %bitcast.47), custom_call_target="tpu_custom_call" | custom-call | bytes 2736128 | tf_op jit(solution)/shard_map/pallas_call | solution.py:29
  61.6 1.3 %collective-permute-start.24 = (bf16[4,160,128]{2,1,0:T(8,128)(2,1)S(1)}, bf16[4,160,128]{2,1,0:T(8,128)(2,1)S(1)}, u32[]{:S(2)}, u32[]{:S(2)}) collective-permute-start(bf16[4,160,128]{2,1,0:T(8,128)(2,1)S(1)} %get-tuple-element.188), channel_id=1, source_target_pairs={{1,2},{2,1},{3,4},{4,3},{5,6},{6,5},{0,8},{7,15},{9,10},{10,9},{11... | collective-permute-start | bytes 491528 | tf_op jit(solution)/shard_map/ppermute | solution.py:447
  63.7 2.1 %shard_map.138 = (f32[1344,128]{1,0:T(8,128)S(1)}, f32[1344,128]{1,0:T(8,128)S(1)}) custom-call(f32[1344,128]{1,0:T(8,128)S(1)} %bitcast.27, f32[1344,128]{1,0:T(8,128)S(1)} %bitcast.28, s32[4,512]{1,0:T(4,128)S(1)} %shard_map.135.refs_2_.refs_1_, f32[4,512]{1,0:T(4,128)S(1)} %bitcast.48), custom_call_target="tpu_custom_call" | custom-call | bytes 2768896 | tf_op jit(solution)/shard_map/pallas_call | solution.py:29
  65.8 1.5 %shard_map.137 = (f32[4,320,128]{2,1,0:T(8,128)S(1)}, f32[4,320,128]{2,1,0:T(8,128)S(1)}, f32[4,320,128]{2,1,0:T(8,128)S(1)}) custom-call(f32[4,336,128]{2,1,0:T(8,128)S(1)} %bitcast.32, f32[4,320,128]{2,1,0:T(8,128)S(1)} %get-tuple-element.143.refs_7_.s2_ref.refs_1_, f32[4,320,128]{2,1,0:T(8,128)S(1)} %get-tuple-element.144.refs_8_.s3_ref.refs_2_, ...), custom_call_target="tpu_custom_call" | custom-call | bytes 6127616 | tf_op jit(solution)/shard_map/pallas_call | solution.py:29
  69.5 1.2 %collective-permute-start.27 = (bf16[4,160,128]{2,1,0:T(8,128)(2,1)S(1)}, bf16[4,160,128]{2,1,0:T(8,128)(2,1)S(1)}, u32[]{:S(2)}, u32[]{:S(2)}) collective-permute-start(bf16[4,160,128]{2,1,0:T(8,128)(2,1)S(1)} %get-tuple-element.205), channel_id=1, source_target_pairs={{1,2},{2,1},{3,4},{4,3},{5,6},{6,5},{0,8},{7,15},{9,10},{10,9},{11... | collective-permute-start | bytes 491528 | tf_op jit(solution)/shard_map/ppermute | solution.py:447
  71.5 1.6 %shard_map.141 = (f32[4,320,128]{2,1,0:T(8,128)S(1)}, f32[4,320,128]{2,1,0:T(8,128)S(1)}, f32[4,320,128]{2,1,0:T(8,128)S(1)}) custom-call(f32[4,336,128]{2,1,0:T(8,128)S(1)} %get-tuple-element.193.refs_0_, f32[4,320,128]{2,1,0:T(8,128)S(1)} %get-tuple-element.143.refs_7_.s2_ref.refs_1_, f32[4,320,128]{2,1,0:T(8,128)S(1)} %get-tuple-element.144.refs_8_.s3_ref.refs_2_, ...), custom_call_target="tpu_custom_call" | custom-call | bytes 7438336 | tf_op jit(solution)/shard_map/pallas_call | solution.py:29
  73.1 1.7 %collective-permute-done.27.refs_2_ = bf16[4,160,128]{2,1,0:T(8,128)(2,1)S(1)} collective-permute-done((bf16[4,160,128]{2,1,0:T(8,128)(2,1)S(1)}, bf16[4,160,128]{2,1,0:T(8,128)(2,1)S(1)}, u32[]{:S(2)}, u32[]{:S(2)}) %collective-permute-start.27) | collective-permute-done | bytes 163872 | tf_op jit(solution)/shard_map/ppermute | solution.py:447
  75.4 1.2 %collective-permute-done.26.refs_2_ = bf16[4,160,128]{2,1,0:T(8,128)(2,1)S(1)} collective-permute-done((bf16[4,160,128]{2,1,0:T(8,128)(2,1)S(1)}, bf16[4,160,128]{2,1,0:T(8,128)(2,1)S(1)}, u32[]{:S(2)}, u32[]{:S(2)}) %collective-permute-start.26) | collective-permute-done | bytes 163872 | tf_op jit(solution)/shard_map/ppermute | solution.py:447
  77.3 1.2 %collective-permute-start.29 = (bf16[4,160,128]{2,1,0:T(8,128)(2,1)S(1)}, bf16[4,160,128]{2,1,0:T(8,128)(2,1)S(1)}, u32[]{:S(2)}, u32[]{:S(2)}) collective-permute-start(bf16[4,160,128]{2,1,0:T(8,128)(2,1)S(1)} %get-tuple-element.212), channel_id=1, source_target_pairs={{1,2},{2,1},{3,4},{4,3},{5,6},{6,5},{0,8},{7,15},{9,10},{10,9},{11... | collective-permute-start | bytes 491528 | tf_op jit(solution)/shard_map/ppermute | solution.py:447
  79.3 1.4 %shard_map.145 = f32[1344,128]{1,0:T(8,128)S(1)} custom-call(f32[1344,128]{1,0:T(8,128)S(1)} %bitcast.26, s32[4,512]{1,0:T(4,128)S(1)} %shard_map.135.refs_2_.refs_1_, f32[4,512]{1,0:T(4,128)S(1)} %bitcast.49), custom_call_target="tpu_custom_call" | custom-call | bytes 1392640 | tf_op jit(solution)/shard_map/pallas_call | solution.py:29
  80.7 1.6 %shard_map.144 = (f32[4,320,128]{2,1,0:T(8,128)S(1)}, f32[4,320,128]{2,1,0:T(8,128)S(1)}, f32[4,320,128]{2,1,0:T(8,128)S(1)}) custom-call(f32[4,336,128]{2,1,0:T(8,128)S(1)} %get-tuple-element.210.refs_0_, f32[4,320,128]{2,1,0:T(8,128)S(1)} %get-tuple-element.143.refs_7_.s2_ref.refs_1_, f32[4,320,128]{2,1,0:T(8,128)S(1)} %get-tuple-element.144.refs_8_.s3_ref.refs_2_, ...), custom_call_target="tpu_custom_call" | custom-call | bytes 7438336 | tf_op jit(solution)/shard_map/pallas_call | solution.py:29
  83.2 1.1 %collective-permute-done.32.refs_2_ = bf16[4,160,128]{2,1,0:T(8,128)(2,1)S(1)} collective-permute-done((bf16[4,160,128]{2,1,0:T(8,128)(2,1)S(1)}, bf16[4,160,128]{2,1,0:T(8,128)(2,1)S(1)}, u32[]{:S(2)}, u32[]{:S(2)}) %collective-permute-start.32) | collective-permute-done | bytes 163872 | tf_op jit(solution)/shard_map/ppermute | solution.py:447
  85.7 1.2 %collective-permute-start.30 = (bf16[4,160,128]{2,1,0:T(8,128)(2,1)S(1)}, bf16[4,160,128]{2,1,0:T(8,128)(2,1)S(1)}, u32[]{:S(2)}, u32[]{:S(2)}) collective-permute-start(bf16[4,160,128]{2,1,0:T(8,128)(2,1)S(1)} %get-tuple-element.224.refs_1_), channel_id=1, source_target_pairs={{0,8},{8,0},{16,24},{24,16},{1,9},{9,1},{17,25},{25,17},{2,10},{10... | collective-permute-start | bytes 491528 | tf_op jit(solution)/shard_map/ppermute | solution.py:428
  87.7 1.2 %collective-permute-start.39 = (bf16[4,160,128]{2,1,0:T(8,128)(2,1)S(1)}, bf16[4,160,128]{2,1,0:T(8,128)(2,1)S(1)}, u32[]{:S(2)}, u32[]{:S(2)}) collective-permute-start(bf16[4,160,128]{2,1,0:T(8,128)(2,1)S(1)} %get-tuple-element.241), channel_id=1, source_target_pairs={{1,2},{2,1},{3,4},{4,3},{5,6},{6,5},{0,8},{7,15},{9,10},{10,9},{11... | collective-permute-start | bytes 491528 | tf_op jit(solution)/shard_map/ppermute | solution.py:447
  88.9 2.8 %collective-permute-done.33.refs_2_ = bf16[4,160,128]{2,1,0:T(8,128)(2,1)S(1)} collective-permute-done((bf16[4,160,128]{2,1,0:T(8,128)(2,1)S(1)}, bf16[4,160,128]{2,1,0:T(8,128)(2,1)S(1)}, u32[]{:S(2)}, u32[]{:S(2)}) %collective-permute-start.33) | collective-permute-done | bytes 163872 | tf_op jit(solution)/shard_map/ppermute | solution.py:428
  91.9 1.3 %collective-permute-start.34 = (bf16[4,160,128]{2,1,0:T(8,128)(2,1)S(1)}, bf16[4,160,128]{2,1,0:T(8,128)(2,1)S(1)}, u32[]{:S(2)}, u32[]{:S(2)}) collective-permute-start(bf16[4,160,128]{2,1,0:T(8,128)(2,1)S(1)} %get-tuple-element.233), channel_id=1, source_target_pairs={{0,8},{8,0},{16,24},{24,16},{1,9},{9,1},{17,25},{25,17},{2,10},{10... | collective-permute-start | bytes 491528 | tf_op jit(solution)/shard_map/ppermute | solution.py:428
  93.1 1.2 %shard_map.150.refs_4_ = f32[4,320,128]{2,1,0:T(8,128)S(1)} custom-call(f32[4,336,128]{2,1,0:T(8,128)S(1)} %get-tuple-element.234.f_ref.refs_0_, bf16[384,256]{1,0:T(8,128)(2,1)S(1)} %copy-done, f32[4,320,128]{2,1,0:T(8,128)S(1)} %get-tuple-element.145.refs_9_.fdy_ref, f32[4,320,128]{2,1,0:T(8,128)S(1)} %get-tuple-element.146.refs_10_.fdz_ref, ...), custom_call_target="tpu_custom_call" | custom-call | bytes 3506176 | tf_op jit(solution)/shard_map/pallas_call | solution.py:29
  97.2 1.9 %collective-permute-start.40 = (bf16[4,160,128]{2,1,0:T(8,128)(2,1)S(1)}, bf16[4,160,128]{2,1,0:T(8,128)(2,1)S(1)}, u32[]{:S(2)}, u32[]{:S(2)}) collective-permute-start(bf16[4,160,128]{2,1,0:T(8,128)(2,1)S(1)} %shard_map.153.refs_1_), channel_id=1, source_target_pairs={{0,16},{8,24},{16,0},{24,8},{1,17},{9,25},{17,1},{25,9},{2,18},{10... | collective-permute-start | bytes 491528 | tf_op jit(solution)/shard_map/ppermute | solution.py:428
  99.1 1.2 %collective-permute-done.34 = bf16[4,160,128]{2,1,0:T(8,128)(2,1)S(1)} collective-permute-done((bf16[4,160,128]{2,1,0:T(8,128)(2,1)S(1)}, bf16[4,160,128]{2,1,0:T(8,128)(2,1)S(1)}, u32[]{:S(2)}, u32[]{:S(2)}) %collective-permute-start.34) | collective-permute-done | bytes 163872 | tf_op jit(solution)/shard_map/ppermute | solution.py:428
  100.4 2.1 %collective-permute-done.37.refs_2_ = bf16[4,160,128]{2,1,0:T(8,128)(2,1)S(1)} collective-permute-done((bf16[4,160,128]{2,1,0:T(8,128)(2,1)S(1)}, bf16[4,160,128]{2,1,0:T(8,128)(2,1)S(1)}, u32[]{:S(2)}, u32[]{:S(2)}) %collective-permute-start.37) | collective-permute-done | bytes 163872 | tf_op jit(solution)/shard_map/ppermute | solution.py:428
  102.7 1.5 %collective-permute-start.38 = (bf16[4,160,128]{2,1,0:T(8,128)(2,1)S(1)}, bf16[4,160,128]{2,1,0:T(8,128)(2,1)S(1)}, u32[]{:S(2)}, u32[]{:S(2)}) collective-permute-start(bf16[4,160,128]{2,1,0:T(8,128)(2,1)S(1)} %get-tuple-element.240), channel_id=1, source_target_pairs={{0,16},{8,24},{16,0},{24,8},{1,17},{9,25},{17,1},{25,9},{2,18},{10... | collective-permute-start | bytes 491528 | tf_op jit(solution)/shard_map/ppermute | solution.py:428
  105.3 1.3 %collective-permute-start.41 = (bf16[4,160,128]{2,1,0:T(8,128)(2,1)S(1)}, bf16[4,160,128]{2,1,0:T(8,128)(2,1)S(1)}, u32[]{:S(2)}, u32[]{:S(2)}) collective-permute-start(bf16[4,160,128]{2,1,0:T(8,128)(2,1)S(1)} %get-tuple-element.243), channel_id=1, source_target_pairs={{0,8},{8,0},{16,24},{24,16},{1,9},{9,1},{17,25},{25,17},{2,10},{10... | collective-permute-start | bytes 491528 | tf_op jit(solution)/shard_map/ppermute | solution.py:428
  106.6 1.4 %collective-permute-done.38 = bf16[4,160,128]{2,1,0:T(8,128)(2,1)S(1)} collective-permute-done((bf16[4,160,128]{2,1,0:T(8,128)(2,1)S(1)}, bf16[4,160,128]{2,1,0:T(8,128)(2,1)S(1)}, u32[]{:S(2)}, u32[]{:S(2)}) %collective-permute-start.38) | collective-permute-done | bytes 163872 | tf_op jit(solution)/shard_map/ppermute | solution.py:428
  108.1 2.6 %collective-permute-done.41 = bf16[4,160,128]{2,1,0:T(8,128)(2,1)S(1)} collective-permute-done((bf16[4,160,128]{2,1,0:T(8,128)(2,1)S(1)}, bf16[4,160,128]{2,1,0:T(8,128)(2,1)S(1)}, u32[]{:S(2)}, u32[]{:S(2)}) %collective-permute-start.41) | collective-permute-done | bytes 163872 | tf_op jit(solution)/shard_map/ppermute | solution.py:428
  (104 shorter events, 28.8 us)
Async XLA Ops:
  0.6 5.7 %copy-start.8 = (bf16[1,4,320,128]{3,2,1,0:T(8,128)(2,1)S(1)}, bf16[1,4,320,128]{3,2,1,0:T(8,128)(2,1)}, u32[]{:S(2)}) copy-start(bf16[1,4,320,128]{3,2,1,0:T(8,128)(2,1)} %param.10) | copy-start | bytes 983044
  0.6 7.0 %copy-start.3 = (f32[1,4,320,128]{3,2,1,0:T(8,128)S(1)}, f32[1,4,320,128]{3,2,1,0:T(8,128)}, u32[]{:S(2)}) copy-start(f32[1,4,320,128]{3,2,1,0:T(8,128)} %param.15) | copy-start | bytes 1966084
  1.8 8.0 %collective-permute-start.1 = (bf16[2,320,128]{2,1,0:T(8,128)(2,1)S(1)}, bf16[2,320,128]{2,1,0:T(8,128)(2,1)S(1)}, u32[]{:S(2)}, u32[]{:S(2)}) collective-permute-start(bf16[2,320,128]{2,1,0:T(8,128)(2,1)S(1)} %get-tuple-element.129.refs_3_.refs_4_), channel_id=1, source_target_pairs={{0,16},{8,24},{16,0},{24,8},{1,17},{9,25},{17,1},{25,9},{2,18},{10... | collective-permute-start | bytes 491528 | tf_op jit(solution)/shard_map/ppermute | solution.py:428
  4.8 7.1 %collective-permute-start = (bf16[2,320,128]{2,1,0:T(8,128)(2,1)S(1)}, bf16[2,320,128]{2,1,0:T(8,128)(2,1)S(1)}, u32[]{:S(2)}, u32[]{:S(2)}) collective-permute-start(bf16[2,320,128]{2,1,0:T(8,128)(2,1)S(1)} %get-tuple-element.127.refs_1_), channel_id=1, source_target_pairs={{0,8},{8,0},{16,24},{24,16},{1,9},{9,1},{17,25},{25,17},{2,10},{10... | collective-permute-start | bytes 491528 | tf_op jit(solution)/shard_map/ppermute | solution.py:428
  6.3 8.0 %collective-permute-start.9 = (bf16[2,320,128]{2,1,0:T(8,128)(2,1)S(1)}, bf16[2,320,128]{2,1,0:T(8,128)(2,1)S(1)}, u32[]{:S(2)}, u32[]{:S(2)}) collective-permute-start(bf16[2,320,128]{2,1,0:T(8,128)(2,1)S(1)} %get-tuple-element.244.refs_3_.refs_4_), channel_id=1, source_target_pairs={{0,16},{8,24},{16,0},{24,8},{1,17},{9,25},{17,1},{25,9},{2,18},{10... | collective-permute-start | bytes 491528 | tf_op jit(solution)/shard_map/ppermute | solution.py:428
  6.9 8.5 %collective-permute-start.8 = (bf16[2,320,128]{2,1,0:T(8,128)(2,1)S(1)}, bf16[2,320,128]{2,1,0:T(8,128)(2,1)S(1)}, u32[]{:S(2)}, u32[]{:S(2)}) collective-permute-start(bf16[2,320,128]{2,1,0:T(8,128)(2,1)S(1)} %get-tuple-element.245.refs_1_), channel_id=1, source_target_pairs={{0,8},{8,0},{16,24},{24,16},{1,9},{9,1},{17,25},{25,17},{2,10},{10... | collective-permute-start | bytes 491528 | tf_op jit(solution)/shard_map/ppermute | solution.py:428
  12.2 7.0 %collective-permute-start.4 = (bf16[2,320,128]{2,1,0:T(8,128)(2,1)S(1)}, bf16[2,320,128]{2,1,0:T(8,128)(2,1)S(1)}, u32[]{:S(2)}, u32[]{:S(2)}) collective-permute-start(bf16[2,320,128]{2,1,0:T(8,128)(2,1)S(1)} %get-tuple-element.131), channel_id=1, source_target_pairs={{0,16},{8,24},{16,0},{24,8},{1,17},{9,25},{17,1},{25,9},{2,18},{10... | collective-permute-start | bytes 491528 | tf_op jit(solution)/shard_map/ppermute | solution.py:428
  12.3 6.9 %collective-permute-start.5 = (bf16[2,320,128]{2,1,0:T(8,128)(2,1)S(1)}, bf16[2,320,128]{2,1,0:T(8,128)(2,1)S(1)}, u32[]{:S(2)}, u32[]{:S(2)}) collective-permute-start(bf16[2,320,128]{2,1,0:T(8,128)(2,1)S(1)} %get-tuple-element.132), channel_id=1, source_target_pairs={{0,8},{8,0},{16,24},{24,16},{1,9},{9,1},{17,25},{25,17},{2,10},{10... | collective-permute-start | bytes 491528 | tf_op jit(solution)/shard_map/ppermute | solution.py:428
  15.7 15.8 %copy-start = (bf16[384,256]{1,0:T(8,128)(2,1)S(1)}, bf16[384,256]{1,0:T(8,128)(2,1)}, u32[]{:S(2)}) copy-start(bf16[384,256]{1,0:T(8,128)(2,1)} %constant.2.clone.matrix_ref.refs_3_) | copy-start | bytes 589828
  15.8 9.2 %collective-permute-start.10 = (bf16[2,320,128]{2,1,0:T(8,128)(2,1)S(1)}, bf16[2,320,128]{2,1,0:T(8,128)(2,1)S(1)}, u32[]{:S(2)}, u32[]{:S(2)}) collective-permute-start(bf16[2,320,128]{2,1,0:T(8,128)(2,1)S(1)} %get-tuple-element.136), channel_id=1, source_target_pairs={{0,16},{8,24},{16,0},{24,8},{1,17},{9,25},{17,1},{25,9},{2,18},{10... | collective-permute-start | bytes 491528 | tf_op jit(solution)/shard_map/ppermute | solution.py:428
  19.7 13.2 %copy-start.1 = (f32[1,4,320,128]{3,2,1,0:T(8,128)S(1)}, f32[1,4,320,128]{3,2,1,0:T(8,128)}, u32[]{:S(2)}) copy-start(f32[1,4,320,128]{3,2,1,0:T(8,128)} %param.16) | copy-start | bytes 1966084
  19.7 15.0 %collective-permute-start.6 = (bf16[4,320,128]{2,1,0:T(8,128)(2,1)S(1)}, bf16[4,320,128]{2,1,0:T(8,128)(2,1)S(1)}, u32[]{:S(2)}, u32[]{:S(2)}) collective-permute-start(bf16[4,320,128]{2,1,0:T(8,128)(2,1)S(1)} %get-tuple-element.133.den_ref.refs_6_), channel_id=1, source_target_pairs={{0,1},{1,0},{2,3},{3,2},{4,5},{5,4},{6,7},{7,6},{8,9},{9,8},{10,11... | collective-permute-start | bytes 983048 | tf_op jit(solution)/shard_map/ppermute | solution.py:433
  19.8 15.3 %collective-permute-start.3 = (bf16[4,320,128]{2,1,0:T(8,128)(2,1)S(1)}, bf16[4,320,128]{2,1,0:T(8,128)(2,1)S(1)}, u32[]{:S(2)}, u32[]{:S(2)}) collective-permute-start(bf16[4,320,128]{2,1,0:T(8,128)(2,1)S(1)} %get-tuple-element.125), channel_id=1, source_target_pairs={{1,2},{2,1},{3,4},{4,3},{5,6},{6,5},{0,7},{7,0},{9,10},{10,9},{11,... | collective-permute-start | bytes 983048 | tf_op jit(solution)/shard_map/ppermute | solution.py:447
  23.5 11.6 %collective-permute-start.2 = (bf16[4,320,128]{2,1,0:T(8,128)(2,1)S(1)}, bf16[4,320,128]{2,1,0:T(8,128)(2,1)S(1)}, u32[]{:S(2)}, u32[]{:S(2)}) collective-permute-start(bf16[4,320,128]{2,1,0:T(8,128)(2,1)S(1)} %get-tuple-element.125), channel_id=1, source_target_pairs={{0,1},{1,0},{2,3},{3,2},{4,5},{5,4},{6,7},{7,6},{8,9},{9,8},{10,11... | collective-permute-start | bytes 983048 | tf_op jit(solution)/shard_map/ppermute | solution.py:433
  23.5 6.6 %collective-permute-start.11 = (bf16[2,320,128]{2,1,0:T(8,128)(2,1)S(1)}, bf16[2,320,128]{2,1,0:T(8,128)(2,1)S(1)}, u32[]{:S(2)}, u32[]{:S(2)}) collective-permute-start(bf16[2,320,128]{2,1,0:T(8,128)(2,1)S(1)} %get-tuple-element.137), channel_id=1, source_target_pairs={{0,8},{8,0},{16,24},{24,16},{1,9},{9,1},{17,25},{25,17},{2,10},{10... | collective-permute-start | bytes 491528 | tf_op jit(solution)/shard_map/ppermute | solution.py:428
  25.0 9.7 %collective-permute-start.12 = (bf16[4,160,128]{2,1,0:T(8,128)(2,1)S(1)}, bf16[4,160,128]{2,1,0:T(8,128)(2,1)S(1)}, u32[]{:S(2)}, u32[]{:S(2)}) collective-permute-start(bf16[4,160,128]{2,1,0:T(8,128)(2,1)S(1)} %get-tuple-element.138), channel_id=1, source_target_pairs={{1,2},{2,1},{3,4},{4,3},{5,6},{6,5},{0,8},{7,15},{9,10},{10,9},{11... | collective-permute-start | bytes 491528 | tf_op jit(solution)/shard_map/ppermute | solution.py:447
  30.1 5.5 %collective-permute-start.7 = (bf16[4,160,128]{2,1,0:T(8,128)(2,1)S(1)}, bf16[4,160,128]{2,1,0:T(8,128)(2,1)S(1)}, u32[]{:S(2)}, u32[]{:S(2)}) collective-permute-start(bf16[4,160,128]{2,1,0:T(8,128)(2,1)S(1)} %get-tuple-element.135), channel_id=1, source_target_pairs={{1,2},{2,1},{3,4},{4,3},{5,6},{6,5},{0,8},{7,15},{9,10},{10,9},{11... | collective-permute-start | bytes 491528 | tf_op jit(solution)/shard_map/ppermute | solution.py:447
  36.6 5.5 %collective-permute-start.13 = (bf16[4,320,128]{2,1,0:T(8,128)(2,1)S(1)}, bf16[4,320,128]{2,1,0:T(8,128)(2,1)S(1)}, u32[]{:S(2)}, u32[]{:S(2)}) collective-permute-start(bf16[4,320,128]{2,1,0:T(8,128)(2,1)S(1)} %get-tuple-element.152), channel_id=1, source_target_pairs={{0,1},{1,0},{2,3},{3,2},{4,5},{5,4},{6,7},{7,6},{8,9},{9,8},{10,11... | collective-permute-start | bytes 983048 | tf_op jit(solution)/shard_map/ppermute | solution.py:433
  36.6 5.4 %collective-permute-start.15 = (bf16[4,160,128]{2,1,0:T(8,128)(2,1)S(1)}, bf16[4,160,128]{2,1,0:T(8,128)(2,1)S(1)}, u32[]{:S(2)}, u32[]{:S(2)}) collective-permute-start(bf16[4,160,128]{2,1,0:T(8,128)(2,1)S(1)} %get-tuple-element.155), channel_id=1, source_target_pairs={{1,2},{2,1},{3,4},{4,3},{5,6},{6,5},{0,8},{7,15},{9,10},{10,9},{11... | collective-permute-start | bytes 491528 | tf_op jit(solution)/shard_map/ppermute | solution.py:447
  37.9 5.8 %collective-permute-start.14 = (bf16[4,160,128]{2,1,0:T(8,128)(2,1)S(1)}, bf16[4,160,128]{2,1,0:T(8,128)(2,1)S(1)}, u32[]{:S(2)}, u32[]{:S(2)}) collective-permute-start(bf16[4,160,128]{2,1,0:T(8,128)(2,1)S(1)} %get-tuple-element.153), channel_id=1, source_target_pairs={{1,2},{2,1},{3,4},{4,3},{5,6},{6,5},{0,8},{7,15},{9,10},{10,9},{11... | collective-permute-start | bytes 491528 | tf_op jit(solution)/shard_map/ppermute | solution.py:447
  44.3 5.5 %collective-permute-start.16 = (bf16[4,320,128]{2,1,0:T(8,128)(2,1)S(1)}, bf16[4,320,128]{2,1,0:T(8,128)(2,1)S(1)}, u32[]{:S(2)}, u32[]{:S(2)}) collective-permute-start(bf16[4,320,128]{2,1,0:T(8,128)(2,1)S(1)} %get-tuple-element.161), channel_id=1, source_target_pairs={{0,1},{1,0},{2,3},{3,2},{4,5},{5,4},{6,7},{7,6},{8,9},{9,8},{10,11... | collective-permute-start | bytes 983048 | tf_op jit(solution)/shard_map/ppermute | solution.py:433
  44.4 5.3 %collective-permute-start.18 = (bf16[4,160,128]{2,1,0:T(8,128)(2,1)S(1)}, bf16[4,160,128]{2,1,0:T(8,128)(2,1)S(1)}, u32[]{:S(2)}, u32[]{:S(2)}) collective-permute-start(bf16[4,160,128]{2,1,0:T(8,128)(2,1)S(1)} %get-tuple-element.164), channel_id=1, source_target_pairs={{1,2},{2,1},{3,4},{4,3},{5,6},{6,5},{0,8},{7,15},{9,10},{10,9},{11... | collective-permute-start | bytes 491528 | tf_op jit(solution)/shard_map/ppermute | solution.py:447
  45.7 5.8 %collective-permute-start.17 = (bf16[4,160,128]{2,1,0:T(8,128)(2,1)S(1)}, bf16[4,160,128]{2,1,0:T(8,128)(2,1)S(1)}, u32[]{:S(2)}, u32[]{:S(2)}) collective-permute-start(bf16[4,160,128]{2,1,0:T(8,128)(2,1)S(1)} %get-tuple-element.162), channel_id=1, source_target_pairs={{1,2},{2,1},{3,4},{4,3},{5,6},{6,5},{0,8},{7,15},{9,10},{10,9},{11... | collective-permute-start | bytes 491528 | tf_op jit(solution)/shard_map/ppermute | solution.py:447
  51.5 3.2 %copy-start.4 = (f32[1,4,320,128]{3,2,1,0:T(8,128)S(1)}, f32[1,4,320,128]{3,2,1,0:T(8,128)}, u32[]{:S(2)}) copy-start(f32[1,4,320,128]{3,2,1,0:T(8,128)} %param.17) | copy-start | bytes 1966084
  52.0 2.2 %copy-start.7 = (s32[1,512]{1,0:T(1,128)S(1)}, s32[1,512]{1,0:T(1,128)}, u32[]{:S(2)}) copy-start(s32[1,512]{1,0:T(1,128)} %rec.1) | copy-start | bytes 6148
  52.0 5.5 %collective-permute-start.19 = (bf16[4,320,128]{2,1,0:T(8,128)(2,1)S(1)}, bf16[4,320,128]{2,1,0:T(8,128)(2,1)S(1)}, u32[]{:S(2)}, u32[]{:S(2)}) collective-permute-start(bf16[4,320,128]{2,1,0:T(8,128)(2,1)S(1)} %get-tuple-element.170), channel_id=1, source_target_pairs={{0,1},{1,0},{2,3},{3,2},{4,5},{5,4},{6,7},{7,6},{8,9},{9,8},{10,11... | collective-permute-start | bytes 983048 | tf_op jit(solution)/shard_map/ppermute | solution.py:433
  52.2 5.3 %collective-permute-start.21 = (bf16[4,160,128]{2,1,0:T(8,128)(2,1)S(1)}, bf16[4,160,128]{2,1,0:T(8,128)(2,1)S(1)}, u32[]{:S(2)}, u32[]{:S(2)}) collective-permute-start(bf16[4,160,128]{2,1,0:T(8,128)(2,1)S(1)} %get-tuple-element.173), channel_id=1, source_target_pairs={{1,2},{2,1},{3,4},{4,3},{5,6},{6,5},{0,8},{7,15},{9,10},{10,9},{11... | collective-permute-start | bytes 491528 | tf_op jit(solution)/shard_map/ppermute | solution.py:447
  53.4 5.8 %collective-permute-start.20 = (bf16[4,160,128]{2,1,0:T(8,128)(2,1)S(1)}, bf16[4,160,128]{2,1,0:T(8,128)(2,1)S(1)}, u32[]{:S(2)}, u32[]{:S(2)}) collective-permute-start(bf16[4,160,128]{2,1,0:T(8,128)(2,1)S(1)} %get-tuple-element.171), channel_id=1, source_target_pairs={{1,2},{2,1},{3,4},{4,3},{5,6},{6,5},{0,8},{7,15},{9,10},{10,9},{11... | collective-permute-start | bytes 491528 | tf_op jit(solution)/shard_map/ppermute | solution.py:447
  61.6 5.8 %collective-permute-start.22 = (bf16[4,320,128]{2,1,0:T(8,128)(2,1)S(1)}, bf16[4,320,128]{2,1,0:T(8,128)(2,1)S(1)}, u32[]{:S(2)}, u32[]{:S(2)}) collective-permute-start(bf16[4,320,128]{2,1,0:T(8,128)(2,1)S(1)} %get-tuple-element.179), channel_id=1, source_target_pairs={{0,1},{1,0},{2,3},{3,2},{4,5},{5,4},{6,7},{7,6},{8,9},{9,8},{10,11... | collective-permute-start | bytes 983048 | tf_op jit(solution)/shard_map/ppermute | solution.py:433
  61.6 5.7 %collective-permute-start.24 = (bf16[4,160,128]{2,1,0:T(8,128)(2,1)S(1)}, bf16[4,160,128]{2,1,0:T(8,128)(2,1)S(1)}, u32[]{:S(2)}, u32[]{:S(2)}) collective-permute-start(bf16[4,160,128]{2,1,0:T(8,128)(2,1)S(1)} %get-tuple-element.188), channel_id=1, source_target_pairs={{1,2},{2,1},{3,4},{4,3},{5,6},{6,5},{0,8},{7,15},{9,10},{10,9},{11... | collective-permute-start | bytes 491528 | tf_op jit(solution)/shard_map/ppermute | solution.py:447
  63.0 5.8 %collective-permute-start.23 = (bf16[4,160,128]{2,1,0:T(8,128)(2,1)S(1)}, bf16[4,160,128]{2,1,0:T(8,128)(2,1)S(1)}, u32[]{:S(2)}, u32[]{:S(2)}) collective-permute-start(bf16[4,160,128]{2,1,0:T(8,128)(2,1)S(1)} %get-tuple-element.180), channel_id=1, source_target_pairs={{1,2},{2,1},{3,4},{4,3},{5,6},{6,5},{0,8},{7,15},{9,10},{10,9},{11... | collective-permute-start | bytes 491528 | tf_op jit(solution)/shard_map/ppermute | solution.py:447
  69.3 5.5 %collective-permute-start.25 = (bf16[4,320,128]{2,1,0:T(8,128)(2,1)S(1)}, bf16[4,320,128]{2,1,0:T(8,128)(2,1)S(1)}, u32[]{:S(2)}, u32[]{:S(2)}) collective-permute-start(bf16[4,320,128]{2,1,0:T(8,128)(2,1)S(1)} %get-tuple-element.194), channel_id=1, source_target_pairs={{0,1},{1,0},{2,3},{3,2},{4,5},{5,4},{6,7},{7,6},{8,9},{9,8},{10,11... | collective-permute-start | bytes 983048 | tf_op jit(solution)/shard_map/ppermute | solution.py:433
  69.5 5.3 %collective-permute-start.27 = (bf16[4,160,128]{2,1,0:T(8,128)(2,1)S(1)}, bf16[4,160,128]{2,1,0:T(8,128)(2,1)S(1)}, u32[]{:S(2)}, u32[]{:S(2)}) collective-permute-start(bf16[4,160,128]{2,1,0:T(8,128)(2,1)S(1)} %get-tuple-element.205), channel_id=1, source_target_pairs={{1,2},{2,1},{3,4},{4,3},{5,6},{6,5},{0,8},{7,15},{9,10},{10,9},{11... | collective-permute-start | bytes 491528 | tf_op jit(solution)/shard_map/ppermute | solution.py:447
  70.7 5.9 %collective-permute-start.26 = (bf16[4,160,128]{2,1,0:T(8,128)(2,1)S(1)}, bf16[4,160,128]{2,1,0:T(8,128)(2,1)S(1)}, u32[]{:S(2)}, u32[]{:S(2)}) collective-permute-start(bf16[4,160,128]{2,1,0:T(8,128)(2,1)S(1)} %get-tuple-element.195), channel_id=1, source_target_pairs={{1,2},{2,1},{3,4},{4,3},{5,6},{6,5},{0,8},{7,15},{9,10},{10,9},{11... | collective-permute-start | bytes 491528 | tf_op jit(solution)/shard_map/ppermute | solution.py:447
  77.1 5.5 %collective-permute-start.28 = (bf16[4,320,128]{2,1,0:T(8,128)(2,1)S(1)}, bf16[4,320,128]{2,1,0:T(8,128)(2,1)S(1)}, u32[]{:S(2)}, u32[]{:S(2)}) collective-permute-start(bf16[4,320,128]{2,1,0:T(8,128)(2,1)S(1)} %get-tuple-element.211), channel_id=1, source_target_pairs={{0,1},{1,0},{2,3},{3,2},{4,5},{5,4},{6,7},{7,6},{8,9},{9,8},{10,11... | collective-permute-start | bytes 983048 | tf_op jit(solution)/shard_map/ppermute | solution.py:433
  77.3 5.3 %collective-permute-start.29 = (bf16[4,160,128]{2,1,0:T(8,128)(2,1)S(1)}, bf16[4,160,128]{2,1,0:T(8,128)(2,1)S(1)}, u32[]{:S(2)}, u32[]{:S(2)}) collective-permute-start(bf16[4,160,128]{2,1,0:T(8,128)(2,1)S(1)} %get-tuple-element.212), channel_id=1, source_target_pairs={{1,2},{2,1},{3,4},{4,3},{5,6},{6,5},{0,8},{7,15},{9,10},{10,9},{11... | collective-permute-start | bytes 491528 | tf_op jit(solution)/shard_map/ppermute | solution.py:447
  78.5 5.9 %collective-permute-start.32 = (bf16[4,160,128]{2,1,0:T(8,128)(2,1)S(1)}, bf16[4,160,128]{2,1,0:T(8,128)(2,1)S(1)}, u32[]{:S(2)}, u32[]{:S(2)}) collective-permute-start(bf16[4,160,128]{2,1,0:T(8,128)(2,1)S(1)} %get-tuple-element.227), channel_id=1, source_target_pairs={{1,2},{2,1},{3,4},{4,3},{5,6},{6,5},{0,8},{7,15},{9,10},{10,9},{11... | collective-permute-start | bytes 491528 | tf_op jit(solution)/shard_map/ppermute | solution.py:447
  85.0 10.2 %collective-permute-start.35 = (bf16[4,320,128]{2,1,0:T(8,128)(2,1)S(1)}, bf16[4,320,128]{2,1,0:T(8,128)(2,1)S(1)}, u32[]{:S(2)}, u32[]{:S(2)}) collective-permute-start(bf16[4,320,128]{2,1,0:T(8,128)(2,1)S(1)} %get-tuple-element.235), channel_id=1, source_target_pairs={{0,1},{1,0},{2,3},{3,2},{4,5},{5,4},{6,7},{7,6},{8,9},{9,8},{10,11... | collective-permute-start | bytes 983048 | tf_op jit(solution)/shard_map/ppermute | solution.py:433
  85.1 6.5 %collective-permute-start.33 = (bf16[4,160,128]{2,1,0:T(8,128)(2,1)S(1)}, bf16[4,160,128]{2,1,0:T(8,128)(2,1)S(1)}, u32[]{:S(2)}, u32[]{:S(2)}) collective-permute-start(bf16[4,160,128]{2,1,0:T(8,128)(2,1)S(1)} %get-tuple-element.231.refs_1_), channel_id=1, source_target_pairs={{0,16},{8,24},{16,0},{24,8},{1,17},{9,25},{17,1},{25,9},{2,18},{10... | collective-permute-start | bytes 491528 | tf_op jit(solution)/shard_map/ppermute | solution.py:428
  85.7 8.7 %collective-permute-start.30 = (bf16[4,160,128]{2,1,0:T(8,128)(2,1)S(1)}, bf16[4,160,128]{2,1,0:T(8,128)(2,1)S(1)}, u32[]{:S(2)}, u32[]{:S(2)}) collective-permute-start(bf16[4,160,128]{2,1,0:T(8,128)(2,1)S(1)} %get-tuple-element.224.refs_1_), channel_id=1, source_target_pairs={{0,8},{8,0},{16,24},{24,16},{1,9},{9,1},{17,25},{25,17},{2,10},{10... | collective-permute-start | bytes 491528 | tf_op jit(solution)/shard_map/ppermute | solution.py:428
  86.9 8.3 %collective-permute-start.36 = (bf16[4,160,128]{2,1,0:T(8,128)(2,1)S(1)}, bf16[4,160,128]{2,1,0:T(8,128)(2,1)S(1)}, u32[]{:S(2)}, u32[]{:S(2)}) collective-permute-start(bf16[4,160,128]{2,1,0:T(8,128)(2,1)S(1)} %get-tuple-element.236), channel_id=1, source_target_pairs={{1,2},{2,1},{3,4},{4,3},{5,6},{6,5},{0,8},{7,15},{9,10},{10,9},{11... | collective-permute-start | bytes 491528 | tf_op jit(solution)/shard_map/ppermute | solution.py:447
  87.7 9.1 %collective-permute-start.39 = (bf16[4,160,128]{2,1,0:T(8,128)(2,1)S(1)}, bf16[4,160,128]{2,1,0:T(8,128)(2,1)S(1)}, u32[]{:S(2)}, u32[]{:S(2)}) collective-permute-start(bf16[4,160,128]{2,1,0:T(8,128)(2,1)S(1)} %get-tuple-element.241), channel_id=1, source_target_pairs={{1,2},{2,1},{3,4},{4,3},{5,6},{6,5},{0,8},{7,15},{9,10},{10,9},{11... | collective-permute-start | bytes 491528 | tf_op jit(solution)/shard_map/ppermute | solution.py:447
  91.9 8.5 %collective-permute-start.34 = (bf16[4,160,128]{2,1,0:T(8,128)(2,1)S(1)}, bf16[4,160,128]{2,1,0:T(8,128)(2,1)S(1)}, u32[]{:S(2)}, u32[]{:S(2)}) collective-permute-start(bf16[4,160,128]{2,1,0:T(8,128)(2,1)S(1)} %get-tuple-element.233), channel_id=1, source_target_pairs={{0,8},{8,0},{16,24},{24,16},{1,9},{9,1},{17,25},{25,17},{2,10},{10... | collective-permute-start | bytes 491528 | tf_op jit(solution)/shard_map/ppermute | solution.py:428
  94.6 9.6 %collective-permute-start.31 = (bf16[4,160,128]{2,1,0:T(8,128)(2,1)S(1)}, bf16[4,160,128]{2,1,0:T(8,128)(2,1)S(1)}, u32[]{:S(2)}, u32[]{:S(2)}) collective-permute-start(bf16[4,160,128]{2,1,0:T(8,128)(2,1)S(1)} %get-tuple-element.226), channel_id=1, source_target_pairs={{0,16},{8,24},{16,0},{24,8},{1,17},{9,25},{17,1},{25,9},{2,18},{10... | collective-permute-start | bytes 491528 | tf_op jit(solution)/shard_map/ppermute | solution.py:428
  95.5 6.9 %collective-permute-start.37 = (bf16[4,160,128]{2,1,0:T(8,128)(2,1)S(1)}, bf16[4,160,128]{2,1,0:T(8,128)(2,1)S(1)}, u32[]{:S(2)}, u32[]{:S(2)}) collective-permute-start(bf16[4,160,128]{2,1,0:T(8,128)(2,1)S(1)} %shard_map.151.refs_1_), channel_id=1, source_target_pairs={{0,8},{8,0},{16,24},{24,16},{1,9},{9,1},{17,25},{25,17},{2,10},{10... | collective-permute-start | bytes 491528 | tf_op jit(solution)/shard_map/ppermute | solution.py:428
  97.2 7.9 %collective-permute-start.40 = (bf16[4,160,128]{2,1,0:T(8,128)(2,1)S(1)}, bf16[4,160,128]{2,1,0:T(8,128)(2,1)S(1)}, u32[]{:S(2)}, u32[]{:S(2)}) collective-permute-start(bf16[4,160,128]{2,1,0:T(8,128)(2,1)S(1)} %shard_map.153.refs_1_), channel_id=1, source_target_pairs={{0,16},{8,24},{16,0},{24,8},{1,17},{9,25},{17,1},{25,9},{2,18},{10... | collective-permute-start | bytes 491528 | tf_op jit(solution)/shard_map/ppermute | solution.py:428
  102.7 5.4 %collective-permute-start.38 = (bf16[4,160,128]{2,1,0:T(8,128)(2,1)S(1)}, bf16[4,160,128]{2,1,0:T(8,128)(2,1)S(1)}, u32[]{:S(2)}, u32[]{:S(2)}) collective-permute-start(bf16[4,160,128]{2,1,0:T(8,128)(2,1)S(1)} %get-tuple-element.240), channel_id=1, source_target_pairs={{0,16},{8,24},{16,0},{24,8},{1,17},{9,25},{17,1},{25,9},{2,18},{10... | collective-permute-start | bytes 491528 | tf_op jit(solution)/shard_map/ppermute | solution.py:428
  105.3 5.4 %collective-permute-start.41 = (bf16[4,160,128]{2,1,0:T(8,128)(2,1)S(1)}, bf16[4,160,128]{2,1,0:T(8,128)(2,1)S(1)}, u32[]{:S(2)}, u32[]{:S(2)}) collective-permute-start(bf16[4,160,128]{2,1,0:T(8,128)(2,1)S(1)} %get-tuple-element.243), channel_id=1, source_target_pairs={{0,8},{8,0},{16,24},{24,16},{1,9},{9,1},{17,25},{25,17},{2,10},{10... | collective-permute-start | bytes 491528 | tf_op jit(solution)/shard_map/ppermute | solution.py:428
  (3 other events, 3.0 us)

commit v7 on v6

--- a/solution.py
+++ b/solution.py
@@ -13,6 +13,7 @@
 SECOND = (-205.0 / 72.0, 8.0 / 5.0, -1.0 / 5.0, 8.0 / 315.0, -1.0 / 560.0)
 FIRST = (4.0 / 5.0, -1.0 / 5.0, 4.0 / 105.0, -1.0 / 280.0)
 SPEED = 0.15
+SHOT, SUB = "shot", "sub"
 PAD = 8
 PARTS = 2
 UNROLL = 4
@@ -79,7 +80,7 @@
 
 
 def where_am_i():
-    column, columns = lax.axis_index("sub"), lax.axis_size("sub")
+    column, columns = lax.axis_index(SUB), lax.axis_size(SUB)
     even = (column & 1) == 0
     valid = jnp.logical_and(column > 0, column < columns - 1)
     return even, valid
@@ -136,7 +137,7 @@
 def list_kernel(rec_ref, layers, width, depth, list_ref):
     total = rec_ref.shape[1]
     cells = layers * width * depth
-    local = rec_ref[...] - lax.axis_index("sub") * cells
+    local = rec_ref[...] - lax.axis_index(SUB) * cells
     inside = jnp.logical_and(local >= 0, local < cells)
     line = lax.shift_right_arithmetic(local, depth.bit_length() - 1)
     row = line + PAD
@@ -165,8 +166,8 @@
     list_ref[3:4, :] = jnp.where(number < count, listed[0:1], depth)
 
 
-def add_receivers(n, field_ref, into_ref, list_ref, observed_ref):
-    depth = field_ref.shape[1]
+def add_receivers(jobs, list_ref, observed_ref):
+    depth = jobs[0][1].shape[1]
     lane = lax.broadcasted_iota(jnp.int32, (1, depth), 1)
     count = list_ref[2, 0]
 
@@ -175,25 +176,32 @@
         rows, terms = [], []
         for k in range(UNROLL):
             row = list_ref[0, c * UNROLL + k]
-            spot = list_ref[3, c * UNROLL + k]
-            seen = observed_ref[n, list_ref[1, c * UNROLL + k]]
+            number = list_ref[1, c * UNROLL + k]
+            here = lane == list_ref[3, c * UNROLL + k]
             rows.append(row)
-            terms.append(jnp.where(lane == spot, field_ref[pl.ds(row, 1), :] - seen, 0.0))
-        for row, term in zip(rows, terms):
-            into_ref[pl.ds(row, 1), :] += term
+            terms.append(
+                [
+                    jnp.where(here, field_ref[pl.ds(row, 1), :] - observed_ref[n, number], 0.0)
+                    for n, field_ref, _ in jobs
+                ]
+            )
+        for row, parts in zip(rows, terms):
+            for (_, _, into_ref), term in zip(jobs, parts):
+                into_ref[pl.ds(row, 1), :] += term
 
 
 def receivers_kernel(first, *refs):
     count = (len(refs) - 2) // 2
     fields, (list_ref, observed_ref), outs = refs[:count], refs[count : count + 2], refs[count + 2 :]
-    for n, (field_ref, source_ref) in enumerate(zip(fields, outs)):
+    for source_ref in outs:
         source_ref[...] = jnp.zeros(source_ref.shape, F32)
-        add_receivers(first + n, field_ref, source_ref, list_ref, observed_ref)
+    steps = range(first, first + count)
+    add_receivers(list(zip(steps, fields, outs)), list_ref, observed_ref)
 
 
 def first_adjoint_kernel(n, p_ref, q_ref, list_ref, observed_ref, a_ref, half_ref, *part_refs):
     a_ref[...] = q_ref[...]
-    add_receivers(n, p_ref, a_ref, list_ref, observed_ref)
+    add_receivers([(n, p_ref, a_ref)], list_ref, observed_ref)
     layers, width, _ = half_ref.shape
     tall = width + 2 * PAD
 
@@ -429,12 +437,12 @@
 
 
 def paired(half):
-    count = lax.axis_size("sub")
-    return lax.ppermute(half, "sub", [(i, i ^ 1) for i in range(count)])
+    count = lax.axis_size(SUB)
+    return lax.ppermute(half, SUB, [(i, i ^ 1) for i in range(count)])
 
 
 def across(half, ring=False):
-    groups, count = lax.axis_size("shot"), lax.axis_size("sub")
+    groups, count = lax.axis_size(SHOT), lax.axis_size(SUB)
     pairs = []
     for s in range(groups):
         for i in range(1, count - 1, 2):
@@ -444,7 +452,7 @@
         elif groups % 2 == 0:
             for i in (0, count - 1):
                 pairs.append((s * count + i, (s ^ 1) * count + i))
-    return lax.ppermute(half, ("shot", "sub"), pairs)
+    return lax.ppermute(half, (SHOT, SUB), pairs)
 
 
 def bits_of(groups):
@@ -452,27 +460,29 @@
 
 
 def routes_kernel(cover_ref, out_ref):
-    column = lax.axis_index("sub")
+    column = lax.axis_index(SUB)
     for g in range(out_ref.shape[0]):
         out_ref[g, :, :] = jnp.full(out_ref.shape[1:], cover_ref[g, column], jnp.int32)
 
 
 def masked_sum(out_ref, first, terms):
     layers, width, _ = terms[0][1].shape
-
-    @pl.loop(0, width // 16)
-    def _(j):
-        rows = pl.ds(pl.multiple_of(16 * j, 16), 16)
-        for l in range(layers):
-            total = None
-            for mask, ref in terms:
-                term = jnp.where(mask, ref[l, rows, :].astype(F32), 0.0)
-                total = term if total is None else total + term
-            out_ref[first + l, rows, :] = total.astype(out_ref.dtype)
+    tiles = next(n for n in (4, 2, 1) if width % (16 * n) == 0)
+
+    @pl.loop(0, width // (16 * tiles))
+    def _(j):
+        for n in range(tiles):
+            rows = pl.ds(pl.multiple_of(16 * tiles * j + 16 * n, 16), 16)
+            for l in range(layers):
+                total = None
+                for mask, ref in terms:
+                    term = jnp.where(mask, ref[l, rows, :].astype(F32), 0.0)
+                    total = term if total is None else total + term
+                out_ref[first + l, rows, :] = total.astype(out_ref.dtype)
 
 
 def pick_kernel(offsets, bits, route_ref, *refs):
-    me = lax.axis_index("shot")
+    me = lax.axis_index(SHOT)
     outs = refs[-2:]
     count = len(refs) // 2 - 1
     for way in range(2):
@@ -482,7 +492,7 @@
 
 
 def gather_kernel(offsets, bits, parts, route_ref, *refs):
-    me = lax.axis_index("shot")
+    me = lax.axis_index(SHOT)
     part_refs = refs[len(refs) - parts :]
     refs = refs[: len(refs) - parts]
     out_ref = refs[-1]
@@ -510,7 +520,7 @@
         for way in range(2):
             bit = ways[way][stage]
             block = jnp.concatenate(held[way], axis=0) if len(held[way]) > 1 else held[way][0]
-            got = swap_over("shot", groups, bit, block)
+            got = swap_over(SHOT, groups, bit, block)
             held[way] = held[way] + [
                 lax.slice_in_dim(got, n * layers, (n + 1) * layers, axis=0)
                 for n in range(len(held[way]))
@@ -522,7 +532,7 @@
         lambda *refs: pick_kernel(offsets, last, *refs),
         [(small, BF16)] * 2, [route, *held[0], *held[1]],
     )
-    far = [swap_over("shot", groups, last[way], sends[way]) for way in range(2)]
+    far = [swap_over(SHOT, groups, last[way], sends[way]) for way in range(2)]
     part_shape = (tile.shape[0], tile.shape[1] // PARTS, tile.shape[2])
     return call(
         lambda *refs: gather_kernel(offsets, last, parts, *refs),
@@ -531,7 +541,7 @@
 
 
 def bucket_kernel(offsets, bit, route_ref, own_ref, got_ref, *outs):
-    me = lax.axis_index("shot")
+    me = lax.axis_index(SHOT)
     mine, theirs = route_ref[me], route_ref[me ^ bit]
     for offset, out in zip(offsets, outs):
         row = me ^ offset
@@ -542,7 +552,7 @@
     groups = route.shape[0]
     layers = part.shape[0]
     bits = bits_of(groups)[:: 1 if way == 0 else -1]
-    got = swap_over("shot", groups, bits[0], part)
+    got = swap_over(SHOT, groups, bits[0], part)
     offsets = [0]
     for b in reversed(bits[1:]):
         offsets = offsets + [o ^ b for o in offsets]
@@ -555,7 +565,7 @@
     for b in bits[1:]:
         away = [o for o in left if o & b]
         block = jnp.concatenate([left[o].astype(BF16) for o in away], axis=0)
-        came = swap_over("shot", groups, b, block)
+        came = swap_over(SHOT, groups, b, block)
         left = {
             o ^ b: left[o ^ b] + came[n * layers : (n + 1) * layers].astype(F32)
             for n, o in enumerate(away)
@@ -698,11 +708,11 @@
 
 
 def solution(mesh):
-    spec = P("shot", "sub", None, None)
+    spec = P(SHOT, SUB, None, None)
     return jax.shard_map(
         inner,
         mesh=mesh,
-        in_specs=(spec, spec, P(), P("shot", None), P("shot", None, None), spec, spec, spec, spec),
+        in_specs=(spec, spec, P(), P(SHOT, None), P(SHOT, None, None), spec, spec, spec, spec),
         out_specs=(spec, spec),
         check_vma=False,
     )

time: 112 us -> 111 us (level)
  Pallas kernels: 30.4 us -> 29.1 us
    pallas_call x42, Pallas kernels: 30.4 us -> 29.1 us  [call(): pl.pallas_call(kernel, out_shape=outs, in_specs=list(specs or [VM] * len(...]
  transfers between devices with their start and end apart: 42 -> 42, of which waited for: 22 -> 23; matrix products, arithmetic and copies ran while one was open for 1% -> 1% of each run, Pallas kernels for 22% -> 21%
where the time goes in v7:
time: 111 us
  starting transfers between devices  39.8 us (36%)
  waiting for transfers between devices  37.7 us (34%)
  Pallas kernels  29.1 us (26%)
  other arithmetic  1.88 us (2%)
  local copies, waits for them, and re-layouts  1.37 us (1%)
  between operations  1.14 us (1%)
    pallas_call x42, Pallas kernels, call(): pl.pallas_call(kernel, out_shape=outs, in_specs=list(specs or [VM] * len(...  29.1 us
    ppermute x16, waiting for transfers between devices, swap_over(): return lax.ppermute(value, axis, [(i, i ^ bit) for i in range(count)])  22.9 us
    ppermute x17, starting transfers between devices, across(): return lax.ppermute(half, (SHOT, SUB), pairs)  20 us
    ppermute x16, starting transfers between devices, swap_over(): return lax.ppermute(value, axis, [(i, i ^ bit) for i in range(count)])  18.6 us
    ppermute x17, waiting for transfers between devices, across(): return lax.ppermute(half, (SHOT, SUB), pairs)  14.8 us
  transfers between devices with their start and end apart: 42, of which 23 were waited for; matrix products, arithmetic and copies ran while one was open for 1% of the time, Pallas kernels for 21%

profile of v7, /device:TPU:0, one launch (start us, length us, event | category | flops | bytes accessed | tf_op | source)
XLA Modules:
  0.0 111.0 jit_solution(11094652740984101415)
XLA Ops:
  1.8 3.1 %collective-permute-start.1 = (bf16[2,320,128]{2,1,0:T(8,128)(2,1)S(1)}, bf16[2,320,128]{2,1,0:T(8,128)(2,1)S(1)}, u32[]{:S(2)}, u32[]{:S(2)}) collective-permute-start(bf16[2,320,128]{2,1,0:T(8,128)(2,1)S(1)} %get-tuple-element.129.refs_3_.refs_4_), channel_id=1, source_target_pairs={{0,16},{8,24},{16,0},{24,8},{1,17},{9,25},{17,1},{25,9},{2,18},{10... | collective-permute-start | bytes 491528 | tf_op jit(solution)/shard_map/ppermute | solution.py:436
  4.8 1.5 %collective-permute-start = (bf16[2,320,128]{2,1,0:T(8,128)(2,1)S(1)}, bf16[2,320,128]{2,1,0:T(8,128)(2,1)S(1)}, u32[]{:S(2)}, u32[]{:S(2)}) collective-permute-start(bf16[2,320,128]{2,1,0:T(8,128)(2,1)S(1)} %get-tuple-element.127.refs_1_), channel_id=1, source_target_pairs={{0,8},{8,0},{16,24},{24,16},{1,9},{9,1},{17,25},{25,17},{2,10},{10... | collective-permute-start | bytes 491528 | tf_op jit(solution)/shard_map/ppermute | solution.py:436
  7.8 2.0 %collective-permute-done.1.refs_4_.refs_5_ = bf16[2,320,128]{2,1,0:T(8,128)(2,1)S(1)} collective-permute-done((bf16[2,320,128]{2,1,0:T(8,128)(2,1)S(1)}, bf16[2,320,128]{2,1,0:T(8,128)(2,1)S(1)}, u32[]{:S(2)}, u32[]{:S(2)}) %collective-permute-start.1) | collective-permute-done | bytes 163872 | tf_op jit(solution)/shard_map/ppermute | solution.py:436
  9.7 2.1 %collective-permute-done.refs_2_ = bf16[2,320,128]{2,1,0:T(8,128)(2,1)S(1)} collective-permute-done((bf16[2,320,128]{2,1,0:T(8,128)(2,1)S(1)}, bf16[2,320,128]{2,1,0:T(8,128)(2,1)S(1)}, u32[]{:S(2)}, u32[]{:S(2)}) %collective-permute-start) | collective-permute-done | bytes 163872 | tf_op jit(solution)/shard_map/ppermute | solution.py:436
  12.1 2.0 %collective-permute-start.5 = (bf16[2,320,128]{2,1,0:T(8,128)(2,1)S(1)}, bf16[2,320,128]{2,1,0:T(8,128)(2,1)S(1)}, u32[]{:S(2)}, u32[]{:S(2)}) collective-permute-start(bf16[2,320,128]{2,1,0:T(8,128)(2,1)S(1)} %get-tuple-element.132), channel_id=1, source_target_pairs={{0,8},{8,0},{16,24},{24,16},{1,9},{9,1},{17,25},{25,17},{2,10},{10... | collective-permute-start | bytes 491528 | tf_op jit(solution)/shard_map/ppermute | solution.py:436
  14.1 1.3 %collective-permute-done.8.refs_2_ = bf16[2,320,128]{2,1,0:T(8,128)(2,1)S(1)} collective-permute-done((bf16[2,320,128]{2,1,0:T(8,128)(2,1)S(1)}, bf16[2,320,128]{2,1,0:T(8,128)(2,1)S(1)}, u32[]{:S(2)}, u32[]{:S(2)}) %collective-permute-start.8) | collective-permute-done | bytes 163872 | tf_op jit(solution)/shard_map/ppermute | solution.py:436
  15.9 3.1 %collective-permute-done.4.refs_3_ = bf16[2,320,128]{2,1,0:T(8,128)(2,1)S(1)} collective-permute-done((bf16[2,320,128]{2,1,0:T(8,128)(2,1)S(1)}, bf16[2,320,128]{2,1,0:T(8,128)(2,1)S(1)}, u32[]{:S(2)}, u32[]{:S(2)}) %collective-permute-start.4) | collective-permute-done | bytes 163872 | tf_op jit(solution)/shard_map/ppermute | solution.py:436
  19.4 3.7 %collective-permute-start.3 = (bf16[4,320,128]{2,1,0:T(8,128)(2,1)S(1)}, bf16[4,320,128]{2,1,0:T(8,128)(2,1)S(1)}, u32[]{:S(2)}, u32[]{:S(2)}) collective-permute-start(bf16[4,320,128]{2,1,0:T(8,128)(2,1)S(1)} %get-tuple-element.125), channel_id=1, source_target_pairs={{1,2},{2,1},{3,4},{4,3},{5,6},{6,5},{0,7},{7,0},{9,10},{10,9},{11,... | collective-permute-start | bytes 983048 | tf_op jit(solution)/shard_map/ppermute | solution.py:455
  23.1 1.5 %collective-permute-start.11 = (bf16[2,320,128]{2,1,0:T(8,128)(2,1)S(1)}, bf16[2,320,128]{2,1,0:T(8,128)(2,1)S(1)}, u32[]{:S(2)}, u32[]{:S(2)}) collective-permute-start(bf16[2,320,128]{2,1,0:T(8,128)(2,1)S(1)} %get-tuple-element.137), channel_id=1, source_target_pairs={{0,8},{8,0},{16,24},{24,16},{1,9},{9,1},{17,25},{25,17},{2,10},{10... | collective-permute-start | bytes 491528 | tf_op jit(solution)/shard_map/ppermute | solution.py:436
  25.2 4.6 %collective-permute-done.11.refs_6_ = bf16[2,320,128]{2,1,0:T(8,128)(2,1)S(1)} collective-permute-done((bf16[2,320,128]{2,1,0:T(8,128)(2,1)S(1)}, bf16[2,320,128]{2,1,0:T(8,128)(2,1)S(1)}, u32[]{:S(2)}, u32[]{:S(2)}) %collective-permute-start.11) | collective-permute-done | bytes 163872 | tf_op jit(solution)/shard_map/ppermute | solution.py:436
  29.7 1.5 %collective-permute-start.7 = (bf16[4,160,128]{2,1,0:T(8,128)(2,1)S(1)}, bf16[4,160,128]{2,1,0:T(8,128)(2,1)S(1)}, u32[]{:S(2)}, u32[]{:S(2)}) collective-permute-start(bf16[4,160,128]{2,1,0:T(8,128)(2,1)S(1)} %get-tuple-element.135), channel_id=1, source_target_pairs={{1,2},{2,1},{3,4},{4,3},{5,6},{6,5},{0,8},{7,15},{9,10},{10,9},{11... | collective-permute-start | bytes 491528 | tf_op jit(solution)/shard_map/ppermute | solution.py:455
  31.2 1.3 %shard_map.115 = (f32[4,320,128]{2,1,0:T(8,128)S(1)}, f32[4,320,128]{2,1,0:T(8,128)S(1)}, f32[4,320,128]{2,1,0:T(8,128)S(1)}) custom-call(f32[4,336,128]{2,1,0:T(8,128)S(1)} %get-tuple-element.124.f_ref.refs_0_.refs_6_, bf16[384,256]{1,0:T(8,128)(2,1)S(1)} %copy-done), custom_call_target="tpu_custom_call" | custom-call | bytes 2850816 | tf_op jit(solution)/shard_map/pallas_call | solution.py:30
  32.5 1.3 %shard_map.118 = (f32[4,336,128]{2,1,0:T(8,128)S(1)}, f32[4,320,128]{2,1,0:T(8,128)S(1)}, f32[4,320,128]{2,1,0:T(8,128)S(1)}) custom-call(bf16[4,320,128]{2,1,0:T(8,128)(2,1)S(1)} %get-tuple-element.133.den_ref.refs_6_, bf16[384,256]{1,0:T(8,128)(2,1)S(1)} %copy-done, f32[4,320,128]{2,1,0:T(8,128)S(1)} %bitcast.35), custom_call_target="tpu_custom_call" | custom-call | bytes 3178496 | tf_op jit(solution)/shard_map/pallas_call | solution.py:30
  36.1 1.5 %collective-permute-start.15 = (bf16[4,160,128]{2,1,0:T(8,128)(2,1)S(1)}, bf16[4,160,128]{2,1,0:T(8,128)(2,1)S(1)}, u32[]{:S(2)}, u32[]{:S(2)}) collective-permute-start(bf16[4,160,128]{2,1,0:T(8,128)(2,1)S(1)} %get-tuple-element.155), channel_id=1, source_target_pairs={{1,2},{2,1},{3,4},{4,3},{5,6},{6,5},{0,8},{7,15},{9,10},{10,9},{11... | collective-permute-start | bytes 491528 | tf_op jit(solution)/shard_map/ppermute | solution.py:455
  38.2 1.4 %shard_map.125 = (f32[4,320,128]{2,1,0:T(8,128)S(1)}, f32[4,320,128]{2,1,0:T(8,128)S(1)}, f32[4,320,128]{2,1,0:T(8,128)S(1)}) custom-call(f32[4,336,128]{2,1,0:T(8,128)S(1)} %get-tuple-element.151.f_ref.refs_0_.refs_6_, f32[4,320,128]{2,1,0:T(8,128)S(1)} %get-tuple-element.143.refs_7_.s2_ref.refs_1_, ...), custom_call_target="tpu_custom_call" | custom-call | bytes 4161536 | tf_op jit(solution)/shard_map/pallas_call | solution.py:30
  39.6 1.9 %collective-permute-done.15.refs_2_ = bf16[4,160,128]{2,1,0:T(8,128)(2,1)S(1)} collective-permute-done((bf16[4,160,128]{2,1,0:T(8,128)(2,1)S(1)}, bf16[4,160,128]{2,1,0:T(8,128)(2,1)S(1)}, u32[]{:S(2)}, u32[]{:S(2)}) %collective-permute-start.15) | collective-permute-done | bytes 163872 | tf_op jit(solution)/shard_map/ppermute | solution.py:455
  42.0 1.3 %collective-permute-done.14.refs_2_ = bf16[4,160,128]{2,1,0:T(8,128)(2,1)S(1)} collective-permute-done((bf16[4,160,128]{2,1,0:T(8,128)(2,1)S(1)}, bf16[4,160,128]{2,1,0:T(8,128)(2,1)S(1)}, u32[]{:S(2)}, u32[]{:S(2)}) %collective-permute-start.14) | collective-permute-done | bytes 163872 | tf_op jit(solution)/shard_map/ppermute | solution.py:455
  43.9 1.4 %collective-permute-start.18 = (bf16[4,160,128]{2,1,0:T(8,128)(2,1)S(1)}, bf16[4,160,128]{2,1,0:T(8,128)(2,1)S(1)}, u32[]{:S(2)}, u32[]{:S(2)}) collective-permute-start(bf16[4,160,128]{2,1,0:T(8,128)(2,1)S(1)} %get-tuple-element.164), channel_id=1, source_target_pairs={{1,2},{2,1},{3,4},{4,3},{5,6},{6,5},{0,8},{7,15},{9,10},{10,9},{11... | collective-permute-start | bytes 491528 | tf_op jit(solution)/shard_map/ppermute | solution.py:455
  45.9 1.4 %shard_map.128 = (f32[4,320,128]{2,1,0:T(8,128)S(1)}, f32[4,320,128]{2,1,0:T(8,128)S(1)}, f32[4,320,128]{2,1,0:T(8,128)S(1)}) custom-call(f32[4,336,128]{2,1,0:T(8,128)S(1)} %get-tuple-element.160.f_ref.refs_0_.refs_6_, f32[4,320,128]{2,1,0:T(8,128)S(1)} %get-tuple-element.143.refs_7_.s2_ref.refs_1_, ...), custom_call_target="tpu_custom_call" | custom-call | bytes 4161536 | tf_op jit(solution)/shard_map/pallas_call | solution.py:30
  47.4 1.9 %collective-permute-done.18.refs_2_ = bf16[4,160,128]{2,1,0:T(8,128)(2,1)S(1)} collective-permute-done((bf16[4,160,128]{2,1,0:T(8,128)(2,1)S(1)}, bf16[4,160,128]{2,1,0:T(8,128)(2,1)S(1)}, u32[]{:S(2)}, u32[]{:S(2)}) %collective-permute-start.18) | collective-permute-done | bytes 163872 | tf_op jit(solution)/shard_map/ppermute | solution.py:455
  49.7 1.3 %collective-permute-done.17.refs_2_ = bf16[4,160,128]{2,1,0:T(8,128)(2,1)S(1)} collective-permute-done((bf16[4,160,128]{2,1,0:T(8,128)(2,1)S(1)}, bf16[4,160,128]{2,1,0:T(8,128)(2,1)S(1)}, u32[]{:S(2)}, u32[]{:S(2)}) %collective-permute-start.17) | collective-permute-done | bytes 163872 | tf_op jit(solution)/shard_map/ppermute | solution.py:455
  51.7 1.4 %collective-permute-start.21 = (bf16[4,160,128]{2,1,0:T(8,128)(2,1)S(1)}, bf16[4,160,128]{2,1,0:T(8,128)(2,1)S(1)}, u32[]{:S(2)}, u32[]{:S(2)}) collective-permute-start(bf16[4,160,128]{2,1,0:T(8,128)(2,1)S(1)} %get-tuple-element.173), channel_id=1, source_target_pairs={{1,2},{2,1},{3,4},{4,3},{5,6},{6,5},{0,8},{7,15},{9,10},{10,9},{11... | collective-permute-start | bytes 491528 | tf_op jit(solution)/shard_map/ppermute | solution.py:455
  54.3 1.4 %shard_map.131 = (f32[4,320,128]{2,1,0:T(8,128)S(1)}, f32[4,320,128]{2,1,0:T(8,128)S(1)}, f32[4,320,128]{2,1,0:T(8,128)S(1)}) custom-call(f32[4,336,128]{2,1,0:T(8,128)S(1)} %get-tuple-element.169.f_ref.refs_0_, f32[4,320,128]{2,1,0:T(8,128)S(1)} %get-tuple-element.143.refs_7_.s2_ref.refs_1_, f32[4,320,128]{2,1,0:T(8,128)S(1)} %get-tuple-element.144.refs_8_.s3_ref.refs_2_, ...), custom_call_target="tpu_custom_call" | custom-call | bytes 4161536 | tf_op jit(solution)/shard_map/pallas_call | solution.py:30
  55.7 1.3 %collective-permute-done.21.refs_2_ = bf16[4,160,128]{2,1,0:T(8,128)(2,1)S(1)} collective-permute-done((bf16[4,160,128]{2,1,0:T(8,128)(2,1)S(1)}, bf16[4,160,128]{2,1,0:T(8,128)(2,1)S(1)}, u32[]{:S(2)}, u32[]{:S(2)}) %collective-permute-start.21) | collective-permute-done | bytes 163872 | tf_op jit(solution)/shard_map/ppermute | solution.py:455
  57.5 1.3 %collective-permute-done.20.refs_2_ = bf16[4,160,128]{2,1,0:T(8,128)(2,1)S(1)} collective-permute-done((bf16[4,160,128]{2,1,0:T(8,128)(2,1)S(1)}, bf16[4,160,128]{2,1,0:T(8,128)(2,1)S(1)}, u32[]{:S(2)}, u32[]{:S(2)}) %collective-permute-start.20) | collective-permute-done | bytes 163872 | tf_op jit(solution)/shard_map/ppermute | solution.py:455
  59.4 1.6 %shard_map.136 = (f32[1344,128]{1,0:T(8,128)S(1)}, bf16[4,320,128]{2,1,0:T(8,128)(2,1)S(1)}, bf16[4,160,128]{2,1,0:T(8,128)(2,1)S(1)}, bf16[4,160,128]{2,1,0:T(8,128)(2,1)S(1)}) custom-call(f32[1344,128]{1,0:T(8,128)S(1)} %bitcast.38, f32[1344,128]{1,0:T(8,128)S(1)} %bitcast.29, s32[4,512]{1,0:T(4,128)S(1)} %shard_map.135.refs_2_.refs_1_, f32[4,512]{1,0:T(4,128)S(1)} %bitcast.47), custom_call_target="tpu_custom_call" | custom-call | bytes 2736128 | tf_op jit(solution)/shard_map/pallas_call | solution.py:30
  61.1 1.5 %collective-permute-start.24 = (bf16[4,160,128]{2,1,0:T(8,128)(2,1)S(1)}, bf16[4,160,128]{2,1,0:T(8,128)(2,1)S(1)}, u32[]{:S(2)}, u32[]{:S(2)}) collective-permute-start(bf16[4,160,128]{2,1,0:T(8,128)(2,1)S(1)} %get-tuple-element.188), channel_id=1, source_target_pairs={{1,2},{2,1},{3,4},{4,3},{5,6},{6,5},{0,8},{7,15},{9,10},{10,9},{11... | collective-permute-start | bytes 491528 | tf_op jit(solution)/shard_map/ppermute | solution.py:455
  63.2 1.7 %shard_map.138 = (f32[1344,128]{1,0:T(8,128)S(1)}, f32[1344,128]{1,0:T(8,128)S(1)}) custom-call(f32[1344,128]{1,0:T(8,128)S(1)} %bitcast.27, f32[1344,128]{1,0:T(8,128)S(1)} %bitcast.28, s32[4,512]{1,0:T(4,128)S(1)} %shard_map.135.refs_2_.refs_1_, f32[4,512]{1,0:T(4,128)S(1)} %bitcast.48), custom_call_target="tpu_custom_call" | custom-call | bytes 2768896 | tf_op jit(solution)/shard_map/pallas_call | solution.py:30
  64.9 1.5 %shard_map.137 = (f32[4,320,128]{2,1,0:T(8,128)S(1)}, f32[4,320,128]{2,1,0:T(8,128)S(1)}, f32[4,320,128]{2,1,0:T(8,128)S(1)}) custom-call(f32[4,336,128]{2,1,0:T(8,128)S(1)} %bitcast.32, f32[4,320,128]{2,1,0:T(8,128)S(1)} %get-tuple-element.143.refs_7_.s2_ref.refs_1_, f32[4,320,128]{2,1,0:T(8,128)S(1)} %get-tuple-element.144.refs_8_.s3_ref.refs_2_, ...), custom_call_target="tpu_custom_call" | custom-call | bytes 6127616 | tf_op jit(solution)/shard_map/pallas_call | solution.py:30
  68.9 1.4 %collective-permute-start.27 = (bf16[4,160,128]{2,1,0:T(8,128)(2,1)S(1)}, bf16[4,160,128]{2,1,0:T(8,128)(2,1)S(1)}, u32[]{:S(2)}, u32[]{:S(2)}) collective-permute-start(bf16[4,160,128]{2,1,0:T(8,128)(2,1)S(1)} %get-tuple-element.205), channel_id=1, source_target_pairs={{1,2},{2,1},{3,4},{4,3},{5,6},{6,5},{0,8},{7,15},{9,10},{10,9},{11... | collective-permute-start | bytes 491528 | tf_op jit(solution)/shard_map/ppermute | solution.py:455
  71.0 1.6 %shard_map.141 = (f32[4,320,128]{2,1,0:T(8,128)S(1)}, f32[4,320,128]{2,1,0:T(8,128)S(1)}, f32[4,320,128]{2,1,0:T(8,128)S(1)}) custom-call(f32[4,336,128]{2,1,0:T(8,128)S(1)} %get-tuple-element.193.refs_0_, f32[4,320,128]{2,1,0:T(8,128)S(1)} %get-tuple-element.143.refs_7_.s2_ref.refs_1_, f32[4,320,128]{2,1,0:T(8,128)S(1)} %get-tuple-element.144.refs_8_.s3_ref.refs_2_, ...), custom_call_target="tpu_custom_call" | custom-call | bytes 7438336 | tf_op jit(solution)/shard_map/pallas_call | solution.py:30
  72.6 1.7 %collective-permute-done.27.refs_2_ = bf16[4,160,128]{2,1,0:T(8,128)(2,1)S(1)} collective-permute-done((bf16[4,160,128]{2,1,0:T(8,128)(2,1)S(1)}, bf16[4,160,128]{2,1,0:T(8,128)(2,1)S(1)}, u32[]{:S(2)}, u32[]{:S(2)}) %collective-permute-start.27) | collective-permute-done | bytes 163872 | tf_op jit(solution)/shard_map/ppermute | solution.py:455
  74.8 1.2 %collective-permute-done.26.refs_2_ = bf16[4,160,128]{2,1,0:T(8,128)(2,1)S(1)} collective-permute-done((bf16[4,160,128]{2,1,0:T(8,128)(2,1)S(1)}, bf16[4,160,128]{2,1,0:T(8,128)(2,1)S(1)}, u32[]{:S(2)}, u32[]{:S(2)}) %collective-permute-start.26) | collective-permute-done | bytes 163872 | tf_op jit(solution)/shard_map/ppermute | solution.py:455
  76.7 1.4 %collective-permute-start.29 = (bf16[4,160,128]{2,1,0:T(8,128)(2,1)S(1)}, bf16[4,160,128]{2,1,0:T(8,128)(2,1)S(1)}, u32[]{:S(2)}, u32[]{:S(2)}) collective-permute-start(bf16[4,160,128]{2,1,0:T(8,128)(2,1)S(1)} %get-tuple-element.212), channel_id=1, source_target_pairs={{1,2},{2,1},{3,4},{4,3},{5,6},{6,5},{0,8},{7,15},{9,10},{10,9},{11... | collective-permute-start | bytes 491528 | tf_op jit(solution)/shard_map/ppermute | solution.py:455
  78.8 1.4 %shard_map.145 = f32[1344,128]{1,0:T(8,128)S(1)} custom-call(f32[1344,128]{1,0:T(8,128)S(1)} %bitcast.26, s32[4,512]{1,0:T(4,128)S(1)} %shard_map.135.refs_2_.refs_1_, f32[4,512]{1,0:T(4,128)S(1)} %bitcast.49), custom_call_target="tpu_custom_call" | custom-call | bytes 1392640 | tf_op jit(solution)/shard_map/pallas_call | solution.py:30
  80.2 1.6 %shard_map.144 = (f32[4,320,128]{2,1,0:T(8,128)S(1)}, f32[4,320,128]{2,1,0:T(8,128)S(1)}, f32[4,320,128]{2,1,0:T(8,128)S(1)}) custom-call(f32[4,336,128]{2,1,0:T(8,128)S(1)} %get-tuple-element.210.refs_0_, f32[4,320,128]{2,1,0:T(8,128)S(1)} %get-tuple-element.143.refs_7_.s2_ref.refs_1_, f32[4,320,128]{2,1,0:T(8,128)S(1)} %get-tuple-element.144.refs_8_.s3_ref.refs_2_, ...), custom_call_target="tpu_custom_call" | custom-call | bytes 7438336 | tf_op jit(solution)/shard_map/pallas_call | solution.py:30
  85.2 1.3 %collective-permute-start.30 = (bf16[4,160,128]{2,1,0:T(8,128)(2,1)S(1)}, bf16[4,160,128]{2,1,0:T(8,128)(2,1)S(1)}, u32[]{:S(2)}, u32[]{:S(2)}) collective-permute-start(bf16[4,160,128]{2,1,0:T(8,128)(2,1)S(1)} %get-tuple-element.224.refs_1_), channel_id=1, source_target_pairs={{0,8},{8,0},{16,24},{24,16},{1,9},{9,1},{17,25},{25,17},{2,10},{10... | collective-permute-start | bytes 491528 | tf_op jit(solution)/shard_map/ppermute | solution.py:436
  87.2 1.3 %collective-permute-start.39 = (bf16[4,160,128]{2,1,0:T(8,128)(2,1)S(1)}, bf16[4,160,128]{2,1,0:T(8,128)(2,1)S(1)}, u32[]{:S(2)}, u32[]{:S(2)}) collective-permute-start(bf16[4,160,128]{2,1,0:T(8,128)(2,1)S(1)} %get-tuple-element.241), channel_id=1, source_target_pairs={{1,2},{2,1},{3,4},{4,3},{5,6},{6,5},{0,8},{7,15},{9,10},{10,9},{11... | collective-permute-start | bytes 491528 | tf_op jit(solution)/shard_map/ppermute | solution.py:455
  88.5 2.6 %collective-permute-done.33.refs_2_ = bf16[4,160,128]{2,1,0:T(8,128)(2,1)S(1)} collective-permute-done((bf16[4,160,128]{2,1,0:T(8,128)(2,1)S(1)}, bf16[4,160,128]{2,1,0:T(8,128)(2,1)S(1)}, u32[]{:S(2)}, u32[]{:S(2)}) %collective-permute-start.33) | collective-permute-done | bytes 163872 | tf_op jit(solution)/shard_map/ppermute | solution.py:436
  91.3 1.5 %collective-permute-start.34 = (bf16[4,160,128]{2,1,0:T(8,128)(2,1)S(1)}, bf16[4,160,128]{2,1,0:T(8,128)(2,1)S(1)}, u32[]{:S(2)}, u32[]{:S(2)}) collective-permute-start(bf16[4,160,128]{2,1,0:T(8,128)(2,1)S(1)} %get-tuple-element.233), channel_id=1, source_target_pairs={{0,8},{8,0},{16,24},{24,16},{1,9},{9,1},{17,25},{25,17},{2,10},{10... | collective-permute-start | bytes 491528 | tf_op jit(solution)/shard_map/ppermute | solution.py:436
  92.7 1.2 %shard_map.150.refs_4_ = f32[4,320,128]{2,1,0:T(8,128)S(1)} custom-call(f32[4,336,128]{2,1,0:T(8,128)S(1)} %get-tuple-element.234.f_ref.refs_0_, bf16[384,256]{1,0:T(8,128)(2,1)S(1)} %copy-done, f32[4,320,128]{2,1,0:T(8,128)S(1)} %get-tuple-element.145.refs_9_.fdy_ref, f32[4,320,128]{2,1,0:T(8,128)S(1)} %get-tuple-element.146.refs_10_.fdz_ref, ...), custom_call_target="tpu_custom_call" | custom-call | bytes 3506176 | tf_op jit(solution)/shard_map/pallas_call | solution.py:30
  96.7 1.9 %collective-permute-start.40 = (bf16[4,160,128]{2,1,0:T(8,128)(2,1)S(1)}, bf16[4,160,128]{2,1,0:T(8,128)(2,1)S(1)}, u32[]{:S(2)}, u32[]{:S(2)}) collective-permute-start(bf16[4,160,128]{2,1,0:T(8,128)(2,1)S(1)} %shard_map.153.refs_1_), channel_id=1, source_target_pairs={{0,16},{8,24},{16,0},{24,8},{1,17},{9,25},{17,1},{25,9},{2,18},{10... | collective-permute-start | bytes 491528 | tf_op jit(solution)/shard_map/ppermute | solution.py:436
  98.5 1.3 %collective-permute-done.34 = bf16[4,160,128]{2,1,0:T(8,128)(2,1)S(1)} collective-permute-done((bf16[4,160,128]{2,1,0:T(8,128)(2,1)S(1)}, bf16[4,160,128]{2,1,0:T(8,128)(2,1)S(1)}, u32[]{:S(2)}, u32[]{:S(2)}) %collective-permute-start.34) | collective-permute-done | bytes 163872 | tf_op jit(solution)/shard_map/ppermute | solution.py:436
  99.9 2.0 %collective-permute-done.37.refs_2_ = bf16[4,160,128]{2,1,0:T(8,128)(2,1)S(1)} collective-permute-done((bf16[4,160,128]{2,1,0:T(8,128)(2,1)S(1)}, bf16[4,160,128]{2,1,0:T(8,128)(2,1)S(1)}, u32[]{:S(2)}, u32[]{:S(2)}) %collective-permute-start.37) | collective-permute-done | bytes 163872 | tf_op jit(solution)/shard_map/ppermute | solution.py:436
  102.1 1.5 %collective-permute-start.38 = (bf16[4,160,128]{2,1,0:T(8,128)(2,1)S(1)}, bf16[4,160,128]{2,1,0:T(8,128)(2,1)S(1)}, u32[]{:S(2)}, u32[]{:S(2)}) collective-permute-start(bf16[4,160,128]{2,1,0:T(8,128)(2,1)S(1)} %get-tuple-element.240), channel_id=1, source_target_pairs={{0,16},{8,24},{16,0},{24,8},{1,17},{9,25},{17,1},{25,9},{2,18},{10... | collective-permute-start | bytes 491528 | tf_op jit(solution)/shard_map/ppermute | solution.py:436
  104.7 1.5 %collective-permute-start.41 = (bf16[4,160,128]{2,1,0:T(8,128)(2,1)S(1)}, bf16[4,160,128]{2,1,0:T(8,128)(2,1)S(1)}, u32[]{:S(2)}, u32[]{:S(2)}) collective-permute-start(bf16[4,160,128]{2,1,0:T(8,128)(2,1)S(1)} %get-tuple-element.243), channel_id=1, source_target_pairs={{0,8},{8,0},{16,24},{24,16},{1,9},{9,1},{17,25},{25,17},{2,10},{10... | collective-permute-start | bytes 491528 | tf_op jit(solution)/shard_map/ppermute | solution.py:436
  106.2 1.3 %collective-permute-done.38 = bf16[4,160,128]{2,1,0:T(8,128)(2,1)S(1)} collective-permute-done((bf16[4,160,128]{2,1,0:T(8,128)(2,1)S(1)}, bf16[4,160,128]{2,1,0:T(8,128)(2,1)S(1)}, u32[]{:S(2)}, u32[]{:S(2)}) %collective-permute-start.38) | collective-permute-done | bytes 163872 | tf_op jit(solution)/shard_map/ppermute | solution.py:436
  107.5 2.6 %collective-permute-done.41 = bf16[4,160,128]{2,1,0:T(8,128)(2,1)S(1)} collective-permute-done((bf16[4,160,128]{2,1,0:T(8,128)(2,1)S(1)}, bf16[4,160,128]{2,1,0:T(8,128)(2,1)S(1)}, u32[]{:S(2)}, u32[]{:S(2)}) %collective-permute-start.41) | collective-permute-done | bytes 163872 | tf_op jit(solution)/shard_map/ppermute | solution.py:436
  (104 shorter events, 26.8 us)
Async XLA Ops:
  0.6 5.7 %copy-start.8 = (bf16[1,4,320,128]{3,2,1,0:T(8,128)(2,1)S(1)}, bf16[1,4,320,128]{3,2,1,0:T(8,128)(2,1)}, u32[]{:S(2)}) copy-start(bf16[1,4,320,128]{3,2,1,0:T(8,128)(2,1)} %param.10) | copy-start | bytes 983044
  0.6 7.0 %copy-start.3 = (f32[1,4,320,128]{3,2,1,0:T(8,128)S(1)}, f32[1,4,320,128]{3,2,1,0:T(8,128)}, u32[]{:S(2)}) copy-start(f32[1,4,320,128]{3,2,1,0:T(8,128)} %param.15) | copy-start | bytes 1966084
  1.8 8.0 %collective-permute-start.1 = (bf16[2,320,128]{2,1,0:T(8,128)(2,1)S(1)}, bf16[2,320,128]{2,1,0:T(8,128)(2,1)S(1)}, u32[]{:S(2)}, u32[]{:S(2)}) collective-permute-start(bf16[2,320,128]{2,1,0:T(8,128)(2,1)S(1)} %get-tuple-element.129.refs_3_.refs_4_), channel_id=1, source_target_pairs={{0,16},{8,24},{16,0},{24,8},{1,17},{9,25},{17,1},{25,9},{2,18},{10... | collective-permute-start | bytes 491528 | tf_op jit(solution)/shard_map/ppermute | solution.py:436
  4.8 7.1 %collective-permute-start = (bf16[2,320,128]{2,1,0:T(8,128)(2,1)S(1)}, bf16[2,320,128]{2,1,0:T(8,128)(2,1)S(1)}, u32[]{:S(2)}, u32[]{:S(2)}) collective-permute-start(bf16[2,320,128]{2,1,0:T(8,128)(2,1)S(1)} %get-tuple-element.127.refs_1_), channel_id=1, source_target_pairs={{0,8},{8,0},{16,24},{24,16},{1,9},{9,1},{17,25},{25,17},{2,10},{10... | collective-permute-start | bytes 491528 | tf_op jit(solution)/shard_map/ppermute | solution.py:436
  6.3 7.8 %collective-permute-start.9 = (bf16[2,320,128]{2,1,0:T(8,128)(2,1)S(1)}, bf16[2,320,128]{2,1,0:T(8,128)(2,1)S(1)}, u32[]{:S(2)}, u32[]{:S(2)}) collective-permute-start(bf16[2,320,128]{2,1,0:T(8,128)(2,1)S(1)} %get-tuple-element.244.refs_3_.refs_4_), channel_id=1, source_target_pairs={{0,16},{8,24},{16,0},{24,8},{1,17},{9,25},{17,1},{25,9},{2,18},{10... | collective-permute-start | bytes 491528 | tf_op jit(solution)/shard_map/ppermute | solution.py:436
  6.9 8.5 %collective-permute-start.8 = (bf16[2,320,128]{2,1,0:T(8,128)(2,1)S(1)}, bf16[2,320,128]{2,1,0:T(8,128)(2,1)S(1)}, u32[]{:S(2)}, u32[]{:S(2)}) collective-permute-start(bf16[2,320,128]{2,1,0:T(8,128)(2,1)S(1)} %get-tuple-element.245.refs_1_), channel_id=1, source_target_pairs={{0,8},{8,0},{16,24},{24,16},{1,9},{9,1},{17,25},{25,17},{2,10},{10... | collective-permute-start | bytes 491528 | tf_op jit(solution)/shard_map/ppermute | solution.py:436
  12.1 7.0 %collective-permute-start.4 = (bf16[2,320,128]{2,1,0:T(8,128)(2,1)S(1)}, bf16[2,320,128]{2,1,0:T(8,128)(2,1)S(1)}, u32[]{:S(2)}, u32[]{:S(2)}) collective-permute-start(bf16[2,320,128]{2,1,0:T(8,128)(2,1)S(1)} %get-tuple-element.131), channel_id=1, source_target_pairs={{0,16},{8,24},{16,0},{24,8},{1,17},{9,25},{17,1},{25,9},{2,18},{10... | collective-permute-start | bytes 491528 | tf_op jit(solution)/shard_map/ppermute | solution.py:436
  12.1 6.9 %collective-permute-start.5 = (bf16[2,320,128]{2,1,0:T(8,128)(2,1)S(1)}, bf16[2,320,128]{2,1,0:T(8,128)(2,1)S(1)}, u32[]{:S(2)}, u32[]{:S(2)}) collective-permute-start(bf16[2,320,128]{2,1,0:T(8,128)(2,1)S(1)} %get-tuple-element.132), channel_id=1, source_target_pairs={{0,8},{8,0},{16,24},{24,16},{1,9},{9,1},{17,25},{25,17},{2,10},{10... | collective-permute-start | bytes 491528 | tf_op jit(solution)/shard_map/ppermute | solution.py:436
  15.6 15.7 %copy-start = (bf16[384,256]{1,0:T(8,128)(2,1)S(1)}, bf16[384,256]{1,0:T(8,128)(2,1)}, u32[]{:S(2)}) copy-start(bf16[384,256]{1,0:T(8,128)(2,1)} %constant.2.clone.matrix_ref.refs_3_) | copy-start | bytes 589828
  15.6 9.0 %collective-permute-start.10 = (bf16[2,320,128]{2,1,0:T(8,128)(2,1)S(1)}, bf16[2,320,128]{2,1,0:T(8,128)(2,1)S(1)}, u32[]{:S(2)}, u32[]{:S(2)}) collective-permute-start(bf16[2,320,128]{2,1,0:T(8,128)(2,1)S(1)} %get-tuple-element.136), channel_id=1, source_target_pairs={{0,16},{8,24},{16,0},{24,8},{1,17},{9,25},{17,1},{25,9},{2,18},{10... | collective-permute-start | bytes 491528 | tf_op jit(solution)/shard_map/ppermute | solution.py:436
  19.3 13.2 %copy-start.1 = (f32[1,4,320,128]{3,2,1,0:T(8,128)S(1)}, f32[1,4,320,128]{3,2,1,0:T(8,128)}, u32[]{:S(2)}) copy-start(f32[1,4,320,128]{3,2,1,0:T(8,128)} %param.16) | copy-start | bytes 1966084
  19.3 14.8 %collective-permute-start.6 = (bf16[4,320,128]{2,1,0:T(8,128)(2,1)S(1)}, bf16[4,320,128]{2,1,0:T(8,128)(2,1)S(1)}, u32[]{:S(2)}, u32[]{:S(2)}) collective-permute-start(bf16[4,320,128]{2,1,0:T(8,128)(2,1)S(1)} %get-tuple-element.133.den_ref.refs_6_), channel_id=1, source_target_pairs={{0,1},{1,0},{2,3},{3,2},{4,5},{5,4},{6,7},{7,6},{8,9},{9,8},{10,11... | collective-permute-start | bytes 983048 | tf_op jit(solution)/shard_map/ppermute | solution.py:441
  19.4 15.1 %collective-permute-start.3 = (bf16[4,320,128]{2,1,0:T(8,128)(2,1)S(1)}, bf16[4,320,128]{2,1,0:T(8,128)(2,1)S(1)}, u32[]{:S(2)}, u32[]{:S(2)}) collective-permute-start(bf16[4,320,128]{2,1,0:T(8,128)(2,1)S(1)} %get-tuple-element.125), channel_id=1, source_target_pairs={{1,2},{2,1},{3,4},{4,3},{5,6},{6,5},{0,7},{7,0},{9,10},{10,9},{11,... | collective-permute-start | bytes 983048 | tf_op jit(solution)/shard_map/ppermute | solution.py:455
  23.1 11.4 %collective-permute-start.2 = (bf16[4,320,128]{2,1,0:T(8,128)(2,1)S(1)}, bf16[4,320,128]{2,1,0:T(8,128)(2,1)S(1)}, u32[]{:S(2)}, u32[]{:S(2)}) collective-permute-start(bf16[4,320,128]{2,1,0:T(8,128)(2,1)S(1)} %get-tuple-element.125), channel_id=1, source_target_pairs={{0,1},{1,0},{2,3},{3,2},{4,5},{5,4},{6,7},{7,6},{8,9},{9,8},{10,11... | collective-permute-start | bytes 983048 | tf_op jit(solution)/shard_map/ppermute | solution.py:441
  23.1 6.6 %collective-permute-start.11 = (bf16[2,320,128]{2,1,0:T(8,128)(2,1)S(1)}, bf16[2,320,128]{2,1,0:T(8,128)(2,1)S(1)}, u32[]{:S(2)}, u32[]{:S(2)}) collective-permute-start(bf16[2,320,128]{2,1,0:T(8,128)(2,1)S(1)} %get-tuple-element.137), channel_id=1, source_target_pairs={{0,8},{8,0},{16,24},{24,16},{1,9},{9,1},{17,25},{25,17},{2,10},{10... | collective-permute-start | bytes 491528 | tf_op jit(solution)/shard_map/ppermute | solution.py:436
  24.6 9.5 %collective-permute-start.12 = (bf16[4,160,128]{2,1,0:T(8,128)(2,1)S(1)}, bf16[4,160,128]{2,1,0:T(8,128)(2,1)S(1)}, u32[]{:S(2)}, u32[]{:S(2)}) collective-permute-start(bf16[4,160,128]{2,1,0:T(8,128)(2,1)S(1)} %get-tuple-element.138), channel_id=1, source_target_pairs={{1,2},{2,1},{3,4},{4,3},{5,6},{6,5},{0,8},{7,15},{9,10},{10,9},{11... | collective-permute-start | bytes 491528 | tf_op jit(solution)/shard_map/ppermute | solution.py:455
  29.7 5.4 %collective-permute-start.7 = (bf16[4,160,128]{2,1,0:T(8,128)(2,1)S(1)}, bf16[4,160,128]{2,1,0:T(8,128)(2,1)S(1)}, u32[]{:S(2)}, u32[]{:S(2)}) collective-permute-start(bf16[4,160,128]{2,1,0:T(8,128)(2,1)S(1)} %get-tuple-element.135), channel_id=1, source_target_pairs={{1,2},{2,1},{3,4},{4,3},{5,6},{6,5},{0,8},{7,15},{9,10},{10,9},{11... | collective-permute-start | bytes 491528 | tf_op jit(solution)/shard_map/ppermute | solution.py:455
  36.0 5.5 %collective-permute-start.13 = (bf16[4,320,128]{2,1,0:T(8,128)(2,1)S(1)}, bf16[4,320,128]{2,1,0:T(8,128)(2,1)S(1)}, u32[]{:S(2)}, u32[]{:S(2)}) collective-permute-start(bf16[4,320,128]{2,1,0:T(8,128)(2,1)S(1)} %get-tuple-element.152), channel_id=1, source_target_pairs={{0,1},{1,0},{2,3},{3,2},{4,5},{5,4},{6,7},{7,6},{8,9},{9,8},{10,11... | collective-permute-start | bytes 983048 | tf_op jit(solution)/shard_map/ppermute | solution.py:441
  36.1 5.4 %collective-permute-start.15 = (bf16[4,160,128]{2,1,0:T(8,128)(2,1)S(1)}, bf16[4,160,128]{2,1,0:T(8,128)(2,1)S(1)}, u32[]{:S(2)}, u32[]{:S(2)}) collective-permute-start(bf16[4,160,128]{2,1,0:T(8,128)(2,1)S(1)} %get-tuple-element.155), channel_id=1, source_target_pairs={{1,2},{2,1},{3,4},{4,3},{5,6},{6,5},{0,8},{7,15},{9,10},{10,9},{11... | collective-permute-start | bytes 491528 | tf_op jit(solution)/shard_map/ppermute | solution.py:455
  37.6 5.6 %collective-permute-start.14 = (bf16[4,160,128]{2,1,0:T(8,128)(2,1)S(1)}, bf16[4,160,128]{2,1,0:T(8,128)(2,1)S(1)}, u32[]{:S(2)}, u32[]{:S(2)}) collective-permute-start(bf16[4,160,128]{2,1,0:T(8,128)(2,1)S(1)} %get-tuple-element.153), channel_id=1, source_target_pairs={{1,2},{2,1},{3,4},{4,3},{5,6},{6,5},{0,8},{7,15},{9,10},{10,9},{11... | collective-permute-start | bytes 491528 | tf_op jit(solution)/shard_map/ppermute | solution.py:455
  43.7 5.5 %collective-permute-start.16 = (bf16[4,320,128]{2,1,0:T(8,128)(2,1)S(1)}, bf16[4,320,128]{2,1,0:T(8,128)(2,1)S(1)}, u32[]{:S(2)}, u32[]{:S(2)}) collective-permute-start(bf16[4,320,128]{2,1,0:T(8,128)(2,1)S(1)} %get-tuple-element.161), channel_id=1, source_target_pairs={{0,1},{1,0},{2,3},{3,2},{4,5},{5,4},{6,7},{7,6},{8,9},{9,8},{10,11... | collective-permute-start | bytes 983048 | tf_op jit(solution)/shard_map/ppermute | solution.py:441
  43.9 5.3 %collective-permute-start.18 = (bf16[4,160,128]{2,1,0:T(8,128)(2,1)S(1)}, bf16[4,160,128]{2,1,0:T(8,128)(2,1)S(1)}, u32[]{:S(2)}, u32[]{:S(2)}) collective-permute-start(bf16[4,160,128]{2,1,0:T(8,128)(2,1)S(1)} %get-tuple-element.164), channel_id=1, source_target_pairs={{1,2},{2,1},{3,4},{4,3},{5,6},{6,5},{0,8},{7,15},{9,10},{10,9},{11... | collective-permute-start | bytes 491528 | tf_op jit(solution)/shard_map/ppermute | solution.py:455
  45.3 5.6 %collective-permute-start.17 = (bf16[4,160,128]{2,1,0:T(8,128)(2,1)S(1)}, bf16[4,160,128]{2,1,0:T(8,128)(2,1)S(1)}, u32[]{:S(2)}, u32[]{:S(2)}) collective-permute-start(bf16[4,160,128]{2,1,0:T(8,128)(2,1)S(1)} %get-tuple-element.162), channel_id=1, source_target_pairs={{1,2},{2,1},{3,4},{4,3},{5,6},{6,5},{0,8},{7,15},{9,10},{10,9},{11... | collective-permute-start | bytes 491528 | tf_op jit(solution)/shard_map/ppermute | solution.py:455
  51.0 3.2 %copy-start.4 = (f32[1,4,320,128]{3,2,1,0:T(8,128)S(1)}, f32[1,4,320,128]{3,2,1,0:T(8,128)}, u32[]{:S(2)}) copy-start(f32[1,4,320,128]{3,2,1,0:T(8,128)} %param.17) | copy-start | bytes 1966084
  51.5 2.2 %copy-start.7 = (s32[1,512]{1,0:T(1,128)S(1)}, s32[1,512]{1,0:T(1,128)}, u32[]{:S(2)}) copy-start(s32[1,512]{1,0:T(1,128)} %rec.1) | copy-start | bytes 6148
  51.5 5.5 %collective-permute-start.19 = (bf16[4,320,128]{2,1,0:T(8,128)(2,1)S(1)}, bf16[4,320,128]{2,1,0:T(8,128)(2,1)S(1)}, u32[]{:S(2)}, u32[]{:S(2)}) collective-permute-start(bf16[4,320,128]{2,1,0:T(8,128)(2,1)S(1)} %get-tuple-element.170), channel_id=1, source_target_pairs={{0,1},{1,0},{2,3},{3,2},{4,5},{5,4},{6,7},{7,6},{8,9},{9,8},{10,11... | collective-permute-start | bytes 983048 | tf_op jit(solution)/shard_map/ppermute | solution.py:441
  51.7 5.3 %collective-permute-start.21 = (bf16[4,160,128]{2,1,0:T(8,128)(2,1)S(1)}, bf16[4,160,128]{2,1,0:T(8,128)(2,1)S(1)}, u32[]{:S(2)}, u32[]{:S(2)}) collective-permute-start(bf16[4,160,128]{2,1,0:T(8,128)(2,1)S(1)} %get-tuple-element.173), channel_id=1, source_target_pairs={{1,2},{2,1},{3,4},{4,3},{5,6},{6,5},{0,8},{7,15},{9,10},{10,9},{11... | collective-permute-start | bytes 491528 | tf_op jit(solution)/shard_map/ppermute | solution.py:455
  53.1 5.6 %collective-permute-start.20 = (bf16[4,160,128]{2,1,0:T(8,128)(2,1)S(1)}, bf16[4,160,128]{2,1,0:T(8,128)(2,1)S(1)}, u32[]{:S(2)}, u32[]{:S(2)}) collective-permute-start(bf16[4,160,128]{2,1,0:T(8,128)(2,1)S(1)} %get-tuple-element.171), channel_id=1, source_target_pairs={{1,2},{2,1},{3,4},{4,3},{5,6},{6,5},{0,8},{7,15},{9,10},{10,9},{11... | collective-permute-start | bytes 491528 | tf_op jit(solution)/shard_map/ppermute | solution.py:455
  61.0 5.5 %collective-permute-start.22 = (bf16[4,320,128]{2,1,0:T(8,128)(2,1)S(1)}, bf16[4,320,128]{2,1,0:T(8,128)(2,1)S(1)}, u32[]{:S(2)}, u32[]{:S(2)}) collective-permute-start(bf16[4,320,128]{2,1,0:T(8,128)(2,1)S(1)} %get-tuple-element.179), channel_id=1, source_target_pairs={{0,1},{1,0},{2,3},{3,2},{4,5},{5,4},{6,7},{7,6},{8,9},{9,8},{10,11... | collective-permute-start | bytes 983048 | tf_op jit(solution)/shard_map/ppermute | solution.py:441
  61.1 5.4 %collective-permute-start.24 = (bf16[4,160,128]{2,1,0:T(8,128)(2,1)S(1)}, bf16[4,160,128]{2,1,0:T(8,128)(2,1)S(1)}, u32[]{:S(2)}, u32[]{:S(2)}) collective-permute-start(bf16[4,160,128]{2,1,0:T(8,128)(2,1)S(1)} %get-tuple-element.188), channel_id=1, source_target_pairs={{1,2},{2,1},{3,4},{4,3},{5,6},{6,5},{0,8},{7,15},{9,10},{10,9},{11... | collective-permute-start | bytes 491528 | tf_op jit(solution)/shard_map/ppermute | solution.py:455
  62.6 5.6 %collective-permute-start.23 = (bf16[4,160,128]{2,1,0:T(8,128)(2,1)S(1)}, bf16[4,160,128]{2,1,0:T(8,128)(2,1)S(1)}, u32[]{:S(2)}, u32[]{:S(2)}) collective-permute-start(bf16[4,160,128]{2,1,0:T(8,128)(2,1)S(1)} %get-tuple-element.180), channel_id=1, source_target_pairs={{1,2},{2,1},{3,4},{4,3},{5,6},{6,5},{0,8},{7,15},{9,10},{10,9},{11... | collective-permute-start | bytes 491528 | tf_op jit(solution)/shard_map/ppermute | solution.py:455
  68.8 5.5 %collective-permute-start.25 = (bf16[4,320,128]{2,1,0:T(8,128)(2,1)S(1)}, bf16[4,320,128]{2,1,0:T(8,128)(2,1)S(1)}, u32[]{:S(2)}, u32[]{:S(2)}) collective-permute-start(bf16[4,320,128]{2,1,0:T(8,128)(2,1)S(1)} %get-tuple-element.194), channel_id=1, source_target_pairs={{0,1},{1,0},{2,3},{3,2},{4,5},{5,4},{6,7},{7,6},{8,9},{9,8},{10,11... | collective-permute-start | bytes 983048 | tf_op jit(solution)/shard_map/ppermute | solution.py:441
  68.9 5.3 %collective-permute-start.27 = (bf16[4,160,128]{2,1,0:T(8,128)(2,1)S(1)}, bf16[4,160,128]{2,1,0:T(8,128)(2,1)S(1)}, u32[]{:S(2)}, u32[]{:S(2)}) collective-permute-start(bf16[4,160,128]{2,1,0:T(8,128)(2,1)S(1)} %get-tuple-element.205), channel_id=1, source_target_pairs={{1,2},{2,1},{3,4},{4,3},{5,6},{6,5},{0,8},{7,15},{9,10},{10,9},{11... | collective-permute-start | bytes 491528 | tf_op jit(solution)/shard_map/ppermute | solution.py:455
  70.3 5.7 %collective-permute-start.26 = (bf16[4,160,128]{2,1,0:T(8,128)(2,1)S(1)}, bf16[4,160,128]{2,1,0:T(8,128)(2,1)S(1)}, u32[]{:S(2)}, u32[]{:S(2)}) collective-permute-start(bf16[4,160,128]{2,1,0:T(8,128)(2,1)S(1)} %get-tuple-element.195), channel_id=1, source_target_pairs={{1,2},{2,1},{3,4},{4,3},{5,6},{6,5},{0,8},{7,15},{9,10},{10,9},{11... | collective-permute-start | bytes 491528 | tf_op jit(solution)/shard_map/ppermute | solution.py:455
  76.6 5.5 %collective-permute-start.28 = (bf16[4,320,128]{2,1,0:T(8,128)(2,1)S(1)}, bf16[4,320,128]{2,1,0:T(8,128)(2,1)S(1)}, u32[]{:S(2)}, u32[]{:S(2)}) collective-permute-start(bf16[4,320,128]{2,1,0:T(8,128)(2,1)S(1)} %get-tuple-element.211), channel_id=1, source_target_pairs={{0,1},{1,0},{2,3},{3,2},{4,5},{5,4},{6,7},{7,6},{8,9},{9,8},{10,11... | collective-permute-start | bytes 983048 | tf_op jit(solution)/shard_map/ppermute | solution.py:441
  76.7 5.3 %collective-permute-start.29 = (bf16[4,160,128]{2,1,0:T(8,128)(2,1)S(1)}, bf16[4,160,128]{2,1,0:T(8,128)(2,1)S(1)}, u32[]{:S(2)}, u32[]{:S(2)}) collective-permute-start(bf16[4,160,128]{2,1,0:T(8,128)(2,1)S(1)} %get-tuple-element.212), channel_id=1, source_target_pairs={{1,2},{2,1},{3,4},{4,3},{5,6},{6,5},{0,8},{7,15},{9,10},{10,9},{11... | collective-permute-start | bytes 491528 | tf_op jit(solution)/shard_map/ppermute | solution.py:455
  78.1 5.7 %collective-permute-start.32 = (bf16[4,160,128]{2,1,0:T(8,128)(2,1)S(1)}, bf16[4,160,128]{2,1,0:T(8,128)(2,1)S(1)}, u32[]{:S(2)}, u32[]{:S(2)}) collective-permute-start(bf16[4,160,128]{2,1,0:T(8,128)(2,1)S(1)} %get-tuple-element.227), channel_id=1, source_target_pairs={{1,2},{2,1},{3,4},{4,3},{5,6},{6,5},{0,8},{7,15},{9,10},{10,9},{11... | collective-permute-start | bytes 491528 | tf_op jit(solution)/shard_map/ppermute | solution.py:455
  84.4 10.3 %collective-permute-start.35 = (bf16[4,320,128]{2,1,0:T(8,128)(2,1)S(1)}, bf16[4,320,128]{2,1,0:T(8,128)(2,1)S(1)}, u32[]{:S(2)}, u32[]{:S(2)}) collective-permute-start(bf16[4,320,128]{2,1,0:T(8,128)(2,1)S(1)} %get-tuple-element.235), channel_id=1, source_target_pairs={{0,1},{1,0},{2,3},{3,2},{4,5},{5,4},{6,7},{7,6},{8,9},{9,8},{10,11... | collective-permute-start | bytes 983048 | tf_op jit(solution)/shard_map/ppermute | solution.py:441
  84.6 6.5 %collective-permute-start.33 = (bf16[4,160,128]{2,1,0:T(8,128)(2,1)S(1)}, bf16[4,160,128]{2,1,0:T(8,128)(2,1)S(1)}, u32[]{:S(2)}, u32[]{:S(2)}) collective-permute-start(bf16[4,160,128]{2,1,0:T(8,128)(2,1)S(1)} %get-tuple-element.231.refs_1_), channel_id=1, source_target_pairs={{0,16},{8,24},{16,0},{24,8},{1,17},{9,25},{17,1},{25,9},{2,18},{10... | collective-permute-start | bytes 491528 | tf_op jit(solution)/shard_map/ppermute | solution.py:436
  85.2 8.8 %collective-permute-start.30 = (bf16[4,160,128]{2,1,0:T(8,128)(2,1)S(1)}, bf16[4,160,128]{2,1,0:T(8,128)(2,1)S(1)}, u32[]{:S(2)}, u32[]{:S(2)}) collective-permute-start(bf16[4,160,128]{2,1,0:T(8,128)(2,1)S(1)} %get-tuple-element.224.refs_1_), channel_id=1, source_target_pairs={{0,8},{8,0},{16,24},{24,16},{1,9},{9,1},{17,25},{25,17},{2,10},{10... | collective-permute-start | bytes 491528 | tf_op jit(solution)/shard_map/ppermute | solution.py:436
  86.5 8.2 %collective-permute-start.36 = (bf16[4,160,128]{2,1,0:T(8,128)(2,1)S(1)}, bf16[4,160,128]{2,1,0:T(8,128)(2,1)S(1)}, u32[]{:S(2)}, u32[]{:S(2)}) collective-permute-start(bf16[4,160,128]{2,1,0:T(8,128)(2,1)S(1)} %get-tuple-element.236), channel_id=1, source_target_pairs={{1,2},{2,1},{3,4},{4,3},{5,6},{6,5},{0,8},{7,15},{9,10},{10,9},{11... | collective-permute-start | bytes 491528 | tf_op jit(solution)/shard_map/ppermute | solution.py:455
  87.2 9.1 %collective-permute-start.39 = (bf16[4,160,128]{2,1,0:T(8,128)(2,1)S(1)}, bf16[4,160,128]{2,1,0:T(8,128)(2,1)S(1)}, u32[]{:S(2)}, u32[]{:S(2)}) collective-permute-start(bf16[4,160,128]{2,1,0:T(8,128)(2,1)S(1)} %get-tuple-element.241), channel_id=1, source_target_pairs={{1,2},{2,1},{3,4},{4,3},{5,6},{6,5},{0,8},{7,15},{9,10},{10,9},{11... | collective-permute-start | bytes 491528 | tf_op jit(solution)/shard_map/ppermute | solution.py:455
  91.3 8.6 %collective-permute-start.34 = (bf16[4,160,128]{2,1,0:T(8,128)(2,1)S(1)}, bf16[4,160,128]{2,1,0:T(8,128)(2,1)S(1)}, u32[]{:S(2)}, u32[]{:S(2)}) collective-permute-start(bf16[4,160,128]{2,1,0:T(8,128)(2,1)S(1)} %get-tuple-element.233), channel_id=1, source_target_pairs={{0,8},{8,0},{16,24},{24,16},{1,9},{9,1},{17,25},{25,17},{2,10},{10... | collective-permute-start | bytes 491528 | tf_op jit(solution)/shard_map/ppermute | solution.py:436
  94.2 9.4 %collective-permute-start.31 = (bf16[4,160,128]{2,1,0:T(8,128)(2,1)S(1)}, bf16[4,160,128]{2,1,0:T(8,128)(2,1)S(1)}, u32[]{:S(2)}, u32[]{:S(2)}) collective-permute-start(bf16[4,160,128]{2,1,0:T(8,128)(2,1)S(1)} %get-tuple-element.226), channel_id=1, source_target_pairs={{0,16},{8,24},{16,0},{24,8},{1,17},{9,25},{17,1},{25,9},{2,18},{10... | collective-permute-start | bytes 491528 | tf_op jit(solution)/shard_map/ppermute | solution.py:436
  95.1 6.8 %collective-permute-start.37 = (bf16[4,160,128]{2,1,0:T(8,128)(2,1)S(1)}, bf16[4,160,128]{2,1,0:T(8,128)(2,1)S(1)}, u32[]{:S(2)}, u32[]{:S(2)}) collective-permute-start(bf16[4,160,128]{2,1,0:T(8,128)(2,1)S(1)} %shard_map.151.refs_1_), channel_id=1, source_target_pairs={{0,8},{8,0},{16,24},{24,16},{1,9},{9,1},{17,25},{25,17},{2,10},{10... | collective-permute-start | bytes 491528 | tf_op jit(solution)/shard_map/ppermute | solution.py:436
  96.7 7.8 %collective-permute-start.40 = (bf16[4,160,128]{2,1,0:T(8,128)(2,1)S(1)}, bf16[4,160,128]{2,1,0:T(8,128)(2,1)S(1)}, u32[]{:S(2)}, u32[]{:S(2)}) collective-permute-start(bf16[4,160,128]{2,1,0:T(8,128)(2,1)S(1)} %shard_map.153.refs_1_), channel_id=1, source_target_pairs={{0,16},{8,24},{16,0},{24,8},{1,17},{9,25},{17,1},{25,9},{2,18},{10... | collective-permute-start | bytes 491528 | tf_op jit(solution)/shard_map/ppermute | solution.py:436
  102.1 5.4 %collective-permute-start.38 = (bf16[4,160,128]{2,1,0:T(8,128)(2,1)S(1)}, bf16[4,160,128]{2,1,0:T(8,128)(2,1)S(1)}, u32[]{:S(2)}, u32[]{:S(2)}) collective-permute-start(bf16[4,160,128]{2,1,0:T(8,128)(2,1)S(1)} %get-tuple-element.240), channel_id=1, source_target_pairs={{0,16},{8,24},{16,0},{24,8},{1,17},{9,25},{17,1},{25,9},{2,18},{10... | collective-permute-start | bytes 491528 | tf_op jit(solution)/shard_map/ppermute | solution.py:436
  104.7 5.4 %collective-permute-start.41 = (bf16[4,160,128]{2,1,0:T(8,128)(2,1)S(1)}, bf16[4,160,128]{2,1,0:T(8,128)(2,1)S(1)}, u32[]{:S(2)}, u32[]{:S(2)}) collective-permute-start(bf16[4,160,128]{2,1,0:T(8,128)(2,1)S(1)} %get-tuple-element.243), channel_id=1, source_target_pairs={{0,8},{8,0},{16,24},{24,16},{1,9},{9,1},{17,25},{25,17},{2,10},{10... | collective-permute-start | bytes 491528 | tf_op jit(solution)/shard_map/ppermute | solution.py:436
  (3 other events, 3.0 us)
